TPU v7x, 32 devices: a whole 2x2x4 slice. The times are simulated.
32 devices in a mesh: slab: 8 (over z, y), sub: 4 (over x, core).
Axes of the slice: x: 2, y: 2, z: 4, core: 2. Of those that a mesh axis runs over, the one named last changes fastest.
Arguments:
- fine_blocks: float32 [64, 64, 64, 64], P('slab', 'sub')
- prolong: float32 [64, 64, 64], P('slab')
- smoother: float32 [64, 64, 64], P('slab')
- right_side: float32 [64, 64, 512], P('slab'), may hold values from -6 to 6
- agg_of: int32 [64], replicated, may hold values from 0 to 3, as said below
- col_slot: int32 [64, 64], P('slab', 'sub'), may hold values from 0 to 23, as said below
- send_rows: int32 [8, 4, 2, 8], replicated, may hold values from 0 to 7, as said below
- send_count: int32 [8, 4, 2], replicated, may hold values from 0 to 8, as said below
Outputs:
- coarse_op: float32 [32, 12, 64, 64], P('slab', 'sub')
- solution: float32 [64, 64, 512], P('slab', None, 'sub')
Inputs may be any that keep to these rules, and one draw needn't show every extreme that they name: `agg_of`: each entry is an aggregate of the block row's own slab, numbered within the slab; every aggregate of every slab holds at least one block row. `send_rows`: each list (slab s, sub index k, direction d) holds distinct block rows of slab s numbered within the slab; direction 0 goes to slab s - 1, direction 1 to slab s + 1; only the first send_count entries are live. `send_count`: the first slab sends nothing down and the last nothing up; some list is 8 long. `col_slot`: every slot named is live; block 0 of each row names the row's own block row; some block names the last slot from each neighbour.
All inputs are finite; a program needn't handle non-finite values.
Results may differ from a plain program's by a relative error of at most 0.0003.
Values sent between devices are 32-bit elements; how exact they have to be, the bound alone decides.
No kernel may reach another device: no remote copies, remote signals or barrier semaphores. Data moves between devices by JAX's collectives and lax.ppermute only.
A program may use at most 128 MiB of HBM per device.

v0:
```python
import jax
import jax.numpy as jnp
from jax import lax
from jax.sharding import PartitionSpec as P

COARSE_SWEEPS = 3


highest = lax.Precision.HIGHEST
coarse_weight = 0.25


def passed_along(value, axis, steps):
    count = lax.axis_size(axis)
    first, last = (max(0, -steps), min(count, count - steps))
    return lax.ppermute(value, axis, [(source, source + steps) for source in range(first, last)])


def padded(array, sides, width):
    for axis, dim in sides:
        size, length = (lax.axis_size(axis), array.shape[dim])
        up = [(i, (i + 1) % size) for i in range(size - 1)]
        down = [(j, i) for i, j in up]
        last = lax.slice_in_dim(array, length - width, length, axis=dim)
        first = lax.slice_in_dim(array, 0, width, axis=dim)
        before = lax.ppermute(last, axis, up)
        after = lax.ppermute(first, axis, down)
        array = jnp.concatenate([before, array, after], axis=dim)
    return array


def own_lists(send_rows, send_count):
    slab_pos = lax.axis_index("slab")
    sub_pos = lax.axis_index("sub")
    return (send_rows[slab_pos, sub_pos], send_count[slab_pos, sub_pos])


def with_ghosts(values, picks, counts):
    places = jnp.arange(picks.shape[1], dtype=jnp.int32)
    keep_mask = (places[None, :] < counts[:, None]).astype(values.dtype)
    packed = values[picks] * keep_mask[:, :, None, None]
    from_lower = passed_along(packed[1], "slab", 1)
    from_upper = passed_along(packed[0], "slab", -1)
    return jnp.concatenate([values, from_lower, from_upper], axis=0)


def slot_maps(agg_of, send_rows, row_count, group_count):
    slab_pos = lax.axis_index("slab")
    sub_pos = lax.axis_index("sub")
    slab_total = lax.axis_size("slab")
    slab_below = jnp.maximum(slab_pos - 1, 0)
    slab_above = jnp.minimum(slab_pos + 1, slab_total - 1)
    own_rows = slab_pos * row_count + jnp.arange(row_count, dtype=jnp.int32)
    lower_rows = slab_below * row_count + send_rows[slab_below, sub_pos, 1]
    upper_rows = slab_above * row_count + send_rows[slab_above, sub_pos, 0]
    own_groups = agg_of[own_rows]
    band_table = jnp.concatenate(
        [own_groups + group_count, agg_of[lower_rows], agg_of[upper_rows] + 2 * group_count]
    )
    return (own_groups, band_table)


def image_part(fine_blocks, field_rows, col_slot):

    def add_block(block_index, running):
        block_now = lax.dynamic_index_in_dim(fine_blocks, block_index, 1, keepdims=False)
        slot_ids = lax.dynamic_index_in_dim(col_slot, block_index, 1, keepdims=False)
        return running + jnp.einsum(
            "eab,ebn->ean", block_now, field_rows[slot_ids], precision=highest
        )

    zero_init = jnp.zeros(
        (fine_blocks.shape[0], fine_blocks.shape[2], field_rows.shape[2]), jnp.float32
    )
    return lax.fori_loop(0, fine_blocks.shape[1], add_block, zero_init)


def summed_rows(partial_image):
    return lax.psum(partial_image, "sub")


def coarse_apply(coarse_full, correction):
    widened = padded(correction, (("slab", 0),), correction.shape[0])
    return jnp.einsum("aqxy,qyn->axn", coarse_full, widened, precision=highest)


def coarse_cycle(coarse_full, prolong, row_hot, weight, residual):
    coarse_rhs = jnp.einsum("ea,edc,edn->acn", row_hot, prolong, residual, precision=highest)
    correction = weight * coarse_rhs
    for sweep_index in range(COARSE_SWEEPS - 1):
        correction = correction + weight * (coarse_rhs - coarse_apply(coarse_full, correction))
    return jnp.einsum("ea,edc,acn->edn", row_hot, prolong, correction, precision=highest)


def per_device(fine_blocks, prolong, smoother, right_side, agg_of, col_slot, send_rows, send_count):
    row_count = prolong.shape[0]
    group_count = row_count // 2
    sub_pos = lax.axis_index("sub")
    sub_total = lax.axis_size("sub")
    picks, counts = own_lists(send_rows, send_count)
    own_groups, band_table = slot_maps(agg_of, send_rows, row_count, group_count)
    prolong_wide = with_ghosts(prolong, picks, counts)
    picked = prolong_wide[col_slot]
    products = jnp.einsum("ejab,ejbc->ejac", fine_blocks, picked, precision=highest)
    term_blocks = jnp.einsum("eba,ejbc->ejac", prolong, products, precision=highest)
    row_hot = (own_groups[:, None] == jnp.arange(group_count, dtype=jnp.int32)[None, :]).astype(
        jnp.float32
    )
    col_hot = (
        band_table[col_slot][:, :, None]
        == jnp.arange(3 * group_count, dtype=jnp.int32)[None, None, :]
    ).astype(jnp.float32)
    coarse_part = jnp.einsum("ea,ejq,ejxy->aqxy", row_hot, col_hot, term_blocks, precision=highest)
    coarse_full = lax.psum(coarse_part, "sub")
    band_share = 3 * group_count // sub_total
    coarse_op = lax.dynamic_slice_in_dim(coarse_full, sub_pos * band_share, band_share, 1)
    weight = (coarse_weight / jnp.sum(row_hot, axis=0))[:, None, None]
    x_first = jnp.einsum("eab,ebn->ean", smoother, right_side, precision=highest)
    image_first = image_part(fine_blocks, with_ghosts(x_first, picks, counts), col_slot)
    column_share = right_side.shape[2] // sub_total
    residual = right_side - summed_rows(image_first)
    x_second = x_first + coarse_cycle(coarse_full, prolong, row_hot, weight, residual)
    image_next = summed_rows(
        image_part(fine_blocks, with_ghosts(x_second, picks, counts), col_slot)
    )
    x_third = x_second + jnp.einsum(
        "eab,ebn->ean", smoother, right_side - image_next, precision=highest
    )
    solution = lax.dynamic_slice_in_dim(x_third, sub_pos * column_share, column_share, 2)
    return (coarse_op, solution)


def solution(mesh):
    placed = (
        P("slab", "sub", None, None),
        P("slab", None, None),
        P("slab", None, None),
        P("slab", None, None),
        P(),
        P("slab", "sub"),
        P(),
        P(),
    )
    return jax.shard_map(
        per_device,
        mesh=mesh,
        in_specs=placed,
        out_specs=(P("slab", "sub", None, None), P("slab", None, "sub")),
        check_vma=False,
    )
```

profile of v0, /device:TPU:8, one launch (start us, length us, event | category | flops | bytes accessed | tf_op | source)
XLA Modules:
  0.0 473.9 jit_solution(11319103451945792552)
XLA Ops:
  11.5 3.3 collective-permute-start.1
  14.8 2.5 collective-permute-start
  21.0 4.2 collective-permute-start.3
  31.5 4.8 %copy.18 = f32[8,16,64,64]{3,2,0,1:T(8,128)} copy(f32[8,16,64,64]{3,2,1,0:T(8,128)} %param.12) | data formatting | bytes 4194304
  36.3 13.6 %collective-permute-done = f32[8,64,64]{2,1,0:T(8,128)} collective-permute-done((f32[8,64,64]{2,1,0:T(8,128)}, f32[8,64,64]{2,1,0:T(8,128)}, u32[]{:S(2)}, u32[]{:S(2)}) %collective-permute-start) | collective-permute-done | bytes 131104 | tf_op jit(solution)/shard_map/ppermute | solution.py:16
  51.0 2.8 gather_fusion.3
  53.8 9.4 %fusion.67 = f32[8,16,64,64]{3,2,1,0:T(8,128)S(1)} fusion(f32[8,16,64,64]{3,2,1,0:T(8,128)} %bitcast.127, f32[8,16,64,64]{3,2,1,0:T(8,128)} %param.12), kind=kOutput, calls=%fused_computation.113 | convolution fusion | flops 402653184 | bytes 6291456 | tf_op jit(solution)/shard_map/ejab,ejbc->ejac/dot_general | solution.py:104
  63.2 5.2 %fusion.12 = f32[8,16,64,64]{2,3,1,0:T(8,128)} fusion(f32[8,16,64,64]{3,2,1,0:T(8,128)S(1)} %fusion.67, f32[8,64,64]{2,1,0:T(8,128)S(1)} %copy-done.7), kind=kOutput, calls=%fused_computation.30 | convolution fusion | flops 402653184 | bytes 4325376 | tf_op jit(solution)/shard_map/eba,ejbc->ejac/dot_general | solution.py:105
  68.4 5.6 %copy.27 = f32[8,16,64,64]{3,1,2,0:T(8,128)} copy(f32[8,16,64,64]{2,3,1,0:T(8,128)} %fusion.12) | data formatting | bytes 4194304 | tf_op jit(solution)/shard_map/eba,ejbc->ejac/transpose | solution.py:105
  74.1 4.4 fusion.46
  78.5 4.5 fusion.20
  83.0 3.8 pad_maximum_fusion
  86.7 74.7 %while.28 = (s32[]{:T(128)}, f32[8,64,512]{2,1,0:T(8,128)S(1)}, f32[8,16,64,64]{3,2,0,1:T(8,128)}, s32[8,16]{0,1:T(8,128)S(1)}, f32[24,64,512]{2,1,0:T(8,128)}, /*index=5*/s32[]{:T(128)}, s32[]{:T(128)}) while((s32[]{:T(128)}, f32[8,64,512]{2,1,0:T(8,128)S(1)}, f32[8,16,64,64]{3,2,0,1:T(8,128)}, s32[8,16]{0,1:T(8,128)S(1)}, ...), condition=%wide.region_3.4_spmd.clone, body=%wide.region_2.3_spmd.clone.sunk | while | flops 201851936 | bytes 5509351 | solution.py:75
  86.8 2.5 gather_fusion
  91.4 2.5 gather_fusion
  96.1 2.5 gather_fusion
  100.8 2.5 gather_fusion
  105.5 2.5 gather_fusion
  110.1 2.5 gather_fusion
  114.8 2.5 gather_fusion
  117.3 2.1 convolution_add_fusion.4
  119.5 2.5 gather_fusion
  124.1 2.5 gather_fusion
  128.8 2.5 gather_fusion
  133.5 2.5 gather_fusion
  138.2 2.5 gather_fusion
  140.7 2.1 convolution_add_fusion.4
  142.8 2.5 gather_fusion
  147.5 2.5 gather_fusion
  152.2 2.5 gather_fusion
  156.9 2.5 gather_fusion
  159.4 2.1 convolution_add_fusion.4
  162.7 61.2 %all-reduce.6.cloned.1.call-done = (f32[4,12,64,64]{3,0,1,2:T(4,128)}, f32[8,64,512]{2,1,0:T(8,128)}) async-done(((f32[4,12,64,64]{3,0,1,2:T(4,128)}, f32[8,64,512]{2,1,0:T(8,128)}), (f32[4,12,64,64]{3,0,1,2:T(4,128)}, f32[8,64,512]{2,1,0:T(8,128)})) %all-reduce.6.cloned.1.call-update) | async-done | bytes 1835024 | tf_op jit(solution)/shard_map/psum | solution.py:114
  223.9 2.3 fusion.34
  227.4 3.5 collective-permute-start.5
  230.9 2.7 collective-permute-start.4
  233.6 20.6 %collective-permute-done.5 = f32[4,64,512]{2,0,1:T(4,128)S(1)} collective-permute-done((f32[4,64,512]{2,0,1:T(4,128)S(1)}, f32[4,64,512]{2,0,1:T(4,128)S(1)}, u32[]{:S(2)}, u32[]{:S(2)}) %collective-permute-start.5) | collective-permute-done | bytes 524320 | tf_op jit(solution)/shard_map/ppermute | solution.py:27
  254.6 2.9 fusion.26
  258.0 4.3 collective-permute-start.7
  264.2 21.4 %collective-permute-done.7 = f32[4,64,512]{2,0,1:T(4,128)S(1)} collective-permute-done((f32[4,64,512]{2,0,1:T(4,128)S(1)}, f32[4,64,512]{2,0,1:T(4,128)S(1)}, u32[]{:S(2)}, u32[]{:S(2)}) %collective-permute-start.7) | collective-permute-done | bytes 524320 | tf_op jit(solution)/shard_map/ppermute | solution.py:27
  286.1 2.9 fusion.17
  297.2 4.3 collective-permute-start.9
  301.6 2.2 collective-permute-start.8
  303.8 43.9 %collective-permute-done.9 = f32[8,64,512]{2,1,0:T(8,128)} collective-permute-done((f32[8,64,512]{2,1,0:T(8,128)}, f32[8,64,512]{2,1,0:T(8,128)}, u32[]{:S(2)}, u32[]{:S(2)}) %collective-permute-start.9) | collective-permute-done | bytes 1048608 | tf_op jit(solution)/shard_map/ppermute | solution.py:16
  347.8 3.8 pad_maximum_fusion.1
  351.5 74.7 %while.29 = (s32[]{:T(128)}, f32[8,64,512]{2,1,0:T(8,128)S(1)}, f32[8,16,64,64]{3,2,0,1:T(8,128)}, s32[8,16]{0,1:T(8,128)S(1)}, f32[24,64,512]{2,1,0:T(8,128)}, /*index=5*/s32[]{:T(128)}, s32[]{:T(128)}) while((s32[]{:T(128)}, f32[8,64,512]{2,1,0:T(8,128)S(1)}, f32[8,16,64,64]{3,2,0,1:T(8,128)}, s32[8,16]{0,1:T(8,128)S(1)}, ...), condition=%wide.region_6.7_spmd.clone, body=%wide.region_5.6_spmd.clone.sunk | while | flops 201851936 | bytes 5509351 | solution.py:75
  351.6 2.5 gather_fusion.1
  356.2 2.5 gather_fusion.1
  360.9 2.5 gather_fusion.1
  365.6 2.5 gather_fusion.1
  370.2 2.5 gather_fusion.1
  374.9 2.5 gather_fusion.1
  379.6 2.5 gather_fusion.1
  384.3 2.5 gather_fusion.1
  388.9 2.5 gather_fusion.1
  393.6 2.5 gather_fusion.1
  398.3 2.5 gather_fusion.1
  403.0 2.5 gather_fusion.1
  407.6 2.5 gather_fusion.1
  412.3 2.5 gather_fusion.1
  417.0 2.5 gather_fusion.1
  421.7 2.5 gather_fusion.1
  429.1 34.8 %all-reduce.4.cloned.1.call-done = f32[8,64,512]{2,1,0:T(8,128)} async-done(((f32[8,64,512]{2,1,0:T(8,128)}), f32[8,64,512]{2,1,0:T(8,128)}) %all-reduce.4.cloned.1.call-update) | async-done | bytes 1048592 | tf_op jit(solution)/shard_map/psum | solution.py:79
  464.0 2.3 convolution_bitcast_fusion
  (172 shorter events, 94.1 us)
Async XLA Ops:
  7.2 10.2 %copy-start = (f32[8,64,64]{2,1,0:T(8,128)S(1)}, f32[8,64,64]{2,1,0:T(8,128)}, u32[]{:S(2)}) copy-start(f32[8,64,64]{2,1,0:T(8,128)} %param.14) | copy-start | bytes 393220
  7.2 10.2 %copy-start.4 = (f32[8,64,512]{2,1,0:T(8,128)S(1)}, f32[8,64,512]{2,1,0:T(8,128)}, u32[]{:S(2)}) copy-start(f32[8,64,512]{2,1,0:T(8,128)} %param.15) | copy-start | bytes 3145732
  7.2 216.7 %all-reduce.6.cloned.1.call-start = ((), (), s32[]{:S(2)}) async-start(), calls=%async_computation.1 | async-start | bytes 5242880 | tf_op jit(solution)/shard_map/psum | solution.py:114
  11.5 24.7 %collective-permute-start.1 = (f32[8,64,64]{2,1,0:T(8,128)}, f32[8,64,64]{2,1,0:T(8,128)}, u32[]{:S(2)}, u32[]{:S(2)}) collective-permute-start(f32[8,64,64]{2,1,0:T(8,128)} %get-tuple-element.279), channel_id=1, source_target_pairs={{4,0},{8,4},{12,8},{16,12},{20,16},{24,20},{28,24},{5,1},{9,5},{13... | collective-permute-start | bytes 393224 | tf_op jit(solution)/shard_map/ppermute | solution.py:16
  14.8 35.1 %collective-permute-start = (f32[8,64,64]{2,1,0:T(8,128)}, f32[8,64,64]{2,1,0:T(8,128)}, u32[]{:S(2)}, u32[]{:S(2)}) collective-permute-start(f32[8,64,64]{2,1,0:T(8,128)} %get-tuple-element.278), channel_id=1, source_target_pairs={{0,4},{4,8},{8,12},{12,16},{16,20},{20,24},{24,28},{1,5},{5,9},{9,... | collective-permute-start | bytes 393224 | tf_op jit(solution)/shard_map/ppermute | solution.py:16
  19.4 7.8 %copy-start.10 = (s32[8,16]{1,0:T(8,128)S(1)}, s32[8,16]{1,0:T(8,128)}, u32[]{:S(2)}) copy-start(s32[8,16]{1,0:T(8,128)} %param.17) | copy-start | bytes 1540
  19.4 8.6 %copy-start.1 = (s32[64]{0:T(128)S(1)}, s32[64]{0:T(128)}, u32[]{:S(2)}) copy-start(s32[64]{0:T(128)} %param.16) | copy-start | bytes 772
  21.0 62.0 %collective-permute-start.3 = (f32[8,64,512]{2,1,0:T(8,128)}, f32[8,64,512]{2,1,0:T(8,128)}, u32[]{:S(2)}, u32[]{:S(2)}) collective-permute-start(f32[8,64,512]{2,1,0:T(8,128)} %get-tuple-element.277), channel_id=1, source_target_pairs={{4,0},{8,4},{12,8},{16,12},{20,16},{24,20},{28,24},{5,1},{9,5},{13... | collective-permute-start | bytes 3145736 | tf_op jit(solution)/shard_map/ppermute | solution.py:16
  25.2 57.8 %collective-permute-start.2 = (f32[8,64,512]{2,1,0:T(8,128)}, f32[8,64,512]{2,1,0:T(8,128)}, u32[]{:S(2)}, u32[]{:S(2)}) collective-permute-start(f32[8,64,512]{2,1,0:T(8,128)} %get-tuple-element.276), channel_id=1, source_target_pairs={{0,4},{4,8},{8,12},{12,16},{16,20},{20,24},{24,28},{1,5},{5,9},{9,... | collective-permute-start | bytes 3145736 | tf_op jit(solution)/shard_map/ppermute | solution.py:16
  31.5 18.4 %copy-start.7 = (f32[8,64,64]{2,1,0:T(8,128)S(1)}, f32[8,64,64]{2,1,0:T(8,128)}, u32[]{:S(2)}) copy-start(f32[8,64,64]{2,1,0:T(8,128)} %param.13) | copy-start | bytes 393220
  161.5 1.0 copy-start.2
  161.5 62.4 %copy-start.5 = (f32[8,64,512]{2,1,0:T(8,128)S(1)}, f32[8,64,512]{2,1,0:T(8,128)}, u32[]{:S(2)}) copy-start(f32[8,64,512]{2,1,0:T(8,128)} %param.15) | copy-start | bytes 3145732
  162.5 301.5 %all-reduce.4.cloned.1.call-start = ((), (), s32[]{:S(2)}) async-start(), calls=%async_computation | async-start | bytes 2097152 | tf_op jit(solution)/shard_map/psum | solution.py:79
  227.4 27.2 %copy-start.9 = (f32[4,12,64,64]{3,0,1,2:T(4,128)S(1)}, f32[4,12,64,64]{3,0,1,2:T(4,128)}, u32[]{:S(2)}) copy-start(f32[4,12,64,64]{3,0,1,2:T(4,128)} %get-tuple-element.272) | copy-start | bytes 2359300
  227.4 26.8 %collective-permute-start.5 = (f32[4,64,512]{2,0,1:T(4,128)S(1)}, f32[4,64,512]{2,0,1:T(4,128)S(1)}, u32[]{:S(2)}, u32[]{:S(2)}) collective-permute-start(f32[4,64,512]{2,0,1:T(4,128)S(1)} %get-tuple-element.282), channel_id=1, source_target_pairs={{4,0},{8,4},{12,8},{16,12},{20,16},{24,20},{28,24},{5,1},{9,5},{13... | collective-permute-start | bytes 1572872 | tf_op jit(solution)/shard_map/ppermute | solution.py:27
  230.9 23.3 %collective-permute-start.4 = (f32[4,64,512]{2,0,1:T(4,128)S(1)}, f32[4,64,512]{2,0,1:T(4,128)S(1)}, u32[]{:S(2)}, u32[]{:S(2)}) collective-permute-start(f32[4,64,512]{2,0,1:T(4,128)S(1)} %get-tuple-element.282), channel_id=1, source_target_pairs={{0,4},{4,8},{8,12},{12,16},{16,20},{20,24},{24,28},{1,5},{5,9},{9,... | collective-permute-start | bytes 1572872 | tf_op jit(solution)/shard_map/ppermute | solution.py:26
  258.0 27.6 %collective-permute-start.7 = (f32[4,64,512]{2,0,1:T(4,128)S(1)}, f32[4,64,512]{2,0,1:T(4,128)S(1)}, u32[]{:S(2)}, u32[]{:S(2)}) collective-permute-start(f32[4,64,512]{2,0,1:T(4,128)S(1)} %fusion.42), channel_id=1, source_target_pairs={{4,0},{8,4},{12,8},{16,12},{20,16},{24,20},{28,24},{5,1},{9,5},{13... | collective-permute-start | bytes 1572872 | tf_op jit(solution)/shard_map/ppermute | solution.py:27
  262.2 23.5 %collective-permute-start.6 = (f32[4,64,512]{2,0,1:T(4,128)S(1)}, f32[4,64,512]{2,0,1:T(4,128)S(1)}, u32[]{:S(2)}, u32[]{:S(2)}) collective-permute-start(f32[4,64,512]{2,0,1:T(4,128)S(1)} %fusion.42), channel_id=1, source_target_pairs={{0,4},{4,8},{8,12},{12,16},{16,20},{20,24},{24,28},{1,5},{5,9},{9,... | collective-permute-start | bytes 1572872 | tf_op jit(solution)/shard_map/ppermute | solution.py:26
  289.0 1.3 copy-start.8
  297.2 50.5 %collective-permute-start.9 = (f32[8,64,512]{2,1,0:T(8,128)}, f32[8,64,512]{2,1,0:T(8,128)}, u32[]{:S(2)}, u32[]{:S(2)}) collective-permute-start(f32[8,64,512]{2,1,0:T(8,128)} %get-tuple-element.275), channel_id=1, source_target_pairs={{4,0},{8,4},{12,8},{16,12},{20,16},{24,20},{28,24},{5,1},{9,5},{13... | collective-permute-start | bytes 3145736 | tf_op jit(solution)/shard_map/ppermute | solution.py:16
  301.6 46.2 %collective-permute-start.8 = (f32[8,64,512]{2,1,0:T(8,128)S(1)}, f32[8,64,512]{2,1,0:T(8,128)}, u32[]{:S(2)}, u32[]{:S(2)}) collective-permute-start(f32[8,64,512]{2,1,0:T(8,128)S(1)} %get-tuple-element.274), channel_id=1, source_target_pairs={{0,4},{4,8},{8,12},{12,16},{16,20},{20,24},{24,28},{1,5},{5,9},{9,... | collective-permute-start | bytes 3145736 | tf_op jit(solution)/shard_map/ppermute | solution.py:16
  426.3 1.0 copy-start.3
  426.3 37.7 %copy-start.6 = (f32[8,64,512]{2,1,0:T(8,128)S(1)}, f32[8,64,512]{2,1,0:T(8,128)}, u32[]{:S(2)}) copy-start(f32[8,64,512]{2,1,0:T(8,128)} %param.15) | copy-start | bytes 3145732
Sparse Core Ops, SparseCore 0:
  162.6 61.1 all-reduce.5
  427.4 36.5 all-reduce.3
where the time goes:
time: 478 us; the launch traced here: 474 us
  waiting for transfers between devices  196 us (41%)
  local copies, waits for them, and re-layouts  109 us (23%)
  matrix products  106 us (22%)
  starting transfers between devices  31.1 us (7%)
  other arithmetic  15.2 us (3%)
  between operations  14.5 us (3%)
    gather x32, local copies, waits for them, and re-layouts, add_block(): field_rows[slot_ids]  80.1 us
    dot_general x32, matrix products, add_block(): jnp.einsum('eab,ebn->ean', block_now, field_rows[slot_ids], precision=hig...  67.3 us
    psum x1, waiting for transfers between devices, per_device(): coarse_full = lax.psum(coarse_part, 'sub')  61.2 us
    ppermute x6, waiting for transfers between devices, passed_along(): lax.ppermute(value, axis, [(source, source + steps) for source in range(f...  57.6 us
    ppermute x2, waiting for transfers between devices, padded(): after = lax.ppermute(first, axis, down)  42 us
    psum x1, waiting for transfers between devices, summed_rows(): return lax.psum(partial_image, 'sub')  34.8 us
    ppermute x6, starting transfers between devices, passed_along(): lax.ppermute(value, axis, [(source, source + steps) for source in range(f...  18.6 us
  transfers between devices with their start and end apart: 12, of which 7 were waited for; matrix products, arithmetic and copies ran while one was open for 10% of the time, Pallas kernels for 0%

commit v1 on v0

v1 whole, which is shorter than its diff:
```python
import functools
import jax
import jax.numpy as jnp
from jax import lax
from jax.experimental import pallas as pl
from jax.experimental.pallas import tpu as pltpu
from jax.sharding import PartitionSpec as P

COARSE_SWEEPS = 3
COARSE_WEIGHT = 0.25
F32 = jnp.float32
BF16 = jnp.bfloat16
VMEM = pl.BlockSpec(memory_space=pltpu.VMEM)
SMEM = pl.BlockSpec(memory_space=pltpu.SMEM)
ROWS = 8
GHOSTS = 8
SLOTS = ROWS + 2 * GHOSTS
GROUPS = 4
BANDS = 3 * GROUPS
DOF = 64
COLS = 128

AT_SUB = 0
AT_COL = 8
AT_LIVE = AT_COL + SLOTS
AT_AGG = AT_LIVE + SLOTS


def params(limit=48):
    return pltpu.CompilerParams(vmem_limit_bytes=limit << 20)


def halves(value):
    high = value.astype(BF16)
    return high, (value - high.astype(F32)).astype(BF16)


def mm(a, b):
    return jnp.dot(a, b, preferred_element_type=F32)


def product(left, right):
    left_high, left_low = left
    right_high, right_low = right
    return mm(left_high, right_high) + (mm(left_high, right_low) + mm(left_low, right_high))


def rows_of(index, size=DOF):
    return slice(index * size, (index + 1) * size)


def first_kernel(meta, smoother, right_own, right_other, prolong, x_ref, packed_ref):
    for e in range(ROWS):
        right = jnp.concatenate([right_own[e], right_other[e]], axis=1)
        x_ref[rows_of(e), :] = product(halves(smoother[e]), halves(right))
    for e in range(ROWS // 2):
        packed_ref[rows_of(e), :] = jnp.concatenate([prolong[e], prolong[e + ROWS // 2]], axis=1)


def first_step(meta, smoother, right_side, prolong):
    whole = lambda shape: pl.BlockSpec(shape, lambda i, meta: (0,) * len(shape))
    chunk = (ROWS, DOF, COLS)
    return pl.pallas_call(
        first_kernel,
        grid_spec=pltpu.PrefetchScalarGridSpec(
            num_scalar_prefetch=1,
            grid=(1,),
            in_specs=[
                whole(smoother.shape),
                pl.BlockSpec(chunk, lambda i, meta: (0, 0, meta[AT_SUB])),
                pl.BlockSpec(chunk, lambda i, meta: (0, 0, meta[AT_SUB + 1])),
                whole(prolong.shape),
            ],
            out_specs=[whole((ROWS * DOF, 2 * COLS)), whole((ROWS * DOF // 2, 2 * DOF))],
        ),
        out_shape=[
            jax.ShapeDtypeStruct((ROWS * DOF, 2 * COLS), F32),
            jax.ShapeDtypeStruct((ROWS * DOF // 2, 2 * DOF), F32),
        ],
        compiler_params=params(),
        name="first_step",
    )(meta, smoother, right_side, right_side, prolong)


def build_kernel(meta, col_slot, blocks, d_ref):
    row = pl.program_id(0)
    d_ref[...] = jnp.zeros_like(d_ref)
    upper = lax.broadcasted_iota(jnp.int32, (DOF, 2 * DOF), 1) >= DOF
    for j in range(blocks.shape[1]):
        slot = col_slot[row, j]
        column = meta[AT_COL + slot]
        live = meta[AT_LIVE + slot].astype(F32)
        block = blocks[0, j]
        doubled = jnp.concatenate([block, block], axis=1)
        odd = lax.rem(column, 2)
        lower_scale = jnp.where(odd == 0, live, 0.0)
        upper_scale = jnp.where(odd == 1, live, 0.0)
        placed = doubled * jnp.where(upper, upper_scale, lower_scale)
        lanes = pl.ds(pl.multiple_of(lax.div(column, 2) * 2 * DOF, 2 * DOF), 2 * DOF)
        d_ref[:, lanes] += placed


def build(meta, col_slot, blocks):
    per_row = blocks.shape[1]
    return pl.pallas_call(
        build_kernel,
        grid=(ROWS,),
        in_specs=[SMEM, SMEM, pl.BlockSpec((1, per_row, DOF, DOF), lambda e: (e, 0, 0, 0))],
        out_specs=pl.BlockSpec((DOF, SLOTS * DOF), lambda e: (e, 0)),
        out_shape=jax.ShapeDtypeStruct((ROWS * DOF, SLOTS * DOF), F32),
        compiler_params=params(),
        name="build",
    )(meta, col_slot, blocks)


def galerkin_kernel(
    meta, d_own, d_other, prolong, below, above, high_ref, low_ref, half_ref, rt_high, rt_low, q_high, q_low
):
    step = pl.program_id(0)
    band_start = meta[AT_SUB + 2] * (BANDS // 2)
    upper = lax.broadcasted_iota(jnp.int32, (DOF, 2 * DOF), 1) >= DOF

    @pl.when(step == 0)
    def _():
        for c in range(SLOTS):
            if c < ROWS:
                piece = jnp.concatenate([prolong[c], prolong[c]], axis=1)
            else:
                packed = below if c < 2 * ROWS else above
                r = c % ROWS
                both = packed[rows_of(r % (ROWS // 2)), :]
                piece = both[:, :DOF] if r < ROWS // 2 else both[:, DOF:]
                piece = jnp.concatenate([piece, piece], axis=1)
            region = (GROUPS, 0, 2 * GROUPS)[c // ROWS]
            band = meta[AT_AGG + c] + region - band_start
            for t in range(BANDS // 4):
                lower_scale = jnp.where(band == 2 * t, 1.0, 0.0)
                upper_scale = jnp.where(band == 2 * t + 1, 1.0, 0.0)
                high, low = halves(piece * jnp.where(upper, upper_scale, lower_scale))
                q_high[rows_of(c), rows_of(t, 2 * DOF)] = high
                q_low[rows_of(c), rows_of(t, 2 * DOF)] = low
        restrict_rows = []
        for e in range(ROWS):
            piece = jnp.concatenate([prolong[e], prolong[e]], axis=1)
            group = meta[AT_AGG + e]
            parts = []
            for t in range(GROUPS // 2):
                lower_scale = jnp.where(group == 2 * t, 1.0, 0.0)
                upper_scale = jnp.where(group == 2 * t + 1, 1.0, 0.0)
                parts.append(piece * jnp.where(upper, upper_scale, lower_scale))
            restrict_rows.append(jnp.concatenate(parts, axis=1))
        high, low = halves(jnp.concatenate(restrict_rows, axis=0).T)
        rt_high[...] = high
        rt_low[...] = low

    high, low = halves(d_own[...] + d_other[...])
    high_ref[...] = high
    low_ref[...] = low
    half_ref[...] = product((high, low), (q_high[...], q_low[...]))


def galerkin(meta, d_own, d_other, prolong, below, above):
    rows, wide = d_own.shape
    steps = 2
    half = BANDS // 2 * DOF
    whole = lambda array: pl.BlockSpec(array.shape, lambda i: (0,) * array.ndim)
    part = lambda width: pl.BlockSpec((rows // steps, width), lambda i: (i, 0))
    restrict_shape = (GROUPS * DOF, rows)
    restrict = pl.BlockSpec(restrict_shape, lambda i: (0, 0))
    return pl.pallas_call(
        galerkin_kernel,
        grid=(steps,),
        in_specs=[SMEM, part(wide), part(wide), whole(prolong), whole(below), whole(above)],
        out_specs=[part(wide), part(wide), part(half), restrict, restrict],
        out_shape=[
            jax.ShapeDtypeStruct((rows, wide), BF16),
            jax.ShapeDtypeStruct((rows, wide), BF16),
            jax.ShapeDtypeStruct((rows, half), F32),
            jax.ShapeDtypeStruct(restrict_shape, BF16),
            jax.ShapeDtypeStruct(restrict_shape, BF16),
        ],
        scratch_shapes=[pltpu.VMEM((wide, half), BF16), pltpu.VMEM((wide, half), BF16)],
        compiler_params=params(),
        name="galerkin",
    )(meta, d_own, d_other, prolong, below, above)


def image_kernel(d_high, d_low, own, below, above, keep_ref, send_ref):
    total = None
    for region, field in enumerate((own, below, above)):
        lanes = rows_of(region, ROWS * DOF)
        part = product((d_high[:, lanes], d_low[:, lanes]), halves(field[...]))
        total = part if total is None else total + part
    keep_ref[...] = total[:, :COLS]
    send_ref[...] = total[:, COLS:]


def image(d_high, d_low, own, below, above):
    shape = jax.ShapeDtypeStruct((d_high.shape[0], COLS), F32)
    return pl.pallas_call(
        image_kernel,
        in_specs=[VMEM] * 5,
        out_specs=[VMEM] * 2,
        out_shape=[shape, shape],
        compiler_params=params(),
        name="image",
    )(d_high, d_low, own, below, above)


def scaled_by_weight(meta, value):
    pieces = []
    for a in range(GROUPS):
        members = jnp.zeros((), jnp.int32)
        for e in range(ROWS):
            members += jnp.where(meta[AT_AGG + e] == a, 1, 0)
        piece = value[rows_of(a), :]
        pieces.append(piece * (COARSE_WEIGHT / jnp.full(piece.shape, members.astype(F32))))
    return jnp.concatenate(pieces, axis=0)


def coarse_kernel(meta, rt_high, rt_low, mine, other, g_high, g_low, m_high, m_low, op_ref):
    core = meta[AT_SUB + 2]
    sub = meta[AT_SUB]
    half = mine.shape[1]
    own_value, other_value = mine[...], other[...]
    is_first = core == 0
    left = jnp.where(is_first, own_value, other_value)
    right = jnp.where(is_first, other_value, own_value)
    for position, value in enumerate((left, right)):
        lanes = rows_of(position, half)
        high, low = halves(value)
        g_high[:, lanes] = high
        g_low[:, lanes] = low
        coarse = product((rt_high[...], rt_low[...]), (high, low))
        high, low = halves(scaled_by_weight(meta, coarse))
        m_high[:, lanes] = high
        m_low[:, lanes] = low
        per_half = op_ref.shape[1]
        for place in range(2):

            @pl.when(sub == 2 * position + place)
            def _():
                for a in range(GROUPS):
                    for q in range(per_half):
                        op_ref[a, q] = coarse[rows_of(a), rows_of(place * per_half + q)]


def coarse_operator(meta, rt_high, rt_low, mine, other):
    rows, half = mine.shape
    field = lambda n, t: jax.ShapeDtypeStruct((n, 2 * half), t)
    return pl.pallas_call(
        coarse_kernel,
        in_specs=[SMEM] + [VMEM] * 4,
        out_specs=[VMEM] * 5,
        out_shape=[
            field(rows, BF16),
            field(rows, BF16),
            field(GROUPS * DOF, BF16),
            field(GROUPS * DOF, BF16),
            jax.ShapeDtypeStruct((GROUPS, BANDS // 4, DOF, DOF), F32),
        ],
        compiler_params=params(),
        name="coarse_operator",
    )(meta, rt_high, rt_low, mine, other)


def residual_kernel(meta, right, keep, received, rt_high, rt_low, residual_ref, first_ref):
    residual = right[...].reshape(keep.shape) - (keep[...] + received[...])
    residual_ref[...] = residual
    coarse_rhs = product((rt_high[...], rt_low[...]), halves(residual))
    first_ref[...] = scaled_by_weight(meta, coarse_rhs)


def residual_step(meta, right_side, keep, received, rt_high, rt_low):
    whole = lambda shape: pl.BlockSpec(shape, lambda i, meta: (0,) * len(shape))
    coarse_shape = (rt_high.shape[0], COLS)
    return pl.pallas_call(
        residual_kernel,
        grid_spec=pltpu.PrefetchScalarGridSpec(
            num_scalar_prefetch=1,
            grid=(1,),
            in_specs=[
                pl.BlockSpec((ROWS, DOF, COLS), lambda i, meta: (0, 0, meta[AT_SUB])),
                whole(keep.shape),
                whole(keep.shape),
                whole(rt_high.shape),
                whole(rt_high.shape),
            ],
            out_specs=[whole(keep.shape), whole(coarse_shape)],
        ),
        out_shape=[jax.ShapeDtypeStruct(keep.shape, F32), jax.ShapeDtypeStruct(coarse_shape, F32)],
        compiler_params=params(),
        name="residual_step",
    )(meta, right_side, keep, received, rt_high, rt_low)


def applied(op_high, op_low, below, own, above):
    total = None
    for region, field in enumerate((below, own, above)):
        lanes = rows_of(region, GROUPS * DOF)
        part = product((op_high[:, lanes], op_low[:, lanes]), halves(field[...]))
        total = part if total is None else total + part
    return total


def sweep_kernel(m_high, m_low, first, below, own, above, next_ref):
    next_ref[...] = own[...] + first[...] - applied(m_high, m_low, below, own, above)


def sweep(m_high, m_low, first, below, own, above):
    return pl.pallas_call(
        sweep_kernel,
        in_specs=[VMEM] * 6,
        out_specs=VMEM,
        out_shape=jax.ShapeDtypeStruct(own.shape, F32),
        compiler_params=params(),
        name="sweep",
    )(m_high, m_low, first, below, own, above)


def last_kernel(meta, g_high, g_low, prolong, smoother, x_first, residual, below, own, above, out_ref):
    remaining = residual[...] - applied(g_high, g_low, below, own, above)
    for e in range(ROWS):
        group = meta[AT_AGG + e]
        correction = own[pl.ds(pl.multiple_of(group * DOF, DOF), DOF), :]
        out_ref[e] = (
            x_first[rows_of(e), :COLS]
            + product(halves(prolong[e]), halves(correction))
            + product(halves(smoother[e]), halves(remaining[rows_of(e), :]))
        )


def last_step(meta, g_high, g_low, prolong, smoother, x_first, residual, below, own, above):
    return pl.pallas_call(
        last_kernel,
        in_specs=[SMEM] + [VMEM] * 9,
        out_specs=VMEM,
        out_shape=jax.ShapeDtypeStruct((ROWS, DOF, COLS), F32),
        compiler_params=params(),
        name="last_step",
    )(meta, g_high, g_low, prolong, smoother, x_first, residual, below, own, above)


def from_neighbours(value):
    size = lax.axis_size("slab")
    up = [(i, i + 1) for i in range(size - 1)]
    down = [(i + 1, i) for i in range(size - 1)]
    return lax.ppermute(value, "slab", up), lax.ppermute(value, "slab", down)


def swapped(value, bit):
    size = lax.axis_size("sub")
    return lax.ppermute(value, "sub", [(i, i ^ bit) for i in range(size)])


def scalars(agg_of, send_rows, send_count):
    slab = lax.axis_index("slab")
    sub = lax.axis_index("sub")
    size = lax.axis_size("slab")
    below = jnp.maximum(slab - 1, 0)
    above = jnp.minimum(slab + 1, size - 1)
    own = jnp.arange(ROWS, dtype=jnp.int32)
    places = jnp.arange(GHOSTS, dtype=jnp.int32)
    lower_live = (places < send_count[below, sub, 1]) & (slab > 0)
    upper_live = (places < send_count[above, sub, 0]) & (slab < size - 1)
    rows_at = lambda which: lax.dynamic_slice_in_dim(agg_of, which * ROWS, ROWS)
    head = jnp.stack([sub, sub ^ 2, sub & 1, slab, slab, slab, slab, slab]).astype(jnp.int32)
    return jnp.concatenate(
        [
            head,
            own,
            ROWS + send_rows[below, sub, 1],
            2 * ROWS + send_rows[above, sub, 0],
            jnp.ones((ROWS,), jnp.int32),
            lower_live.astype(jnp.int32),
            upper_live.astype(jnp.int32),
            rows_at(slab),
            rows_at(below),
            rows_at(above),
        ]
    )


def per_device(fine_blocks, prolong, smoother, right_side, agg_of, col_slot, send_rows, send_count):
    meta = scalars(agg_of, send_rows, send_count)
    x_first, packed = first_step(meta, smoother, right_side, prolong)
    packed_below, packed_above = from_neighbours(packed)
    x_below, x_above = from_neighbours(x_first)
    d_own = build(meta, col_slot, fine_blocks)
    d_other = swapped(d_own, 1)
    d_high, d_low, half, rt_high, rt_low = galerkin(meta, d_own, d_other, prolong, packed_below, packed_above)
    half = half + swapped(half, 2)
    g_high, g_low, m_high, m_low, coarse_op = coarse_operator(meta, rt_high, rt_low, half, swapped(half, 1))
    keep, send = image(d_high, d_low, x_first, x_below, x_above)
    residual, first = residual_step(meta, right_side, keep, swapped(send, 2), rt_high, rt_low)
    correction = first
    for _ in range(COARSE_SWEEPS - 1):
        below, above = from_neighbours(correction)
        correction = sweep(m_high, m_low, first, below, correction, above)
    below, above = from_neighbours(correction)
    solution = last_step(meta, g_high, g_low, prolong, smoother, x_first, residual, below, correction, above)
    return coarse_op, solution


def solution(mesh):
    placed = (
        P("slab", "sub", None, None),
        P("slab", None, None),
        P("slab", None, None),
        P("slab", None, None),
        P(),
        P("slab", "sub"),
        P(),
        P(),
    )
    return jax.shard_map(
        per_device,
        mesh=mesh,
        in_specs=placed,
        out_specs=(P("slab", "sub", None, None), P("slab", None, "sub")),
        check_vma=False,
    )
```

time: 478 us -> 108 us (0.23)
  waiting for transfers between devices: 196 us -> 42 us
  matrix products: 106 us -> 0 us
  local copies, waits for them, and re-layouts: 109 us -> 4.74 us
  Pallas kernels: 0 us -> 20.6 us
  between operations: 14.5 us -> 0.86 us
  other arithmetic: 15.2 us -> 2.08 us
  starting transfers between devices: 31.1 us -> 36 us
    dot_general x44 -> x0, matrix products: 106 us -> none  [the longest x32 67.3 us: add_block(): jnp.einsum('eab,ebn->ean', block_now, field_rows[slot_ids], precision=hig...]
    psum x2 -> x0, waiting for transfers between devices: 96 us -> none  [the longest x1 61.2 us: per_device(): coarse_full = lax.psum(coarse_part, 'sub')]
    gather x41 -> x0, local copies, waits for them, and re-layouts: 90.4 us -> none  [the longest x32 80.1 us: add_block(): field_rows[slot_ids]]
    ppermute x10 -> x14, waiting for transfers between devices: 99.8 us -> 42 us  [the longest x10 23.2 us: from_neighbours(): return (lax.ppermute(value, 'slab', up), lax.ppermute(value, 'slab', down))]
    pallas_call x0 -> x9, Pallas kernels: none -> 20.6 us  [the longest x1 5.58 us: build(): pl.pallas_call(build_kernel, grid=(ROWS,), in_specs=[SMEM, SMEM, pl.Block...]
    concatenate x6 -> x0, other arithmetic: 9.45 us -> none  [the longest x3 8.65 us: with_ghosts(): return jnp.concatenate([values, from_lower, from_upper], axis=0)]
    transpose x1 -> x0, local copies, waits for them, and re-layouts: 5.64 us -> none  [per_device(): jnp.einsum('eba,ejbc->ejac', prolong, products, precision=highest)]
    unnamed x25 -> x12, local copies, waits for them, and re-layouts: 7.59 us -> 2.36 us
  transfers between devices with their start and end apart: 12 -> 14, of which waited for: 7 -> 11; matrix products, arithmetic and copies ran while one was open for 10% -> 0% of each run, Pallas kernels for 0% -> 6%
where the time goes in v1:
time: 108 us; the launch traced here: 106 us
  waiting for transfers between devices  42 us (39%)
  starting transfers between devices  36 us (33%)
  Pallas kernels  20.6 us (19%)
  local copies, waits for them, and re-layouts  4.74 us (4%)
  other arithmetic  2.08 us (2%)
    ppermute x10, starting transfers between devices, from_neighbours(): return (lax.ppermute(value, 'slab', up), lax.ppermute(value, 'slab', down))  33.7 us
    ppermute x10, waiting for transfers between devices, from_neighbours(): return (lax.ppermute(value, 'slab', up), lax.ppermute(value, 'slab', down))  23.2 us
    ppermute x4, waiting for transfers between devices, swapped(): return lax.ppermute(value, 'sub', [(i, i ^ bit) for i in range(size)])  18.8 us
    pallas_call x1, Pallas kernels, build(): pl.pallas_call(build_kernel, grid=(ROWS,), in_specs=[SMEM, SMEM, pl.Block...  5.58 us
    pallas_call x1, Pallas kernels, galerkin(): pl.pallas_call(galerkin_kernel, grid=(steps,), in_specs=[SMEM, part(wide)...  5.51 us
    pallas_call x1, Pallas kernels, coarse_operator(): pl.pallas_call(coarse_kernel, in_specs=[SMEM] + [VMEM] * 4, out_specs=[VM...  2.72 us
    pallas_call x1, Pallas kernels, last_step(): pl.pallas_call(last_kernel, in_specs=[SMEM] + [VMEM] * 9, out_specs=VMEM,...  2.59 us
    unnamed x12, local copies, waits for them, and re-layouts  2.36 us
  transfers between devices with their start and end apart: 14, of which 11 were waited for; matrix products, arithmetic and copies ran while one was open for 0% of the time, Pallas kernels for 6%

profile of v1, /device:TPU:8, one launch (start us, length us, event | category | flops | bytes accessed | tf_op | source)
XLA Modules:
  0.0 106.3 jit_solution(14251954527829969923)
XLA Ops:
  0.6 1.4 %constant_dynamic-slice_fusion = (s32[1,1,1]{0,2,1:T(1,128)}, s32[1,1,1]{0,2,1:T(1,128)}) fusion(s32[8,4,2]{0,2,1:T(2,128)} %param.15, s32[]{:T(128)S(6)} %select_n.22, s32[]{:T(128)S(6)} %select_n.10, s32[]{:T(128)S(6)} %max.3), kind=kLoop, calls=%fused_computation.2 | loop fusion | bytes 28 | tf_op jit(solution)/shard_map/dynamic_slice | solution.py:365
  2.1 0.7 fusion.3
  2.8 1.3 %and_convert_fusion = (s32[8]{0:T(128)S(1)}, s32[8]{0:T(128)S(1)}) fusion(pred[]{:T(512)S(6)} %lt.42, s32[]{:T(128)} %bitcast.7, pred[]{:T(512)S(6)} %gt.3, s32[]{:T(128)} %bitcast.6), kind=kLoop, calls=%fused_computation | loop fusion | flops 48 | bytes 74 | tf_op jit(solution)/shard_map/convert_element_type | solution.py:376
  4.1 0.9 fusion.4
  4.9 0.1 concatenate.3.meta
  5.0 0.0 copy-start.4
  5.0 0.7 copy-done.4
  5.7 0.0 copy-start.1
  5.7 0.0 copy-start.2
  5.7 0.0 copy-start.3
  5.7 5.6 %build.1.d_own = f32[512,1536]{1,0:T(8,128)S(1)} custom-call(s32[80]{0:T(128)S(1)} %concatenate.3.meta, s32[8,16]{1,0:T(8,128)S(1)} %copy-done.4, f32[8,16,64,64]{3,2,1,0:T(8,128)} %blocks.1), custom_call_target="tpu_custom_call" | custom-call | tf_op jit(solution)/shard_map/build/pallas_call | solution.py:105
  11.3 0.0 copy-start
  11.3 0.1 collective-permute-start
  11.4 0.0 copy-done.1
  11.4 0.0 copy-done.2
  11.4 0.0 copy-done.3
  11.4 0.9 first_step.1
  12.3 3.4 %collective-permute-start.1 = (f32[256,128]{1,0:T(8,128)S(1)}, f32[256,128]{1,0:T(8,128)S(1)}, u32[]{:S(2)}, u32[]{:S(2)}) collective-permute-start(f32[256,128]{1,0:T(8,128)S(1)} %get-tuple-element.18), channel_id=1, source_target_pairs={{0,4},{4,8},{8,12},{12,16},{16,20},{20,24},{24,28},{1,5},{5,9},{9,... | collective-permute-start | bytes 393224 | tf_op jit(solution)/shard_map/ppermute | solution.py:348
  15.8 3.3 %collective-permute-start.2 = (f32[256,128]{1,0:T(8,128)S(1)}, f32[256,128]{1,0:T(8,128)S(1)}, u32[]{:S(2)}, u32[]{:S(2)}) collective-permute-start(f32[256,128]{1,0:T(8,128)S(1)} %get-tuple-element.18), channel_id=1, source_target_pairs={{4,0},{8,4},{12,8},{16,12},{20,16},{24,20},{28,24},{5,1},{9,5},{13... | collective-permute-start | bytes 393224 | tf_op jit(solution)/shard_map/ppermute | solution.py:348
  19.1 2.0 %collective-permute-done.1.below = f32[256,128]{1,0:T(8,128)S(1)} collective-permute-done((f32[256,128]{1,0:T(8,128)S(1)}, f32[256,128]{1,0:T(8,128)S(1)}, u32[]{:S(2)}, u32[]{:S(2)}) %collective-permute-start.1) | collective-permute-done | bytes 131104 | tf_op jit(solution)/shard_map/ppermute | solution.py:348
  21.1 2.8 %collective-permute-done.2.above = f32[256,128]{1,0:T(8,128)S(1)} collective-permute-done((f32[256,128]{1,0:T(8,128)S(1)}, f32[256,128]{1,0:T(8,128)S(1)}, u32[]{:S(2)}, u32[]{:S(2)}) %collective-permute-start.2) | collective-permute-done | bytes 131104 | tf_op jit(solution)/shard_map/ppermute | solution.py:348
  23.8 0.0 collective-permute-done.d_other
  23.8 0.0 copy-done
  23.8 0.0 copy-start.5
  23.8 1.7 %copy-done.5 = f32[512,1536]{1,0:T(8,128)} copy-done((f32[512,1536]{1,0:T(8,128)}, f32[512,1536]{1,0:T(8,128)S(1)}, u32[]{:S(2)}) %copy-start.5) | copy-done | bytes 3145752
  25.5 5.5 %galerkin.1 = (bf16[512,1536]{1,0:T(8,128)(2,1)S(1)}, bf16[512,1536]{1,0:T(8,128)(2,1)S(1)}, f32[512,384]{1,0:T(8,128)S(1)}, bf16[256,512]{1,0:T(8,128)(2,1)S(1)}, bf16[256,512]{1,0:T(8,128)(2,1)S(1)}) custom-call(s32[80]{0:T(128)S(1)} %concatenate.3.meta, f32[512,1536]{1,0:T(8,128)} %copy-done, f32[512,1536]{1,0:T(8,128)} %copy-done.5, ...), custom_call_target="tpu_custom_call" | custom-call | tf_op jit(solution)/shard_map/galerkin/pallas_call | solution.py:170
  31.0 1.6 %collective-permute-start.3 = (f32[512,384]{1,0:T(8,128)S(1)}, f32[512,384]{1,0:T(8,128)S(1)}, u32[]{:S(2)}, u32[]{:S(2)}) collective-permute-start(f32[512,384]{1,0:T(8,128)S(1)} %get-tuple-element.21), channel_id=1, source_target_pairs={{0,2},{1,3},{2,0},{3,1},{4,6},{5,7},{6,4},{7,5},{8,10},{9,11},{10,... | collective-permute-start | bytes 2359304 | tf_op jit(solution)/shard_map/ppermute | solution.py:353
  32.6 3.8 %collective-permute-start.5 = (f32[512,256]{1,0:T(8,128)S(1)}, f32[512,256]{1,0:T(8,128)S(1)}, u32[]{:S(2)}, u32[]{:S(2)}) collective-permute-start(f32[512,256]{1,0:T(8,128)S(1)} %get-tuple-element.25.own.x_first), channel_id=1, source_target_pairs={{0,4},{4,8},{8,12},{12,16},{16,20},{20,24},{24,28},{1,5},{5,9},{9,... | collective-permute-start | bytes 1572872 | tf_op jit(solution)/shard_map/ppermute | solution.py:348
  36.3 3.0 %collective-permute-start.6 = (f32[512,256]{1,0:T(8,128)S(1)}, f32[512,256]{1,0:T(8,128)S(1)}, u32[]{:S(2)}, u32[]{:S(2)}) collective-permute-start(f32[512,256]{1,0:T(8,128)S(1)} %get-tuple-element.25.own.x_first), channel_id=1, source_target_pairs={{4,0},{8,4},{12,8},{16,12},{20,16},{24,20},{28,24},{5,1},{9,5},{13... | collective-permute-start | bytes 1572872 | tf_op jit(solution)/shard_map/ppermute | solution.py:348
  39.3 11.1 %collective-permute-done.3 = f32[512,384]{1,0:T(8,128)S(1)} collective-permute-done((f32[512,384]{1,0:T(8,128)S(1)}, f32[512,384]{1,0:T(8,128)S(1)}, u32[]{:S(2)}, u32[]{:S(2)}) %collective-permute-start.3) | collective-permute-done | bytes 786464 | tf_op jit(solution)/shard_map/ppermute | solution.py:353
  50.4 0.1 add.50.mine
  50.5 0.1 collective-permute-start.4
  50.6 7.4 %collective-permute-done.5.below = f32[512,256]{1,0:T(8,128)S(1)} collective-permute-done((f32[512,256]{1,0:T(8,128)S(1)}, f32[512,256]{1,0:T(8,128)S(1)}, u32[]{:S(2)}, u32[]{:S(2)}) %collective-permute-start.5) | collective-permute-done | bytes 524320 | tf_op jit(solution)/shard_map/ppermute | solution.py:348
  58.0 2.0 %collective-permute-done.6.above = f32[512,256]{1,0:T(8,128)S(1)} collective-permute-done((f32[512,256]{1,0:T(8,128)S(1)}, f32[512,256]{1,0:T(8,128)S(1)}, u32[]{:S(2)}, u32[]{:S(2)}) %collective-permute-start.6) | collective-permute-done | bytes 524320 | tf_op jit(solution)/shard_map/ppermute | solution.py:348
  60.0 1.4 %image.1 = (f32[512,128]{1,0:T(8,128)S(1)}, f32[512,128]{1,0:T(8,128)S(1)}) custom-call(bf16[512,1536]{1,0:T(8,128)(2,1)S(1)} %get-tuple-element.26.d_high, bf16[512,1536]{1,0:T(8,128)(2,1)S(1)} %get-tuple-element.27.d_low, f32[512,256]{1,0:T(8,128)S(1)} %get-tuple-element.25.own.x_first, f32[512,256]{1,0:T(8,128)S(1)} %collective-permute-done.5.below, ...), custom_call_target="tpu_custom_call" | custom-call | tf_op jit(solution)/shard_map/image/pallas_call | solution.py:200
  61.4 0.6 collective-permute-start.7
  62.0 7.7 %collective-permute-done.7.received = f32[512,128]{1,0:T(8,128)S(1)} collective-permute-done((f32[512,128]{1,0:T(8,128)S(1)}, f32[512,128]{1,0:T(8,128)S(1)}, u32[]{:S(2)}, u32[]{:S(2)}) %collective-permute-start.7) | collective-permute-done | bytes 262176 | tf_op jit(solution)/shard_map/ppermute | solution.py:353
  69.7 0.9 residual_step.1
  70.7 1.9 %collective-permute-start.8 = (f32[256,128]{1,0:T(8,128)S(1)}, f32[256,128]{1,0:T(8,128)S(1)}, u32[]{:S(2)}, u32[]{:S(2)}) collective-permute-start(f32[256,128]{1,0:T(8,128)S(1)} %get-tuple-element.33.first.own), channel_id=1, source_target_pairs={{0,4},{4,8},{8,12},{12,16},{16,20},{20,24},{24,28},{1,5},{5,9},{9,... | collective-permute-start | bytes 393224 | tf_op jit(solution)/shard_map/ppermute | solution.py:348
  72.6 4.8 %collective-permute-start.9 = (f32[256,128]{1,0:T(8,128)S(1)}, f32[256,128]{1,0:T(8,128)S(1)}, u32[]{:S(2)}, u32[]{:S(2)}) collective-permute-start(f32[256,128]{1,0:T(8,128)S(1)} %get-tuple-element.33.first.own), channel_id=1, source_target_pairs={{4,0},{8,4},{12,8},{16,12},{20,16},{24,20},{28,24},{5,1},{9,5},{13... | collective-permute-start | bytes 393224 | tf_op jit(solution)/shard_map/ppermute | solution.py:348
  77.4 0.0 collective-permute-done.4.other
  77.4 2.7 %coarse_operator.1 = (bf16[512,768]{1,0:T(8,128)(2,1)S(1)}, bf16[512,768]{1,0:T(8,128)(2,1)S(1)}, bf16[256,768]{1,0:T(8,128)(2,1)S(1)}, bf16[256,768]{1,0:T(8,128)(2,1)S(1)}, f32[4,3,64,64]{3,2,1,0:T(8,128)}) custom-call(s32[80]{0:T(128)S(1)} %concatenate.3.meta, bf16[256,512]{1,0:T(8,128)(2,1)S(1)} %get-tuple-element.19.rt_high, ...), custom_call_target="tpu_custom_call" | custom-call | tf_op jit(solution)/shard_map/coarse_operator/pallas_call | solution.py:251
  80.2 0.0 collective-permute-done.8.below
  80.2 1.1 %collective-permute-done.9.above = f32[256,128]{1,0:T(8,128)S(1)} collective-permute-done((f32[256,128]{1,0:T(8,128)S(1)}, f32[256,128]{1,0:T(8,128)S(1)}, u32[]{:S(2)}, u32[]{:S(2)}) %collective-permute-start.9) | collective-permute-done | bytes 131104 | tf_op jit(solution)/shard_map/ppermute | solution.py:348
  81.2 0.5 sweep.2.own
  81.7 4.0 %collective-permute-start.10 = (f32[256,128]{1,0:T(8,128)S(1)}, f32[256,128]{1,0:T(8,128)S(1)}, u32[]{:S(2)}, u32[]{:S(2)}) collective-permute-start(f32[256,128]{1,0:T(8,128)S(1)} %sweep.2.own), channel_id=1, source_target_pairs={{0,4},{4,8},{8,12},{12,16},{16,20},{20,24},{24,28},{1,5},{5,9},{9,... | collective-permute-start | bytes 393224 | tf_op jit(solution)/shard_map/ppermute | solution.py:348
  85.8 2.7 %collective-permute-start.11 = (f32[256,128]{1,0:T(8,128)S(1)}, f32[256,128]{1,0:T(8,128)S(1)}, u32[]{:S(2)}, u32[]{:S(2)}) collective-permute-start(f32[256,128]{1,0:T(8,128)S(1)} %sweep.2.own), channel_id=1, source_target_pairs={{4,0},{8,4},{12,8},{16,12},{20,16},{24,20},{28,24},{5,1},{9,5},{13... | collective-permute-start | bytes 393224 | tf_op jit(solution)/shard_map/ppermute | solution.py:348
  88.5 1.1 %collective-permute-done.10.below = f32[256,128]{1,0:T(8,128)S(1)} collective-permute-done((f32[256,128]{1,0:T(8,128)S(1)}, f32[256,128]{1,0:T(8,128)S(1)}, u32[]{:S(2)}, u32[]{:S(2)}) %collective-permute-start.10) | collective-permute-done | bytes 131104 | tf_op jit(solution)/shard_map/ppermute | solution.py:348
  89.6 3.1 %collective-permute-done.11.above = f32[256,128]{1,0:T(8,128)S(1)} collective-permute-done((f32[256,128]{1,0:T(8,128)S(1)}, f32[256,128]{1,0:T(8,128)S(1)}, u32[]{:S(2)}, u32[]{:S(2)}) %collective-permute-start.11) | collective-permute-done | bytes 131104 | tf_op jit(solution)/shard_map/ppermute | solution.py:348
  92.6 0.5 sweep.3.own
  93.1 3.7 %collective-permute-start.12 = (f32[256,128]{1,0:T(8,128)S(1)}, f32[256,128]{1,0:T(8,128)S(1)}, u32[]{:S(2)}, u32[]{:S(2)}) collective-permute-start(f32[256,128]{1,0:T(8,128)S(1)} %sweep.3.own), channel_id=1, source_target_pairs={{0,4},{4,8},{8,12},{12,16},{16,20},{20,24},{24,28},{1,5},{5,9},{9,... | collective-permute-start | bytes 393224 | tf_op jit(solution)/shard_map/ppermute | solution.py:348
  96.8 3.0 %collective-permute-start.13 = (f32[256,128]{1,0:T(8,128)S(1)}, f32[256,128]{1,0:T(8,128)S(1)}, u32[]{:S(2)}, u32[]{:S(2)}) collective-permute-start(f32[256,128]{1,0:T(8,128)S(1)} %sweep.3.own), channel_id=1, source_target_pairs={{4,0},{8,4},{12,8},{16,12},{20,16},{24,20},{28,24},{5,1},{9,5},{13... | collective-permute-start | bytes 393224 | tf_op jit(solution)/shard_map/ppermute | solution.py:348
  99.9 1.1 %collective-permute-done.12.below = f32[256,128]{1,0:T(8,128)S(1)} collective-permute-done((f32[256,128]{1,0:T(8,128)S(1)}, f32[256,128]{1,0:T(8,128)S(1)}, u32[]{:S(2)}, u32[]{:S(2)}) %collective-permute-start.12) | collective-permute-done | bytes 131104 | tf_op jit(solution)/shard_map/ppermute | solution.py:348
  101.0 2.7 %collective-permute-done.13.above = f32[256,128]{1,0:T(8,128)S(1)} collective-permute-done((f32[256,128]{1,0:T(8,128)S(1)}, f32[256,128]{1,0:T(8,128)S(1)}, u32[]{:S(2)}, u32[]{:S(2)}) %collective-permute-start.13) | collective-permute-done | bytes 131104 | tf_op jit(solution)/shard_map/ppermute | solution.py:348
  103.7 2.6 %last_step.1 = f32[8,64,128]{2,1,0:T(8,128)} custom-call(s32[80]{0:T(128)S(1)} %concatenate.3.meta, bf16[512,768]{1,0:T(8,128)(2,1)S(1)} %get-tuple-element.23.g_high, bf16[512,768]{1,0:T(8,128)(2,1)S(1)} %get-tuple-element.24.g_low, f32[8,64,64]{2,1,0:T(8,128)S(1)} %copy-done.2, f32[8,64,64]{2,1,0:T(8,128)S(1)} %copy-done.3, ...), custom_call_target="tpu_custom_call" | custom-call | tf_op jit(solution)/shard_map/last_step/pallas_call | solution.py:334
  (2 shorter events, 0.0 us)
Async XLA Ops:
  5.0 0.7 copy-start.4
  5.7 5.7 %copy-start.1 = (f32[8,64,512]{2,1,0:T(8,128)S(1)}, f32[8,64,512]{2,1,0:T(8,128)}, u32[]{:S(2)}) copy-start(f32[8,64,512]{2,1,0:T(8,128)} %right.1) | copy-start | bytes 3145732
  5.7 5.7 %copy-start.2 = (f32[8,64,64]{2,1,0:T(8,128)S(1)}, f32[8,64,64]{2,1,0:T(8,128)}, u32[]{:S(2)}) copy-start(f32[8,64,64]{2,1,0:T(8,128)} %prolong.5) | copy-start | bytes 393220
  5.7 5.7 %copy-start.3 = (f32[8,64,64]{2,1,0:T(8,128)S(1)}, f32[8,64,64]{2,1,0:T(8,128)}, u32[]{:S(2)}) copy-start(f32[8,64,64]{2,1,0:T(8,128)} %smoother.3) | copy-start | bytes 393220
  11.3 12.5 %copy-start = (f32[512,1536]{1,0:T(8,128)}, f32[512,1536]{1,0:T(8,128)S(1)}, u32[]{:S(2)}) copy-start(f32[512,1536]{1,0:T(8,128)S(1)} %build.1.d_own) | copy-start | bytes 9437188
  11.3 12.5 %collective-permute-start = (f32[512,1536]{1,0:T(8,128)S(1)}, f32[512,1536]{1,0:T(8,128)S(1)}, u32[]{:S(2)}, u32[]{:S(2)}) collective-permute-start(f32[512,1536]{1,0:T(8,128)S(1)} %build.1.d_own), channel_id=1, source_target_pairs={{0,1},{1,0},{2,3},{3,2},{4,5},{5,4},{6,7},{7,6},{8,9},{9,8},{10,11... | collective-permute-start | bytes 9437192 | tf_op jit(solution)/shard_map/ppermute | solution.py:353
  12.3 8.7 %collective-permute-start.1 = (f32[256,128]{1,0:T(8,128)S(1)}, f32[256,128]{1,0:T(8,128)S(1)}, u32[]{:S(2)}, u32[]{:S(2)}) collective-permute-start(f32[256,128]{1,0:T(8,128)S(1)} %get-tuple-element.18), channel_id=1, source_target_pairs={{0,4},{4,8},{8,12},{12,16},{16,20},{20,24},{24,28},{1,5},{5,9},{9,... | collective-permute-start | bytes 393224 | tf_op jit(solution)/shard_map/ppermute | solution.py:348
  15.8 8.0 %collective-permute-start.2 = (f32[256,128]{1,0:T(8,128)S(1)}, f32[256,128]{1,0:T(8,128)S(1)}, u32[]{:S(2)}, u32[]{:S(2)}) collective-permute-start(f32[256,128]{1,0:T(8,128)S(1)} %get-tuple-element.18), channel_id=1, source_target_pairs={{4,0},{8,4},{12,8},{16,12},{20,16},{24,20},{28,24},{5,1},{9,5},{13... | collective-permute-start | bytes 393224 | tf_op jit(solution)/shard_map/ppermute | solution.py:348
  23.8 1.7 %copy-start.5 = (f32[512,1536]{1,0:T(8,128)}, f32[512,1536]{1,0:T(8,128)S(1)}, u32[]{:S(2)}) copy-start(f32[512,1536]{1,0:T(8,128)S(1)} %collective-permute-done.d_other) | copy-start | bytes 9437188
  31.0 19.4 %collective-permute-start.3 = (f32[512,384]{1,0:T(8,128)S(1)}, f32[512,384]{1,0:T(8,128)S(1)}, u32[]{:S(2)}, u32[]{:S(2)}) collective-permute-start(f32[512,384]{1,0:T(8,128)S(1)} %get-tuple-element.21), channel_id=1, source_target_pairs={{0,2},{1,3},{2,0},{3,1},{4,6},{5,7},{6,4},{7,5},{8,10},{9,11},{10,... | collective-permute-start | bytes 2359304 | tf_op jit(solution)/shard_map/ppermute | solution.py:353
  32.6 25.4 %collective-permute-start.5 = (f32[512,256]{1,0:T(8,128)S(1)}, f32[512,256]{1,0:T(8,128)S(1)}, u32[]{:S(2)}, u32[]{:S(2)}) collective-permute-start(f32[512,256]{1,0:T(8,128)S(1)} %get-tuple-element.25.own.x_first), channel_id=1, source_target_pairs={{0,4},{4,8},{8,12},{12,16},{16,20},{20,24},{24,28},{1,5},{5,9},{9,... | collective-permute-start | bytes 1572872 | tf_op jit(solution)/shard_map/ppermute | solution.py:348
  36.3 23.7 %collective-permute-start.6 = (f32[512,256]{1,0:T(8,128)S(1)}, f32[512,256]{1,0:T(8,128)S(1)}, u32[]{:S(2)}, u32[]{:S(2)}) collective-permute-start(f32[512,256]{1,0:T(8,128)S(1)} %get-tuple-element.25.own.x_first), channel_id=1, source_target_pairs={{4,0},{8,4},{12,8},{16,12},{20,16},{24,20},{28,24},{5,1},{9,5},{13... | collective-permute-start | bytes 1572872 | tf_op jit(solution)/shard_map/ppermute | solution.py:348
  50.5 26.9 %collective-permute-start.4 = (f32[512,384]{1,0:T(8,128)S(1)}, f32[512,384]{1,0:T(8,128)S(1)}, u32[]{:S(2)}, u32[]{:S(2)}) collective-permute-start(f32[512,384]{1,0:T(8,128)S(1)} %add.50.mine), channel_id=1, source_target_pairs={{0,1},{1,0},{2,3},{3,2},{4,5},{5,4},{6,7},{7,6},{8,9},{9,8},{10,11... | collective-permute-start | bytes 2359304 | tf_op jit(solution)/shard_map/ppermute | solution.py:353
  61.4 8.3 %collective-permute-start.7 = (f32[512,128]{1,0:T(8,128)S(1)}, f32[512,128]{1,0:T(8,128)S(1)}, u32[]{:S(2)}, u32[]{:S(2)}) collective-permute-start(f32[512,128]{1,0:T(8,128)S(1)} %get-tuple-element.29), channel_id=1, source_target_pairs={{0,2},{1,3},{2,0},{3,1},{4,6},{5,7},{6,4},{7,5},{8,10},{9,11},{10,... | collective-permute-start | bytes 786440 | tf_op jit(solution)/shard_map/ppermute | solution.py:353
  70.7 9.5 %collective-permute-start.8 = (f32[256,128]{1,0:T(8,128)S(1)}, f32[256,128]{1,0:T(8,128)S(1)}, u32[]{:S(2)}, u32[]{:S(2)}) collective-permute-start(f32[256,128]{1,0:T(8,128)S(1)} %get-tuple-element.33.first.own), channel_id=1, source_target_pairs={{0,4},{4,8},{8,12},{12,16},{16,20},{20,24},{24,28},{1,5},{5,9},{9,... | collective-permute-start | bytes 393224 | tf_op jit(solution)/shard_map/ppermute | solution.py:348
  72.6 8.6 %collective-permute-start.9 = (f32[256,128]{1,0:T(8,128)S(1)}, f32[256,128]{1,0:T(8,128)S(1)}, u32[]{:S(2)}, u32[]{:S(2)}) collective-permute-start(f32[256,128]{1,0:T(8,128)S(1)} %get-tuple-element.33.first.own), channel_id=1, source_target_pairs={{4,0},{8,4},{12,8},{16,12},{20,16},{24,20},{28,24},{5,1},{9,5},{13... | collective-permute-start | bytes 393224 | tf_op jit(solution)/shard_map/ppermute | solution.py:348
  81.7 7.9 %collective-permute-start.10 = (f32[256,128]{1,0:T(8,128)S(1)}, f32[256,128]{1,0:T(8,128)S(1)}, u32[]{:S(2)}, u32[]{:S(2)}) collective-permute-start(f32[256,128]{1,0:T(8,128)S(1)} %sweep.2.own), channel_id=1, source_target_pairs={{0,4},{4,8},{8,12},{12,16},{16,20},{20,24},{24,28},{1,5},{5,9},{9,... | collective-permute-start | bytes 393224 | tf_op jit(solution)/shard_map/ppermute | solution.py:348
  85.8 6.9 %collective-permute-start.11 = (f32[256,128]{1,0:T(8,128)S(1)}, f32[256,128]{1,0:T(8,128)S(1)}, u32[]{:S(2)}, u32[]{:S(2)}) collective-permute-start(f32[256,128]{1,0:T(8,128)S(1)} %sweep.2.own), channel_id=1, source_target_pairs={{4,0},{8,4},{12,8},{16,12},{20,16},{24,20},{28,24},{5,1},{9,5},{13... | collective-permute-start | bytes 393224 | tf_op jit(solution)/shard_map/ppermute | solution.py:348
  93.1 7.9 %collective-permute-start.12 = (f32[256,128]{1,0:T(8,128)S(1)}, f32[256,128]{1,0:T(8,128)S(1)}, u32[]{:S(2)}, u32[]{:S(2)}) collective-permute-start(f32[256,128]{1,0:T(8,128)S(1)} %sweep.3.own), channel_id=1, source_target_pairs={{0,4},{4,8},{8,12},{12,16},{16,20},{20,24},{24,28},{1,5},{5,9},{9,... | collective-permute-start | bytes 393224 | tf_op jit(solution)/shard_map/ppermute | solution.py:348
  96.8 6.9 %collective-permute-start.13 = (f32[256,128]{1,0:T(8,128)S(1)}, f32[256,128]{1,0:T(8,128)S(1)}, u32[]{:S(2)}, u32[]{:S(2)}) collective-permute-start(f32[256,128]{1,0:T(8,128)S(1)} %sweep.3.own), channel_id=1, source_target_pairs={{4,0},{8,4},{12,8},{16,12},{20,16},{24,20},{28,24},{5,1},{9,5},{13... | collective-permute-start | bytes 393224 | tf_op jit(solution)/shard_map/ppermute | solution.py:348

commit v2 on v0

v2 whole, which is shorter than its diff:
```python
import functools
import jax
import jax.numpy as jnp
from jax import lax
from jax.experimental import pallas as pl
from jax.experimental.pallas import tpu as pltpu
from jax.sharding import PartitionSpec as P

COARSE_SWEEPS = 3
COARSE_WEIGHT = 0.25
F32 = jnp.float32
BF16 = jnp.bfloat16
VMEM = pl.BlockSpec(memory_space=pltpu.VMEM)
SMEM = pl.BlockSpec(memory_space=pltpu.SMEM)
ANY = pl.BlockSpec(memory_space=pl.ANY)
ROWS = 8
GHOSTS = 8
SLOTS = ROWS + 2 * GHOSTS
GROUPS = 4
BANDS = 3 * GROUPS
DOF = 64
COLS = 128
SUBS = 4


def params(limit=48):
    return pltpu.CompilerParams(vmem_limit_bytes=limit << 20)


def halves(value):
    high = value.astype(BF16)
    return high, (value - high.astype(F32)).astype(BF16)


def mm(a, b):
    return jnp.dot(a, b, preferred_element_type=F32)


def product(left, right):
    left_high, left_low = left
    right_high, right_low = right
    return mm(left_high, right_high) + (mm(left_high, right_low) + mm(left_low, right_high))


def rows_of(index, size=DOF):
    return slice(index * size, (index + 1) * size)


def place_of(slab, size):
    odd = slab & 1
    near = jnp.minimum(slab ^ 1, size - 1)
    far = jnp.where(odd == 1, jnp.minimum(slab + 1, size - 1), jnp.maximum(slab - 1, 0))
    return odd, near, far


def here():
    slab = lax.axis_index("slab")
    return slab, lax.axis_size("slab"), lax.axis_index("sub")


def start_kernel(
    col_slot, rows_hbm, counts_hbm, blocks, smoother, right_side, prolong,
    d_ref, x_ref, packed_ref, rows, counts, sems, *parts
):
    step = pl.program_id(0)
    slab, size, sub = here()
    below = jnp.maximum(slab - 1, 0)
    above = jnp.minimum(slab + 1, size - 1)

    @pl.when(step == 0)
    def _():
        copies = [
            pltpu.make_async_copy(rows_hbm.at[below, sub], rows.at[0], sems.at[0]),
            pltpu.make_async_copy(rows_hbm.at[above, sub], rows.at[1], sems.at[1]),
            pltpu.make_async_copy(counts_hbm.at[below], counts.at[0], sems.at[2]),
            pltpu.make_async_copy(counts_hbm.at[above], counts.at[1], sems.at[3]),
        ]
        for copy in copies:
            copy.start()
        start = (sub & 1) * (ROWS // 2)
        packed_ref[...] = jnp.concatenate([prolong[start + i] for i in range(ROWS // 2)], axis=1)
        for copy in copies:
            copy.wait()

    own = pl.ds(pl.multiple_of(sub * COLS, COLS), COLS)
    other = pl.ds(pl.multiple_of((sub ^ 2) * COLS, COLS), COLS)
    for e in range(len(parts)):
        right = jnp.concatenate([right_side[e, :, own], right_side[e, :, other]], axis=1)
        x_ref[rows_of(e), :] = product(halves(smoother[e]), halves(right))
    lower_count = jnp.where(slab > 0, counts[0, sub, 1], 0)
    upper_count = jnp.where(slab < size - 1, counts[1, sub, 0], 0)
    odd = slab & 1
    lower_start = (2 - odd) * ROWS
    upper_start = (1 + odd) * ROWS
    upper_lanes = lax.broadcasted_iota(jnp.int32, (DOF, 2 * DOF), 1) >= DOF
    for part in parts:
        part[...] = jnp.zeros_like(part)
    for j in range(blocks.shape[1]):
        for position, part in enumerate(parts):
            slot = col_slot[step * len(parts) + position, j]
            ghost = jnp.maximum(slot - ROWS, 0)
            is_own = slot < ROWS
            is_upper = slot >= ROWS + GHOSTS
            side = jnp.where(is_upper, 1, 0)
            at = jnp.where(is_upper, ghost - GHOSTS, ghost)
            at = jnp.where(is_own, 0, at)
            listed = rows[side, 1 - side, at] + jnp.where(is_upper, upper_start, lower_start)
            column = jnp.where(is_own, slot, listed)
            count = jnp.where(is_upper, upper_count, lower_count)
            live = jnp.where(is_own | (at < count), 1.0, 0.0)
            block = blocks[position, j]
            doubled = jnp.concatenate([block, block], axis=1)
            odd_column = column & 1
            lower_scale = jnp.where(odd_column == 0, live, 0.0)
            upper_scale = jnp.where(odd_column == 1, live, 0.0)
            placed = doubled * jnp.where(upper_lanes, upper_scale, lower_scale)
            lanes = pl.ds(pl.multiple_of((column >> 1) * 2 * DOF, 2 * DOF), 2 * DOF)
            part[:, lanes] += placed
    for position, part in enumerate(parts):
        d_ref[rows_of(position), :] = part[...]


def start_step(col_slot, send_rows, send_count, blocks, smoother, right_side, prolong):
    per_row, columns = blocks.shape[1], right_side.shape[2]
    at_once = 4
    by_rows = lambda *shape: pl.BlockSpec((at_once,) + shape, lambda e: (e,) + (0,) * len(shape))
    return pl.pallas_call(
        start_kernel,
        grid=(ROWS // at_once,),
        in_specs=[
            SMEM,
            ANY,
            ANY,
            by_rows(per_row, DOF, DOF),
            by_rows(DOF, DOF),
            by_rows(DOF, columns),
            pl.BlockSpec(prolong.shape, lambda e: (0, 0, 0)),
        ],
        out_specs=[
            pl.BlockSpec((at_once * DOF, SLOTS * DOF), lambda e: (e, 0)),
            pl.BlockSpec((at_once * DOF, 2 * COLS), lambda e: (e, 0)),
            pl.BlockSpec((DOF, 2 * COLS), lambda e: (0, 0)),
        ],
        out_shape=[
            jax.ShapeDtypeStruct((ROWS * DOF, SLOTS * DOF), F32),
            jax.ShapeDtypeStruct((ROWS * DOF, 2 * COLS), F32),
            jax.ShapeDtypeStruct((DOF, 2 * COLS), F32),
        ],
        scratch_shapes=[
            pltpu.SMEM((2, 2, GHOSTS), jnp.int32),
            pltpu.SMEM((2, SUBS, 2), jnp.int32),
            pltpu.SemaphoreType.DMA((4,)),
        ]
        + [pltpu.VMEM((DOF, SLOTS * DOF), F32)] * at_once,
        compiler_params=params(),
        name="start_step",
    )(col_slot, send_rows, send_count, blocks, smoother, right_side, prolong)


def placed_pairs(piece, index, count):
    upper = lax.broadcasted_iota(jnp.int32, (DOF, 2 * DOF), 1) >= DOF
    doubled = jnp.concatenate([piece, piece], axis=1)
    for t in range(count):
        lower_scale = jnp.where(index == 2 * t, 1.0, 0.0)
        upper_scale = jnp.where(index == 2 * t + 1, 1.0, 0.0)
        yield t, doubled * jnp.where(upper, upper_scale, lower_scale)


def own_kernel(
    agg_of, d_own, d_other, prolong, own, high_ref, low_ref, half_ref, image_ref, rt_high, rt_low, q_high, q_low
):
    step = pl.program_id(0)
    slab, size, sub = here()
    band_start = (sub & 1) * (BANDS // 2)

    @pl.when(step == 0)
    def _():
        restrict_rows = []
        for e in range(ROWS):
            group = agg_of[slab * ROWS + e]
            for t, value in placed_pairs(prolong[e], group + GROUPS - band_start, BANDS // 4):
                high, low = halves(value)
                q_high[rows_of(e), rows_of(t, 2 * DOF)] = high
                q_low[rows_of(e), rows_of(t, 2 * DOF)] = low
            parts = [value for _, value in placed_pairs(prolong[e], group, GROUPS // 2)]
            restrict_rows.append(jnp.concatenate(parts, axis=1))
        high, low = halves(jnp.concatenate(restrict_rows, axis=0).T)
        rt_high[...] = high
        rt_low[...] = low

    high, low = halves(d_own[...] + d_other[...])
    high_ref[...] = high
    low_ref[...] = low
    width = ROWS * DOF
    pair = (high[:, :width], low[:, :width])
    half_ref[...] = product(pair, (q_high[...], q_low[...]))
    image_ref[...] = product(pair, halves(own[...]))


def own_step(agg_of, d_own, d_other, prolong, x_message):
    rows, wide = d_own.shape
    steps = 2
    half = BANDS // 2 * DOF
    whole = lambda shape: pl.BlockSpec(shape, lambda i: (0,) * len(shape))
    part = lambda width: pl.BlockSpec((rows // steps, width), lambda i: (i, 0))
    restrict_shape = (GROUPS * DOF, rows)
    return pl.pallas_call(
        own_kernel,
        grid=(steps,),
        in_specs=[SMEM, part(wide), part(wide), whole(prolong.shape), whole((rows, 2 * COLS))],
        out_specs=[part(wide), part(wide), part(half), part(2 * COLS)] + [whole(restrict_shape)] * 2,
        out_shape=[
            jax.ShapeDtypeStruct((rows, wide), BF16),
            jax.ShapeDtypeStruct((rows, wide), BF16),
            jax.ShapeDtypeStruct((rows, half), F32),
            jax.ShapeDtypeStruct((rows, 2 * COLS), F32),
            jax.ShapeDtypeStruct(restrict_shape, BF16),
            jax.ShapeDtypeStruct(restrict_shape, BF16),
        ],
        scratch_shapes=[pltpu.VMEM((rows, half), BF16), pltpu.VMEM((rows, half), BF16)],
        compiler_params=params(),
        name="own_step",
    )(agg_of, d_own, d_other, prolong, x_message)


def ghost_lanes(side):
    return rows_of(1 + side, ROWS * DOF)


def image_kernel(d_high, d_low, own_image, near, far, keep_ref, send_ref):
    rows = own_image.shape[0]
    for place, target in ((1, send_ref), (0, keep_ref)):
        columns = rows_of(place, COLS)
        total = own_image[:, columns]
        for side, message in enumerate((near, far)):
            lanes = ghost_lanes(side)
            total += product((d_high[:, lanes], d_low[:, lanes]), halves(message[:rows, columns]))
        target[...] = total


def image(d_high, d_low, own_image, near, far):
    shape = jax.ShapeDtypeStruct((d_high.shape[0], COLS), F32)
    return pl.pallas_call(
        image_kernel,
        in_specs=[VMEM] * 5,
        out_specs=[VMEM] * 2,
        out_shape=[shape, shape],
        compiler_params=params(),
        name="image",
    )(d_high, d_low, own_image, near, far)


def ghost_kernel(agg_of, d_high, d_low, own_half, mine, other, rt_high, rt_low, half_ref, coarse_ref, q_high, q_low):
    slab, size, sub = here()
    core = sub & 1
    odd, near, far = place_of(slab, size)
    band_start = core * (BANDS // 2)
    for side, (which, region) in enumerate(((near, (1 - odd) * 2 * GROUPS), (far, odd * 2 * GROUPS))):
        for r in range(ROWS):
            columns = rows_of(r % (ROWS // 2))
            piece = jnp.where(core == r // (ROWS // 2), mine[side, :, columns], other[side, :, columns])
            band = agg_of[which * ROWS + r] + region - band_start
            for t, value in placed_pairs(piece, band, BANDS // 4):
                high, low = halves(value)
                q_high[rows_of(side * ROWS + r), rows_of(t, 2 * DOF)] = high
                q_low[rows_of(side * ROWS + r), rows_of(t, 2 * DOF)] = low
    lanes = slice(ROWS * DOF, SLOTS * DOF)
    half = own_half[...] + product((d_high[:, lanes], d_low[:, lanes]), (q_high[...], q_low[...]))
    half_ref[...] = half
    coarse_ref[...] = product((rt_high[...], rt_low[...]), halves(half))


def ghost_step(agg_of, d_high, d_low, own_half, mine, other, rt_high, rt_low):
    rows, half = own_half.shape
    return pl.pallas_call(
        ghost_kernel,
        in_specs=[SMEM] + [VMEM] * 7,
        out_specs=[VMEM] * 2,
        out_shape=[
            jax.ShapeDtypeStruct((rows, half), F32),
            jax.ShapeDtypeStruct((GROUPS * DOF, half), F32),
        ],
        scratch_shapes=[pltpu.VMEM((2 * ROWS * DOF, half), BF16)] * 2,
        compiler_params=params(),
        name="ghost_step",
    )(agg_of, d_high, d_low, own_half, mine, other, rt_high, rt_low)


def scaled_by_weight(agg_of, value):
    start = lax.axis_index("slab") * ROWS
    pieces = []
    for a in range(GROUPS):
        members = jnp.zeros((), jnp.int32)
        for e in range(ROWS):
            members += jnp.where(agg_of[start + e] == a, 1, 0)
        piece = value[rows_of(a), :]
        pieces.append(piece * (COARSE_WEIGHT / jnp.full(piece.shape, members.astype(F32))))
    return jnp.concatenate(pieces, axis=0)


def region_lanes(width):
    odd = lax.axis_index("slab") & 1
    near = pl.ds(pl.multiple_of((1 - odd) * 2 * width, width), width)
    far = pl.ds(pl.multiple_of(odd * 2 * width, width), width)
    return near, slice(width, 2 * width), far


def coarse_kernel(agg_of, mine, other, m_high, m_low, op_ref, natural):
    sub = lax.axis_index("sub")
    half = mine.shape[1]
    is_first = (sub & 1) == 0
    left = jnp.where(is_first, mine[...], other[...])
    right = jnp.where(is_first, other[...], mine[...])
    per_share = op_ref.shape[1]
    for position, value in enumerate((left, right)):
        natural[:, rows_of(position, half)] = scaled_by_weight(agg_of, value)
        for place in range(2):

            @pl.when(sub == 2 * position + place)
            def _():
                for a in range(GROUPS):
                    for q in range(per_share):
                        op_ref[a, q] = value[rows_of(a), rows_of(place * per_share + q)]

    width = GROUPS * DOF
    for region, lanes in enumerate(region_lanes(width)):
        high, low = halves(natural[:, lanes])
        m_high[:, rows_of(region, width)] = high
        m_low[:, rows_of(region, width)] = low


def coarse_operator(agg_of, mine, other):
    rows, half = mine.shape
    field = jax.ShapeDtypeStruct((rows, 2 * half), BF16)
    return pl.pallas_call(
        coarse_kernel,
        in_specs=[SMEM] + [VMEM] * 2,
        out_specs=[VMEM] * 3,
        out_shape=[field, field, jax.ShapeDtypeStruct((GROUPS, BANDS // 4, DOF, DOF), F32)],
        scratch_shapes=[pltpu.VMEM((rows, 2 * half), F32)],
        compiler_params=params(),
        name="coarse_operator",
    )(agg_of, mine, other)


def lift_kernel(agg_of, mine, other, smoother, prolong, w_high, w_low, natural):
    half = mine.shape[1]
    width = GROUPS * DOF
    slab, size, sub = here()
    is_first = (sub & 1) == 0
    for e in range(ROWS):
        own_value, other_value = mine[rows_of(e), :], other[rows_of(e), :]
        left = jnp.where(is_first, own_value, other_value)
        right = jnp.where(is_first, other_value, own_value)
        smooth = halves(smoother[e])
        natural[rows_of(e), :half] = -product(smooth, halves(left))
        natural[rows_of(e), half:] = -product(smooth, halves(right))
        for t, value in placed_pairs(prolong[e], agg_of[slab * ROWS + e], GROUPS // 2):
            lanes = slice(width + t * 2 * DOF, width + (t + 1) * 2 * DOF)
            natural[rows_of(e), lanes] += value
    for region, lanes in enumerate(region_lanes(width)):
        high, low = halves(natural[:, lanes])
        w_high[:, rows_of(region, width)] = high
        w_low[:, rows_of(region, width)] = low


def lift_operator(agg_of, mine, other, smoother, prolong):
    rows, half = mine.shape
    field = jax.ShapeDtypeStruct((rows, 2 * half), BF16)
    return pl.pallas_call(
        lift_kernel,
        in_specs=[SMEM] + [VMEM] * 4,
        out_specs=[VMEM] * 2,
        out_shape=[field, field],
        scratch_shapes=[pltpu.VMEM((rows, 2 * half), F32)],
        compiler_params=params(),
        name="lift_operator",
    )(agg_of, mine, other, smoother, prolong)


def residual_kernel(agg_of, right_side, keep, received, rt_high, rt_low, residual_ref, first_ref):
    own = pl.ds(pl.multiple_of(lax.axis_index("sub") * COLS, COLS), COLS)
    residual = right_side[:, :, own].reshape(keep.shape) - (keep[...] + received[...])
    residual_ref[...] = residual
    coarse_rhs = product((rt_high[...], rt_low[...]), halves(residual))
    first_ref[...] = scaled_by_weight(agg_of, coarse_rhs)


def residual_step(agg_of, right_side, keep, received, rt_high, rt_low):
    return pl.pallas_call(
        residual_kernel,
        in_specs=[SMEM] + [VMEM] * 5,
        out_specs=[VMEM] * 2,
        out_shape=[
            jax.ShapeDtypeStruct(keep.shape, F32),
            jax.ShapeDtypeStruct((rt_high.shape[0], COLS), F32),
        ],
        compiler_params=params(),
        name="residual_step",
    )(agg_of, right_side, keep, received, rt_high, rt_low)


def base_kernel(smoother, x_first, residual, base_ref):
    for e in range(ROWS):
        smoothed = product(halves(smoother[e]), halves(residual[rows_of(e), :]))
        base_ref[rows_of(e), :] = x_first[rows_of(e), :COLS] + smoothed


def base_step(smoother, x_first, residual):
    return pl.pallas_call(
        base_kernel,
        in_specs=[VMEM] * 3,
        out_specs=VMEM,
        out_shape=jax.ShapeDtypeStruct(residual.shape, F32),
        compiler_params=params(),
        name="base_step",
    )(smoother, x_first, residual)


def applied(op_high, op_low, near, own, far):
    total = None
    for region, field in enumerate((near, own, far)):
        lanes = rows_of(region, GROUPS * DOF)
        part = product((op_high[:, lanes], op_low[:, lanes]), halves(field[...]))
        total = part if total is None else total + part
    return total


def sweep_kernel(m_high, m_low, first, near, own, far, next_ref):
    next_ref[...] = own[...] + first[...] - applied(m_high, m_low, near, own, far)


def sweep(m_high, m_low, first, near, own, far):
    return pl.pallas_call(
        sweep_kernel,
        in_specs=[VMEM] * 6,
        out_specs=VMEM,
        out_shape=jax.ShapeDtypeStruct(own.shape, F32),
        compiler_params=params(),
        name="sweep",
    )(m_high, m_low, first, near, own, far)


def last_kernel(w_high, w_low, base, near, own, far, out_ref):
    out_ref[...] = base[...] + applied(w_high, w_low, near, own, far)


def last_step(w_high, w_low, base, near, own, far):
    return pl.pallas_call(
        last_kernel,
        in_specs=[VMEM] * 6,
        out_specs=VMEM,
        out_shape=jax.ShapeDtypeStruct(base.shape, F32),
        compiler_params=params(),
        name="last_step",
    )(w_high, w_low, base, near, own, far)


def swaps(size, start):
    pairs = [(i, i + 1) for i in range(start, size - 1, 2)]
    return pairs + [(j, i) for i, j in pairs]


def from_neighbours(value):
    size = lax.axis_size("slab")
    far = lax.ppermute(value, "slab", swaps(size, 1))
    near = lax.ppermute(value, "slab", swaps(size, 0))
    return near, far


def swapped(value, bit):
    size = lax.axis_size("sub")
    return lax.ppermute(value, "sub", [(i, i ^ bit) for i in range(size)])


def per_device(fine_blocks, prolong, smoother, right_side, agg_of, col_slot, send_rows, send_count):
    d_own, x_first, packed = start_step(
        col_slot, send_rows, send_count, fine_blocks, smoother, right_side, prolong
    )
    x_message = jnp.concatenate([x_first, packed], axis=0)
    near_message, far_message = from_neighbours(x_message)
    d_other = swapped(d_own, 1)
    d_high, d_low, half, own_image, rt_high, rt_low = own_step(agg_of, d_own, d_other, prolong, x_first)
    near_message, far_message, own_image = lax.optimization_barrier((near_message, far_message, own_image))
    keep, send = image(d_high, d_low, own_image, near_message, far_message)
    received = swapped(send, 2)
    ghosts = jnp.stack([near_message[ROWS * DOF :], far_message[ROWS * DOF :]])
    half, coarse = ghost_step(agg_of, d_high, d_low, half, ghosts, swapped(ghosts, 1), rt_high, rt_low)
    coarse_other = swapped(coarse, 2)
    residual, first = residual_step(agg_of, right_side, keep, received, rt_high, rt_low)
    base = base_step(smoother, x_first, residual)
    near, far = from_neighbours(first)
    near, far, coarse_other = lax.optimization_barrier((near, far, coarse_other))
    coarse = coarse + coarse_other
    half, coarse = lax.optimization_barrier((half, coarse))
    half_other = swapped(half, 2)
    m_high, m_low, coarse_op = coarse_operator(agg_of, coarse, swapped(coarse, 1))
    correction = first
    for index in range(COARSE_SWEEPS - 1):
        if index > 0:
            near, far = from_neighbours(correction)
        correction = sweep(m_high, m_low, first, near, correction, far)
    half_other, correction = lax.optimization_barrier((half_other, correction))
    half = half + half_other
    w_high, w_low = lift_operator(agg_of, half, swapped(half, 1), smoother, prolong)
    near, far = from_neighbours(correction)
    solution = last_step(w_high, w_low, base, near, correction, far)
    return coarse_op, solution.reshape(ROWS, DOF, COLS)


def solution(mesh):
    placed = (
        P("slab", "sub", None, None),
        P("slab", None, None),
        P("slab", None, None),
        P("slab", None, None),
        P(),
        P("slab", "sub"),
        P(),
        P(),
    )
    return jax.shard_map(
        per_device,
        mesh=mesh,
        in_specs=placed,
        out_specs=(P("slab", "sub", None, None), P("slab", None, "sub")),
        check_vma=False,
    )
```

time: 478 us -> 89.3 us (0.19)
  waiting for transfers between devices: 196 us -> 43.6 us
  matrix products: 106 us -> 0 us
  local copies, waits for them, and re-layouts: 109 us -> 7.12 us
  Pallas kernels: 0 us -> 20.6 us
  other arithmetic: 15.2 us -> 0.13 us
  starting transfers between devices: 31.1 us -> 16.5 us
  between operations: 14.5 us -> 0.84 us
    dot_general x44 -> x0, matrix products: 106 us -> none  [the longest x32 67.3 us: add_block(): jnp.einsum('eab,ebn->ean', block_now, field_rows[slot_ids], precision=hig...]
    psum x2 -> x0, waiting for transfers between devices: 96 us -> none  [the longest x1 61.2 us: per_device(): coarse_full = lax.psum(coarse_part, 'sub')]
    gather x41 -> x0, local copies, waits for them, and re-layouts: 90.4 us -> none  [the longest x32 80.1 us: add_block(): field_rows[slot_ids]]
    ppermute x10 -> x15, waiting for transfers between devices: 99.8 us -> 43.6 us  [the longest x4 22.1 us: from_neighbours(): near = lax.ppermute(value, 'slab', swaps(size, 0))]
    pallas_call x0 -> x11, Pallas kernels: none -> 20.6 us  [the longest x1 4.68 us: own_step(): pl.pallas_call(own_kernel, grid=(steps,), in_specs=[SMEM, part(wide), par...]
    ppermute x10 -> x15, starting transfers between devices: 31 us -> 16.5 us  [the longest x4 7.63 us: from_neighbours(): far = lax.ppermute(value, 'slab', swaps(size, 1))]
    concatenate x6 -> x0, other arithmetic: 9.45 us -> none  [the longest x3 8.65 us: with_ghosts(): return jnp.concatenate([values, from_lower, from_upper], axis=0)]
    transpose x1 -> x0, local copies, waits for them, and re-layouts: 5.64 us -> none  [per_device(): jnp.einsum('eba,ejbc->ejac', prolong, products, precision=highest)]
  transfers between devices with their start and end apart: 12 -> 15, of which waited for: 7 -> 11; matrix products, arithmetic and copies ran while one was open for 10% -> 0% of each run, Pallas kernels for 0% -> 17%
where the time goes in v2:
time: 89.3 us; the launch traced here: 88.9 us
  waiting for transfers between devices  43.6 us (49%)
  Pallas kernels  20.6 us (23%)
  starting transfers between devices  16.5 us (18%)
  local copies, waits for them, and re-layouts  7.12 us (8%)
    ppermute x4, waiting for transfers between devices, from_neighbours(): near = lax.ppermute(value, 'slab', swaps(size, 0))  22.1 us
    ppermute x4, waiting for transfers between devices, from_neighbours(): far = lax.ppermute(value, 'slab', swaps(size, 1))  10.9 us
    ppermute x7, waiting for transfers between devices, swapped(): return lax.ppermute(value, 'sub', [(i, i ^ bit) for i in range(size)])  10.6 us
    ppermute x4, starting transfers between devices, from_neighbours(): far = lax.ppermute(value, 'slab', swaps(size, 1))  7.63 us
    unnamed x24, local copies, waits for them, and re-layouts  7.11 us
    ppermute x4, starting transfers between devices, from_neighbours(): near = lax.ppermute(value, 'slab', swaps(size, 0))  4.96 us
    pallas_call x1, Pallas kernels, own_step(): pl.pallas_call(own_kernel, grid=(steps,), in_specs=[SMEM, part(wide), par...  4.68 us
    pallas_call x1, Pallas kernels, start_step(): pl.pallas_call(start_kernel, grid=(ROWS // at_once,), in_specs=[SMEM, ANY...  4.24 us
  transfers between devices with their start and end apart: 15, of which 11 were waited for; matrix products, arithmetic and copies ran while one was open for 0% of the time, Pallas kernels for 17%

profile of v2, /device:TPU:8, one launch (start us, length us, event | category | flops | bytes accessed | tf_op | source)
XLA Modules:
  0.0 88.9 jit_solution(9871924004574976723)
XLA Ops:
  0.6 0.8 copy.10.counts_hbm
  1.4 0.0 copy-start
  1.4 1.2 %copy-done = f32[8,64,512]{2,1,0:T(8,128)S(1)} copy-done((f32[8,64,512]{2,1,0:T(8,128)S(1)}, f32[8,64,512]{2,1,0:T(8,128)}, u32[]{:S(2)}) %copy-start) | copy-done | bytes 1048600
  2.6 0.0 copy-start.3
  2.6 0.9 %copy-done.3 = f32[8,64,64]{2,1,0:T(8,128)S(1)} copy-done((f32[8,64,64]{2,1,0:T(8,128)S(1)}, f32[8,64,64]{2,1,0:T(8,128)}, u32[]{:S(2)}) %copy-start.3) | copy-done | bytes 131096
  3.6 0.0 copy-start.5
  3.6 0.9 %copy-done.5 = f32[8,64,64]{2,1,0:T(8,128)S(1)} copy-done((f32[8,64,64]{2,1,0:T(8,128)S(1)}, f32[8,64,64]{2,1,0:T(8,128)}, u32[]{:S(2)}) %copy-start.5) | copy-done | bytes 131096
  4.5 0.0 copy-start.7
  4.5 0.8 copy-done.7
  5.3 0.0 copy-start.9
  5.3 0.7 copy-done.9
  6.0 0.0 copy-start.4
  6.0 0.0 copy-start.8
  6.0 4.2 %start_step.1 = (f32[512,1536]{1,0:T(8,128)S(1)}, f32[512,256]{1,0:T(8,128)S(1)}, f32[64,256]{1,0:T(8,128)S(1)}) custom-call(s32[8,16]{1,0:T(8,128)S(1)} %copy-done.9, s32[8,4,2,8]{3,2,1,0:T(2,128)S(1)} %copy-done.7, s32[8,4,2]{2,1,0:T(4,128)S(1)} %copy.10.counts_hbm, f32[8,16,64,64]{3,2,1,0:T(8,128)} %blocks.1, f32[8,64,64]{2,1,0:T(8,128)S(1)} %copy-done.5, ...), custom_call_target="tpu_custom_call" | custom-call | tf_op jit(solution)/shard_map/start_step/pallas_call | solution.py:127
  10.2 0.0 copy-start.2
  10.2 0.1 collective-permute-start
  10.4 1.6 %collective-permute-start.1 = (f32[576,256]{1,0:T(8,128)S(1)}, f32[576,256]{1,0:T(8,128)S(1)}, u32[]{:S(2)}, u32[]{:S(2)}) collective-permute-start(f32[576,256]{1,0:T(8,128)S(1)} %constant_dynamic-update-slice_fusion), channel_id=1, source_target_pairs={{0,4},{8,12},{16,20},{24,28},{4,0},{12,8},{20,16},{28,24},{1,5},{9... | collective-permute-start | bytes 1769480 | tf_op jit(solution)/shard_map/ppermute | solution.py:467
  12.0 1.9 %collective-permute-start.2 = (f32[576,256]{1,0:T(8,128)S(1)}, f32[576,256]{1,0:T(8,128)S(1)}, u32[]{:S(2)}, u32[]{:S(2)}) collective-permute-start(f32[576,256]{1,0:T(8,128)S(1)} %constant_dynamic-update-slice_fusion), channel_id=1, source_target_pairs={{4,8},{12,16},{20,24},{8,4},{16,12},{24,20},{5,9},{13,17},{21,25},... | collective-permute-start | bytes 1769480 | tf_op jit(solution)/shard_map/ppermute | solution.py:466
  13.9 2.1 %collective-permute-done.d_other = f32[512,1536]{1,0:T(8,128)S(1)} collective-permute-done((f32[512,1536]{1,0:T(8,128)S(1)}, f32[512,1536]{1,0:T(8,128)S(1)}, u32[]{:S(2)}, u32[]{:S(2)}) %collective-permute-start) | collective-permute-done | bytes 3145760 | tf_op jit(solution)/shard_map/ppermute | solution.py:473
  16.0 0.0 copy-done.2
  16.0 1.7 %copy-done.10 = f32[512,1536]{1,0:T(8,128)} copy-done((f32[512,1536]{1,0:T(8,128)}, f32[512,1536]{1,0:T(8,128)S(1)}, u32[]{:S(2)}) %copy-start.10) | copy-done | bytes 3145752
  17.7 0.0 copy-done.4
  17.7 0.0 copy-done.8
  17.7 4.7 %own_step.1 = (bf16[512,1536]{1,0:T(8,128)(2,1)S(1)}, bf16[512,1536]{1,0:T(8,128)(2,1)S(1)}, f32[512,384]{1,0:T(8,128)S(1)}, f32[512,256]{1,0:T(8,128)S(1)}, bf1...) custom-call(s32[64]{0:T(128)S(1)} %copy-done.8, f32[512,1536]{1,0:T(8,128)} %copy-done.2, f32[512,1536]{1,0:T(8,128)} %copy-done.10, ...), custom_call_target="tpu_custom_call" | custom-call | tf_op jit(solution)/shard_map/own_step/pallas_call | solution.py:207
  22.4 16.5 %collective-permute-done.1.near = f32[576,256]{1,0:T(8,128)S(1)} collective-permute-done((f32[576,256]{1,0:T(8,128)S(1)}, f32[576,256]{1,0:T(8,128)S(1)}, u32[]{:S(2)}, u32[]{:S(2)}) %collective-permute-start.1) | collective-permute-done | bytes 589856 | tf_op jit(solution)/shard_map/ppermute | solution.py:467
  38.8 0.0 collective-permute-done.2.far
  38.9 0.1 collective-permute-start.3
  38.9 1.8 %image.1 = (f32[512,128]{1,0:T(8,128)S(1)}, f32[512,128]{1,0:T(8,128)S(1)}) custom-call(bf16[512,1536]{1,0:T(8,128)(2,1)S(1)} %get-tuple-element.34.d_high, bf16[512,1536]{1,0:T(8,128)(2,1)S(1)} %get-tuple-element.35.d_low, f32[512,256]{1,0:T(8,128)S(1)} %get-tuple-element.45.own_image, f32[576,256]{1,0:T(8,128)S(1)} %collective-permute-done.1.near, ...), custom_call_target="tpu_custom_call" | custom-call | tf_op jit(solution)/shard_map/image/pallas_call | solution.py:243
  40.7 0.0 copy-start.1
  40.7 1.6 %collective-permute-start.4 = (f32[512,128]{1,0:T(8,128)S(1)}, f32[512,128]{1,0:T(8,128)S(1)}, u32[]{:S(2)}, u32[]{:S(2)}) collective-permute-start(f32[512,128]{1,0:T(8,128)S(1)} %get-tuple-element.47), channel_id=1, source_target_pairs={{0,2},{1,3},{2,0},{3,1},{4,6},{5,7},{6,4},{7,5},{8,10},{9,11},{10,... | collective-permute-start | bytes 786440 | tf_op jit(solution)/shard_map/ppermute | solution.py:473
  42.3 0.0 collective-permute-done.3.other
  42.3 3.1 %ghost_step.1 = (f32[512,384]{1,0:T(8,128)S(1)}, f32[256,384]{1,0:T(8,128)S(1)}) custom-call(s32[64]{0:T(128)S(1)} %copy-done.8, bf16[512,1536]{1,0:T(8,128)(2,1)S(1)} %get-tuple-element.34.d_high, bf16[512,1536]{1,0:T(8,128)(2,1)S(1)} %get-tuple-element.35.d_low, f32[512,384]{1,0:T(8,128)S(1)} %get-tuple-element.36.own_half, ...), custom_call_target="tpu_custom_call" | custom-call | tf_op jit(solution)/shard_map/ghost_step/pallas_call | solution.py:275
  45.5 0.6 collective-permute-start.7
  46.1 3.9 %collective-permute-done.4.received = f32[512,128]{1,0:T(8,128)S(1)} collective-permute-done((f32[512,128]{1,0:T(8,128)S(1)}, f32[512,128]{1,0:T(8,128)S(1)}, u32[]{:S(2)}, u32[]{:S(2)}) %collective-permute-start.4) | collective-permute-done | bytes 262176 | tf_op jit(solution)/shard_map/ppermute | solution.py:473
  49.9 0.0 copy-done.1
  49.9 0.9 %residual_step.1 = (f32[512,128]{1,0:T(8,128)S(1)}, f32[256,128]{1,0:T(8,128)S(1)}) custom-call(s32[64]{0:T(128)S(1)} %copy-done.8, f32[8,64,512]{2,1,0:T(8,128)S(1)} %copy-done.1, f32[512,128]{1,0:T(8,128)S(1)} %get-tuple-element.46.keep, f32[512,128]{1,0:T(8,128)S(1)} %collective-permute-done.4.received, bf16[256,512]{1,0:T(8,128)(2,1)S(1)} %get-tuple-element.41.rt_high, ...), custom_call_target="tpu_custom_call" | custom-call | tf_op jit(solution)/shard_map/residual_step/pallas_call | solution.py:390
  50.9 1.6 %collective-permute-start.5 = (f32[256,128]{1,0:T(8,128)S(1)}, f32[256,128]{1,0:T(8,128)S(1)}, u32[]{:S(2)}, u32[]{:S(2)}) collective-permute-start(f32[256,128]{1,0:T(8,128)S(1)} %get-tuple-element.48.first.own), channel_id=1, source_target_pairs={{0,4},{8,12},{16,20},{24,28},{4,0},{12,8},{20,16},{28,24},{1,5},{9... | collective-permute-start | bytes 393224 | tf_op jit(solution)/shard_map/ppermute | solution.py:467
  52.5 1.9 %collective-permute-start.6 = (f32[256,128]{1,0:T(8,128)S(1)}, f32[256,128]{1,0:T(8,128)S(1)}, u32[]{:S(2)}, u32[]{:S(2)}) collective-permute-start(f32[256,128]{1,0:T(8,128)S(1)} %get-tuple-element.48.first.own), channel_id=1, source_target_pairs={{4,8},{12,16},{20,24},{8,4},{16,12},{24,20},{5,9},{13,17},{21,25},... | collective-permute-start | bytes 393224 | tf_op jit(solution)/shard_map/ppermute | solution.py:466
  54.4 1.5 %collective-permute-done.5.near = f32[256,128]{1,0:T(8,128)S(1)} collective-permute-done((f32[256,128]{1,0:T(8,128)S(1)}, f32[256,128]{1,0:T(8,128)S(1)}, u32[]{:S(2)}, u32[]{:S(2)}) %collective-permute-start.5) | collective-permute-done | bytes 131104 | tf_op jit(solution)/shard_map/ppermute | solution.py:467
  55.9 4.3 %collective-permute-done.6.far = f32[256,128]{1,0:T(8,128)S(1)} collective-permute-done((f32[256,128]{1,0:T(8,128)S(1)}, f32[256,128]{1,0:T(8,128)S(1)}, u32[]{:S(2)}, u32[]{:S(2)}) %collective-permute-start.6) | collective-permute-done | bytes 131104 | tf_op jit(solution)/shard_map/ppermute | solution.py:466
  60.2 0.0 collective-permute-done.7
  60.3 0.0 copy-start.6
  60.3 1.6 %collective-permute-start.9 = (f32[512,384]{1,0:T(8,128)S(1)}, f32[512,384]{1,0:T(8,128)S(1)}, u32[]{:S(2)}, u32[]{:S(2)}) collective-permute-start(f32[512,384]{1,0:T(8,128)S(1)} %get-tuple-element.52), channel_id=1, source_target_pairs={{0,2},{1,3},{2,0},{3,1},{4,6},{5,7},{6,4},{7,5},{8,10},{9,11},{10,... | collective-permute-start | bytes 2359304 | tf_op jit(solution)/shard_map/ppermute | solution.py:473
  61.8 0.0 collective-permute-start.8
  61.8 1.7 %collective-permute-done.8.other = f32[256,384]{1,0:T(8,128)S(1)} collective-permute-done((f32[256,384]{1,0:T(8,128)S(1)}, f32[256,384]{1,0:T(8,128)S(1)}, u32[]{:S(2)}, u32[]{:S(2)}) %collective-permute-start.8) | collective-permute-done | bytes 393248 | tf_op jit(solution)/shard_map/ppermute | solution.py:473
  63.6 1.6 %coarse_operator.1 = (bf16[256,768]{1,0:T(8,128)(2,1)S(1)}, bf16[256,768]{1,0:T(8,128)(2,1)S(1)}, f32[4,3,64,64]{3,2,1,0:T(8,128)}) custom-call(s32[64]{0:T(128)S(1)} %copy-done.8, f32[256,384]{1,0:T(8,128)S(1)} %add.6.mine, f32[256,384]{1,0:T(8,128)S(1)} %collective-permute-done.8.other), custom_call_target="tpu_custom_call" | custom-call | tf_op jit(solution)/shard_map/coarse_operator/pallas_call | solution.py:335
  65.1 0.5 sweep.2.own
  65.6 0.6 collective-permute-start.10
  66.2 1.9 %collective-permute-start.11 = (f32[256,128]{1,0:T(8,128)S(1)}, f32[256,128]{1,0:T(8,128)S(1)}, u32[]{:S(2)}, u32[]{:S(2)}) collective-permute-start(f32[256,128]{1,0:T(8,128)S(1)} %sweep.2.own), channel_id=1, source_target_pairs={{4,8},{12,16},{20,24},{8,4},{16,12},{24,20},{5,9},{13,17},{21,25},... | collective-permute-start | bytes 393224 | tf_op jit(solution)/shard_map/ppermute | solution.py:466
  68.1 3.1 %collective-permute-done.10.near = f32[256,128]{1,0:T(8,128)S(1)} collective-permute-done((f32[256,128]{1,0:T(8,128)S(1)}, f32[256,128]{1,0:T(8,128)S(1)}, u32[]{:S(2)}, u32[]{:S(2)}) %collective-permute-start.10) | collective-permute-done | bytes 131104 | tf_op jit(solution)/shard_map/ppermute | solution.py:467
  71.2 3.0 %collective-permute-done.11.far = f32[256,128]{1,0:T(8,128)S(1)} collective-permute-done((f32[256,128]{1,0:T(8,128)S(1)}, f32[256,128]{1,0:T(8,128)S(1)}, u32[]{:S(2)}, u32[]{:S(2)}) %collective-permute-start.11) | collective-permute-done | bytes 131104 | tf_op jit(solution)/shard_map/ppermute | solution.py:466
  74.3 0.5 sweep.3.own
  74.7 3.0 %collective-permute-done.9 = f32[512,384]{1,0:T(8,128)S(1)} collective-permute-done((f32[512,384]{1,0:T(8,128)S(1)}, f32[512,384]{1,0:T(8,128)S(1)}, u32[]{:S(2)}, u32[]{:S(2)}) %collective-permute-start.9) | collective-permute-done | bytes 786464 | tf_op jit(solution)/shard_map/ppermute | solution.py:473
  77.7 0.1 add.7.mine
  77.8 0.1 collective-permute-start.12
  77.9 1.1 %collective-permute-start.13 = (f32[256,128]{1,0:T(8,128)S(1)}, f32[256,128]{1,0:T(8,128)S(1)}, u32[]{:S(2)}, u32[]{:S(2)}) collective-permute-start(f32[256,128]{1,0:T(8,128)S(1)} %sweep.3.own), channel_id=1, source_target_pairs={{0,4},{8,12},{16,20},{24,28},{4,0},{12,8},{20,16},{28,24},{1,5},{9... | collective-permute-start | bytes 393224 | tf_op jit(solution)/shard_map/ppermute | solution.py:467
  79.0 1.9 %collective-permute-start.14 = (f32[256,128]{1,0:T(8,128)S(1)}, f32[256,128]{1,0:T(8,128)S(1)}, u32[]{:S(2)}, u32[]{:S(2)}) collective-permute-start(f32[256,128]{1,0:T(8,128)S(1)} %sweep.3.own), channel_id=1, source_target_pairs={{4,8},{12,16},{20,24},{8,4},{16,12},{24,20},{5,9},{13,17},{21,25},... | collective-permute-start | bytes 393224 | tf_op jit(solution)/shard_map/ppermute | solution.py:466
  80.9 0.0 copy-done.6
  80.9 0.2 base_step.1.base
  81.2 0.0 collective-permute-done.12.other
  81.2 1.6 %lift_operator.1 = (bf16[512,768]{1,0:T(8,128)(2,1)S(1)}, bf16[512,768]{1,0:T(8,128)(2,1)S(1)}) custom-call(s32[64]{0:T(128)S(1)} %copy-done.8, f32[512,384]{1,0:T(8,128)S(1)} %add.7.mine, f32[512,384]{1,0:T(8,128)S(1)} %collective-permute-done.12.other, f32[8,64,64]{2,1,0:T(8,128)S(1)} %copy-done.6, f32[8,64,64]{2,1,0:T(8,128)S(1)} %copy-done.4), custom_call_target="tpu_custom_call" | custom-call | tf_op jit(solution)/shard_map/lift_operator/pallas_call | solution.py:370
  82.8 1.0 %collective-permute-done.13.near = f32[256,128]{1,0:T(8,128)S(1)} collective-permute-done((f32[256,128]{1,0:T(8,128)S(1)}, f32[256,128]{1,0:T(8,128)S(1)}, u32[]{:S(2)}, u32[]{:S(2)}) %collective-permute-start.13) | collective-permute-done | bytes 131104 | tf_op jit(solution)/shard_map/ppermute | solution.py:467
  83.8 3.6 %collective-permute-done.14.far = f32[256,128]{1,0:T(8,128)S(1)} collective-permute-done((f32[256,128]{1,0:T(8,128)S(1)}, f32[256,128]{1,0:T(8,128)S(1)}, u32[]{:S(2)}, u32[]{:S(2)}) %collective-permute-start.14) | collective-permute-done | bytes 131104 | tf_op jit(solution)/shard_map/ppermute | solution.py:466
  87.3 1.5 %last_step.1 = f32[512,128]{1,0:T(8,128)} custom-call(bf16[512,768]{1,0:T(8,128)(2,1)S(1)} %get-tuple-element.58.w_high, bf16[512,768]{1,0:T(8,128)(2,1)S(1)} %get-tuple-element.59.w_low, f32[512,128]{1,0:T(8,128)S(1)} %base_step.1.base, f32[256,128]{1,0:T(8,128)S(1)} %collective-permute-done.13.near, f32[256,128]{1,0:T(8,128)S(1)} %sweep.3.own, ...), custom_call_target="tpu_custom_call" | custom-call | tf_op jit(solution)/shard_map/last_step/pallas_call | solution.py:449
  (6 shorter events, 0.1 us)
Async XLA Ops:
  1.4 1.2 %copy-start = (f32[8,64,512]{2,1,0:T(8,128)S(1)}, f32[8,64,512]{2,1,0:T(8,128)}, u32[]{:S(2)}) copy-start(f32[8,64,512]{2,1,0:T(8,128)} %right_side.3) | copy-start | bytes 3145732
  2.6 0.9 %copy-start.3 = (f32[8,64,64]{2,1,0:T(8,128)S(1)}, f32[8,64,64]{2,1,0:T(8,128)}, u32[]{:S(2)}) copy-start(f32[8,64,64]{2,1,0:T(8,128)} %prolong.5) | copy-start | bytes 393220
  3.6 0.9 %copy-start.5 = (f32[8,64,64]{2,1,0:T(8,128)S(1)}, f32[8,64,64]{2,1,0:T(8,128)}, u32[]{:S(2)}) copy-start(f32[8,64,64]{2,1,0:T(8,128)} %smoother.5) | copy-start | bytes 393220
  4.5 0.8 copy-start.7
  5.3 0.7 copy-start.9
  6.0 11.7 %copy-start.4 = (f32[8,64,64]{2,1,0:T(8,128)S(1)}, f32[8,64,64]{2,1,0:T(8,128)}, u32[]{:S(2)}) copy-start(f32[8,64,64]{2,1,0:T(8,128)} %prolong.5) | copy-start | bytes 393220
  6.0 11.7 %copy-start.8 = (s32[64]{0:T(128)S(1)}, s32[64]{0:T(128)}, u32[]{:S(2)}) copy-start(s32[64]{0:T(128)} %agg_of.9) | copy-start | bytes 772
  10.2 5.7 %copy-start.2 = (f32[512,1536]{1,0:T(8,128)}, f32[512,1536]{1,0:T(8,128)S(1)}, u32[]{:S(2)}) copy-start(f32[512,1536]{1,0:T(8,128)S(1)} %get-tuple-element.32.d_own) | copy-start | bytes 9437188
  10.2 5.7 %collective-permute-start = (f32[512,1536]{1,0:T(8,128)S(1)}, f32[512,1536]{1,0:T(8,128)S(1)}, u32[]{:S(2)}, u32[]{:S(2)}) collective-permute-start(f32[512,1536]{1,0:T(8,128)S(1)} %get-tuple-element.32.d_own), channel_id=1, source_target_pairs={{0,1},{1,0},{2,3},{3,2},{4,5},{5,4},{6,7},{7,6},{8,9},{9,8},{10,11... | collective-permute-start | bytes 9437192 | tf_op jit(solution)/shard_map/ppermute | solution.py:473
  10.4 28.4 %collective-permute-start.1 = (f32[576,256]{1,0:T(8,128)S(1)}, f32[576,256]{1,0:T(8,128)S(1)}, u32[]{:S(2)}, u32[]{:S(2)}) collective-permute-start(f32[576,256]{1,0:T(8,128)S(1)} %constant_dynamic-update-slice_fusion), channel_id=1, source_target_pairs={{0,4},{8,12},{16,20},{24,28},{4,0},{12,8},{20,16},{28,24},{1,5},{9... | collective-permute-start | bytes 1769480 | tf_op jit(solution)/shard_map/ppermute | solution.py:467
  12.0 26.8 %collective-permute-start.2 = (f32[576,256]{1,0:T(8,128)S(1)}, f32[576,256]{1,0:T(8,128)S(1)}, u32[]{:S(2)}, u32[]{:S(2)}) collective-permute-start(f32[576,256]{1,0:T(8,128)S(1)} %constant_dynamic-update-slice_fusion), channel_id=1, source_target_pairs={{4,8},{12,16},{20,24},{8,4},{16,12},{24,20},{5,9},{13,17},{21,25},... | collective-permute-start | bytes 1769480 | tf_op jit(solution)/shard_map/ppermute | solution.py:466
  16.0 1.7 %copy-start.10 = (f32[512,1536]{1,0:T(8,128)}, f32[512,1536]{1,0:T(8,128)S(1)}, u32[]{:S(2)}) copy-start(f32[512,1536]{1,0:T(8,128)S(1)} %collective-permute-done.d_other) | copy-start | bytes 9437188
  38.9 3.5 %collective-permute-start.3 = (f32[2,64,256]{2,1,0:T(8,128)S(1)}, f32[2,64,256]{2,1,0:T(8,128)S(1)}, u32[]{:S(2)}, u32[]{:S(2)}) collective-permute-start(f32[2,64,256]{2,1,0:T(8,128)S(1)} %pad_maximum_fusion.mine), channel_id=1, source_target_pairs={{0,1},{1,0},{2,3},{3,2},{4,5},{5,4},{6,7},{7,6},{8,9},{9,8},{10,11... | collective-permute-start | bytes 393224 | tf_op jit(solution)/shard_map/ppermute | solution.py:473
  40.7 9.2 %copy-start.1 = (f32[8,64,512]{2,1,0:T(8,128)S(1)}, f32[8,64,512]{2,1,0:T(8,128)}, u32[]{:S(2)}) copy-start(f32[8,64,512]{2,1,0:T(8,128)} %right_side.3) | copy-start | bytes 3145732
  40.7 9.2 %collective-permute-start.4 = (f32[512,128]{1,0:T(8,128)S(1)}, f32[512,128]{1,0:T(8,128)S(1)}, u32[]{:S(2)}, u32[]{:S(2)}) collective-permute-start(f32[512,128]{1,0:T(8,128)S(1)} %get-tuple-element.47), channel_id=1, source_target_pairs={{0,2},{1,3},{2,0},{3,1},{4,6},{5,7},{6,4},{7,5},{8,10},{9,11},{10,... | collective-permute-start | bytes 786440 | tf_op jit(solution)/shard_map/ppermute | solution.py:473
  45.5 14.7 %collective-permute-start.7 = (f32[256,384]{1,0:T(8,128)S(1)}, f32[256,384]{1,0:T(8,128)S(1)}, u32[]{:S(2)}, u32[]{:S(2)}) collective-permute-start(f32[256,384]{1,0:T(8,128)S(1)} %get-tuple-element.44), channel_id=1, source_target_pairs={{0,2},{1,3},{2,0},{3,1},{4,6},{5,7},{6,4},{7,5},{8,10},{9,11},{10,... | collective-permute-start | bytes 1179656 | tf_op jit(solution)/shard_map/ppermute | solution.py:473
  50.9 5.0 %collective-permute-start.5 = (f32[256,128]{1,0:T(8,128)S(1)}, f32[256,128]{1,0:T(8,128)S(1)}, u32[]{:S(2)}, u32[]{:S(2)}) collective-permute-start(f32[256,128]{1,0:T(8,128)S(1)} %get-tuple-element.48.first.own), channel_id=1, source_target_pairs={{0,4},{8,12},{16,20},{24,28},{4,0},{12,8},{20,16},{28,24},{1,5},{9... | collective-permute-start | bytes 393224 | tf_op jit(solution)/shard_map/ppermute | solution.py:467
  52.5 7.7 %collective-permute-start.6 = (f32[256,128]{1,0:T(8,128)S(1)}, f32[256,128]{1,0:T(8,128)S(1)}, u32[]{:S(2)}, u32[]{:S(2)}) collective-permute-start(f32[256,128]{1,0:T(8,128)S(1)} %get-tuple-element.48.first.own), channel_id=1, source_target_pairs={{4,8},{12,16},{20,24},{8,4},{16,12},{24,20},{5,9},{13,17},{21,25},... | collective-permute-start | bytes 393224 | tf_op jit(solution)/shard_map/ppermute | solution.py:466
  60.3 20.6 %copy-start.6 = (f32[8,64,64]{2,1,0:T(8,128)S(1)}, f32[8,64,64]{2,1,0:T(8,128)}, u32[]{:S(2)}) copy-start(f32[8,64,64]{2,1,0:T(8,128)} %smoother.5) | copy-start | bytes 393220
  60.3 17.4 %collective-permute-start.9 = (f32[512,384]{1,0:T(8,128)S(1)}, f32[512,384]{1,0:T(8,128)S(1)}, u32[]{:S(2)}, u32[]{:S(2)}) collective-permute-start(f32[512,384]{1,0:T(8,128)S(1)} %get-tuple-element.52), channel_id=1, source_target_pairs={{0,2},{1,3},{2,0},{3,1},{4,6},{5,7},{6,4},{7,5},{8,10},{9,11},{10,... | collective-permute-start | bytes 2359304 | tf_op jit(solution)/shard_map/ppermute | solution.py:473
  61.8 1.7 %collective-permute-start.8 = (f32[256,384]{1,0:T(8,128)S(1)}, f32[256,384]{1,0:T(8,128)S(1)}, u32[]{:S(2)}, u32[]{:S(2)}) collective-permute-start(f32[256,384]{1,0:T(8,128)S(1)} %add.6.mine), channel_id=1, source_target_pairs={{0,1},{1,0},{2,3},{3,2},{4,5},{5,4},{6,7},{7,6},{8,9},{9,8},{10,11... | collective-permute-start | bytes 1179656 | tf_op jit(solution)/shard_map/ppermute | solution.py:473
  65.6 5.6 %collective-permute-start.10 = (f32[256,128]{1,0:T(8,128)S(1)}, f32[256,128]{1,0:T(8,128)S(1)}, u32[]{:S(2)}, u32[]{:S(2)}) collective-permute-start(f32[256,128]{1,0:T(8,128)S(1)} %sweep.2.own), channel_id=1, source_target_pairs={{0,4},{8,12},{16,20},{24,28},{4,0},{12,8},{20,16},{28,24},{1,5},{9... | collective-permute-start | bytes 393224 | tf_op jit(solution)/shard_map/ppermute | solution.py:467
  66.2 8.1 %collective-permute-start.11 = (f32[256,128]{1,0:T(8,128)S(1)}, f32[256,128]{1,0:T(8,128)S(1)}, u32[]{:S(2)}, u32[]{:S(2)}) collective-permute-start(f32[256,128]{1,0:T(8,128)S(1)} %sweep.2.own), channel_id=1, source_target_pairs={{4,8},{12,16},{20,24},{8,4},{16,12},{24,20},{5,9},{13,17},{21,25},... | collective-permute-start | bytes 393224 | tf_op jit(solution)/shard_map/ppermute | solution.py:466
  77.8 3.4 %collective-permute-start.12 = (f32[512,384]{1,0:T(8,128)S(1)}, f32[512,384]{1,0:T(8,128)S(1)}, u32[]{:S(2)}, u32[]{:S(2)}) collective-permute-start(f32[512,384]{1,0:T(8,128)S(1)} %add.7.mine), channel_id=1, source_target_pairs={{0,1},{1,0},{2,3},{3,2},{4,5},{5,4},{6,7},{7,6},{8,9},{9,8},{10,11... | collective-permute-start | bytes 2359304 | tf_op jit(solution)/shard_map/ppermute | solution.py:473
  77.9 5.9 %collective-permute-start.13 = (f32[256,128]{1,0:T(8,128)S(1)}, f32[256,128]{1,0:T(8,128)S(1)}, u32[]{:S(2)}, u32[]{:S(2)}) collective-permute-start(f32[256,128]{1,0:T(8,128)S(1)} %sweep.3.own), channel_id=1, source_target_pairs={{0,4},{8,12},{16,20},{24,28},{4,0},{12,8},{20,16},{28,24},{1,5},{9... | collective-permute-start | bytes 393224 | tf_op jit(solution)/shard_map/ppermute | solution.py:467
  79.0 8.3 %collective-permute-start.14 = (f32[256,128]{1,0:T(8,128)S(1)}, f32[256,128]{1,0:T(8,128)S(1)}, u32[]{:S(2)}, u32[]{:S(2)}) collective-permute-start(f32[256,128]{1,0:T(8,128)S(1)} %sweep.3.own), channel_id=1, source_target_pairs={{4,8},{12,16},{20,24},{8,4},{16,12},{24,20},{5,9},{13,17},{21,25},... | collective-permute-start | bytes 393224 | tf_op jit(solution)/shard_map/ppermute | solution.py:466

commit v3 on v0

v3 whole, which is shorter than its diff:
```python
import jax
import jax.numpy as jnp
from jax import lax
from jax.experimental import pallas as pl
from jax.experimental.pallas import tpu as pltpu
from jax.sharding import PartitionSpec as P

COARSE_SWEEPS = 3
COARSE_WEIGHT = 0.25
F32 = jnp.float32
BF16 = jnp.bfloat16
VMEM = pl.BlockSpec(memory_space=pltpu.VMEM)
SMEM = pl.BlockSpec(memory_space=pltpu.SMEM)
HBM = pl.BlockSpec(memory_space=pltpu.HBM)
ROWS = 8
GHOSTS = 8
SLOTS = ROWS + 2 * GHOSTS
GROUPS = 4
BANDS = 3 * GROUPS
DOF = 64
COLS = 128
SUBS = 4
HALF_ROWS = ROWS // 2
WIDE = ROWS * DOF
PAIR = 2 * DOF
COARSE = GROUPS * DOF


def params(limit=24):
    return pltpu.CompilerParams(vmem_limit_bytes=limit << 20)


def shape(*dims, dtype=F32):
    return jax.ShapeDtypeStruct(dims, dtype)


def halves(value):
    high = value.astype(BF16)
    return high, (value - high.astype(F32)).astype(BF16)


def mm(a, b):
    return jnp.dot(a, b, preferred_element_type=F32)


def product(left, right):
    left_high, left_low = left
    right_high, right_low = right
    return mm(left_high, right_high) + (mm(left_high, right_low) + mm(left_low, right_high))


def narrow_product(left, value):
    left_high, left_low = left
    high, low = halves(value)
    width = value.shape[1]
    both = mm(left_high, jnp.concatenate([high, low], axis=1))
    return both[:, :width] + (both[:, width:] + mm(left_low, high))


def span(index, size=DOF):
    return slice(index * size, (index + 1) * size)


def aligned(index, size):
    return pl.ds(pl.multiple_of(index * size, size), size)


def neighbours():
    slab, size = lax.axis_index("slab"), lax.axis_size("slab")
    odd = slab & 1
    near = jnp.minimum(slab ^ 1, size - 1)
    far = jnp.where(odd == 1, jnp.minimum(slab + 1, size - 1), jnp.maximum(slab - 1, 0))
    return slab, near, far


def start_kernel(
    col_hbm, rows_hbm, counts_hbm, blocks_hbm, smoother_hbm, right_hbm, prolong_hbm,
    pair_ref, mine_ref, theirs_ref, message_ref, right_ref,
    col_slot, rows, counts, blocks, smoother, right, prolong, sems, block_sems, *parts
):
    slab, size, sub = lax.axis_index("slab"), lax.axis_size("slab"), lax.axis_index("sub")
    below = jnp.maximum(slab - 1, 0)
    above = jnp.minimum(slab + 1, size - 1)
    core = sub & 1
    chip = (sub >> 1) & 1
    sources = [
        (smoother_hbm, smoother),
        (right_hbm.at[:, :, aligned(sub, COLS)], right.at[0]),
        (right_hbm.at[:, :, aligned(sub ^ 2, COLS)], right.at[1]),
        (prolong_hbm.at[pl.ds(core * HALF_ROWS, HALF_ROWS)], prolong),
        (col_hbm, col_slot),
        (rows_hbm.at[below, sub], rows.at[0]),
        (rows_hbm.at[above, sub], rows.at[1]),
        (counts_hbm.at[sub], counts),
    ]
    copies = [pltpu.make_async_copy(s, d, sems.at[i]) for i, (s, d) in enumerate(sources)]
    block_copies = [
        pltpu.make_async_copy(blocks_hbm.at[e], blocks.at[e], block_sems.at[e]) for e in range(ROWS)
    ]
    for copy in copies + block_copies:
        copy.start()
    for copy in copies:
        copy.wait()

    for e in range(ROWS):
        right_ref[span(e), :] = right[0, e]
        wide = jnp.concatenate([right[0, e], right[1, e]], axis=1)
        message_ref[span(e), :] = product(halves(smoother[e]), halves(wide))
    message_ref[span(ROWS), :] = jnp.concatenate([prolong[i] for i in range(HALF_ROWS)], axis=1)

    lower_count = jnp.where(slab > 0, counts[1, below], 0)
    upper_count = jnp.where(slab < size - 1, counts[0, above], 0)
    lower_region = 1 + (1 - (slab & 1) ^ chip)
    lower_start = lower_region * ROWS
    upper_start = (3 - lower_region) * ROWS
    upper_lanes = lax.broadcasted_iota(jnp.int32, (DOF, PAIR), 1) >= DOF
    for group in range(ROWS // HALF_ROWS):
        for position, part in enumerate(parts):
            part[...] = jnp.zeros_like(part)
            block_copies[group * HALF_ROWS + position].wait()
        for j in range(blocks.shape[1]):
            for position, part in enumerate(parts):
                e = group * HALF_ROWS + position
                slot = col_slot[e, j]
                is_own = slot < ROWS
                is_upper = slot >= ROWS + GHOSTS
                side = jnp.where(is_upper, 1, 0)
                place = jnp.where(is_own, 0, slot - ROWS - side * GHOSTS)
                listed = rows[side, 1 - side, place] + jnp.where(is_upper, upper_start, lower_start)
                column = jnp.where(is_own, slot, listed)
                count = jnp.where(is_upper, upper_count, lower_count)
                live = jnp.where(is_own | (place < count), 1.0, 0.0)
                odd_column = column & 1
                lower_scale = jnp.where(odd_column == 0, live, 0.0)
                upper_scale = jnp.where(odd_column == 1, live, 0.0)
                block = blocks[e, j]
                doubled = jnp.concatenate([block, block], axis=1)
                part[:, aligned(column >> 1, PAIR)] += doubled * jnp.where(upper_lanes, upper_scale, lower_scale)
        for position, part in enumerate(parts):
            pair_ref[span(group * HALF_ROWS + position), :] = part[:, : 2 * WIDE]

        @pl.when(core == group)
        def _():
            for position, part in enumerate(parts):
                mine_ref[span(position), :] = part[:, 2 * WIDE :]

        @pl.when(core != group)
        def _():
            for position, part in enumerate(parts):
                theirs_ref[span(position), :] = part[:, 2 * WIDE :]


def start_step(col_slot, send_rows, send_count, blocks, smoother, right_side, prolong):
    counts = jnp.transpose(send_count, (1, 2, 0))
    arrays = (col_slot, send_rows, counts, blocks, smoother, right_side, prolong)
    return pl.pallas_call(
        start_kernel,
        in_specs=[HBM] * 7,
        out_specs=[VMEM] * 5,
        out_shape=[
            shape(WIDE, 2 * WIDE),
            shape(WIDE // 2, WIDE),
            shape(WIDE // 2, WIDE),
            shape(WIDE + DOF, 2 * COLS),
            shape(WIDE, COLS),
        ],
        scratch_shapes=[
            pltpu.SMEM(col_slot.shape, jnp.int32),
            pltpu.SMEM((2, 2, GHOSTS), jnp.int32),
            pltpu.SMEM((2, send_count.shape[0]), jnp.int32),
            pltpu.VMEM(blocks.shape, F32),
            pltpu.VMEM(smoother.shape, F32),
            pltpu.VMEM((2, ROWS, DOF, COLS), F32),
            pltpu.VMEM((HALF_ROWS, DOF, DOF), F32),
            pltpu.SemaphoreType.DMA((8,)),
            pltpu.SemaphoreType.DMA((ROWS,)),
        ]
        + [pltpu.VMEM((DOF, 3 * WIDE), F32)] * HALF_ROWS,
        compiler_params=params(),
        name="start_step",
    )(*(pltpu.with_memory_space_constraint(a, pltpu.HBM) for a in arrays))


def placed(piece, index):
    upper = lax.broadcasted_iota(jnp.int32, (DOF, PAIR), 1) >= DOF
    doubled = jnp.concatenate([piece, piece], axis=1)
    lower_scale = jnp.where(index == 0, 1.0, 0.0)
    upper_scale = jnp.where(index == 1, 1.0, 0.0)
    return doubled * jnp.where(upper, upper_scale, lower_scale)


def own_kernel(
    agg_of, prolong, field, right, pair, pair_other, side_ref, half_ref, image_ref, rt_high, rt_low, q_high, q_low
):
    start = lax.axis_index("slab") * ROWS
    core = lax.axis_index("sub") & 1

    @pl.when(pl.program_id(0) == 0)
    def _():
        restrict_rows = []
        for e in range(ROWS):
            group = agg_of[start + e]
            high, low = halves(placed(prolong[e], group - 2 * core))
            q_high[span(e), :] = high
            q_low[span(e), :] = low
            parts = [placed(prolong[e], group - 2 * t) for t in range(GROUPS // 2)]
            restrict_rows.append(jnp.concatenate(parts, axis=1))
        high, low = halves(jnp.concatenate(restrict_rows, axis=0).T)
        rt_high[...] = high
        rt_low[...] = low

    side_ref[...] = pair[:, WIDE:] + pair_other[:, WIDE:]
    own = halves(pair[:, :WIDE] + pair_other[:, :WIDE])
    half_ref[...] = product(own, (q_high[...], q_low[...]))
    total = product(own, halves(field[...]))
    image_ref[:, :COLS] = total[:, :COLS] - right[...]
    image_ref[:, COLS:] = total[:, COLS:]


def own_step(agg_of, prolong, message, right, pair, pair_other):
    steps = 2
    whole = lambda *dims: pl.BlockSpec(dims, lambda i: (0,) * len(dims))
    part = lambda width: pl.BlockSpec((WIDE // steps, width), lambda i: (i, 0))
    return pl.pallas_call(
        own_kernel,
        grid=(steps,),
        in_specs=[SMEM, whole(*prolong.shape), whole(WIDE, 2 * COLS), part(COLS)] + [part(2 * WIDE)] * 2,
        out_specs=[part(WIDE), part(PAIR), part(2 * COLS)] + [whole(COARSE, WIDE)] * 2,
        out_shape=[
            shape(WIDE, WIDE),
            shape(WIDE, PAIR),
            shape(WIDE, 2 * COLS),
            shape(COARSE, WIDE, dtype=BF16),
            shape(COARSE, WIDE, dtype=BF16),
        ],
        scratch_shapes=[pltpu.VMEM((WIDE, PAIR), BF16)] * 2,
        compiler_params=params(),
        name="own_step",
    )(agg_of, prolong, message, right, pair, pair_other)


def image_kernel(own_image, side, received, received_other, message, keep_ref, send_ref, high_ref, low_ref):
    core = lax.axis_index("sub") & 1
    field = halves(message[:WIDE, :])
    rows = WIDE // 2
    for group in range(2):
        part = span(group, rows)
        extra = jnp.where(core == group, received[...], received_other[...])
        high, low = halves(side[part, :] + extra)
        high_ref[part, :] = high
        low_ref[part, :] = low
        total = own_image[part, :] + product((high, low), field)
        keep_ref[part, :] = total[:, :COLS]
        send_ref[part, :] = total[:, COLS:]


def image(own_image, side, received, received_other, message):
    return pl.pallas_call(
        image_kernel,
        in_specs=[VMEM] * 5,
        out_specs=[VMEM] * 4,
        out_shape=[shape(WIDE, COLS)] * 2 + [shape(WIDE, WIDE, dtype=BF16)] * 2,
        compiler_params=params(),
        name="image",
    )(own_image, side, received, received_other, message)


def ghost_kernel(agg_of, d_high, d_low, own_half, mine, other, rt_high, rt_low, half_ref, coarse_ref, q_high, q_low):
    _, near, far = neighbours()
    sub = lax.axis_index("sub")
    core = sub & 1
    start = jnp.where(((sub >> 1) & 1) == 0, near, far) * ROWS
    for r in range(ROWS):
        columns = span(r % HALF_ROWS)
        piece = jnp.where(core == r // HALF_ROWS, mine[:, columns], other[:, columns])
        high, low = halves(placed(piece, agg_of[start + r] - 2 * core))
        q_high[span(r), :] = high
        q_low[span(r), :] = low
    half_ref[:, :PAIR] = own_half[...]
    half_ref[:, PAIR:] = product((d_high[...], d_low[...]), (q_high[...], q_low[...]))
    coarse_ref[...] = product((rt_high[...], rt_low[...]), halves(half_ref[...]))


def ghost_step(agg_of, d_high, d_low, own_half, mine, other, rt_high, rt_low):
    return pl.pallas_call(
        ghost_kernel,
        in_specs=[SMEM] + [VMEM] * 7,
        out_specs=[VMEM] * 2,
        out_shape=[shape(WIDE, 2 * PAIR), shape(COARSE, 2 * PAIR)],
        scratch_shapes=[pltpu.VMEM((WIDE, PAIR), BF16)] * 2,
        compiler_params=params(),
        name="ghost_step",
    )(agg_of, d_high, d_low, own_half, mine, other, rt_high, rt_low)


def scaled_by_weight(agg_of, value):
    start = lax.axis_index("slab") * ROWS
    pieces = []
    for a in range(GROUPS):
        members = jnp.zeros((), jnp.int32)
        for e in range(ROWS):
            members += jnp.where(agg_of[start + e] == a, 1, 0)
        piece = value[span(a), :]
        pieces.append(piece * (COARSE_WEIGHT / jnp.full(piece.shape, members.astype(F32))))
    return jnp.concatenate(pieces, axis=0)


def coarse_kernel(agg_of, mine, other, m_high, m_low, op_ref, natural):
    sub = lax.axis_index("sub")
    odd = lax.axis_index("slab") & 1
    is_first = (sub & 1) == 0
    first = jnp.where(is_first, mine[...], other[...])
    second = jnp.where(is_first, other[...], mine[...])
    places = (2 * (1 - odd), 1, 2 * odd)
    for region, place in enumerate(places):
        value = jnp.concatenate([first[:, span(region, PAIR)], second[:, span(region, PAIR)]], axis=1)
        natural[:, aligned(place, COARSE)] = value
        high, low = halves(scaled_by_weight(agg_of, value))
        m_high[:, span(region, COARSE)] = high
        m_low[:, span(region, COARSE)] = low
    share = op_ref.shape[1]
    for k in range(BANDS // share):

        @pl.when(sub == k)
        def _():
            for a in range(GROUPS):
                for q in range(share):
                    op_ref[a, q] = natural[span(a), span(k * share + q)]


def coarse_operator(agg_of, mine, other):
    return pl.pallas_call(
        coarse_kernel,
        in_specs=[SMEM] + [VMEM] * 2,
        out_specs=[VMEM] * 3,
        out_shape=[shape(COARSE, 3 * COARSE, dtype=BF16)] * 2 + [shape(GROUPS, BANDS // SUBS, DOF, DOF)],
        scratch_shapes=[pltpu.VMEM((COARSE, 3 * COARSE), F32)],
        compiler_params=params(),
        name="coarse_operator",
    )(agg_of, mine, other)


def lift_kernel(agg_of, mine, other, smoother, prolong, w_high, w_low):
    start = lax.axis_index("slab") * ROWS
    is_first = (lax.axis_index("sub") & 1) == 0
    for e in range(ROWS):
        smooth = halves(smoother[e])
        from_mine = product(smooth, halves(mine[span(e), :]))
        from_other = product(smooth, halves(other[span(e), :]))
        first = jnp.where(is_first, from_mine, from_other)
        second = jnp.where(is_first, from_other, from_mine)
        for region in range(3):
            for t, value in enumerate((first, second)):
                value = -value[:, span(region, PAIR)]
                if region == 1:
                    value += placed(prolong[e], agg_of[start + e] - 2 * t)
                high, low = halves(value)
                w_high[span(e), span(2 * region + t, PAIR)] = high
                w_low[span(e), span(2 * region + t, PAIR)] = low


def lift_operator(agg_of, mine, other, smoother, prolong):
    return pl.pallas_call(
        lift_kernel,
        in_specs=[SMEM] + [VMEM] * 4,
        out_specs=[VMEM] * 2,
        out_shape=[shape(WIDE, 3 * COARSE, dtype=BF16)] * 2,
        compiler_params=params(),
        name="lift_operator",
    )(agg_of, mine, other, smoother, prolong)


def residual_kernel(agg_of, keep, received, rt_high, rt_low, residual_ref, first_ref):
    residual = -(keep[...] + received[...])
    residual_ref[...] = residual
    first_ref[...] = scaled_by_weight(agg_of, narrow_product((rt_high[...], rt_low[...]), residual))


def residual_step(agg_of, keep, received, rt_high, rt_low):
    return pl.pallas_call(
        residual_kernel,
        in_specs=[SMEM] + [VMEM] * 4,
        out_specs=[VMEM] * 2,
        out_shape=[shape(WIDE, COLS), shape(COARSE, COLS)],
        compiler_params=params(),
        name="residual_step",
    )(agg_of, keep, received, rt_high, rt_low)


def base_kernel(smoother, message, residual, base_ref):
    for e in range(ROWS):
        smoothed = narrow_product(halves(smoother[e]), residual[span(e), :])
        base_ref[span(e), :] = message[span(e), :COLS] + smoothed


def base_step(smoother, message, residual):
    return pl.pallas_call(
        base_kernel,
        in_specs=[VMEM] * 3,
        out_specs=VMEM,
        out_shape=shape(WIDE, COLS),
        compiler_params=params(),
        name="base_step",
    )(smoother, message, residual)


def applied(op_high, op_low, fields):
    total = None
    for region, field in fields:
        lanes = span(region, COARSE)
        part = narrow_product((op_high[:, lanes], op_low[:, lanes]), field[...])
        total = part if total is None else total + part
    return total


def sweep_kernel(m_high, m_low, first, near, own, far, next_ref):
    fields = ((0, near), (1, own), (2, far))
    next_ref[...] = own[...] + first[...] - applied(m_high, m_low, fields)


def sweep(m_high, m_low, first, near, own, far):
    return pl.pallas_call(
        sweep_kernel,
        in_specs=[VMEM] * 6,
        out_specs=VMEM,
        out_shape=shape(COARSE, COLS),
        compiler_params=params(),
        name="sweep",
    )(m_high, m_low, first, near, own, far)


def lifted_kernel(w_high, w_low, base, own, out_ref):
    out_ref[...] = base[...] + applied(w_high, w_low, ((1, own),))


def lifted(w_high, w_low, base, own):
    return pl.pallas_call(
        lifted_kernel,
        in_specs=[VMEM] * 4,
        out_specs=VMEM,
        out_shape=shape(WIDE, COLS),
        compiler_params=params(),
        name="lifted",
    )(w_high, w_low, base, own)


def last_kernel(w_high, w_low, base, near, far, out_ref):
    out_ref[...] = base[...] + applied(w_high, w_low, ((0, near), (2, far)))


def last_step(w_high, w_low, base, near, far):
    return pl.pallas_call(
        last_kernel,
        in_specs=[VMEM] * 5,
        out_specs=VMEM,
        out_shape=shape(WIDE, COLS),
        compiler_params=params(),
        name="last_step",
    )(w_high, w_low, base, near, far)


def swaps(size, start):
    pairs = [(i, i + 1) for i in range(start, size - 1, 2)]
    return pairs + [(j, i) for i, j in pairs]


def from_neighbours(value):
    size = lax.axis_size("slab")
    far = lax.ppermute(value, "slab", swaps(size, 1))
    near = lax.ppermute(value, "slab", swaps(size, 0))
    return near, far


def from_side(value):
    size, subs = lax.axis_size("slab"), lax.axis_size("sub")
    pairs = [
        (i * subs + k, j * subs + k) for k in range(subs) for i, j in swaps(size, (k >> 1) & 1)
    ]
    return lax.ppermute(value, ("slab", "sub"), pairs)


def swapped(value, bit):
    size = lax.axis_size("sub")
    return lax.ppermute(value, "sub", [(i, i ^ bit) for i in range(size)])


def summed_regions(mine, received):
    is_near = ((lax.axis_index("sub") >> 1) & 1) == 0
    own = mine[:, :PAIR] + received[:, :PAIR]
    near = jnp.where(is_near, mine[:, PAIR:], received[:, PAIR:])
    far = jnp.where(is_near, received[:, PAIR:], mine[:, PAIR:])
    return jnp.concatenate([near, own, far], axis=1)


def per_device(fine_blocks, prolong, smoother, right_side, agg_of, col_slot, send_rows, send_count):
    pair, mine, theirs, message, right = start_step(
        col_slot, send_rows, send_count, fine_blocks, smoother, right_side, prolong
    )
    side_message = from_side(message)
    received = swapped(mine + swapped(theirs, 1), 2)
    received_other = swapped(received, 1)
    side, half, own_image, rt_high, rt_low = own_step(agg_of, prolong, message, right, pair, swapped(pair, 1))
    keep, send, d_high, d_low = image(own_image, side, received, received_other, side_message)
    image_received = swapped(send, 2)
    ghosts = side_message[WIDE:]
    half, coarse = ghost_step(agg_of, d_high, d_low, half, ghosts, swapped(ghosts, 1), rt_high, rt_low)
    coarse_received = swapped(coarse, 2)
    residual, first = residual_step(agg_of, keep, image_received, rt_high, rt_low)
    base = base_step(smoother, message, residual)
    half, first = lax.optimization_barrier((half, first))
    half_received = swapped(half, 2)
    near, far = from_neighbours(first)
    near, far, coarse_received = lax.optimization_barrier((near, far, coarse_received))
    coarse = summed_regions(coarse, coarse_received)
    m_high, m_low, coarse_op = coarse_operator(agg_of, coarse, swapped(coarse, 1))
    correction = first
    for index in range(COARSE_SWEEPS - 1):
        if index > 0:
            near, far = from_neighbours(correction)
        correction = sweep(m_high, m_low, first, near, correction, far)
    half_received, correction = lax.optimization_barrier((half_received, correction))
    half = summed_regions(half, half_received)
    w_high, w_low = lift_operator(agg_of, half, swapped(half, 1), smoother, prolong)
    near, far = from_neighbours(correction)
    base = lifted(w_high, w_low, base, correction)
    solution = last_step(w_high, w_low, base, near, far)
    return coarse_op, solution.reshape(ROWS, DOF, COLS)


def solution(mesh):
    placed_args = (
        P("slab", "sub", None, None),
        P("slab", None, None),
        P("slab", None, None),
        P("slab", None, None),
        P(),
        P("slab", "sub"),
        P(),
        P(),
    )
    return jax.shard_map(
        per_device,
        mesh=mesh,
        in_specs=placed_args,
        out_specs=(P("slab", "sub", None, None), P("slab", None, "sub")),
        check_vma=False,
    )
```

time: 478 us -> 72.2 us (0.15)
  waiting for transfers between devices: 196 us -> 34.7 us
  local copies, waits for them, and re-layouts: 109 us -> 0.02 us
  matrix products: 106 us -> 0 us
  Pallas kernels: 0 us -> 15.2 us
  other arithmetic: 15.2 us -> 0.25 us
  between operations: 14.5 us -> 0.86 us
  starting transfers between devices: 31.1 us -> 20.5 us
    dot_general x44 -> x0, matrix products: 106 us -> none  [the longest x32 67.3 us: add_block(): jnp.einsum('eab,ebn->ean', block_now, field_rows[slot_ids], precision=hig...]
    psum x2 -> x0, waiting for transfers between devices: 96 us -> none  [the longest x1 61.2 us: per_device(): coarse_full = lax.psum(coarse_part, 'sub')]
    gather x41 -> x0, local copies, waits for them, and re-layouts: 90.4 us -> none  [the longest x32 80.1 us: add_block(): field_rows[slot_ids]]
    ppermute x10 -> x17, waiting for transfers between devices: 99.8 us -> 34.7 us  [the longest x10 18.4 us: swapped(): return lax.ppermute(value, 'sub', [(i, i ^ bit) for i in range(size)])]
    pallas_call x0 -> x12, Pallas kernels: none -> 15.2 us  [the longest x1 4.14 us: start_step(): pl.pallas_call(start_kernel, in_specs=[HBM] * 7, out_specs=[VMEM] * 5, ou...]
    ppermute x10 -> x17, starting transfers between devices: 31 us -> 20.5 us  [the longest x3 7.97 us: from_neighbours(): far = lax.ppermute(value, 'slab', swaps(size, 1))]
    concatenate x6 -> x2, other arithmetic: 9.45 us -> 0.08 us  [summed_regions(): return jnp.concatenate([near, own, far], axis=1)]
    unnamed x25 -> x6, local copies, waits for them, and re-layouts: 7.59 us -> 0.01 us
  transfers between devices with their start and end apart: 12 -> 17, of which waited for: 7 -> 13; matrix products, arithmetic and copies ran while one was open for 10% -> 0% of each run, Pallas kernels for 0% -> 13%
where the time goes in v3:
time: 72.2 us; the launch traced here: 71.6 us
  waiting for transfers between devices  34.7 us (48%)
  starting transfers between devices  20.5 us (28%)
  Pallas kernels  15.2 us (21%)
  between operations  0.86 us (1%)
    ppermute x10, waiting for transfers between devices, swapped(): return lax.ppermute(value, 'sub', [(i, i ^ bit) for i in range(size)])  18.4 us
    ppermute x3, waiting for transfers between devices, from_neighbours(): far = lax.ppermute(value, 'slab', swaps(size, 1))  8.78 us
    ppermute x3, starting transfers between devices, from_neighbours(): far = lax.ppermute(value, 'slab', swaps(size, 1))  7.97 us
    ppermute x10, starting transfers between devices, swapped(): return lax.ppermute(value, 'sub', [(i, i ^ bit) for i in range(size)])  6.57 us
    ppermute x3, waiting for transfers between devices, from_neighbours(): near = lax.ppermute(value, 'slab', swaps(size, 0))  5.26 us
    pallas_call x1, Pallas kernels, start_step(): pl.pallas_call(start_kernel, in_specs=[HBM] * 7, out_specs=[VMEM] * 5, ou...  4.14 us
    ppermute x1, starting transfers between devices, from_side(): return lax.ppermute(value, ('slab', 'sub'), pairs)  3.39 us
    ppermute x3, starting transfers between devices, from_neighbours(): near = lax.ppermute(value, 'slab', swaps(size, 0))  2.6 us
  transfers between devices with their start and end apart: 17, of which 13 were waited for; matrix products, arithmetic and copies ran while one was open for 0% of the time, Pallas kernels for 13%

profile of v3, /device:TPU:8, one launch (start us, length us, event | category | flops | bytes accessed | tf_op | source)
XLA Modules:
  0.0 71.6 jit_solution(11495085322314462020)
XLA Ops:
  0.6 0.0 copy-start
  0.6 0.0 copy-start.2
  0.7 4.1 %start_step.1 = (f32[512,1024]{1,0:T(8,128)S(1)}, f32[256,512]{1,0:T(8,128)S(1)}, f32[256,512]{1,0:T(8,128)S(1)}, f32[576,256]{1,0:T(8,128)S(1)}, f32[512,128]{1,0:T(8,128)S(1)}) custom-call(s32[8,16]{1,0:T(8,128)} %col_hbm.1, s32[8,4,2,8]{3,2,1,0:T(2,128)} %rows_hbm.1, s32[4,2,8]{2,1,0:T(2,128)} %bitcast.3, f32[8,16,64,64]{3,2,1,0:T(8,128)} %blocks_hbm.1, ...), custom_call_target="tpu_custom_call" | custom-call | tf_op jit(solution)/shard_map/start_step/pallas_call | solution.py:156
  4.8 0.1 collective-permute-start
  4.9 0.5 collective-permute-start.1
  5.4 4.4 %collective-permute-done.1 = f32[256,512]{1,0:T(8,128)S(1)} collective-permute-done((f32[256,512]{1,0:T(8,128)S(1)}, f32[256,512]{1,0:T(8,128)S(1)}, u32[]{:S(2)}, u32[]{:S(2)}) %collective-permute-start.1) | collective-permute-done | bytes 524320 | tf_op jit(solution)/shard_map/ppermute | solution.py:484
  9.8 0.1 add.9
  9.9 1.6 %collective-permute-start.2 = (f32[256,512]{1,0:T(8,128)S(1)}, f32[256,512]{1,0:T(8,128)S(1)}, u32[]{:S(2)}, u32[]{:S(2)}) collective-permute-start(f32[256,512]{1,0:T(8,128)S(1)} %add.9), channel_id=1, source_target_pairs={{0,2},{1,3},{2,0},{3,1},{4,6},{5,7},{6,4},{7,5},{8,10},{9,11},{10,... | collective-permute-start | bytes 1572872 | tf_op jit(solution)/shard_map/ppermute | solution.py:484
  11.4 3.4 %collective-permute-start.4 = (f32[576,256]{1,0:T(8,128)S(1)}, f32[576,256]{1,0:T(8,128)S(1)}, u32[]{:S(2)}, u32[]{:S(2)}) collective-permute-start(f32[576,256]{1,0:T(8,128)S(1)} %get-tuple-element.32.field.message), channel_id=1, source_target_pairs={{0,4},{8,12},{16,20},{24,28},{4,0},{12,8},{20,16},{28,24},{1,5},{9... | collective-permute-start | bytes 1769480 | tf_op jit(solution)/shard_map/ppermute | solution.py:479
  14.8 9.1 %collective-permute-done.2.received = f32[256,512]{1,0:T(8,128)S(1)} collective-permute-done((f32[256,512]{1,0:T(8,128)S(1)}, f32[256,512]{1,0:T(8,128)S(1)}, u32[]{:S(2)}, u32[]{:S(2)}) %collective-permute-start.2) | collective-permute-done | bytes 524320 | tf_op jit(solution)/shard_map/ppermute | solution.py:484
  23.9 0.0 collective-permute-start.3
  23.9 0.0 collective-permute-done.pair_other
  23.9 0.0 copy-done
  23.9 0.0 copy-done.2
  23.9 2.3 %own_step.1 = (f32[512,512]{1,0:T(8,128)S(1)}, f32[512,128]{1,0:T(8,128)S(1)}, f32[512,256]{1,0:T(8,128)S(1)}, bf16[256,512]{1,0:T(8,128)(2,1)S(1)}, bf16[256,512]{1,0:T(8,128)(2,1)S(1)}) custom-call(s32[64]{0:T(128)S(1)} %copy-done.2, f32[8,64,64]{2,1,0:T(8,128)S(1)} %copy-done, f32[576,256]{1,0:T(8,128)S(1)} %get-tuple-element.32.field.message, ...), custom_call_target="tpu_custom_call" | custom-call | tf_op jit(solution)/shard_map/own_step/pallas_call | solution.py:224
  26.2 2.2 %collective-permute-done.4.message = f32[576,256]{1,0:T(8,128)S(1)} collective-permute-done((f32[576,256]{1,0:T(8,128)S(1)}, f32[576,256]{1,0:T(8,128)S(1)}, u32[]{:S(2)}, u32[]{:S(2)}) %collective-permute-start.4) | collective-permute-done | bytes 589856 | tf_op jit(solution)/shard_map/ppermute | solution.py:479
  28.4 0.0 collective-permute-done.3.received_other
  28.4 0.7 image.1
  29.1 1.5 %collective-permute-start.6 = (f32[512,128]{1,0:T(8,128)S(1)}, f32[512,128]{1,0:T(8,128)S(1)}, u32[]{:S(2)}, u32[]{:S(2)}) collective-permute-start(f32[512,128]{1,0:T(8,128)S(1)} %get-tuple-element.47), channel_id=1, source_target_pairs={{0,2},{1,3},{2,0},{3,1},{4,6},{5,7},{6,4},{7,5},{8,10},{9,11},{10,... | collective-permute-start | bytes 786440 | tf_op jit(solution)/shard_map/ppermute | solution.py:484
  30.6 0.0 collective-permute-start.5
  30.6 1.2 %collective-permute-done.5.other = f32[64,256]{1,0:T(8,128)S(1)} collective-permute-done((f32[64,256]{1,0:T(8,128)S(1)}, f32[64,256]{1,0:T(8,128)S(1)}, u32[]{:S(2)}, u32[]{:S(2)}) %collective-permute-start.5) | collective-permute-done | bytes 65568 | tf_op jit(solution)/shard_map/ppermute | solution.py:484
  31.9 1.9 %ghost_step.1 = (f32[512,256]{1,0:T(8,128)S(1)}, f32[256,256]{1,0:T(8,128)S(1)}) custom-call(s32[64]{0:T(128)S(1)} %copy-done.2, bf16[512,512]{1,0:T(8,128)(2,1)S(1)} %get-tuple-element.39.d_high, bf16[512,512]{1,0:T(8,128)(2,1)S(1)} %get-tuple-element.40.d_low, f32[512,128]{1,0:T(8,128)S(1)} %get-tuple-element.41.own_half, f32[64,256]{1,0:T(8,128)S(1)} %slice.40.mine, ...), custom_call_target="tpu_custom_call" | custom-call | tf_op jit(solution)/shard_map/ghost_step/pallas_call | solution.py:285
  33.7 0.7 collective-permute-start.9
  34.4 2.0 %collective-permute-done.6.received = f32[512,128]{1,0:T(8,128)S(1)} collective-permute-done((f32[512,128]{1,0:T(8,128)S(1)}, f32[512,128]{1,0:T(8,128)S(1)}, u32[]{:S(2)}, u32[]{:S(2)}) %collective-permute-start.6) | collective-permute-done | bytes 262176 | tf_op jit(solution)/shard_map/ppermute | solution.py:484
  36.4 0.8 %residual_step.1 = (f32[512,128]{1,0:T(8,128)S(1)}, f32[256,128]{1,0:T(8,128)S(1)}) custom-call(s32[64]{0:T(128)S(1)} %copy-done.2, f32[512,128]{1,0:T(8,128)S(1)} %get-tuple-element.46.keep, f32[512,128]{1,0:T(8,128)S(1)} %collective-permute-done.6.received, bf16[256,512]{1,0:T(8,128)(2,1)S(1)} %get-tuple-element.42.rt_high, ...), custom_call_target="tpu_custom_call" | custom-call | tf_op jit(solution)/shard_map/residual_step/pallas_call | solution.py:380
  37.2 1.6 %collective-permute-start.7 = (f32[256,128]{1,0:T(8,128)S(1)}, f32[256,128]{1,0:T(8,128)S(1)}, u32[]{:S(2)}, u32[]{:S(2)}) collective-permute-start(f32[256,128]{1,0:T(8,128)S(1)} %get-tuple-element.49.first.own), channel_id=1, source_target_pairs={{0,4},{8,12},{16,20},{24,28},{4,0},{12,8},{20,16},{28,24},{1,5},{9... | collective-permute-start | bytes 393224 | tf_op jit(solution)/shard_map/ppermute | solution.py:470
  38.8 3.2 %collective-permute-start.8 = (f32[256,128]{1,0:T(8,128)S(1)}, f32[256,128]{1,0:T(8,128)S(1)}, u32[]{:S(2)}, u32[]{:S(2)}) collective-permute-start(f32[256,128]{1,0:T(8,128)S(1)} %get-tuple-element.49.first.own), channel_id=1, source_target_pairs={{4,8},{12,16},{20,24},{8,4},{16,12},{24,20},{5,9},{13,17},{21,25},... | collective-permute-start | bytes 393224 | tf_op jit(solution)/shard_map/ppermute | solution.py:469
  42.0 0.2 collective-permute-done.9
  42.2 1.5 %collective-permute-done.7.near = f32[256,128]{1,0:T(8,128)S(1)} collective-permute-done((f32[256,128]{1,0:T(8,128)S(1)}, f32[256,128]{1,0:T(8,128)S(1)}, u32[]{:S(2)}, u32[]{:S(2)}) %collective-permute-start.7) | collective-permute-done | bytes 131104 | tf_op jit(solution)/shard_map/ppermute | solution.py:470
  43.7 2.9 %collective-permute-done.8.far = f32[256,128]{1,0:T(8,128)S(1)} collective-permute-done((f32[256,128]{1,0:T(8,128)S(1)}, f32[256,128]{1,0:T(8,128)S(1)}, u32[]{:S(2)}, u32[]{:S(2)}) %collective-permute-start.8) | collective-permute-done | bytes 131104 | tf_op jit(solution)/shard_map/ppermute | solution.py:469
  46.6 0.1 collective-permute-start.10
  46.7 2.1 %collective-permute-start.11 = (f32[512,256]{1,0:T(8,128)S(1)}, f32[512,256]{1,0:T(8,128)S(1)}, u32[]{:S(2)}, u32[]{:S(2)}) collective-permute-start(f32[512,256]{1,0:T(8,128)S(1)} %get-tuple-element.52), channel_id=1, source_target_pairs={{0,2},{1,3},{2,0},{3,1},{4,6},{5,7},{6,4},{7,5},{8,10},{9,11},{10,... | collective-permute-start | bytes 1572872 | tf_op jit(solution)/shard_map/ppermute | solution.py:484
  48.8 0.0 collective-permute-done.10.other
  48.8 1.6 %coarse_operator.1 = (bf16[256,768]{1,0:T(8,128)(2,1)S(1)}, bf16[256,768]{1,0:T(8,128)(2,1)S(1)}, f32[4,3,64,64]{3,2,1,0:T(8,128)}) custom-call(s32[64]{0:T(128)S(1)} %copy-done.2, f32[256,384]{1,0:T(8,128)S(1)} %pad_maximum_fusion.1.mine, f32[256,384]{1,0:T(8,128)S(1)} %collective-permute-done.10.other), custom_call_target="tpu_custom_call" | custom-call | tf_op jit(solution)/shard_map/coarse_operator/pallas_call | solution.py:332
  50.4 0.4 sweep.2.own
  50.8 0.0 copy-start.1
  50.8 0.5 collective-permute-start.12
  51.3 2.3 %collective-permute-start.13 = (f32[256,128]{1,0:T(8,128)S(1)}, f32[256,128]{1,0:T(8,128)S(1)}, u32[]{:S(2)}, u32[]{:S(2)}) collective-permute-start(f32[256,128]{1,0:T(8,128)S(1)} %sweep.2.own), channel_id=1, source_target_pairs={{4,8},{12,16},{20,24},{8,4},{16,12},{24,20},{5,9},{13,17},{21,25},... | collective-permute-start | bytes 393224 | tf_op jit(solution)/shard_map/ppermute | solution.py:469
  53.7 2.8 %collective-permute-done.12.near = f32[256,128]{1,0:T(8,128)S(1)} collective-permute-done((f32[256,128]{1,0:T(8,128)S(1)}, f32[256,128]{1,0:T(8,128)S(1)}, u32[]{:S(2)}, u32[]{:S(2)}) %collective-permute-start.12) | collective-permute-done | bytes 131104 | tf_op jit(solution)/shard_map/ppermute | solution.py:470
  56.5 3.0 %collective-permute-done.13.far = f32[256,128]{1,0:T(8,128)S(1)} collective-permute-done((f32[256,128]{1,0:T(8,128)S(1)}, f32[256,128]{1,0:T(8,128)S(1)}, u32[]{:S(2)}, u32[]{:S(2)}) %collective-permute-start.13) | collective-permute-done | bytes 131104 | tf_op jit(solution)/shard_map/ppermute | solution.py:469
  59.4 0.4 sweep.3.own
  59.8 1.6 %collective-permute-done.11 = f32[512,256]{1,0:T(8,128)S(1)} collective-permute-done((f32[512,256]{1,0:T(8,128)S(1)}, f32[512,256]{1,0:T(8,128)S(1)}, u32[]{:S(2)}, u32[]{:S(2)}) %collective-permute-start.11) | collective-permute-done | bytes 524320 | tf_op jit(solution)/shard_map/ppermute | solution.py:484
  61.3 0.1 slice_select_fusion.1
  61.4 0.1 pad_maximum_fusion.mine
  61.5 0.1 collective-permute-start.14
  61.5 0.5 collective-permute-start.15
  62.1 2.5 %collective-permute-start.16 = (f32[256,128]{1,0:T(8,128)S(1)}, f32[256,128]{1,0:T(8,128)S(1)}, u32[]{:S(2)}, u32[]{:S(2)}) collective-permute-start(f32[256,128]{1,0:T(8,128)S(1)} %sweep.3.own), channel_id=1, source_target_pairs={{4,8},{12,16},{20,24},{8,4},{16,12},{24,20},{5,9},{13,17},{21,25},... | collective-permute-start | bytes 393224 | tf_op jit(solution)/shard_map/ppermute | solution.py:469
  64.5 0.0 copy-done.1
  64.5 0.3 base_step.1.base
  64.8 0.0 collective-permute-done.14.other
  64.8 1.4 %lift_operator.1 = (bf16[512,768]{1,0:T(8,128)(2,1)S(1)}, bf16[512,768]{1,0:T(8,128)(2,1)S(1)}) custom-call(s32[64]{0:T(128)S(1)} %copy-done.2, f32[512,384]{1,0:T(8,128)S(1)} %pad_maximum_fusion.mine, f32[512,384]{1,0:T(8,128)S(1)} %collective-permute-done.14.other, f32[8,64,64]{2,1,0:T(8,128)S(1)} %copy-done.1, f32[8,64,64]{2,1,0:T(8,128)S(1)} %copy-done), custom_call_target="tpu_custom_call" | custom-call | tf_op jit(solution)/shard_map/lift_operator/pallas_call | solution.py:363
  66.2 0.3 lifted.1.base
  66.5 1.0 %collective-permute-done.15.near = f32[256,128]{1,0:T(8,128)S(1)} collective-permute-done((f32[256,128]{1,0:T(8,128)S(1)}, f32[256,128]{1,0:T(8,128)S(1)}, u32[]{:S(2)}, u32[]{:S(2)}) %collective-permute-start.15) | collective-permute-done | bytes 131104 | tf_op jit(solution)/shard_map/ppermute | solution.py:470
  67.4 3.0 %collective-permute-done.16.far = f32[256,128]{1,0:T(8,128)S(1)} collective-permute-done((f32[256,128]{1,0:T(8,128)S(1)}, f32[256,128]{1,0:T(8,128)S(1)}, u32[]{:S(2)}, u32[]{:S(2)}) %collective-permute-start.16) | collective-permute-done | bytes 131104 | tf_op jit(solution)/shard_map/ppermute | solution.py:469
  70.4 1.2 %last_step.1 = f32[512,128]{1,0:T(8,128)} custom-call(bf16[512,768]{1,0:T(8,128)(2,1)S(1)} %get-tuple-element.58.w_high, bf16[512,768]{1,0:T(8,128)(2,1)S(1)} %get-tuple-element.59.w_low, f32[512,128]{1,0:T(8,128)S(1)} %lifted.1.base, f32[256,128]{1,0:T(8,128)S(1)} %collective-permute-done.15.near, f32[256,128]{1,0:T(8,128)S(1)} %collective-permute-done.16.far), custom_call_target="tpu_custom_call" | custom-call | tf_op jit(solution)/shard_map/last_step/pallas_call | solution.py:452
  (3 shorter events, 0.1 us)
Async XLA Ops:
  0.6 23.3 %copy-start = (f32[8,64,64]{2,1,0:T(8,128)S(1)}, f32[8,64,64]{2,1,0:T(8,128)}, u32[]{:S(2)}) copy-start(f32[8,64,64]{2,1,0:T(8,128)} %prolong.3) | copy-start | bytes 393220
  0.6 23.3 %copy-start.2 = (s32[64]{0:T(128)S(1)}, s32[64]{0:T(128)}, u32[]{:S(2)}) copy-start(s32[64]{0:T(128)} %agg_of.9) | copy-start | bytes 772
  4.8 19.1 %collective-permute-start = (f32[512,1024]{1,0:T(8,128)S(1)}, f32[512,1024]{1,0:T(8,128)S(1)}, u32[]{:S(2)}, u32[]{:S(2)}) collective-permute-start(f32[512,1024]{1,0:T(8,128)S(1)} %get-tuple-element.34.pair), channel_id=1, source_target_pairs={{0,1},{1,0},{2,3},{3,2},{4,5},{5,4},{6,7},{7,6},{8,9},{9,8},{10,11... | collective-permute-start | bytes 6291464 | tf_op jit(solution)/shard_map/ppermute | solution.py:484
  4.9 4.9 %collective-permute-start.1 = (f32[256,512]{1,0:T(8,128)S(1)}, f32[256,512]{1,0:T(8,128)S(1)}, u32[]{:S(2)}, u32[]{:S(2)}) collective-permute-start(f32[256,512]{1,0:T(8,128)S(1)} %get-tuple-element.38), channel_id=1, source_target_pairs={{0,1},{1,0},{2,3},{3,2},{4,5},{5,4},{6,7},{7,6},{8,9},{9,8},{10,11... | collective-permute-start | bytes 1572872 | tf_op jit(solution)/shard_map/ppermute | solution.py:484
  9.9 14.0 %collective-permute-start.2 = (f32[256,512]{1,0:T(8,128)S(1)}, f32[256,512]{1,0:T(8,128)S(1)}, u32[]{:S(2)}, u32[]{:S(2)}) collective-permute-start(f32[256,512]{1,0:T(8,128)S(1)} %add.9), channel_id=1, source_target_pairs={{0,2},{1,3},{2,0},{3,1},{4,6},{5,7},{6,4},{7,5},{8,10},{9,11},{10,... | collective-permute-start | bytes 1572872 | tf_op jit(solution)/shard_map/ppermute | solution.py:484
  11.4 17.0 %collective-permute-start.4 = (f32[576,256]{1,0:T(8,128)S(1)}, f32[576,256]{1,0:T(8,128)S(1)}, u32[]{:S(2)}, u32[]{:S(2)}) collective-permute-start(f32[576,256]{1,0:T(8,128)S(1)} %get-tuple-element.32.field.message), channel_id=1, source_target_pairs={{0,4},{8,12},{16,20},{24,28},{4,0},{12,8},{20,16},{28,24},{1,5},{9... | collective-permute-start | bytes 1769480 | tf_op jit(solution)/shard_map/ppermute | solution.py:479
  23.9 4.5 %collective-permute-start.3 = (f32[256,512]{1,0:T(8,128)S(1)}, f32[256,512]{1,0:T(8,128)S(1)}, u32[]{:S(2)}, u32[]{:S(2)}) collective-permute-start(f32[256,512]{1,0:T(8,128)S(1)} %collective-permute-done.2.received), channel_id=1, source_target_pairs={{0,1},{1,0},{2,3},{3,2},{4,5},{5,4},{6,7},{7,6},{8,9},{9,8},{10,11... | collective-permute-start | bytes 1572872 | tf_op jit(solution)/shard_map/ppermute | solution.py:484
  29.1 7.3 %collective-permute-start.6 = (f32[512,128]{1,0:T(8,128)S(1)}, f32[512,128]{1,0:T(8,128)S(1)}, u32[]{:S(2)}, u32[]{:S(2)}) collective-permute-start(f32[512,128]{1,0:T(8,128)S(1)} %get-tuple-element.47), channel_id=1, source_target_pairs={{0,2},{1,3},{2,0},{3,1},{4,6},{5,7},{6,4},{7,5},{8,10},{9,11},{10,... | collective-permute-start | bytes 786440 | tf_op jit(solution)/shard_map/ppermute | solution.py:484
  30.6 1.3 %collective-permute-start.5 = (f32[64,256]{1,0:T(8,128)S(1)}, f32[64,256]{1,0:T(8,128)S(1)}, u32[]{:S(2)}, u32[]{:S(2)}) collective-permute-start(f32[64,256]{1,0:T(8,128)S(1)} %slice.40.mine), channel_id=1, source_target_pairs={{0,1},{1,0},{2,3},{3,2},{4,5},{5,4},{6,7},{7,6},{8,9},{9,8},{10,11... | collective-permute-start | bytes 196616 | tf_op jit(solution)/shard_map/ppermute | solution.py:484
  33.7 8.4 %collective-permute-start.9 = (f32[256,256]{1,0:T(8,128)S(1)}, f32[256,256]{1,0:T(8,128)S(1)}, u32[]{:S(2)}, u32[]{:S(2)}) collective-permute-start(f32[256,256]{1,0:T(8,128)S(1)} %get-tuple-element.44), channel_id=1, source_target_pairs={{0,2},{1,3},{2,0},{3,1},{4,6},{5,7},{6,4},{7,5},{8,10},{9,11},{10,... | collective-permute-start | bytes 786440 | tf_op jit(solution)/shard_map/ppermute | solution.py:484
  37.2 6.4 %collective-permute-start.7 = (f32[256,128]{1,0:T(8,128)S(1)}, f32[256,128]{1,0:T(8,128)S(1)}, u32[]{:S(2)}, u32[]{:S(2)}) collective-permute-start(f32[256,128]{1,0:T(8,128)S(1)} %get-tuple-element.49.first.own), channel_id=1, source_target_pairs={{0,4},{8,12},{16,20},{24,28},{4,0},{12,8},{20,16},{28,24},{1,5},{9... | collective-permute-start | bytes 393224 | tf_op jit(solution)/shard_map/ppermute | solution.py:470
  38.8 7.7 %collective-permute-start.8 = (f32[256,128]{1,0:T(8,128)S(1)}, f32[256,128]{1,0:T(8,128)S(1)}, u32[]{:S(2)}, u32[]{:S(2)}) collective-permute-start(f32[256,128]{1,0:T(8,128)S(1)} %get-tuple-element.49.first.own), channel_id=1, source_target_pairs={{4,8},{12,16},{20,24},{8,4},{16,12},{24,20},{5,9},{13,17},{21,25},... | collective-permute-start | bytes 393224 | tf_op jit(solution)/shard_map/ppermute | solution.py:469
  46.6 2.2 %collective-permute-start.10 = (f32[256,384]{1,0:T(8,128)S(1)}, f32[256,384]{1,0:T(8,128)S(1)}, u32[]{:S(2)}, u32[]{:S(2)}) collective-permute-start(f32[256,384]{1,0:T(8,128)S(1)} %pad_maximum_fusion.1.mine), channel_id=1, source_target_pairs={{0,1},{1,0},{2,3},{3,2},{4,5},{5,4},{6,7},{7,6},{8,9},{9,8},{10,11... | collective-permute-start | bytes 1179656 | tf_op jit(solution)/shard_map/ppermute | solution.py:484
  46.7 14.6 %collective-permute-start.11 = (f32[512,256]{1,0:T(8,128)S(1)}, f32[512,256]{1,0:T(8,128)S(1)}, u32[]{:S(2)}, u32[]{:S(2)}) collective-permute-start(f32[512,256]{1,0:T(8,128)S(1)} %get-tuple-element.52), channel_id=1, source_target_pairs={{0,2},{1,3},{2,0},{3,1},{4,6},{5,7},{6,4},{7,5},{8,10},{9,11},{10,... | collective-permute-start | bytes 1572872 | tf_op jit(solution)/shard_map/ppermute | solution.py:484
  50.8 13.7 %copy-start.1 = (f32[8,64,64]{2,1,0:T(8,128)S(1)}, f32[8,64,64]{2,1,0:T(8,128)}, u32[]{:S(2)}) copy-start(f32[8,64,64]{2,1,0:T(8,128)} %smoother.3) | copy-start | bytes 393220
  50.8 5.7 %collective-permute-start.12 = (f32[256,128]{1,0:T(8,128)S(1)}, f32[256,128]{1,0:T(8,128)S(1)}, u32[]{:S(2)}, u32[]{:S(2)}) collective-permute-start(f32[256,128]{1,0:T(8,128)S(1)} %sweep.2.own), channel_id=1, source_target_pairs={{0,4},{8,12},{16,20},{24,28},{4,0},{12,8},{20,16},{28,24},{1,5},{9... | collective-permute-start | bytes 393224 | tf_op jit(solution)/shard_map/ppermute | solution.py:470
  51.3 8.1 %collective-permute-start.13 = (f32[256,128]{1,0:T(8,128)S(1)}, f32[256,128]{1,0:T(8,128)S(1)}, u32[]{:S(2)}, u32[]{:S(2)}) collective-permute-start(f32[256,128]{1,0:T(8,128)S(1)} %sweep.2.own), channel_id=1, source_target_pairs={{4,8},{12,16},{20,24},{8,4},{16,12},{24,20},{5,9},{13,17},{21,25},... | collective-permute-start | bytes 393224 | tf_op jit(solution)/shard_map/ppermute | solution.py:469
  61.5 3.3 %collective-permute-start.14 = (f32[512,384]{1,0:T(8,128)S(1)}, f32[512,384]{1,0:T(8,128)S(1)}, u32[]{:S(2)}, u32[]{:S(2)}) collective-permute-start(f32[512,384]{1,0:T(8,128)S(1)} %pad_maximum_fusion.mine), channel_id=1, source_target_pairs={{0,1},{1,0},{2,3},{3,2},{4,5},{5,4},{6,7},{7,6},{8,9},{9,8},{10,11... | collective-permute-start | bytes 2359304 | tf_op jit(solution)/shard_map/ppermute | solution.py:484
  61.5 5.9 %collective-permute-start.15 = (f32[256,128]{1,0:T(8,128)S(1)}, f32[256,128]{1,0:T(8,128)S(1)}, u32[]{:S(2)}, u32[]{:S(2)}) collective-permute-start(f32[256,128]{1,0:T(8,128)S(1)} %sweep.3.own), channel_id=1, source_target_pairs={{0,4},{8,12},{16,20},{24,28},{4,0},{12,8},{20,16},{28,24},{1,5},{9... | collective-permute-start | bytes 393224 | tf_op jit(solution)/shard_map/ppermute | solution.py:470
  62.1 8.3 %collective-permute-start.16 = (f32[256,128]{1,0:T(8,128)S(1)}, f32[256,128]{1,0:T(8,128)S(1)}, u32[]{:S(2)}, u32[]{:S(2)}) collective-permute-start(f32[256,128]{1,0:T(8,128)S(1)} %sweep.3.own), channel_id=1, source_target_pairs={{4,8},{12,16},{20,24},{8,4},{16,12},{24,20},{5,9},{13,17},{21,25},... | collective-permute-start | bytes 393224 | tf_op jit(solution)/shard_map/ppermute | solution.py:469

commit v4 on v3

--- a/solution.py
+++ b/solution.py
@@ -265,7 +265,7 @@
     )(own_image, side, received, received_other, message)
 
 
-def ghost_kernel(agg_of, d_high, d_low, own_half, mine, other, rt_high, rt_low, half_ref, coarse_ref, q_high, q_low):
+def ghost_kernel(agg_of, d_high, d_low, mine, other, half_ref, q_high, q_low):
     _, near, far = neighbours()
     sub = lax.axis_index("sub")
     core = sub & 1
@@ -276,21 +276,19 @@
         high, low = halves(placed(piece, agg_of[start + r] - 2 * core))
         q_high[span(r), :] = high
         q_low[span(r), :] = low
-    half_ref[:, :PAIR] = own_half[...]
-    half_ref[:, PAIR:] = product((d_high[...], d_low[...]), (q_high[...], q_low[...]))
-    coarse_ref[...] = product((rt_high[...], rt_low[...]), halves(half_ref[...]))
-
-
-def ghost_step(agg_of, d_high, d_low, own_half, mine, other, rt_high, rt_low):
+    half_ref[...] = product((d_high[...], d_low[...]), (q_high[...], q_low[...]))
+
+
+def ghost_step(agg_of, d_high, d_low, mine, other):
     return pl.pallas_call(
         ghost_kernel,
-        in_specs=[SMEM] + [VMEM] * 7,
-        out_specs=[VMEM] * 2,
-        out_shape=[shape(WIDE, 2 * PAIR), shape(COARSE, 2 * PAIR)],
+        in_specs=[SMEM] + [VMEM] * 4,
+        out_specs=VMEM,
+        out_shape=shape(WIDE, PAIR),
         scratch_shapes=[pltpu.VMEM((WIDE, PAIR), BF16)] * 2,
         compiler_params=params(),
         name="ghost_step",
-    )(agg_of, d_high, d_low, own_half, mine, other, rt_high, rt_low)
+    )(agg_of, d_high, d_low, mine, other)
 
 
 def scaled_by_weight(agg_of, value):
@@ -305,7 +303,26 @@
     return jnp.concatenate(pieces, axis=0)
 
 
-def coarse_kernel(agg_of, mine, other, m_high, m_low, op_ref, natural):
+def coarse_kernel(own, own_received, side, side_received, rt_high, rt_low, g_ref, coarse_ref):
+    is_near = ((lax.axis_index("sub") >> 1) & 1) == 0
+    g_ref[:, span(0, PAIR)] = jnp.where(is_near, side[...], side_received[...])
+    g_ref[:, span(1, PAIR)] = own[...] + own_received[...]
+    g_ref[:, span(2, PAIR)] = jnp.where(is_near, side_received[...], side[...])
+    coarse_ref[...] = product((rt_high[...], rt_low[...]), halves(g_ref[...]))
+
+
+def coarse_half(own, own_received, side, side_received, rt_high, rt_low):
+    return pl.pallas_call(
+        coarse_kernel,
+        in_specs=[VMEM] * 6,
+        out_specs=[VMEM] * 2,
+        out_shape=[shape(WIDE, 3 * PAIR), shape(COARSE, 3 * PAIR)],
+        compiler_params=params(),
+        name="coarse_half",
+    )(own, own_received, side, side_received, rt_high, rt_low)
+
+
+def share_kernel(mine, other, op_ref, natural):
     sub = lax.axis_index("sub")
     odd = lax.axis_index("slab") & 1
     is_first = (sub & 1) == 0
@@ -315,9 +332,6 @@
     for region, place in enumerate(places):
         value = jnp.concatenate([first[:, span(region, PAIR)], second[:, span(region, PAIR)]], axis=1)
         natural[:, aligned(place, COARSE)] = value
-        high, low = halves(scaled_by_weight(agg_of, value))
-        m_high[:, span(region, COARSE)] = high
-        m_low[:, span(region, COARSE)] = low
     share = op_ref.shape[1]
     for k in range(BANDS // share):
 
@@ -328,46 +342,35 @@
                     op_ref[a, q] = natural[span(a), span(k * share + q)]
 
 
-def coarse_operator(agg_of, mine, other):
-    return pl.pallas_call(
-        coarse_kernel,
-        in_specs=[SMEM] + [VMEM] * 2,
-        out_specs=[VMEM] * 3,
-        out_shape=[shape(COARSE, 3 * COARSE, dtype=BF16)] * 2 + [shape(GROUPS, BANDS // SUBS, DOF, DOF)],
+def coarse_share(mine, other):
+    return pl.pallas_call(
+        share_kernel,
+        in_specs=[VMEM] * 2,
+        out_specs=VMEM,
+        out_shape=shape(GROUPS, BANDS // SUBS, DOF, DOF),
         scratch_shapes=[pltpu.VMEM((COARSE, 3 * COARSE), F32)],
         compiler_params=params(),
-        name="coarse_operator",
-    )(agg_of, mine, other)
-
-
-def lift_kernel(agg_of, mine, other, smoother, prolong, w_high, w_low):
+        name="coarse_share",
+    )(mine, other)
+
+
+def lift_kernel(agg_of, g_half, smoother, prolong, w_ref):
     start = lax.axis_index("slab") * ROWS
-    is_first = (lax.axis_index("sub") & 1) == 0
+    core = lax.axis_index("sub") & 1
     for e in range(ROWS):
-        smooth = halves(smoother[e])
-        from_mine = product(smooth, halves(mine[span(e), :]))
-        from_other = product(smooth, halves(other[span(e), :]))
-        first = jnp.where(is_first, from_mine, from_other)
-        second = jnp.where(is_first, from_other, from_mine)
-        for region in range(3):
-            for t, value in enumerate((first, second)):
-                value = -value[:, span(region, PAIR)]
-                if region == 1:
-                    value += placed(prolong[e], agg_of[start + e] - 2 * t)
-                high, low = halves(value)
-                w_high[span(e), span(2 * region + t, PAIR)] = high
-                w_low[span(e), span(2 * region + t, PAIR)] = low
-
-
-def lift_operator(agg_of, mine, other, smoother, prolong):
+        w_ref[span(e), :] = -product(halves(smoother[e]), halves(g_half[span(e), :]))
+        w_ref[span(e), span(1, PAIR)] += placed(prolong[e], agg_of[start + e] - 2 * core)
+
+
+def lift_half(agg_of, g_half, smoother, prolong):
     return pl.pallas_call(
         lift_kernel,
-        in_specs=[SMEM] + [VMEM] * 4,
-        out_specs=[VMEM] * 2,
-        out_shape=[shape(WIDE, 3 * COARSE, dtype=BF16)] * 2,
-        compiler_params=params(),
-        name="lift_operator",
-    )(agg_of, mine, other, smoother, prolong)
+        in_specs=[SMEM] + [VMEM] * 3,
+        out_specs=VMEM,
+        out_shape=shape(WIDE, 3 * PAIR),
+        compiler_params=params(),
+        name="lift_half",
+    )(agg_of, g_half, smoother, prolong)
 
 
 def residual_kernel(agg_of, keep, received, rt_high, rt_low, residual_ref, first_ref):
@@ -404,48 +407,56 @@
     )(smoother, message, residual)
 
 
-def applied(op_high, op_low, fields):
+def core_parts(*fields):
+    core = lax.axis_index("sub") & 1
+    for which in (core, 1 - core):
+        yield jnp.concatenate([field[aligned(which, PAIR), :] for field in fields], axis=0)
+
+
+def sweep_kernel(agg_of, mine, other, first, near, own, far, next_ref):
     total = None
-    for region, field in fields:
-        lanes = span(region, COARSE)
-        part = narrow_product((op_high[:, lanes], op_low[:, lanes]), field[...])
+    for operator, field in zip((mine, other), core_parts(near, own, far)):
+        part = narrow_product(halves(operator[...]), field)
         total = part if total is None else total + part
-    return total
-
-
-def sweep_kernel(m_high, m_low, first, near, own, far, next_ref):
-    fields = ((0, near), (1, own), (2, far))
-    next_ref[...] = own[...] + first[...] - applied(m_high, m_low, fields)
-
-
-def sweep(m_high, m_low, first, near, own, far):
+    next_ref[...] = own[...] + first[...] - scaled_by_weight(agg_of, total)
+
+
+def sweep(agg_of, mine, other, first, near, own, far):
     return pl.pallas_call(
         sweep_kernel,
-        in_specs=[VMEM] * 6,
+        in_specs=[SMEM] + [VMEM] * 6,
         out_specs=VMEM,
         out_shape=shape(COARSE, COLS),
         compiler_params=params(),
         name="sweep",
-    )(m_high, m_low, first, near, own, far)
-
-
-def lifted_kernel(w_high, w_low, base, own, out_ref):
-    out_ref[...] = base[...] + applied(w_high, w_low, ((1, own),))
-
-
-def lifted(w_high, w_low, base, own):
+    )(agg_of, mine, other, first, near, own, far)
+
+
+def lifted_kernel(mine, other, base, own, base_ref, high_ref, low_ref):
+    total = base[...]
+    for place, (operator, field) in enumerate(zip((mine, other), core_parts(own))):
+        total += narrow_product(halves(operator[:, span(1, PAIR)]), field)
+        for t, region in enumerate((0, 2)):
+            high, low = halves(operator[:, span(region, PAIR)])
+            high_ref[:, span(2 * place + t, PAIR)] = high
+            low_ref[:, span(2 * place + t, PAIR)] = low
+    base_ref[...] = total
+
+
+def lifted(mine, other, base, own):
     return pl.pallas_call(
         lifted_kernel,
         in_specs=[VMEM] * 4,
-        out_specs=VMEM,
-        out_shape=shape(WIDE, COLS),
+        out_specs=[VMEM] * 3,
+        out_shape=[shape(WIDE, COLS)] + [shape(WIDE, 2 * COARSE, dtype=BF16)] * 2,
         compiler_params=params(),
         name="lifted",
-    )(w_high, w_low, base, own)
+    )(mine, other, base, own)
 
 
 def last_kernel(w_high, w_low, base, near, far, out_ref):
-    out_ref[...] = base[...] + applied(w_high, w_low, ((0, near), (2, far)))
+    field = jnp.concatenate(list(core_parts(near, far)), axis=0)
+    out_ref[...] = base[...] + narrow_product((w_high[...], w_low[...]), field)
 
 
 def last_step(w_high, w_low, base, near, far):
@@ -484,45 +495,42 @@
     return lax.ppermute(value, "sub", [(i, i ^ bit) for i in range(size)])
 
 
-def summed_regions(mine, received):
-    is_near = ((lax.axis_index("sub") >> 1) & 1) == 0
-    own = mine[:, :PAIR] + received[:, :PAIR]
-    near = jnp.where(is_near, mine[:, PAIR:], received[:, PAIR:])
-    far = jnp.where(is_near, received[:, PAIR:], mine[:, PAIR:])
-    return jnp.concatenate([near, own, far], axis=1)
-
-
 def per_device(fine_blocks, prolong, smoother, right_side, agg_of, col_slot, send_rows, send_count):
     pair, mine, theirs, message, right = start_step(
         col_slot, send_rows, send_count, fine_blocks, smoother, right_side, prolong
     )
     side_message = from_side(message)
-    received = swapped(mine + swapped(theirs, 1), 2)
-    received_other = swapped(received, 1)
-    side, half, own_image, rt_high, rt_low = own_step(agg_of, prolong, message, right, pair, swapped(pair, 1))
-    keep, send, d_high, d_low = image(own_image, side, received, received_other, side_message)
+    theirs = swapped(theirs, 1)
+    received = swapped(mine + theirs, 2)
+    pair, theirs = lax.optimization_barrier((pair, theirs))
+    side, own_half, own_image, rt_high, rt_low = own_step(agg_of, prolong, message, right, pair, swapped(pair, 1))
+    received, side, side_message, own_half = lax.optimization_barrier((received, side, side_message, own_half))
+    own_received = swapped(own_half, 2)
+    keep, send, d_high, d_low = image(own_image, side, received, swapped(received, 1), side_message)
     image_received = swapped(send, 2)
     ghosts = side_message[WIDE:]
-    half, coarse = ghost_step(agg_of, d_high, d_low, half, ghosts, swapped(ghosts, 1), rt_high, rt_low)
-    coarse_received = swapped(coarse, 2)
+    side_half = ghost_step(agg_of, d_high, d_low, ghosts, swapped(ghosts, 1))
+    side_received = swapped(side_half, 2)
     residual, first = residual_step(agg_of, keep, image_received, rt_high, rt_low)
     base = base_step(smoother, message, residual)
-    half, first = lax.optimization_barrier((half, first))
-    half_received = swapped(half, 2)
     near, far = from_neighbours(first)
-    near, far, coarse_received = lax.optimization_barrier((near, far, coarse_received))
-    coarse = summed_regions(coarse, coarse_received)
-    m_high, m_low, coarse_op = coarse_operator(agg_of, coarse, swapped(coarse, 1))
+    near, far, side_received = lax.optimization_barrier((near, far, side_received))
+    g_half, coarse = coarse_half(own_half, own_received, side_half, side_received, rt_high, rt_low)
+    coarse_other = swapped(coarse, 1)
+    coarse_op = coarse_share(coarse, coarse_other)
     correction = first
     for index in range(COARSE_SWEEPS - 1):
         if index > 0:
             near, far = from_neighbours(correction)
-        correction = sweep(m_high, m_low, first, near, correction, far)
-    half_received, correction = lax.optimization_barrier((half_received, correction))
-    half = summed_regions(half, half_received)
-    w_high, w_low = lift_operator(agg_of, half, swapped(half, 1), smoother, prolong)
+        if index == 1:
+            lift_other, near, far = lax.optimization_barrier((lift_other, near, far))
+        correction = sweep(agg_of, coarse, coarse_other, first, near, correction, far)
+        if index == 0:
+            g_half, correction = lax.optimization_barrier((g_half, correction))
+            lift = lift_half(agg_of, g_half, smoother, prolong)
+            lift_other = swapped(lift, 1)
     near, far = from_neighbours(correction)
-    base = lifted(w_high, w_low, base, correction)
+    base, w_high, w_low = lifted(lift, lift_other, base, correction)
     solution = last_step(w_high, w_low, base, near, far)
     return coarse_op, solution.reshape(ROWS, DOF, COLS)
 

time: 72.2 us -> 72.6 us (level)
  waiting for transfers between devices: 34.7 us -> 36.2 us
  starting transfers between devices: 20.5 us -> 19.3 us
    ppermute x1, waiting for transfers between devices: 2.23 us -> 10.3 us  [from_side(): return lax.ppermute(value, ('slab', 'sub'), pairs)]
    ppermute x10, waiting for transfers between devices: 18.4 us -> 11 us  [swapped(): return lax.ppermute(value, 'sub', [(i, i ^ bit) for i in range(size)])]
    ppermute x3, starting transfers between devices: 7.97 us -> 5.77 us  [from_neighbours(): far = lax.ppermute(value, 'slab', swaps(size, 1))]
    ppermute x3, waiting for transfers between devices: 8.78 us -> 10.2 us  [from_neighbours(): far = lax.ppermute(value, 'slab', swaps(size, 1))]
    ppermute x3, starting transfers between devices: 2.6 us -> 3.7 us  [from_neighbours(): near = lax.ppermute(value, 'slab', swaps(size, 0))]
    pallas_call x6 -> x7, Pallas kernels: 5.86 us -> 6.3 us  [the longest x2 1.9 us: sweep(): pl.pallas_call(sweep_kernel, in_specs=[SMEM] + [VMEM] * 6, out_specs=VMEM...]
  transfers between devices with their start and end apart: 17 -> 17, of which waited for: 13 -> 14; matrix products, arithmetic and copies ran while one was open for 0% -> 0% of each run, Pallas kernels for 13% -> 9%
where the time goes in v4:
time: 72.6 us; the launch traced here: 72.2 us
  waiting for transfers between devices  36.2 us (50%)
  starting transfers between devices  19.3 us (27%)
  Pallas kernels  15.7 us (22%)
  between operations  0.81 us (1%)
    ppermute x10, waiting for transfers between devices, swapped(): return lax.ppermute(value, 'sub', [(i, i ^ bit) for i in range(size)])  11 us
    ppermute x1, waiting for transfers between devices, from_side(): return lax.ppermute(value, ('slab', 'sub'), pairs)  10.3 us
    ppermute x3, waiting for transfers between devices, from_neighbours(): far = lax.ppermute(value, 'slab', swaps(size, 1))  10.2 us
    ppermute x10, starting transfers between devices, swapped(): return lax.ppermute(value, 'sub', [(i, i ^ bit) for i in range(size)])  6.42 us
    ppermute x3, starting transfers between devices, from_neighbours(): far = lax.ppermute(value, 'slab', swaps(size, 1))  5.77 us
    ppermute x3, waiting for transfers between devices, from_neighbours(): near = lax.ppermute(value, 'slab', swaps(size, 0))  4.73 us
    pallas_call x1, Pallas kernels, start_step(): pl.pallas_call(start_kernel, in_specs=[HBM] * 7, out_specs=[VMEM] * 5, ou...  4.17 us
    ppermute x3, starting transfers between devices, from_neighbours(): near = lax.ppermute(value, 'slab', swaps(size, 0))  3.7 us
  transfers between devices with their start and end apart: 17, of which 14 were waited for; matrix products, arithmetic and copies ran while one was open for 0% of the time, Pallas kernels for 9%

profile of v4, /device:TPU:8, one launch (start us, length us, event | category | flops | bytes accessed | tf_op | source)
XLA Modules:
  0.0 72.2 jit_solution(13567922273171759852)
XLA Ops:
  0.6 0.0 copy-start
  0.6 0.0 copy-start.2
  0.7 4.2 %start_step.1 = (f32[512,1024]{1,0:T(8,128)S(1)}, f32[256,512]{1,0:T(8,128)S(1)}, f32[256,512]{1,0:T(8,128)S(1)}, f32[576,256]{1,0:T(8,128)S(1)}, f32[512,128]{1,0:T(8,128)S(1)}) custom-call(s32[8,16]{1,0:T(8,128)} %col_hbm.1, s32[8,4,2,8]{3,2,1,0:T(2,128)} %rows_hbm.1, s32[4,2,8]{2,1,0:T(2,128)} %bitcast.3, f32[8,16,64,64]{3,2,1,0:T(8,128)} %blocks_hbm.1, ...), custom_call_target="tpu_custom_call" | custom-call | tf_op jit(solution)/shard_map/start_step/pallas_call | solution.py:156
  4.8 0.1 collective-permute-start
  4.9 1.9 %collective-permute-done = f32[256,512]{1,0:T(8,128)S(1)} collective-permute-done((f32[256,512]{1,0:T(8,128)S(1)}, f32[256,512]{1,0:T(8,128)S(1)}, u32[]{:S(2)}, u32[]{:S(2)}) %collective-permute-start) | collective-permute-done | bytes 524320 | tf_op jit(solution)/shard_map/ppermute | solution.py:495
  6.8 0.1 collective-permute-start.2
  6.9 3.4 %collective-permute-start.3 = (f32[576,256]{1,0:T(8,128)S(1)}, f32[576,256]{1,0:T(8,128)S(1)}, u32[]{:S(2)}, u32[]{:S(2)}) collective-permute-start(f32[576,256]{1,0:T(8,128)S(1)} %get-tuple-element.38.field.message), channel_id=1, source_target_pairs={{0,4},{8,12},{16,20},{24,28},{4,0},{12,8},{20,16},{28,24},{1,5},{9... | collective-permute-start | bytes 1769480 | tf_op jit(solution)/shard_map/ppermute | solution.py:490
  10.4 0.1 add.3
  10.5 1.4 %collective-permute-start.1 = (f32[256,512]{1,0:T(8,128)S(1)}, f32[256,512]{1,0:T(8,128)S(1)}, u32[]{:S(2)}, u32[]{:S(2)}) collective-permute-start(f32[256,512]{1,0:T(8,128)S(1)} %add.3), channel_id=1, source_target_pairs={{0,2},{1,3},{2,0},{3,1},{4,6},{5,7},{6,4},{7,5},{8,10},{9,11},{10,... | collective-permute-start | bytes 1572872 | tf_op jit(solution)/shard_map/ppermute | solution.py:495
  11.9 0.0 collective-permute-done.2.pair_other
  11.9 0.0 copy-done
  11.9 0.0 copy-done.2
  11.9 2.3 %own_step.1 = (f32[512,512]{1,0:T(8,128)S(1)}, f32[512,128]{1,0:T(8,128)S(1)}, f32[512,256]{1,0:T(8,128)S(1)}, bf16[256,512]{1,0:T(8,128)(2,1)S(1)}, bf16[256,512]{1,0:T(8,128)(2,1)S(1)}) custom-call(s32[64]{0:T(128)S(1)} %copy-done.2, f32[8,64,64]{2,1,0:T(8,128)S(1)} %copy-done, f32[576,256]{1,0:T(8,128)S(1)} %get-tuple-element.38.field.message, ...), custom_call_target="tpu_custom_call" | custom-call | tf_op jit(solution)/shard_map/own_step/pallas_call | solution.py:224
  14.2 10.3 %collective-permute-done.3.message = f32[576,256]{1,0:T(8,128)S(1)} collective-permute-done((f32[576,256]{1,0:T(8,128)S(1)}, f32[576,256]{1,0:T(8,128)S(1)}, u32[]{:S(2)}, u32[]{:S(2)}) %collective-permute-start.3) | collective-permute-done | bytes 589856 | tf_op jit(solution)/shard_map/ppermute | solution.py:490
  24.4 0.0 collective-permute-done.1.received
  24.4 0.0 collective-permute-start.5
  24.4 1.9 %collective-permute-done.5.received_other = f32[256,512]{1,0:T(8,128)S(1)} collective-permute-done((f32[256,512]{1,0:T(8,128)S(1)}, f32[256,512]{1,0:T(8,128)S(1)}, u32[]{:S(2)}, u32[]{:S(2)}) %collective-permute-start.5) | collective-permute-done | bytes 524320 | tf_op jit(solution)/shard_map/ppermute | solution.py:495
  26.4 0.7 image.1
  27.1 2.4 %collective-permute-start.7 = (f32[512,128]{1,0:T(8,128)S(1)}, f32[512,128]{1,0:T(8,128)S(1)}, u32[]{:S(2)}, u32[]{:S(2)}) collective-permute-start(f32[512,128]{1,0:T(8,128)S(1)} %get-tuple-element.52), channel_id=1, source_target_pairs={{0,2},{1,3},{2,0},{3,1},{4,6},{5,7},{6,4},{7,5},{8,10},{9,11},{10,... | collective-permute-start | bytes 786440 | tf_op jit(solution)/shard_map/ppermute | solution.py:495
  29.5 0.0 collective-permute-start.6
  29.5 1.2 %collective-permute-done.6.other = f32[64,256]{1,0:T(8,128)S(1)} collective-permute-done((f32[64,256]{1,0:T(8,128)S(1)}, f32[64,256]{1,0:T(8,128)S(1)}, u32[]{:S(2)}, u32[]{:S(2)}) %collective-permute-start.6) | collective-permute-done | bytes 65568 | tf_op jit(solution)/shard_map/ppermute | solution.py:495
  30.8 1.3 %ghost_step.1.side = f32[512,128]{1,0:T(8,128)S(1)} custom-call(s32[64]{0:T(128)S(1)} %copy-done.2, bf16[512,512]{1,0:T(8,128)(2,1)S(1)} %get-tuple-element.49.d_high, bf16[512,512]{1,0:T(8,128)(2,1)S(1)} %get-tuple-element.50.d_low, f32[64,256]{1,0:T(8,128)S(1)} %slice.3.mine, f32[64,256]{1,0:T(8,128)S(1)} %collective-permute-done.6.other), custom_call_target="tpu_custom_call" | custom-call | tf_op jit(solution)/shard_map/ghost_step/pallas_call | solution.py:283
  32.0 0.0 copy-start.1
  32.0 0.2 collective-permute-start.10
  32.2 1.9 %collective-permute-start.4 = (f32[512,128]{1,0:T(8,128)S(1)}, f32[512,128]{1,0:T(8,128)S(1)}, u32[]{:S(2)}, u32[]{:S(2)}) collective-permute-start(f32[512,128]{1,0:T(8,128)S(1)} %get-tuple-element.44.own), channel_id=1, source_target_pairs={{0,2},{1,3},{2,0},{3,1},{4,6},{5,7},{6,4},{7,5},{8,10},{9,11},{10,... | collective-permute-start | bytes 786440 | tf_op jit(solution)/shard_map/ppermute | solution.py:495
  34.1 2.5 %collective-permute-done.7.received = f32[512,128]{1,0:T(8,128)S(1)} collective-permute-done((f32[512,128]{1,0:T(8,128)S(1)}, f32[512,128]{1,0:T(8,128)S(1)}, u32[]{:S(2)}, u32[]{:S(2)}) %collective-permute-start.7) | collective-permute-done | bytes 262176 | tf_op jit(solution)/shard_map/ppermute | solution.py:495
  36.6 0.8 %residual_step.1 = (f32[512,128]{1,0:T(8,128)S(1)}, f32[256,128]{1,0:T(8,128)S(1)}) custom-call(s32[64]{0:T(128)S(1)} %copy-done.2, f32[512,128]{1,0:T(8,128)S(1)} %get-tuple-element.51.keep, f32[512,128]{1,0:T(8,128)S(1)} %collective-permute-done.7.received, bf16[256,512]{1,0:T(8,128)(2,1)S(1)} %get-tuple-element.53.rt_high, ...), custom_call_target="tpu_custom_call" | custom-call | tf_op jit(solution)/shard_map/residual_step/pallas_call | solution.py:383
  37.4 1.6 %collective-permute-start.8 = (f32[256,128]{1,0:T(8,128)S(1)}, f32[256,128]{1,0:T(8,128)S(1)}, u32[]{:S(2)}, u32[]{:S(2)}) collective-permute-start(f32[256,128]{1,0:T(8,128)S(1)} %get-tuple-element.55.first.own), channel_id=1, source_target_pairs={{0,4},{8,12},{16,20},{24,28},{4,0},{12,8},{20,16},{28,24},{1,5},{9... | collective-permute-start | bytes 393224 | tf_op jit(solution)/shard_map/ppermute | solution.py:481
  39.0 2.0 %collective-permute-start.9 = (f32[256,128]{1,0:T(8,128)S(1)}, f32[256,128]{1,0:T(8,128)S(1)}, u32[]{:S(2)}, u32[]{:S(2)}) collective-permute-start(f32[256,128]{1,0:T(8,128)S(1)} %get-tuple-element.55.first.own), channel_id=1, source_target_pairs={{4,8},{12,16},{20,24},{8,4},{16,12},{24,20},{5,9},{13,17},{21,25},... | collective-permute-start | bytes 393224 | tf_op jit(solution)/shard_map/ppermute | solution.py:480
  41.0 1.2 %collective-permute-done.10.side_received = f32[512,128]{1,0:T(8,128)S(1)} collective-permute-done((f32[512,128]{1,0:T(8,128)S(1)}, f32[512,128]{1,0:T(8,128)S(1)}, u32[]{:S(2)}, u32[]{:S(2)}) %collective-permute-start.10) | collective-permute-done | bytes 262176 | tf_op jit(solution)/shard_map/ppermute | solution.py:495
  42.2 0.3 collective-permute-done.8.near
  42.5 4.3 %collective-permute-done.9.far = f32[256,128]{1,0:T(8,128)S(1)} collective-permute-done((f32[256,128]{1,0:T(8,128)S(1)}, f32[256,128]{1,0:T(8,128)S(1)}, u32[]{:S(2)}, u32[]{:S(2)}) %collective-permute-start.9) | collective-permute-done | bytes 131104 | tf_op jit(solution)/shard_map/ppermute | solution.py:480
  46.8 0.6 collective-permute-done.4.own_received
  47.3 0.6 coarse_half.1
  48.0 0.1 collective-permute-start.11
  48.0 1.7 %collective-permute-done.11.other = f32[256,384]{1,0:T(8,128)S(1)} collective-permute-done((f32[256,384]{1,0:T(8,128)S(1)}, f32[256,384]{1,0:T(8,128)S(1)}, u32[]{:S(2)}, u32[]{:S(2)}) %collective-permute-start.11) | collective-permute-done | bytes 393248 | tf_op jit(solution)/shard_map/ppermute | solution.py:495
  49.7 0.9 %sweep.2.own = f32[256,128]{1,0:T(8,128)S(1)} custom-call(s32[64]{0:T(128)S(1)} %copy-done.2, f32[256,384]{1,0:T(8,128)S(1)} %get-tuple-element.57.mine, f32[256,384]{1,0:T(8,128)S(1)} %collective-permute-done.11.other, f32[256,128]{1,0:T(8,128)S(1)} %get-tuple-element.55.first.own, f32[256,128]{1,0:T(8,128)S(1)} %collective-permute-done.8.near, ...), custom_call_target="tpu_custom_call" | custom-call | tf_op jit(solution)/shard_map/sweep/pallas_call | solution.py:425
  50.7 0.0 copy-done.1
  50.7 1.0 %lift_half.1.mine = f32[512,384]{1,0:T(8,128)S(1)} custom-call(s32[64]{0:T(128)S(1)} %copy-done.2, f32[512,384]{1,0:T(8,128)S(1)} %get-tuple-element.61.g_half, f32[8,64,64]{2,1,0:T(8,128)S(1)} %copy-done.1, f32[8,64,64]{2,1,0:T(8,128)S(1)} %copy-done), custom_call_target="tpu_custom_call" | custom-call | tf_op jit(solution)/shard_map/lift_half/pallas_call | solution.py:366
  51.7 0.2 collective-permute-start.12
  51.9 1.5 %collective-permute-start.13 = (f32[256,128]{1,0:T(8,128)S(1)}, f32[256,128]{1,0:T(8,128)S(1)}, u32[]{:S(2)}, u32[]{:S(2)}) collective-permute-start(f32[256,128]{1,0:T(8,128)S(1)} %sweep.2.own), channel_id=1, source_target_pairs={{0,4},{8,12},{16,20},{24,28},{4,0},{12,8},{20,16},{28,24},{1,5},{9... | collective-permute-start | bytes 393224 | tf_op jit(solution)/shard_map/ppermute | solution.py:481
  53.5 1.9 %collective-permute-start.14 = (f32[256,128]{1,0:T(8,128)S(1)}, f32[256,128]{1,0:T(8,128)S(1)}, u32[]{:S(2)}, u32[]{:S(2)}) collective-permute-start(f32[256,128]{1,0:T(8,128)S(1)} %sweep.2.own), channel_id=1, source_target_pairs={{4,8},{12,16},{20,24},{8,4},{16,12},{24,20},{5,9},{13,17},{21,25},... | collective-permute-start | bytes 393224 | tf_op jit(solution)/shard_map/ppermute | solution.py:480
  55.4 2.3 %collective-permute-done.13.near = f32[256,128]{1,0:T(8,128)S(1)} collective-permute-done((f32[256,128]{1,0:T(8,128)S(1)}, f32[256,128]{1,0:T(8,128)S(1)}, u32[]{:S(2)}, u32[]{:S(2)}) %collective-permute-start.13) | collective-permute-done | bytes 131104 | tf_op jit(solution)/shard_map/ppermute | solution.py:481
  57.7 4.0 %collective-permute-done.14.far = f32[256,128]{1,0:T(8,128)S(1)} collective-permute-done((f32[256,128]{1,0:T(8,128)S(1)}, f32[256,128]{1,0:T(8,128)S(1)}, u32[]{:S(2)}, u32[]{:S(2)}) %collective-permute-start.14) | collective-permute-done | bytes 131104 | tf_op jit(solution)/shard_map/ppermute | solution.py:480
  61.7 0.0 collective-permute-done.12.other
  61.7 1.0 %sweep.3.own = f32[256,128]{1,0:T(8,128)S(1)} custom-call(s32[64]{0:T(128)S(1)} %copy-done.2, f32[256,384]{1,0:T(8,128)S(1)} %get-tuple-element.57.mine, f32[256,384]{1,0:T(8,128)S(1)} %collective-permute-done.11.other, f32[256,128]{1,0:T(8,128)S(1)} %get-tuple-element.55.first.own, f32[256,128]{1,0:T(8,128)S(1)} %collective-permute-done.13.near, ...), custom_call_target="tpu_custom_call" | custom-call | tf_op jit(solution)/shard_map/sweep/pallas_call | solution.py:425
  62.7 0.6 collective-permute-start.15
  63.3 1.9 %collective-permute-start.16 = (f32[256,128]{1,0:T(8,128)S(1)}, f32[256,128]{1,0:T(8,128)S(1)}, u32[]{:S(2)}, u32[]{:S(2)}) collective-permute-start(f32[256,128]{1,0:T(8,128)S(1)} %sweep.3.own), channel_id=1, source_target_pairs={{4,8},{12,16},{20,24},{8,4},{16,12},{24,20},{5,9},{13,17},{21,25},... | collective-permute-start | bytes 393224 | tf_op jit(solution)/shard_map/ppermute | solution.py:480
  65.2 0.3 base_step.1.base
  65.4 0.9 %coarse_share.1 = f32[4,3,64,64]{3,2,1,0:T(8,128)} custom-call(f32[256,384]{1,0:T(8,128)S(1)} %get-tuple-element.57.mine, f32[256,384]{1,0:T(8,128)S(1)} %collective-permute-done.11.other), custom_call_target="tpu_custom_call" | custom-call | tf_op jit(solution)/shard_map/coarse_share/pallas_call | solution.py:346
  66.4 0.6 lifted.1
  67.0 2.2 %collective-permute-done.15.near = f32[256,128]{1,0:T(8,128)S(1)} collective-permute-done((f32[256,128]{1,0:T(8,128)S(1)}, f32[256,128]{1,0:T(8,128)S(1)}, u32[]{:S(2)}, u32[]{:S(2)}) %collective-permute-start.15) | collective-permute-done | bytes 131104 | tf_op jit(solution)/shard_map/ppermute | solution.py:481
  69.1 1.9 %collective-permute-done.16.far = f32[256,128]{1,0:T(8,128)S(1)} collective-permute-done((f32[256,128]{1,0:T(8,128)S(1)}, f32[256,128]{1,0:T(8,128)S(1)}, u32[]{:S(2)}, u32[]{:S(2)}) %collective-permute-start.16) | collective-permute-done | bytes 131104 | tf_op jit(solution)/shard_map/ppermute | solution.py:480
  71.0 1.1 %last_step.1 = f32[512,128]{1,0:T(8,128)} custom-call(bf16[512,512]{1,0:T(8,128)(2,1)S(1)} %get-tuple-element.67.w_high, bf16[512,512]{1,0:T(8,128)(2,1)S(1)} %get-tuple-element.68.w_low, f32[512,128]{1,0:T(8,128)S(1)} %get-tuple-element.69.base, f32[256,128]{1,0:T(8,128)S(1)} %collective-permute-done.15.near, f32[256,128]{1,0:T(8,128)S(1)} %collective-permute-done.16.far), custom_call_target="tpu_custom_call" | custom-call | tf_op jit(solution)/shard_map/last_step/pallas_call | solution.py:463
  (1 shorter events, 0.0 us)
Async XLA Ops:
  0.6 11.2 %copy-start = (f32[8,64,64]{2,1,0:T(8,128)S(1)}, f32[8,64,64]{2,1,0:T(8,128)}, u32[]{:S(2)}) copy-start(f32[8,64,64]{2,1,0:T(8,128)} %prolong.3) | copy-start | bytes 393220
  0.6 11.2 %copy-start.2 = (s32[64]{0:T(128)S(1)}, s32[64]{0:T(128)}, u32[]{:S(2)}) copy-start(s32[64]{0:T(128)} %agg_of.11) | copy-start | bytes 772
  4.8 2.0 %collective-permute-start = (f32[256,512]{1,0:T(8,128)S(1)}, f32[256,512]{1,0:T(8,128)S(1)}, u32[]{:S(2)}, u32[]{:S(2)}) collective-permute-start(f32[256,512]{1,0:T(8,128)S(1)} %get-tuple-element.37), channel_id=1, source_target_pairs={{0,1},{1,0},{2,3},{3,2},{4,5},{5,4},{6,7},{7,6},{8,9},{9,8},{10,11... | collective-permute-start | bytes 1572872 | tf_op jit(solution)/shard_map/ppermute | solution.py:495
  6.8 5.1 %collective-permute-start.2 = (f32[512,1024]{1,0:T(8,128)S(1)}, f32[512,1024]{1,0:T(8,128)S(1)}, u32[]{:S(2)}, u32[]{:S(2)}) collective-permute-start(f32[512,1024]{1,0:T(8,128)S(1)} %get-tuple-element.41.pair), channel_id=1, source_target_pairs={{0,1},{1,0},{2,3},{3,2},{4,5},{5,4},{6,7},{7,6},{8,9},{9,8},{10,11... | collective-permute-start | bytes 6291464 | tf_op jit(solution)/shard_map/ppermute | solution.py:495
  6.9 17.5 %collective-permute-start.3 = (f32[576,256]{1,0:T(8,128)S(1)}, f32[576,256]{1,0:T(8,128)S(1)}, u32[]{:S(2)}, u32[]{:S(2)}) collective-permute-start(f32[576,256]{1,0:T(8,128)S(1)} %get-tuple-element.38.field.message), channel_id=1, source_target_pairs={{0,4},{8,12},{16,20},{24,28},{4,0},{12,8},{20,16},{28,24},{1,5},{9... | collective-permute-start | bytes 1769480 | tf_op jit(solution)/shard_map/ppermute | solution.py:490
  10.5 14.0 %collective-permute-start.1 = (f32[256,512]{1,0:T(8,128)S(1)}, f32[256,512]{1,0:T(8,128)S(1)}, u32[]{:S(2)}, u32[]{:S(2)}) collective-permute-start(f32[256,512]{1,0:T(8,128)S(1)} %add.3), channel_id=1, source_target_pairs={{0,2},{1,3},{2,0},{3,1},{4,6},{5,7},{6,4},{7,5},{8,10},{9,11},{10,... | collective-permute-start | bytes 1572872 | tf_op jit(solution)/shard_map/ppermute | solution.py:495
  24.4 1.9 %collective-permute-start.5 = (f32[256,512]{1,0:T(8,128)S(1)}, f32[256,512]{1,0:T(8,128)S(1)}, u32[]{:S(2)}, u32[]{:S(2)}) collective-permute-start(f32[256,512]{1,0:T(8,128)S(1)} %collective-permute-done.1.received), channel_id=1, source_target_pairs={{0,1},{1,0},{2,3},{3,2},{4,5},{5,4},{6,7},{7,6},{8,9},{9,8},{10,11... | collective-permute-start | bytes 1572872 | tf_op jit(solution)/shard_map/ppermute | solution.py:495
  27.1 9.5 %collective-permute-start.7 = (f32[512,128]{1,0:T(8,128)S(1)}, f32[512,128]{1,0:T(8,128)S(1)}, u32[]{:S(2)}, u32[]{:S(2)}) collective-permute-start(f32[512,128]{1,0:T(8,128)S(1)} %get-tuple-element.52), channel_id=1, source_target_pairs={{0,2},{1,3},{2,0},{3,1},{4,6},{5,7},{6,4},{7,5},{8,10},{9,11},{10,... | collective-permute-start | bytes 786440 | tf_op jit(solution)/shard_map/ppermute | solution.py:495
  29.5 1.3 %collective-permute-start.6 = (f32[64,256]{1,0:T(8,128)S(1)}, f32[64,256]{1,0:T(8,128)S(1)}, u32[]{:S(2)}, u32[]{:S(2)}) collective-permute-start(f32[64,256]{1,0:T(8,128)S(1)} %slice.3.mine), channel_id=1, source_target_pairs={{0,1},{1,0},{2,3},{3,2},{4,5},{5,4},{6,7},{7,6},{8,9},{9,8},{10,11... | collective-permute-start | bytes 196616 | tf_op jit(solution)/shard_map/ppermute | solution.py:495
  32.0 18.7 %copy-start.1 = (f32[8,64,64]{2,1,0:T(8,128)S(1)}, f32[8,64,64]{2,1,0:T(8,128)}, u32[]{:S(2)}) copy-start(f32[8,64,64]{2,1,0:T(8,128)} %smoother.3) | copy-start | bytes 393220
  32.0 10.2 %collective-permute-start.10 = (f32[512,128]{1,0:T(8,128)S(1)}, f32[512,128]{1,0:T(8,128)S(1)}, u32[]{:S(2)}, u32[]{:S(2)}) collective-permute-start(f32[512,128]{1,0:T(8,128)S(1)} %ghost_step.1.side), channel_id=1, source_target_pairs={{0,2},{1,3},{2,0},{3,1},{4,6},{5,7},{6,4},{7,5},{8,10},{9,11},{10,... | collective-permute-start | bytes 786440 | tf_op jit(solution)/shard_map/ppermute | solution.py:495
  32.2 15.2 %collective-permute-start.4 = (f32[512,128]{1,0:T(8,128)S(1)}, f32[512,128]{1,0:T(8,128)S(1)}, u32[]{:S(2)}, u32[]{:S(2)}) collective-permute-start(f32[512,128]{1,0:T(8,128)S(1)} %get-tuple-element.44.own), channel_id=1, source_target_pairs={{0,2},{1,3},{2,0},{3,1},{4,6},{5,7},{6,4},{7,5},{8,10},{9,11},{10,... | collective-permute-start | bytes 786440 | tf_op jit(solution)/shard_map/ppermute | solution.py:495
  37.4 5.0 %collective-permute-start.8 = (f32[256,128]{1,0:T(8,128)S(1)}, f32[256,128]{1,0:T(8,128)S(1)}, u32[]{:S(2)}, u32[]{:S(2)}) collective-permute-start(f32[256,128]{1,0:T(8,128)S(1)} %get-tuple-element.55.first.own), channel_id=1, source_target_pairs={{0,4},{8,12},{16,20},{24,28},{4,0},{12,8},{20,16},{28,24},{1,5},{9... | collective-permute-start | bytes 393224 | tf_op jit(solution)/shard_map/ppermute | solution.py:481
  39.0 7.7 %collective-permute-start.9 = (f32[256,128]{1,0:T(8,128)S(1)}, f32[256,128]{1,0:T(8,128)S(1)}, u32[]{:S(2)}, u32[]{:S(2)}) collective-permute-start(f32[256,128]{1,0:T(8,128)S(1)} %get-tuple-element.55.first.own), channel_id=1, source_target_pairs={{4,8},{12,16},{20,24},{8,4},{16,12},{24,20},{5,9},{13,17},{21,25},... | collective-permute-start | bytes 393224 | tf_op jit(solution)/shard_map/ppermute | solution.py:480
  48.0 1.8 %collective-permute-start.11 = (f32[256,384]{1,0:T(8,128)S(1)}, f32[256,384]{1,0:T(8,128)S(1)}, u32[]{:S(2)}, u32[]{:S(2)}) collective-permute-start(f32[256,384]{1,0:T(8,128)S(1)} %get-tuple-element.57.mine), channel_id=1, source_target_pairs={{0,1},{1,0},{2,3},{3,2},{4,5},{5,4},{6,7},{7,6},{8,9},{9,8},{10,11... | collective-permute-start | bytes 1179656 | tf_op jit(solution)/shard_map/ppermute | solution.py:495
  51.7 10.0 %collective-permute-start.12 = (f32[512,384]{1,0:T(8,128)S(1)}, f32[512,384]{1,0:T(8,128)S(1)}, u32[]{:S(2)}, u32[]{:S(2)}) collective-permute-start(f32[512,384]{1,0:T(8,128)S(1)} %lift_half.1.mine), channel_id=1, source_target_pairs={{0,1},{1,0},{2,3},{3,2},{4,5},{5,4},{6,7},{7,6},{8,9},{9,8},{10,11... | collective-permute-start | bytes 2359304 | tf_op jit(solution)/shard_map/ppermute | solution.py:495
  51.9 5.8 %collective-permute-start.13 = (f32[256,128]{1,0:T(8,128)S(1)}, f32[256,128]{1,0:T(8,128)S(1)}, u32[]{:S(2)}, u32[]{:S(2)}) collective-permute-start(f32[256,128]{1,0:T(8,128)S(1)} %sweep.2.own), channel_id=1, source_target_pairs={{0,4},{8,12},{16,20},{24,28},{4,0},{12,8},{20,16},{28,24},{1,5},{9... | collective-permute-start | bytes 393224 | tf_op jit(solution)/shard_map/ppermute | solution.py:481
  53.5 8.3 %collective-permute-start.14 = (f32[256,128]{1,0:T(8,128)S(1)}, f32[256,128]{1,0:T(8,128)S(1)}, u32[]{:S(2)}, u32[]{:S(2)}) collective-permute-start(f32[256,128]{1,0:T(8,128)S(1)} %sweep.2.own), channel_id=1, source_target_pairs={{4,8},{12,16},{20,24},{8,4},{16,12},{24,20},{5,9},{13,17},{21,25},... | collective-permute-start | bytes 393224 | tf_op jit(solution)/shard_map/ppermute | solution.py:480
  62.7 6.4 %collective-permute-start.15 = (f32[256,128]{1,0:T(8,128)S(1)}, f32[256,128]{1,0:T(8,128)S(1)}, u32[]{:S(2)}, u32[]{:S(2)}) collective-permute-start(f32[256,128]{1,0:T(8,128)S(1)} %sweep.3.own), channel_id=1, source_target_pairs={{0,4},{8,12},{16,20},{24,28},{4,0},{12,8},{20,16},{28,24},{1,5},{9... | collective-permute-start | bytes 393224 | tf_op jit(solution)/shard_map/ppermute | solution.py:481
  63.3 7.7 %collective-permute-start.16 = (f32[256,128]{1,0:T(8,128)S(1)}, f32[256,128]{1,0:T(8,128)S(1)}, u32[]{:S(2)}, u32[]{:S(2)}) collective-permute-start(f32[256,128]{1,0:T(8,128)S(1)} %sweep.3.own), channel_id=1, source_target_pairs={{4,8},{12,16},{20,24},{8,4},{16,12},{24,20},{5,9},{13,17},{21,25},... | collective-permute-start | bytes 393224 | tf_op jit(solution)/shard_map/ppermute | solution.py:480

commit v5 on v4

--- a/solution.py
+++ b/solution.py
@@ -477,8 +477,8 @@
 
 def from_neighbours(value):
     size = lax.axis_size("slab")
+    near = lax.ppermute(value, "slab", swaps(size, 0))
     far = lax.ppermute(value, "slab", swaps(size, 1))
-    near = lax.ppermute(value, "slab", swaps(size, 0))
     return near, far
 
 
@@ -504,9 +504,10 @@
     received = swapped(mine + theirs, 2)
     pair, theirs = lax.optimization_barrier((pair, theirs))
     side, own_half, own_image, rt_high, rt_low = own_step(agg_of, prolong, message, right, pair, swapped(pair, 1))
-    received, side, side_message, own_half = lax.optimization_barrier((received, side, side_message, own_half))
+    received, side, own_half = lax.optimization_barrier((received, side, own_half))
     own_received = swapped(own_half, 2)
     keep, send, d_high, d_low = image(own_image, side, received, swapped(received, 1), side_message)
+    send, own_received = lax.optimization_barrier((send, own_received))
     image_received = swapped(send, 2)
     ghosts = side_message[WIDE:]
     side_half = ghost_step(agg_of, d_high, d_low, ghosts, swapped(ghosts, 1))
@@ -514,21 +515,18 @@
     residual, first = residual_step(agg_of, keep, image_received, rt_high, rt_low)
     base = base_step(smoother, message, residual)
     near, far = from_neighbours(first)
-    near, far, side_received = lax.optimization_barrier((near, far, side_received))
     g_half, coarse = coarse_half(own_half, own_received, side_half, side_received, rt_high, rt_low)
+    near, far, coarse = lax.optimization_barrier((near, far, coarse))
     coarse_other = swapped(coarse, 1)
     coarse_op = coarse_share(coarse, coarse_other)
+    lift = lift_half(agg_of, g_half, smoother, prolong)
     correction = first
     for index in range(COARSE_SWEEPS - 1):
         if index > 0:
             near, far = from_neighbours(correction)
-        if index == 1:
-            lift_other, near, far = lax.optimization_barrier((lift_other, near, far))
+            lift, near, far = lax.optimization_barrier((lift, near, far))
         correction = sweep(agg_of, coarse, coarse_other, first, near, correction, far)
-        if index == 0:
-            g_half, correction = lax.optimization_barrier((g_half, correction))
-            lift = lift_half(agg_of, g_half, smoother, prolong)
-            lift_other = swapped(lift, 1)
+    lift_other = swapped(lift, 1)
     near, far = from_neighbours(correction)
     base, w_high, w_low = lifted(lift, lift_other, base, correction)
     solution = last_step(w_high, w_low, base, near, far)

time: 72.6 us -> 73 us (level)
  waiting for transfers between devices: 36.2 us -> 37.8 us
  starting transfers between devices: 19.3 us -> 18.2 us
    ppermute x10, waiting for transfers between devices: 11 us -> 20 us  [swapped(): return lax.ppermute(value, 'sub', [(i, i ^ bit) for i in range(size)])]
    ppermute x1, waiting for transfers between devices: 10.3 us -> 3 us  [from_side(): return lax.ppermute(value, ('slab', 'sub'), pairs)]
    ppermute x10, starting transfers between devices: 6.42 us -> 5.32 us  [swapped(): return lax.ppermute(value, 'sub', [(i, i ^ bit) for i in range(size)])]
  transfers between devices with their start and end apart: 17 -> 17, of which waited for: 14 -> 14; matrix products, arithmetic and copies ran while one was open for 0% -> 0% of each run, Pallas kernels for 9% -> 13%
where the time goes in v5:
time: 73 us; the launch traced here: 72.6 us
  waiting for transfers between devices  37.8 us (52%)
  starting transfers between devices  18.2 us (25%)
  Pallas kernels  15.7 us (22%)
  between operations  0.82 us (1%)
    ppermute x10, waiting for transfers between devices, swapped(): return lax.ppermute(value, 'sub', [(i, i ^ bit) for i in range(size)])  20 us
    ppermute x3, waiting for transfers between devices, from_neighbours(): far = lax.ppermute(value, 'slab', swaps(size, 1))  9.91 us
    ppermute x3, starting transfers between devices, from_neighbours(): far = lax.ppermute(value, 'slab', swaps(size, 1))  5.73 us
    ppermute x10, starting transfers between devices, swapped(): return lax.ppermute(value, 'sub', [(i, i ^ bit) for i in range(size)])  5.32 us
    ppermute x3, waiting for transfers between devices, from_neighbours(): near = lax.ppermute(value, 'slab', swaps(size, 0))  4.86 us
    pallas_call x1, Pallas kernels, start_step(): pl.pallas_call(start_kernel, in_specs=[HBM] * 7, out_specs=[VMEM] * 5, ou...  4.15 us
    ppermute x3, starting transfers between devices, from_neighbours(): near = lax.ppermute(value, 'slab', swaps(size, 0))  3.73 us
    ppermute x1, starting transfers between devices, from_side(): return lax.ppermute(value, ('slab', 'sub'), pairs)  3.43 us
  transfers between devices with their start and end apart: 17, of which 14 were waited for; matrix products, arithmetic and copies ran while one was open for 0% of the time, Pallas kernels for 13%

profile of v5, /device:TPU:8, one launch (start us, length us, event | category | flops | bytes accessed | tf_op | source)
XLA Modules:
  0.0 72.6 jit_solution(6913064599904536117)
XLA Ops:
  0.6 0.0 copy-start
  0.6 0.0 copy-start.2
  0.7 4.2 %start_step.1 = (f32[512,1024]{1,0:T(8,128)S(1)}, f32[256,512]{1,0:T(8,128)S(1)}, f32[256,512]{1,0:T(8,128)S(1)}, f32[576,256]{1,0:T(8,128)S(1)}, f32[512,128]{1,0:T(8,128)S(1)}) custom-call(s32[8,16]{1,0:T(8,128)} %col_hbm.1, s32[8,4,2,8]{3,2,1,0:T(2,128)} %rows_hbm.1, s32[4,2,8]{2,1,0:T(2,128)} %bitcast.3, f32[8,16,64,64]{3,2,1,0:T(8,128)} %blocks_hbm.1, ...), custom_call_target="tpu_custom_call" | custom-call | tf_op jit(solution)/shard_map/start_step/pallas_call | solution.py:156
  4.8 0.1 collective-permute-start
  4.9 1.9 %collective-permute-done = f32[256,512]{1,0:T(8,128)S(1)} collective-permute-done((f32[256,512]{1,0:T(8,128)S(1)}, f32[256,512]{1,0:T(8,128)S(1)}, u32[]{:S(2)}, u32[]{:S(2)}) %collective-permute-start) | collective-permute-done | bytes 524320 | tf_op jit(solution)/shard_map/ppermute | solution.py:495
  6.8 0.1 collective-permute-start.1
  6.9 0.1 add.3
  7.0 1.5 %collective-permute-start.2 = (f32[256,512]{1,0:T(8,128)S(1)}, f32[256,512]{1,0:T(8,128)S(1)}, u32[]{:S(2)}, u32[]{:S(2)}) collective-permute-start(f32[256,512]{1,0:T(8,128)S(1)} %add.3), channel_id=1, source_target_pairs={{0,2},{1,3},{2,0},{3,1},{4,6},{5,7},{6,4},{7,5},{8,10},{9,11},{10,... | collective-permute-start | bytes 1572872 | tf_op jit(solution)/shard_map/ppermute | solution.py:495
  8.6 3.4 %collective-permute-start.4 = (f32[576,256]{1,0:T(8,128)S(1)}, f32[576,256]{1,0:T(8,128)S(1)}, u32[]{:S(2)}, u32[]{:S(2)}) collective-permute-start(f32[576,256]{1,0:T(8,128)S(1)} %get-tuple-element.35.field.message), channel_id=1, source_target_pairs={{0,4},{8,12},{16,20},{24,28},{4,0},{12,8},{20,16},{28,24},{1,5},{9... | collective-permute-start | bytes 1769480 | tf_op jit(solution)/shard_map/ppermute | solution.py:490
  12.0 0.0 collective-permute-done.1.pair_other
  12.0 0.0 copy-done
  12.0 0.0 copy-done.2
  12.0 2.3 %own_step.1 = (f32[512,512]{1,0:T(8,128)S(1)}, f32[512,128]{1,0:T(8,128)S(1)}, f32[512,256]{1,0:T(8,128)S(1)}, bf16[256,512]{1,0:T(8,128)(2,1)S(1)}, bf16[256,512]{1,0:T(8,128)(2,1)S(1)}) custom-call(s32[64]{0:T(128)S(1)} %copy-done.2, f32[8,64,64]{2,1,0:T(8,128)S(1)} %copy-done, f32[576,256]{1,0:T(8,128)S(1)} %get-tuple-element.35.field.message, ...), custom_call_target="tpu_custom_call" | custom-call | tf_op jit(solution)/shard_map/own_step/pallas_call | solution.py:224
  14.3 7.0 %collective-permute-done.2.received = f32[256,512]{1,0:T(8,128)S(1)} collective-permute-done((f32[256,512]{1,0:T(8,128)S(1)}, f32[256,512]{1,0:T(8,128)S(1)}, u32[]{:S(2)}, u32[]{:S(2)}) %collective-permute-start.2) | collective-permute-done | bytes 524320 | tf_op jit(solution)/shard_map/ppermute | solution.py:495
  21.3 0.0 collective-permute-start.3
  21.3 1.5 %collective-permute-start.5 = (f32[512,128]{1,0:T(8,128)S(1)}, f32[512,128]{1,0:T(8,128)S(1)}, u32[]{:S(2)}, u32[]{:S(2)}) collective-permute-start(f32[512,128]{1,0:T(8,128)S(1)} %get-tuple-element.48.own), channel_id=1, source_target_pairs={{0,2},{1,3},{2,0},{3,1},{4,6},{5,7},{6,4},{7,5},{8,10},{9,11},{10,... | collective-permute-start | bytes 786440 | tf_op jit(solution)/shard_map/ppermute | solution.py:495
  22.7 3.0 %collective-permute-done.4.message = f32[576,256]{1,0:T(8,128)S(1)} collective-permute-done((f32[576,256]{1,0:T(8,128)S(1)}, f32[576,256]{1,0:T(8,128)S(1)}, u32[]{:S(2)}, u32[]{:S(2)}) %collective-permute-start.4) | collective-permute-done | bytes 589856 | tf_op jit(solution)/shard_map/ppermute | solution.py:490
  25.8 0.0 collective-permute-done.3.received_other
  25.8 0.7 image.1
  26.5 3.5 %collective-permute-done.5.own_received = f32[512,128]{1,0:T(8,128)S(1)} collective-permute-done((f32[512,128]{1,0:T(8,128)S(1)}, f32[512,128]{1,0:T(8,128)S(1)}, u32[]{:S(2)}, u32[]{:S(2)}) %collective-permute-start.5) | collective-permute-done | bytes 262176 | tf_op jit(solution)/shard_map/ppermute | solution.py:495
  30.0 1.5 %collective-permute-start.6 = (f32[512,128]{1,0:T(8,128)S(1)}, f32[512,128]{1,0:T(8,128)S(1)}, u32[]{:S(2)}, u32[]{:S(2)}) collective-permute-start(f32[512,128]{1,0:T(8,128)S(1)} %get-tuple-element.49), channel_id=1, source_target_pairs={{0,2},{1,3},{2,0},{3,1},{4,6},{5,7},{6,4},{7,5},{8,10},{9,11},{10,... | collective-permute-start | bytes 786440 | tf_op jit(solution)/shard_map/ppermute | solution.py:495
  31.5 0.0 collective-permute-start.9
  31.5 1.2 %collective-permute-done.9.other = f32[64,256]{1,0:T(8,128)S(1)} collective-permute-done((f32[64,256]{1,0:T(8,128)S(1)}, f32[64,256]{1,0:T(8,128)S(1)}, u32[]{:S(2)}, u32[]{:S(2)}) %collective-permute-start.9) | collective-permute-done | bytes 65568 | tf_op jit(solution)/shard_map/ppermute | solution.py:495
  32.7 1.3 %ghost_step.1.side = f32[512,128]{1,0:T(8,128)S(1)} custom-call(s32[64]{0:T(128)S(1)} %copy-done.2, bf16[512,512]{1,0:T(8,128)(2,1)S(1)} %get-tuple-element.54.d_high, bf16[512,512]{1,0:T(8,128)(2,1)S(1)} %get-tuple-element.55.d_low, f32[64,256]{1,0:T(8,128)S(1)} %slice.4.mine, f32[64,256]{1,0:T(8,128)S(1)} %collective-permute-done.9.other), custom_call_target="tpu_custom_call" | custom-call | tf_op jit(solution)/shard_map/ghost_step/pallas_call | solution.py:283
  34.0 0.0 copy-start.1
  34.0 0.6 collective-permute-start.10
  34.6 4.4 %collective-permute-done.6.received = f32[512,128]{1,0:T(8,128)S(1)} collective-permute-done((f32[512,128]{1,0:T(8,128)S(1)}, f32[512,128]{1,0:T(8,128)S(1)}, u32[]{:S(2)}, u32[]{:S(2)}) %collective-permute-start.6) | collective-permute-done | bytes 262176 | tf_op jit(solution)/shard_map/ppermute | solution.py:495
  39.0 0.8 %residual_step.1 = (f32[512,128]{1,0:T(8,128)S(1)}, f32[256,128]{1,0:T(8,128)S(1)}) custom-call(s32[64]{0:T(128)S(1)} %copy-done.2, f32[512,128]{1,0:T(8,128)S(1)} %get-tuple-element.46.keep, f32[512,128]{1,0:T(8,128)S(1)} %collective-permute-done.6.received, bf16[256,512]{1,0:T(8,128)(2,1)S(1)} %get-tuple-element.50.rt_high, ...), custom_call_target="tpu_custom_call" | custom-call | tf_op jit(solution)/shard_map/residual_step/pallas_call | solution.py:383
  39.8 1.6 %collective-permute-start.7 = (f32[256,128]{1,0:T(8,128)S(1)}, f32[256,128]{1,0:T(8,128)S(1)}, u32[]{:S(2)}, u32[]{:S(2)}) collective-permute-start(f32[256,128]{1,0:T(8,128)S(1)} %get-tuple-element.52.first.own), channel_id=1, source_target_pairs={{0,4},{8,12},{16,20},{24,28},{4,0},{12,8},{20,16},{28,24},{1,5},{9... | collective-permute-start | bytes 393224 | tf_op jit(solution)/shard_map/ppermute | solution.py:480
  41.4 1.9 %collective-permute-start.8 = (f32[256,128]{1,0:T(8,128)S(1)}, f32[256,128]{1,0:T(8,128)S(1)}, u32[]{:S(2)}, u32[]{:S(2)}) collective-permute-start(f32[256,128]{1,0:T(8,128)S(1)} %get-tuple-element.52.first.own), channel_id=1, source_target_pairs={{4,8},{12,16},{20,24},{8,4},{16,12},{24,20},{5,9},{13,17},{21,25},... | collective-permute-start | bytes 393224 | tf_op jit(solution)/shard_map/ppermute | solution.py:481
  43.3 0.2 collective-permute-done.10.side_received
  43.6 0.6 coarse_half.1
  44.2 2.1 %collective-permute-done.7.near = f32[256,128]{1,0:T(8,128)S(1)} collective-permute-done((f32[256,128]{1,0:T(8,128)S(1)}, f32[256,128]{1,0:T(8,128)S(1)}, u32[]{:S(2)}, u32[]{:S(2)}) %collective-permute-start.7) | collective-permute-done | bytes 131104 | tf_op jit(solution)/shard_map/ppermute | solution.py:480
  46.3 2.9 %collective-permute-done.8.far = f32[256,128]{1,0:T(8,128)S(1)} collective-permute-done((f32[256,128]{1,0:T(8,128)S(1)}, f32[256,128]{1,0:T(8,128)S(1)}, u32[]{:S(2)}, u32[]{:S(2)}) %collective-permute-start.8) | collective-permute-done | bytes 131104 | tf_op jit(solution)/shard_map/ppermute | solution.py:481
  49.2 0.0 collective-permute-start.11
  49.2 1.7 %collective-permute-done.11.other = f32[256,384]{1,0:T(8,128)S(1)} collective-permute-done((f32[256,384]{1,0:T(8,128)S(1)}, f32[256,384]{1,0:T(8,128)S(1)}, u32[]{:S(2)}, u32[]{:S(2)}) %collective-permute-start.11) | collective-permute-done | bytes 393248 | tf_op jit(solution)/shard_map/ppermute | solution.py:495
  50.9 0.9 %sweep.2.own = f32[256,128]{1,0:T(8,128)S(1)} custom-call(s32[64]{0:T(128)S(1)} %copy-done.2, f32[256,384]{1,0:T(8,128)S(1)} %get-tuple-element.57.mine, f32[256,384]{1,0:T(8,128)S(1)} %collective-permute-done.11.other, f32[256,128]{1,0:T(8,128)S(1)} %get-tuple-element.52.first.own, f32[256,128]{1,0:T(8,128)S(1)} %collective-permute-done.7.near, ...), custom_call_target="tpu_custom_call" | custom-call | tf_op jit(solution)/shard_map/sweep/pallas_call | solution.py:425
  51.8 0.6 collective-permute-start.12
  52.4 1.9 %collective-permute-start.13 = (f32[256,128]{1,0:T(8,128)S(1)}, f32[256,128]{1,0:T(8,128)S(1)}, u32[]{:S(2)}, u32[]{:S(2)}) collective-permute-start(f32[256,128]{1,0:T(8,128)S(1)} %sweep.2.own), channel_id=1, source_target_pairs={{4,8},{12,16},{20,24},{8,4},{16,12},{24,20},{5,9},{13,17},{21,25},... | collective-permute-start | bytes 393224 | tf_op jit(solution)/shard_map/ppermute | solution.py:481
  54.3 0.0 copy-done.1
  54.3 1.0 %lift_half.1.mine = f32[512,384]{1,0:T(8,128)S(1)} custom-call(s32[64]{0:T(128)S(1)} %copy-done.2, f32[512,384]{1,0:T(8,128)S(1)} %get-tuple-element.58.g_half, f32[8,64,64]{2,1,0:T(8,128)S(1)} %copy-done.1, f32[8,64,64]{2,1,0:T(8,128)S(1)} %copy-done), custom_call_target="tpu_custom_call" | custom-call | tf_op jit(solution)/shard_map/lift_half/pallas_call | solution.py:366
  55.4 2.1 %collective-permute-done.12.near = f32[256,128]{1,0:T(8,128)S(1)} collective-permute-done((f32[256,128]{1,0:T(8,128)S(1)}, f32[256,128]{1,0:T(8,128)S(1)}, u32[]{:S(2)}, u32[]{:S(2)}) %collective-permute-start.12) | collective-permute-done | bytes 131104 | tf_op jit(solution)/shard_map/ppermute | solution.py:480
  57.4 3.0 %collective-permute-done.13.far = f32[256,128]{1,0:T(8,128)S(1)} collective-permute-done((f32[256,128]{1,0:T(8,128)S(1)}, f32[256,128]{1,0:T(8,128)S(1)}, u32[]{:S(2)}, u32[]{:S(2)}) %collective-permute-start.13) | collective-permute-done | bytes 131104 | tf_op jit(solution)/shard_map/ppermute | solution.py:481
  60.5 0.0 collective-permute-start.14
  60.5 0.9 %sweep.3.own = f32[256,128]{1,0:T(8,128)S(1)} custom-call(s32[64]{0:T(128)S(1)} %copy-done.2, f32[256,384]{1,0:T(8,128)S(1)} %get-tuple-element.57.mine, f32[256,384]{1,0:T(8,128)S(1)} %collective-permute-done.11.other, f32[256,128]{1,0:T(8,128)S(1)} %get-tuple-element.52.first.own, f32[256,128]{1,0:T(8,128)S(1)} %collective-permute-done.12.near, ...), custom_call_target="tpu_custom_call" | custom-call | tf_op jit(solution)/shard_map/sweep/pallas_call | solution.py:425
  61.4 1.6 %collective-permute-start.15 = (f32[256,128]{1,0:T(8,128)S(1)}, f32[256,128]{1,0:T(8,128)S(1)}, u32[]{:S(2)}, u32[]{:S(2)}) collective-permute-start(f32[256,128]{1,0:T(8,128)S(1)} %sweep.3.own), channel_id=1, source_target_pairs={{0,4},{8,12},{16,20},{24,28},{4,0},{12,8},{20,16},{28,24},{1,5},{9... | collective-permute-start | bytes 393224 | tf_op jit(solution)/shard_map/ppermute | solution.py:480
  63.0 1.9 %collective-permute-start.16 = (f32[256,128]{1,0:T(8,128)S(1)}, f32[256,128]{1,0:T(8,128)S(1)}, u32[]{:S(2)}, u32[]{:S(2)}) collective-permute-start(f32[256,128]{1,0:T(8,128)S(1)} %sweep.3.own), channel_id=1, source_target_pairs={{4,8},{12,16},{20,24},{8,4},{16,12},{24,20},{5,9},{13,17},{21,25},... | collective-permute-start | bytes 393224 | tf_op jit(solution)/shard_map/ppermute | solution.py:481
  64.9 0.3 base_step.1.base
  65.2 0.9 %coarse_share.1 = f32[4,3,64,64]{3,2,1,0:T(8,128)} custom-call(f32[256,384]{1,0:T(8,128)S(1)} %get-tuple-element.57.mine, f32[256,384]{1,0:T(8,128)S(1)} %collective-permute-done.11.other), custom_call_target="tpu_custom_call" | custom-call | tf_op jit(solution)/shard_map/coarse_share/pallas_call | solution.py:346
  66.1 0.0 collective-permute-done.14.other
  66.1 0.6 lifted.1
  66.7 0.7 collective-permute-done.15.near
  67.4 4.0 %collective-permute-done.16.far = f32[256,128]{1,0:T(8,128)S(1)} collective-permute-done((f32[256,128]{1,0:T(8,128)S(1)}, f32[256,128]{1,0:T(8,128)S(1)}, u32[]{:S(2)}, u32[]{:S(2)}) %collective-permute-start.16) | collective-permute-done | bytes 131104 | tf_op jit(solution)/shard_map/ppermute | solution.py:481
  71.4 1.1 %last_step.1 = f32[512,128]{1,0:T(8,128)} custom-call(bf16[512,512]{1,0:T(8,128)(2,1)S(1)} %get-tuple-element.65.w_high, bf16[512,512]{1,0:T(8,128)(2,1)S(1)} %get-tuple-element.66.w_low, f32[512,128]{1,0:T(8,128)S(1)} %get-tuple-element.67.base, f32[256,128]{1,0:T(8,128)S(1)} %collective-permute-done.15.near, f32[256,128]{1,0:T(8,128)S(1)} %collective-permute-done.16.far), custom_call_target="tpu_custom_call" | custom-call | tf_op jit(solution)/shard_map/last_step/pallas_call | solution.py:463
  (1 shorter events, 0.0 us)
Async XLA Ops:
  0.6 11.4 %copy-start = (f32[8,64,64]{2,1,0:T(8,128)S(1)}, f32[8,64,64]{2,1,0:T(8,128)}, u32[]{:S(2)}) copy-start(f32[8,64,64]{2,1,0:T(8,128)} %prolong.3) | copy-start | bytes 393220
  0.6 11.4 %copy-start.2 = (s32[64]{0:T(128)S(1)}, s32[64]{0:T(128)}, u32[]{:S(2)}) copy-start(s32[64]{0:T(128)} %agg_of.11) | copy-start | bytes 772
  4.8 2.0 %collective-permute-start = (f32[256,512]{1,0:T(8,128)S(1)}, f32[256,512]{1,0:T(8,128)S(1)}, u32[]{:S(2)}, u32[]{:S(2)}) collective-permute-start(f32[256,512]{1,0:T(8,128)S(1)} %get-tuple-element.38), channel_id=1, source_target_pairs={{0,1},{1,0},{2,3},{3,2},{4,5},{5,4},{6,7},{7,6},{8,9},{9,8},{10,11... | collective-permute-start | bytes 1572872 | tf_op jit(solution)/shard_map/ppermute | solution.py:495
  6.8 5.2 %collective-permute-start.1 = (f32[512,1024]{1,0:T(8,128)S(1)}, f32[512,1024]{1,0:T(8,128)S(1)}, u32[]{:S(2)}, u32[]{:S(2)}) collective-permute-start(f32[512,1024]{1,0:T(8,128)S(1)} %get-tuple-element.39.pair), channel_id=1, source_target_pairs={{0,1},{1,0},{2,3},{3,2},{4,5},{5,4},{6,7},{7,6},{8,9},{9,8},{10,11... | collective-permute-start | bytes 6291464 | tf_op jit(solution)/shard_map/ppermute | solution.py:495
  7.0 14.3 %collective-permute-start.2 = (f32[256,512]{1,0:T(8,128)S(1)}, f32[256,512]{1,0:T(8,128)S(1)}, u32[]{:S(2)}, u32[]{:S(2)}) collective-permute-start(f32[256,512]{1,0:T(8,128)S(1)} %add.3), channel_id=1, source_target_pairs={{0,2},{1,3},{2,0},{3,1},{4,6},{5,7},{6,4},{7,5},{8,10},{9,11},{10,... | collective-permute-start | bytes 1572872 | tf_op jit(solution)/shard_map/ppermute | solution.py:495
  8.6 17.2 %collective-permute-start.4 = (f32[576,256]{1,0:T(8,128)S(1)}, f32[576,256]{1,0:T(8,128)S(1)}, u32[]{:S(2)}, u32[]{:S(2)}) collective-permute-start(f32[576,256]{1,0:T(8,128)S(1)} %get-tuple-element.35.field.message), channel_id=1, source_target_pairs={{0,4},{8,12},{16,20},{24,28},{4,0},{12,8},{20,16},{28,24},{1,5},{9... | collective-permute-start | bytes 1769480 | tf_op jit(solution)/shard_map/ppermute | solution.py:490
  21.3 4.5 %collective-permute-start.3 = (f32[256,512]{1,0:T(8,128)S(1)}, f32[256,512]{1,0:T(8,128)S(1)}, u32[]{:S(2)}, u32[]{:S(2)}) collective-permute-start(f32[256,512]{1,0:T(8,128)S(1)} %collective-permute-done.2.received), channel_id=1, source_target_pairs={{0,1},{1,0},{2,3},{3,2},{4,5},{5,4},{6,7},{7,6},{8,9},{9,8},{10,11... | collective-permute-start | bytes 1572872 | tf_op jit(solution)/shard_map/ppermute | solution.py:495
  21.3 8.7 %collective-permute-start.5 = (f32[512,128]{1,0:T(8,128)S(1)}, f32[512,128]{1,0:T(8,128)S(1)}, u32[]{:S(2)}, u32[]{:S(2)}) collective-permute-start(f32[512,128]{1,0:T(8,128)S(1)} %get-tuple-element.48.own), channel_id=1, source_target_pairs={{0,2},{1,3},{2,0},{3,1},{4,6},{5,7},{6,4},{7,5},{8,10},{9,11},{10,... | collective-permute-start | bytes 786440 | tf_op jit(solution)/shard_map/ppermute | solution.py:495
  30.0 9.0 %collective-permute-start.6 = (f32[512,128]{1,0:T(8,128)S(1)}, f32[512,128]{1,0:T(8,128)S(1)}, u32[]{:S(2)}, u32[]{:S(2)}) collective-permute-start(f32[512,128]{1,0:T(8,128)S(1)} %get-tuple-element.49), channel_id=1, source_target_pairs={{0,2},{1,3},{2,0},{3,1},{4,6},{5,7},{6,4},{7,5},{8,10},{9,11},{10,... | collective-permute-start | bytes 786440 | tf_op jit(solution)/shard_map/ppermute | solution.py:495
  31.5 1.3 %collective-permute-start.9 = (f32[64,256]{1,0:T(8,128)S(1)}, f32[64,256]{1,0:T(8,128)S(1)}, u32[]{:S(2)}, u32[]{:S(2)}) collective-permute-start(f32[64,256]{1,0:T(8,128)S(1)} %slice.4.mine), channel_id=1, source_target_pairs={{0,1},{1,0},{2,3},{3,2},{4,5},{5,4},{6,7},{7,6},{8,9},{9,8},{10,11... | collective-permute-start | bytes 196616 | tf_op jit(solution)/shard_map/ppermute | solution.py:495
  34.0 20.4 %copy-start.1 = (f32[8,64,64]{2,1,0:T(8,128)S(1)}, f32[8,64,64]{2,1,0:T(8,128)}, u32[]{:S(2)}) copy-start(f32[8,64,64]{2,1,0:T(8,128)} %smoother.3) | copy-start | bytes 393220
  34.0 9.6 %collective-permute-start.10 = (f32[512,128]{1,0:T(8,128)S(1)}, f32[512,128]{1,0:T(8,128)S(1)}, u32[]{:S(2)}, u32[]{:S(2)}) collective-permute-start(f32[512,128]{1,0:T(8,128)S(1)} %ghost_step.1.side), channel_id=1, source_target_pairs={{0,2},{1,3},{2,0},{3,1},{4,6},{5,7},{6,4},{7,5},{8,10},{9,11},{10,... | collective-permute-start | bytes 786440 | tf_op jit(solution)/shard_map/ppermute | solution.py:495
  39.8 6.4 %collective-permute-start.7 = (f32[256,128]{1,0:T(8,128)S(1)}, f32[256,128]{1,0:T(8,128)S(1)}, u32[]{:S(2)}, u32[]{:S(2)}) collective-permute-start(f32[256,128]{1,0:T(8,128)S(1)} %get-tuple-element.52.first.own), channel_id=1, source_target_pairs={{0,4},{8,12},{16,20},{24,28},{4,0},{12,8},{20,16},{28,24},{1,5},{9... | collective-permute-start | bytes 393224 | tf_op jit(solution)/shard_map/ppermute | solution.py:480
  41.4 7.7 %collective-permute-start.8 = (f32[256,128]{1,0:T(8,128)S(1)}, f32[256,128]{1,0:T(8,128)S(1)}, u32[]{:S(2)}, u32[]{:S(2)}) collective-permute-start(f32[256,128]{1,0:T(8,128)S(1)} %get-tuple-element.52.first.own), channel_id=1, source_target_pairs={{4,8},{12,16},{20,24},{8,4},{16,12},{24,20},{5,9},{13,17},{21,25},... | collective-permute-start | bytes 393224 | tf_op jit(solution)/shard_map/ppermute | solution.py:481
  49.2 1.7 %collective-permute-start.11 = (f32[256,384]{1,0:T(8,128)S(1)}, f32[256,384]{1,0:T(8,128)S(1)}, u32[]{:S(2)}, u32[]{:S(2)}) collective-permute-start(f32[256,384]{1,0:T(8,128)S(1)} %get-tuple-element.57.mine), channel_id=1, source_target_pairs={{0,1},{1,0},{2,3},{3,2},{4,5},{5,4},{6,7},{7,6},{8,9},{9,8},{10,11... | collective-permute-start | bytes 1179656 | tf_op jit(solution)/shard_map/ppermute | solution.py:495
  51.8 5.6 %collective-permute-start.12 = (f32[256,128]{1,0:T(8,128)S(1)}, f32[256,128]{1,0:T(8,128)S(1)}, u32[]{:S(2)}, u32[]{:S(2)}) collective-permute-start(f32[256,128]{1,0:T(8,128)S(1)} %sweep.2.own), channel_id=1, source_target_pairs={{0,4},{8,12},{16,20},{24,28},{4,0},{12,8},{20,16},{28,24},{1,5},{9... | collective-permute-start | bytes 393224 | tf_op jit(solution)/shard_map/ppermute | solution.py:480
  52.4 8.0 %collective-permute-start.13 = (f32[256,128]{1,0:T(8,128)S(1)}, f32[256,128]{1,0:T(8,128)S(1)}, u32[]{:S(2)}, u32[]{:S(2)}) collective-permute-start(f32[256,128]{1,0:T(8,128)S(1)} %sweep.2.own), channel_id=1, source_target_pairs={{4,8},{12,16},{20,24},{8,4},{16,12},{24,20},{5,9},{13,17},{21,25},... | collective-permute-start | bytes 393224 | tf_op jit(solution)/shard_map/ppermute | solution.py:481
  60.5 5.6 %collective-permute-start.14 = (f32[512,384]{1,0:T(8,128)S(1)}, f32[512,384]{1,0:T(8,128)S(1)}, u32[]{:S(2)}, u32[]{:S(2)}) collective-permute-start(f32[512,384]{1,0:T(8,128)S(1)} %lift_half.1.mine), channel_id=1, source_target_pairs={{0,1},{1,0},{2,3},{3,2},{4,5},{5,4},{6,7},{7,6},{8,9},{9,8},{10,11... | collective-permute-start | bytes 2359304 | tf_op jit(solution)/shard_map/ppermute | solution.py:495
  61.4 6.0 %collective-permute-start.15 = (f32[256,128]{1,0:T(8,128)S(1)}, f32[256,128]{1,0:T(8,128)S(1)}, u32[]{:S(2)}, u32[]{:S(2)}) collective-permute-start(f32[256,128]{1,0:T(8,128)S(1)} %sweep.3.own), channel_id=1, source_target_pairs={{0,4},{8,12},{16,20},{24,28},{4,0},{12,8},{20,16},{28,24},{1,5},{9... | collective-permute-start | bytes 393224 | tf_op jit(solution)/shard_map/ppermute | solution.py:480
  63.0 8.4 %collective-permute-start.16 = (f32[256,128]{1,0:T(8,128)S(1)}, f32[256,128]{1,0:T(8,128)S(1)}, u32[]{:S(2)}, u32[]{:S(2)}) collective-permute-start(f32[256,128]{1,0:T(8,128)S(1)} %sweep.3.own), channel_id=1, source_target_pairs={{4,8},{12,16},{20,24},{8,4},{16,12},{24,20},{5,9},{13,17},{21,25},... | collective-permute-start | bytes 393224 | tf_op jit(solution)/shard_map/ppermute | solution.py:481

commit v6 on v5

--- a/solution.py
+++ b/solution.py
@@ -265,7 +265,7 @@
     )(own_image, side, received, received_other, message)
 
 
-def ghost_kernel(agg_of, d_high, d_low, mine, other, half_ref, q_high, q_low):
+def ghost_kernel(agg_of, d_high, d_low, own_half, mine, other, rt_high, rt_low, parts_ref, coarse_ref, q_high, q_low):
     _, near, far = neighbours()
     sub = lax.axis_index("sub")
     core = sub & 1
@@ -276,19 +276,21 @@
         high, low = halves(placed(piece, agg_of[start + r] - 2 * core))
         q_high[span(r), :] = high
         q_low[span(r), :] = low
-    half_ref[...] = product((d_high[...], d_low[...]), (q_high[...], q_low[...]))
-
-
-def ghost_step(agg_of, d_high, d_low, mine, other):
+    parts_ref[:, :PAIR] = own_half[...]
+    parts_ref[:, PAIR:] = product((d_high[...], d_low[...]), (q_high[...], q_low[...]))
+    coarse_ref[...] = product((rt_high[...], rt_low[...]), halves(parts_ref[...]))
+
+
+def ghost_step(agg_of, d_high, d_low, own_half, mine, other, rt_high, rt_low):
     return pl.pallas_call(
         ghost_kernel,
-        in_specs=[SMEM] + [VMEM] * 4,
-        out_specs=VMEM,
-        out_shape=shape(WIDE, PAIR),
+        in_specs=[SMEM] + [VMEM] * 7,
+        out_specs=[VMEM] * 2,
+        out_shape=[shape(WIDE, 2 * PAIR), shape(COARSE, 2 * PAIR)],
         scratch_shapes=[pltpu.VMEM((WIDE, PAIR), BF16)] * 2,
         compiler_params=params(),
         name="ghost_step",
-    )(agg_of, d_high, d_low, mine, other)
+    )(agg_of, d_high, d_low, own_half, mine, other, rt_high, rt_low)
 
 
 def scaled_by_weight(agg_of, value):
@@ -303,26 +305,33 @@
     return jnp.concatenate(pieces, axis=0)
 
 
-def coarse_kernel(own, own_received, side, side_received, rt_high, rt_low, g_ref, coarse_ref):
+def summed_regions(mine, received):
     is_near = ((lax.axis_index("sub") >> 1) & 1) == 0
-    g_ref[:, span(0, PAIR)] = jnp.where(is_near, side[...], side_received[...])
-    g_ref[:, span(1, PAIR)] = own[...] + own_received[...]
-    g_ref[:, span(2, PAIR)] = jnp.where(is_near, side_received[...], side[...])
-    coarse_ref[...] = product((rt_high[...], rt_low[...]), halves(g_ref[...]))
-
-
-def coarse_half(own, own_received, side, side_received, rt_high, rt_low):
+    own = mine[:, :PAIR] + received[:, :PAIR]
+    near = jnp.where(is_near, mine[:, PAIR:], received[:, PAIR:])
+    far = jnp.where(is_near, received[:, PAIR:], mine[:, PAIR:])
+    return jnp.concatenate([near, own, far], axis=1)
+
+
+def coarse_kernel(mine, received, coarse_ref, high_ref, low_ref):
+    coarse = summed_regions(mine[...], received[...])
+    coarse_ref[...] = coarse
+    high_ref[...], low_ref[...] = halves(coarse)
+
+
+def coarse_half(mine, received):
     return pl.pallas_call(
         coarse_kernel,
-        in_specs=[VMEM] * 6,
-        out_specs=[VMEM] * 2,
-        out_shape=[shape(WIDE, 3 * PAIR), shape(COARSE, 3 * PAIR)],
+        in_specs=[VMEM] * 2,
+        out_specs=[VMEM] * 3,
+        out_shape=[shape(COARSE, 3 * PAIR)] + [shape(COARSE, 3 * PAIR, dtype=BF16)] * 2,
         compiler_params=params(),
         name="coarse_half",
-    )(own, own_received, side, side_received, rt_high, rt_low)
-
-
-def share_kernel(mine, other, op_ref, natural):
+    )(mine, received)
+
+
+def share_kernel(mine, other, op_ref, high_ref, low_ref, natural):
+    high_ref[...], low_ref[...] = halves(other[...])
     sub = lax.axis_index("sub")
     odd = lax.axis_index("slab") & 1
     is_first = (sub & 1) == 0
@@ -346,31 +355,32 @@
     return pl.pallas_call(
         share_kernel,
         in_specs=[VMEM] * 2,
-        out_specs=VMEM,
-        out_shape=shape(GROUPS, BANDS // SUBS, DOF, DOF),
+        out_specs=[VMEM] * 3,
+        out_shape=[shape(GROUPS, BANDS // SUBS, DOF, DOF)] + [shape(COARSE, 3 * PAIR, dtype=BF16)] * 2,
         scratch_shapes=[pltpu.VMEM((COARSE, 3 * COARSE), F32)],
         compiler_params=params(),
         name="coarse_share",
     )(mine, other)
 
 
-def lift_kernel(agg_of, g_half, smoother, prolong, w_ref):
+def lift_kernel(agg_of, mine, received, smoother, prolong, w_ref):
     start = lax.axis_index("slab") * ROWS
     core = lax.axis_index("sub") & 1
     for e in range(ROWS):
-        w_ref[span(e), :] = -product(halves(smoother[e]), halves(g_half[span(e), :]))
+        g_half = summed_regions(mine[span(e), :], received[span(e), :])
+        w_ref[span(e), :] = -product(halves(smoother[e]), halves(g_half))
         w_ref[span(e), span(1, PAIR)] += placed(prolong[e], agg_of[start + e] - 2 * core)
 
 
-def lift_half(agg_of, g_half, smoother, prolong):
+def lift_half(agg_of, mine, received, smoother, prolong):
     return pl.pallas_call(
         lift_kernel,
-        in_specs=[SMEM] + [VMEM] * 3,
+        in_specs=[SMEM] + [VMEM] * 4,
         out_specs=VMEM,
         out_shape=shape(WIDE, 3 * PAIR),
         compiler_params=params(),
         name="lift_half",
-    )(agg_of, g_half, smoother, prolong)
+    )(agg_of, mine, received, smoother, prolong)
 
 
 def residual_kernel(agg_of, keep, received, rt_high, rt_low, residual_ref, first_ref):
@@ -413,23 +423,26 @@
         yield jnp.concatenate([field[aligned(which, PAIR), :] for field in fields], axis=0)
 
 
-def sweep_kernel(agg_of, mine, other, first, near, own, far, next_ref):
+def sweep_kernel(agg_of, *refs):
+    operators, (first, far, near, own, next_ref) = refs[:-5], refs[-5:]
+    mine = (operators[0][...], operators[1][...])
+    other = halves(operators[2][...]) if len(operators) == 3 else (operators[2][...], operators[3][...])
     total = None
     for operator, field in zip((mine, other), core_parts(near, own, far)):
-        part = narrow_product(halves(operator[...]), field)
+        part = narrow_product(operator, field)
         total = part if total is None else total + part
     next_ref[...] = own[...] + first[...] - scaled_by_weight(agg_of, total)
 
 
-def sweep(agg_of, mine, other, first, near, own, far):
+def sweep(agg_of, operators, first, near, own, far):
     return pl.pallas_call(
         sweep_kernel,
-        in_specs=[SMEM] + [VMEM] * 6,
+        in_specs=[SMEM] + [VMEM] * (len(operators) + 4),
         out_specs=VMEM,
         out_shape=shape(COARSE, COLS),
         compiler_params=params(),
         name="sweep",
-    )(agg_of, mine, other, first, near, own, far)
+    )(agg_of, *operators, first, far, near, own)
 
 
 def lifted_kernel(mine, other, base, own, base_ref, high_ref, low_ref):
@@ -454,7 +467,7 @@
     )(mine, other, base, own)
 
 
-def last_kernel(w_high, w_low, base, near, far, out_ref):
+def last_kernel(w_high, w_low, base, far, near, out_ref):
     field = jnp.concatenate(list(core_parts(near, far)), axis=0)
     out_ref[...] = base[...] + narrow_product((w_high[...], w_low[...]), field)
 
@@ -467,7 +480,7 @@
         out_shape=shape(WIDE, COLS),
         compiler_params=params(),
         name="last_step",
-    )(w_high, w_low, base, near, far)
+    )(w_high, w_low, base, far, near)
 
 
 def swaps(size, start):
@@ -479,7 +492,7 @@
     size = lax.axis_size("slab")
     near = lax.ppermute(value, "slab", swaps(size, 0))
     far = lax.ppermute(value, "slab", swaps(size, 1))
-    return near, far
+    return far, near
 
 
 def from_side(value):
@@ -504,30 +517,32 @@
     received = swapped(mine + theirs, 2)
     pair, theirs = lax.optimization_barrier((pair, theirs))
     side, own_half, own_image, rt_high, rt_low = own_step(agg_of, prolong, message, right, pair, swapped(pair, 1))
-    received, side, own_half = lax.optimization_barrier((received, side, own_half))
-    own_received = swapped(own_half, 2)
+    received, side = lax.optimization_barrier((received, side))
     keep, send, d_high, d_low = image(own_image, side, received, swapped(received, 1), side_message)
-    send, own_received = lax.optimization_barrier((send, own_received))
     image_received = swapped(send, 2)
     ghosts = side_message[WIDE:]
-    side_half = ghost_step(agg_of, d_high, d_low, ghosts, swapped(ghosts, 1))
-    side_received = swapped(side_half, 2)
+    parts, coarse = ghost_step(agg_of, d_high, d_low, own_half, ghosts, swapped(ghosts, 1), rt_high, rt_low)
+    coarse_received = swapped(coarse, 2)
     residual, first = residual_step(agg_of, keep, image_received, rt_high, rt_low)
     base = base_step(smoother, message, residual)
-    near, far = from_neighbours(first)
-    g_half, coarse = coarse_half(own_half, own_received, side_half, side_received, rt_high, rt_low)
-    near, far, coarse = lax.optimization_barrier((near, far, coarse))
+    far, near = from_neighbours(first)
+    parts, coarse_received = lax.optimization_barrier((parts, coarse_received))
+    parts_received = swapped(parts, 2)
+    coarse, mine_high, mine_low = coarse_half(coarse, coarse_received)
+    far, near, coarse = lax.optimization_barrier((far, near, coarse))
     coarse_other = swapped(coarse, 1)
-    coarse_op = coarse_share(coarse, coarse_other)
-    lift = lift_half(agg_of, g_half, smoother, prolong)
-    correction = first
-    for index in range(COARSE_SWEEPS - 1):
-        if index > 0:
-            near, far = from_neighbours(correction)
-            lift, near, far = lax.optimization_barrier((lift, near, far))
-        correction = sweep(agg_of, coarse, coarse_other, first, near, correction, far)
+    correction = sweep(agg_of, (mine_high, mine_low, coarse_other), first, near, first, far)
+    coarse_op, other_high, other_low = coarse_share(coarse, coarse_other)
+    lift = lift_half(agg_of, parts, parts_received, smoother, prolong)
+    for index in range(1, COARSE_SWEEPS - 1):
+        far, near = from_neighbours(correction)
+        if index == 1:
+            shadowed = (far, near, lift, other_high, other_low)
+            far, near, lift, other_high, other_low = lax.optimization_barrier(shadowed)
+        operators = (mine_high, mine_low, other_high, other_low)
+        correction = sweep(agg_of, operators, first, near, correction, far)
     lift_other = swapped(lift, 1)
-    near, far = from_neighbours(correction)
+    far, near = from_neighbours(correction)
     base, w_high, w_low = lifted(lift, lift_other, base, correction)
     solution = last_step(w_high, w_low, base, near, far)
     return coarse_op, solution.reshape(ROWS, DOF, COLS)

time: 73 us -> 75.2 us (1.030)
  starting transfers between devices: 18.2 us -> 24.5 us
  waiting for transfers between devices: 37.8 us -> 33.2 us
    ppermute x3, waiting for transfers between devices: 9.91 us -> 5.62 us  [from_neighbours(): far = lax.ppermute(value, 'slab', swaps(size, 1))]
    ppermute x3, starting transfers between devices: 5.73 us -> 9.92 us  [from_neighbours(): far = lax.ppermute(value, 'slab', swaps(size, 1))]
    ppermute x1, waiting for transfers between devices: 3 us -> 4.48 us  [from_side(): return lax.ppermute(value, ('slab', 'sub'), pairs)]
    ppermute x3, starting transfers between devices: 3.73 us -> 5.14 us  [from_neighbours(): near = lax.ppermute(value, 'slab', swaps(size, 0))]
    ppermute x10, waiting for transfers between devices: 20 us -> 19 us  [swapped(): return lax.ppermute(value, 'sub', [(i, i ^ bit) for i in range(size)])]
    ppermute x10, starting transfers between devices: 5.32 us -> 6.07 us  [swapped(): return lax.ppermute(value, 'sub', [(i, i ^ bit) for i in range(size)])]
  transfers between devices with their start and end apart: 17 -> 17, of which waited for: 14 -> 10; matrix products, arithmetic and copies ran while one was open for 0% -> 0% of each run, Pallas kernels for 13% -> 13%
where the time goes in v6:
time: 75.2 us; the launch traced here: 74.5 us
  waiting for transfers between devices  33.2 us (44%)
  starting transfers between devices  24.5 us (33%)
  Pallas kernels  15.9 us (21%)
  between operations  0.83 us (1%)
    ppermute x10, waiting for transfers between devices, swapped(): return lax.ppermute(value, 'sub', [(i, i ^ bit) for i in range(size)])  19 us
    ppermute x3, starting transfers between devices, from_neighbours(): far = lax.ppermute(value, 'slab', swaps(size, 1))  9.92 us
    ppermute x10, starting transfers between devices, swapped(): return lax.ppermute(value, 'sub', [(i, i ^ bit) for i in range(size)])  6.07 us
    ppermute x3, waiting for transfers between devices, from_neighbours(): far = lax.ppermute(value, 'slab', swaps(size, 1))  5.62 us
    ppermute x3, starting transfers between devices, from_neighbours(): near = lax.ppermute(value, 'slab', swaps(size, 0))  5.14 us
    ppermute x1, waiting for transfers between devices, from_side(): return lax.ppermute(value, ('slab', 'sub'), pairs)  4.48 us
    pallas_call x1, Pallas kernels, start_step(): pl.pallas_call(start_kernel, in_specs=[HBM] * 7, out_specs=[VMEM] * 5, ou...  4.16 us
    ppermute x3, waiting for transfers between devices, from_neighbours(): near = lax.ppermute(value, 'slab', swaps(size, 0))  4.16 us
  transfers between devices with their start and end apart: 17, of which 10 were waited for; matrix products, arithmetic and copies ran while one was open for 0% of the time, Pallas kernels for 13%

profile of v6, /device:TPU:8, one launch (start us, length us, event | category | flops | bytes accessed | tf_op | source)
XLA Modules:
  0.0 74.5 jit_solution(14052873862612392444)
XLA Ops:
  0.6 0.0 copy-start
  0.6 0.0 copy-start.2
  0.7 4.2 %start_step.1 = (f32[512,1024]{1,0:T(8,128)S(1)}, f32[256,512]{1,0:T(8,128)S(1)}, f32[256,512]{1,0:T(8,128)S(1)}, f32[576,256]{1,0:T(8,128)S(1)}, f32[512,128]{1,0:T(8,128)S(1)}) custom-call(s32[8,16]{1,0:T(8,128)} %col_hbm.1, s32[8,4,2,8]{3,2,1,0:T(2,128)} %rows_hbm.1, s32[4,2,8]{2,1,0:T(2,128)} %bitcast.3, f32[8,16,64,64]{3,2,1,0:T(8,128)} %blocks_hbm.1, ...), custom_call_target="tpu_custom_call" | custom-call | tf_op jit(solution)/shard_map/start_step/pallas_call | solution.py:156
  4.8 0.1 collective-permute-start
  4.9 1.9 %collective-permute-done = f32[256,512]{1,0:T(8,128)S(1)} collective-permute-done((f32[256,512]{1,0:T(8,128)S(1)}, f32[256,512]{1,0:T(8,128)S(1)}, u32[]{:S(2)}, u32[]{:S(2)}) %collective-permute-start) | collective-permute-done | bytes 524320 | tf_op jit(solution)/shard_map/ppermute | solution.py:508
  6.8 0.1 collective-permute-start.1
  6.9 0.1 add.3
  7.0 1.6 %collective-permute-start.2 = (f32[256,512]{1,0:T(8,128)S(1)}, f32[256,512]{1,0:T(8,128)S(1)}, u32[]{:S(2)}, u32[]{:S(2)}) collective-permute-start(f32[256,512]{1,0:T(8,128)S(1)} %add.3), channel_id=1, source_target_pairs={{0,2},{1,3},{2,0},{3,1},{4,6},{5,7},{6,4},{7,5},{8,10},{9,11},{10,... | collective-permute-start | bytes 1572872 | tf_op jit(solution)/shard_map/ppermute | solution.py:508
  8.6 3.4 %collective-permute-start.4 = (f32[576,256]{1,0:T(8,128)S(1)}, f32[576,256]{1,0:T(8,128)S(1)}, u32[]{:S(2)}, u32[]{:S(2)}) collective-permute-start(f32[576,256]{1,0:T(8,128)S(1)} %get-tuple-element.42.field.message), channel_id=1, source_target_pairs={{0,4},{8,12},{16,20},{24,28},{4,0},{12,8},{20,16},{28,24},{1,5},{9... | collective-permute-start | bytes 1769480 | tf_op jit(solution)/shard_map/ppermute | solution.py:503
  12.0 0.0 collective-permute-done.1.pair_other
  12.0 0.0 copy-done
  12.0 0.0 copy-done.2
  12.0 2.3 %own_step.1 = (f32[512,512]{1,0:T(8,128)S(1)}, f32[512,128]{1,0:T(8,128)S(1)}, f32[512,256]{1,0:T(8,128)S(1)}, bf16[256,512]{1,0:T(8,128)(2,1)S(1)}, bf16[256,512]{1,0:T(8,128)(2,1)S(1)}) custom-call(s32[64]{0:T(128)S(1)} %copy-done.2, f32[8,64,64]{2,1,0:T(8,128)S(1)} %copy-done, f32[576,256]{1,0:T(8,128)S(1)} %get-tuple-element.42.field.message, ...), custom_call_target="tpu_custom_call" | custom-call | tf_op jit(solution)/shard_map/own_step/pallas_call | solution.py:224
  14.3 7.0 %collective-permute-done.2.received = f32[256,512]{1,0:T(8,128)S(1)} collective-permute-done((f32[256,512]{1,0:T(8,128)S(1)}, f32[256,512]{1,0:T(8,128)S(1)}, u32[]{:S(2)}, u32[]{:S(2)}) %collective-permute-start.2) | collective-permute-done | bytes 524320 | tf_op jit(solution)/shard_map/ppermute | solution.py:508
  21.3 0.0 collective-permute-start.3
  21.3 4.5 %collective-permute-done.4.message = f32[576,256]{1,0:T(8,128)S(1)} collective-permute-done((f32[576,256]{1,0:T(8,128)S(1)}, f32[576,256]{1,0:T(8,128)S(1)}, u32[]{:S(2)}, u32[]{:S(2)}) %collective-permute-start.4) | collective-permute-done | bytes 589856 | tf_op jit(solution)/shard_map/ppermute | solution.py:503
  25.8 0.0 collective-permute-done.3.received_other
  25.8 0.7 image.1
  26.5 1.5 %collective-permute-start.5 = (f32[512,128]{1,0:T(8,128)S(1)}, f32[512,128]{1,0:T(8,128)S(1)}, u32[]{:S(2)}, u32[]{:S(2)}) collective-permute-start(f32[512,128]{1,0:T(8,128)S(1)} %get-tuple-element.53), channel_id=1, source_target_pairs={{0,2},{1,3},{2,0},{3,1},{4,6},{5,7},{6,4},{7,5},{8,10},{9,11},{10,... | collective-permute-start | bytes 786440 | tf_op jit(solution)/shard_map/ppermute | solution.py:508
  28.0 0.0 collective-permute-start.8
  28.0 1.2 %collective-permute-done.8.other = f32[64,256]{1,0:T(8,128)S(1)} collective-permute-done((f32[64,256]{1,0:T(8,128)S(1)}, f32[64,256]{1,0:T(8,128)S(1)}, u32[]{:S(2)}, u32[]{:S(2)}) %collective-permute-start.8) | collective-permute-done | bytes 65568 | tf_op jit(solution)/shard_map/ppermute | solution.py:508
  29.3 0.0 copy-start.1
  29.3 1.9 %ghost_step.1 = (f32[512,256]{1,0:T(8,128)S(1)}, f32[256,256]{1,0:T(8,128)S(1)}) custom-call(s32[64]{0:T(128)S(1)} %copy-done.2, bf16[512,512]{1,0:T(8,128)(2,1)S(1)} %get-tuple-element.57.d_high, bf16[512,512]{1,0:T(8,128)(2,1)S(1)} %get-tuple-element.58.d_low, f32[512,128]{1,0:T(8,128)S(1)} %get-tuple-element.59.own_half, f32[64,256]{1,0:T(8,128)S(1)} %slice.4.mine, ...), custom_call_target="tpu_custom_call" | custom-call | tf_op jit(solution)/shard_map/ghost_step/pallas_call | solution.py:285
  31.1 0.6 collective-permute-start.9
  31.8 2.2 %collective-permute-done.5.received = f32[512,128]{1,0:T(8,128)S(1)} collective-permute-done((f32[512,128]{1,0:T(8,128)S(1)}, f32[512,128]{1,0:T(8,128)S(1)}, u32[]{:S(2)}, u32[]{:S(2)}) %collective-permute-start.5) | collective-permute-done | bytes 262176 | tf_op jit(solution)/shard_map/ppermute | solution.py:508
  34.0 0.8 %residual_step.1 = (f32[512,128]{1,0:T(8,128)S(1)}, f32[256,128]{1,0:T(8,128)S(1)}) custom-call(s32[64]{0:T(128)S(1)} %copy-done.2, f32[512,128]{1,0:T(8,128)S(1)} %get-tuple-element.52.keep, f32[512,128]{1,0:T(8,128)S(1)} %collective-permute-done.5.received, bf16[256,512]{1,0:T(8,128)(2,1)S(1)} %get-tuple-element.54.rt_high, ...), custom_call_target="tpu_custom_call" | custom-call | tf_op jit(solution)/shard_map/residual_step/pallas_call | solution.py:393
  34.8 3.3 %collective-permute-start.6 = (f32[256,128]{1,0:T(8,128)S(1)}, f32[256,128]{1,0:T(8,128)S(1)}, u32[]{:S(2)}, u32[]{:S(2)}) collective-permute-start(f32[256,128]{1,0:T(8,128)S(1)} %get-tuple-element.56.refs_3_.refs_6_.refs_4_), channel_id=1, source_target_pairs={{4,8},{12,16},{20,24},{8,4},{16,12},{24,20},{5,9},{13,17},{21,25},... | collective-permute-start | bytes 393224 | tf_op jit(solution)/shard_map/ppermute | solution.py:494
  38.2 1.7 %collective-permute-start.7 = (f32[256,128]{1,0:T(8,128)S(1)}, f32[256,128]{1,0:T(8,128)S(1)}, u32[]{:S(2)}, u32[]{:S(2)}) collective-permute-start(f32[256,128]{1,0:T(8,128)S(1)} %get-tuple-element.56.refs_3_.refs_6_.refs_4_), channel_id=1, source_target_pairs={{0,4},{8,12},{16,20},{24,28},{4,0},{12,8},{20,16},{28,24},{1,5},{9... | collective-permute-start | bytes 393224 | tf_op jit(solution)/shard_map/ppermute | solution.py:493
  39.9 0.0 collective-permute-done.9.received
  39.9 0.1 coarse_half.1
  40.0 2.7 %collective-permute-done.6.refs_4_ = f32[256,128]{1,0:T(8,128)S(1)} collective-permute-done((f32[256,128]{1,0:T(8,128)S(1)}, f32[256,128]{1,0:T(8,128)S(1)}, u32[]{:S(2)}, u32[]{:S(2)}) %collective-permute-start.6) | collective-permute-done | bytes 131104 | tf_op jit(solution)/shard_map/ppermute | solution.py:494
  42.7 1.5 %collective-permute-done.7.refs_5_ = f32[256,128]{1,0:T(8,128)S(1)} collective-permute-done((f32[256,128]{1,0:T(8,128)S(1)}, f32[256,128]{1,0:T(8,128)S(1)}, u32[]{:S(2)}, u32[]{:S(2)}) %collective-permute-start.7) | collective-permute-done | bytes 131104 | tf_op jit(solution)/shard_map/ppermute | solution.py:493
  44.2 0.0 collective-permute-start.10
  44.2 2.1 %collective-permute-start.13 = (f32[512,256]{1,0:T(8,128)S(1)}, f32[512,256]{1,0:T(8,128)S(1)}, u32[]{:S(2)}, u32[]{:S(2)}) collective-permute-start(f32[512,256]{1,0:T(8,128)S(1)} %get-tuple-element.70.mine), channel_id=1, source_target_pairs={{0,2},{1,3},{2,0},{3,1},{4,6},{5,7},{6,4},{7,5},{8,10},{9,11},{10,... | collective-permute-start | bytes 1572872 | tf_op jit(solution)/shard_map/ppermute | solution.py:508
  46.3 0.0 collective-permute-done.10.other.refs_2_
  46.3 0.9 %sweep.2.refs_7_ = f32[256,128]{1,0:T(8,128)S(1)} custom-call(s32[64]{0:T(128)S(1)} %copy-done.2, bf16[256,384]{1,0:T(8,128)(2,1)S(1)} %get-tuple-element.66.refs_0_, bf16[256,384]{1,0:T(8,128)(2,1)S(1)} %get-tuple-element.67.refs_1_, f32[256,384]{1,0:T(8,128)S(1)} %collective-permute-done.10.other.refs_2_, ...), custom_call_target="tpu_custom_call" | custom-call | tf_op jit(solution)/shard_map/sweep/pallas_call | solution.py:438
  47.3 3.3 %collective-permute-start.11 = (f32[256,128]{1,0:T(8,128)S(1)}, f32[256,128]{1,0:T(8,128)S(1)}, u32[]{:S(2)}, u32[]{:S(2)}) collective-permute-start(f32[256,128]{1,0:T(8,128)S(1)} %sweep.2.refs_7_), channel_id=1, source_target_pairs={{4,8},{12,16},{20,24},{8,4},{16,12},{24,20},{5,9},{13,17},{21,25},... | collective-permute-start | bytes 393224 | tf_op jit(solution)/shard_map/ppermute | solution.py:494
  50.6 1.8 %collective-permute-start.12 = (f32[256,128]{1,0:T(8,128)S(1)}, f32[256,128]{1,0:T(8,128)S(1)}, u32[]{:S(2)}, u32[]{:S(2)}) collective-permute-start(f32[256,128]{1,0:T(8,128)S(1)} %sweep.2.refs_7_), channel_id=1, source_target_pairs={{0,4},{8,12},{16,20},{24,28},{4,0},{12,8},{20,16},{28,24},{1,5},{9... | collective-permute-start | bytes 393224 | tf_op jit(solution)/shard_map/ppermute | solution.py:493
  52.3 6.6 %collective-permute-done.13.received = f32[512,256]{1,0:T(8,128)S(1)} collective-permute-done((f32[512,256]{1,0:T(8,128)S(1)}, f32[512,256]{1,0:T(8,128)S(1)}, u32[]{:S(2)}, u32[]{:S(2)}) %collective-permute-start.13) | collective-permute-done | bytes 524320 | tf_op jit(solution)/shard_map/ppermute | solution.py:508
  58.9 0.0 copy-done.1
  58.9 1.0 %lift_half.1.mine = f32[512,384]{1,0:T(8,128)S(1)} custom-call(s32[64]{0:T(128)S(1)} %copy-done.2, f32[512,256]{1,0:T(8,128)S(1)} %get-tuple-element.70.mine, f32[512,256]{1,0:T(8,128)S(1)} %collective-permute-done.13.received, f32[8,64,64]{2,1,0:T(8,128)S(1)} %copy-done.1, f32[8,64,64]{2,1,0:T(8,128)S(1)} %copy-done), custom_call_target="tpu_custom_call" | custom-call | tf_op jit(solution)/shard_map/lift_half/pallas_call | solution.py:376
  59.9 1.0 %coarse_share.1 = (f32[4,3,64,64]{3,2,1,0:T(8,128)}, bf16[256,384]{1,0:T(8,128)(2,1)S(1)}, bf16[256,384]{1,0:T(8,128)(2,1)S(1)}) custom-call(f32[256,384]{1,0:T(8,128)S(1)} %get-tuple-element.64.mine, f32[256,384]{1,0:T(8,128)S(1)} %collective-permute-done.10.other.refs_2_), custom_call_target="tpu_custom_call" | custom-call | tf_op jit(solution)/shard_map/coarse_share/pallas_call | solution.py:355
  60.9 0.0 collective-permute-done.11.refs_5_
  60.9 0.0 collective-permute-done.12.refs_6_
  60.9 0.0 collective-permute-start.14
  60.9 0.9 %sweep.3.own = f32[256,128]{1,0:T(8,128)S(1)} custom-call(s32[64]{0:T(128)S(1)} %copy-done.2, bf16[256,384]{1,0:T(8,128)(2,1)S(1)} %get-tuple-element.66.refs_0_, bf16[256,384]{1,0:T(8,128)(2,1)S(1)} %get-tuple-element.67.refs_1_, bf16[256,384]{1,0:T(8,128)(2,1)S(1)} %get-tuple-element.75.refs_2_, bf16[256,384]{1,0:T(8,128)(2,1)S(1)} %get-tuple-element.76.refs_3_, ...), custom_call_target="tpu_custom_call" | custom-call | tf_op jit(solution)/shard_map/sweep/pallas_call | solution.py:438
  61.9 3.3 %collective-permute-start.15 = (f32[256,128]{1,0:T(8,128)S(1)}, f32[256,128]{1,0:T(8,128)S(1)}, u32[]{:S(2)}, u32[]{:S(2)}) collective-permute-start(f32[256,128]{1,0:T(8,128)S(1)} %sweep.3.own), channel_id=1, source_target_pairs={{4,8},{12,16},{20,24},{8,4},{16,12},{24,20},{5,9},{13,17},{21,25},... | collective-permute-start | bytes 393224 | tf_op jit(solution)/shard_map/ppermute | solution.py:494
  65.2 1.7 %collective-permute-start.16 = (f32[256,128]{1,0:T(8,128)S(1)}, f32[256,128]{1,0:T(8,128)S(1)}, u32[]{:S(2)}, u32[]{:S(2)}) collective-permute-start(f32[256,128]{1,0:T(8,128)S(1)} %sweep.3.own), channel_id=1, source_target_pairs={{0,4},{8,12},{16,20},{24,28},{4,0},{12,8},{20,16},{28,24},{1,5},{9... | collective-permute-start | bytes 393224 | tf_op jit(solution)/shard_map/ppermute | solution.py:493
  66.9 0.3 base_step.1.base
  67.2 0.0 collective-permute-done.14.other
  67.2 0.6 lifted.1
  67.8 2.9 %collective-permute-done.15.far = f32[256,128]{1,0:T(8,128)S(1)} collective-permute-done((f32[256,128]{1,0:T(8,128)S(1)}, f32[256,128]{1,0:T(8,128)S(1)}, u32[]{:S(2)}, u32[]{:S(2)}) %collective-permute-start.15) | collective-permute-done | bytes 131104 | tf_op jit(solution)/shard_map/ppermute | solution.py:494
  70.7 2.7 %collective-permute-done.16.near = f32[256,128]{1,0:T(8,128)S(1)} collective-permute-done((f32[256,128]{1,0:T(8,128)S(1)}, f32[256,128]{1,0:T(8,128)S(1)}, u32[]{:S(2)}, u32[]{:S(2)}) %collective-permute-start.16) | collective-permute-done | bytes 131104 | tf_op jit(solution)/shard_map/ppermute | solution.py:493
  73.4 1.1 %last_step.1 = f32[512,128]{1,0:T(8,128)} custom-call(bf16[512,512]{1,0:T(8,128)(2,1)S(1)} %get-tuple-element.79.w_high, bf16[512,512]{1,0:T(8,128)(2,1)S(1)} %get-tuple-element.80.w_low, f32[512,128]{1,0:T(8,128)S(1)} %get-tuple-element.81.base, f32[256,128]{1,0:T(8,128)S(1)} %collective-permute-done.15.far, f32[256,128]{1,0:T(8,128)S(1)} %collective-permute-done.16.near), custom_call_target="tpu_custom_call" | custom-call | tf_op jit(solution)/shard_map/last_step/pallas_call | solution.py:476
  (1 shorter events, 0.0 us)
Async XLA Ops:
  0.6 11.4 %copy-start = (f32[8,64,64]{2,1,0:T(8,128)S(1)}, f32[8,64,64]{2,1,0:T(8,128)}, u32[]{:S(2)}) copy-start(f32[8,64,64]{2,1,0:T(8,128)} %prolong.3) | copy-start | bytes 393220
  0.6 11.4 %copy-start.2 = (s32[64]{0:T(128)S(1)}, s32[64]{0:T(128)}, u32[]{:S(2)}) copy-start(s32[64]{0:T(128)} %agg_of.11) | copy-start | bytes 772
  4.8 2.0 %collective-permute-start = (f32[256,512]{1,0:T(8,128)S(1)}, f32[256,512]{1,0:T(8,128)S(1)}, u32[]{:S(2)}, u32[]{:S(2)}) collective-permute-start(f32[256,512]{1,0:T(8,128)S(1)} %get-tuple-element.45), channel_id=1, source_target_pairs={{0,1},{1,0},{2,3},{3,2},{4,5},{5,4},{6,7},{7,6},{8,9},{9,8},{10,11... | collective-permute-start | bytes 1572872 | tf_op jit(solution)/shard_map/ppermute | solution.py:508
  6.8 5.2 %collective-permute-start.1 = (f32[512,1024]{1,0:T(8,128)S(1)}, f32[512,1024]{1,0:T(8,128)S(1)}, u32[]{:S(2)}, u32[]{:S(2)}) collective-permute-start(f32[512,1024]{1,0:T(8,128)S(1)} %get-tuple-element.46.pair), channel_id=1, source_target_pairs={{0,1},{1,0},{2,3},{3,2},{4,5},{5,4},{6,7},{7,6},{8,9},{9,8},{10,11... | collective-permute-start | bytes 6291464 | tf_op jit(solution)/shard_map/ppermute | solution.py:508
  7.0 14.3 %collective-permute-start.2 = (f32[256,512]{1,0:T(8,128)S(1)}, f32[256,512]{1,0:T(8,128)S(1)}, u32[]{:S(2)}, u32[]{:S(2)}) collective-permute-start(f32[256,512]{1,0:T(8,128)S(1)} %add.3), channel_id=1, source_target_pairs={{0,2},{1,3},{2,0},{3,1},{4,6},{5,7},{6,4},{7,5},{8,10},{9,11},{10,... | collective-permute-start | bytes 1572872 | tf_op jit(solution)/shard_map/ppermute | solution.py:508
  8.6 17.2 %collective-permute-start.4 = (f32[576,256]{1,0:T(8,128)S(1)}, f32[576,256]{1,0:T(8,128)S(1)}, u32[]{:S(2)}, u32[]{:S(2)}) collective-permute-start(f32[576,256]{1,0:T(8,128)S(1)} %get-tuple-element.42.field.message), channel_id=1, source_target_pairs={{0,4},{8,12},{16,20},{24,28},{4,0},{12,8},{20,16},{28,24},{1,5},{9... | collective-permute-start | bytes 1769480 | tf_op jit(solution)/shard_map/ppermute | solution.py:503
  21.3 4.5 %collective-permute-start.3 = (f32[256,512]{1,0:T(8,128)S(1)}, f32[256,512]{1,0:T(8,128)S(1)}, u32[]{:S(2)}, u32[]{:S(2)}) collective-permute-start(f32[256,512]{1,0:T(8,128)S(1)} %collective-permute-done.2.received), channel_id=1, source_target_pairs={{0,1},{1,0},{2,3},{3,2},{4,5},{5,4},{6,7},{7,6},{8,9},{9,8},{10,11... | collective-permute-start | bytes 1572872 | tf_op jit(solution)/shard_map/ppermute | solution.py:508
  26.5 7.5 %collective-permute-start.5 = (f32[512,128]{1,0:T(8,128)S(1)}, f32[512,128]{1,0:T(8,128)S(1)}, u32[]{:S(2)}, u32[]{:S(2)}) collective-permute-start(f32[512,128]{1,0:T(8,128)S(1)} %get-tuple-element.53), channel_id=1, source_target_pairs={{0,2},{1,3},{2,0},{3,1},{4,6},{5,7},{6,4},{7,5},{8,10},{9,11},{10,... | collective-permute-start | bytes 786440 | tf_op jit(solution)/shard_map/ppermute | solution.py:508
  28.0 1.3 %collective-permute-start.8 = (f32[64,256]{1,0:T(8,128)S(1)}, f32[64,256]{1,0:T(8,128)S(1)}, u32[]{:S(2)}, u32[]{:S(2)}) collective-permute-start(f32[64,256]{1,0:T(8,128)S(1)} %slice.4.mine), channel_id=1, source_target_pairs={{0,1},{1,0},{2,3},{3,2},{4,5},{5,4},{6,7},{7,6},{8,9},{9,8},{10,11... | collective-permute-start | bytes 196616 | tf_op jit(solution)/shard_map/ppermute | solution.py:508
  29.3 29.6 %copy-start.1 = (f32[8,64,64]{2,1,0:T(8,128)S(1)}, f32[8,64,64]{2,1,0:T(8,128)}, u32[]{:S(2)}) copy-start(f32[8,64,64]{2,1,0:T(8,128)} %smoother.3) | copy-start | bytes 393220
  31.1 8.7 %collective-permute-start.9 = (f32[256,256]{1,0:T(8,128)S(1)}, f32[256,256]{1,0:T(8,128)S(1)}, u32[]{:S(2)}, u32[]{:S(2)}) collective-permute-start(f32[256,256]{1,0:T(8,128)S(1)} %get-tuple-element.60.mine), channel_id=1, source_target_pairs={{0,2},{1,3},{2,0},{3,1},{4,6},{5,7},{6,4},{7,5},{8,10},{9,11},{10,... | collective-permute-start | bytes 786440 | tf_op jit(solution)/shard_map/ppermute | solution.py:508
  34.8 7.9 %collective-permute-start.6 = (f32[256,128]{1,0:T(8,128)S(1)}, f32[256,128]{1,0:T(8,128)S(1)}, u32[]{:S(2)}, u32[]{:S(2)}) collective-permute-start(f32[256,128]{1,0:T(8,128)S(1)} %get-tuple-element.56.refs_3_.refs_6_.refs_4_), channel_id=1, source_target_pairs={{4,8},{12,16},{20,24},{8,4},{16,12},{24,20},{5,9},{13,17},{21,25},... | collective-permute-start | bytes 393224 | tf_op jit(solution)/shard_map/ppermute | solution.py:494
  38.2 6.0 %collective-permute-start.7 = (f32[256,128]{1,0:T(8,128)S(1)}, f32[256,128]{1,0:T(8,128)S(1)}, u32[]{:S(2)}, u32[]{:S(2)}) collective-permute-start(f32[256,128]{1,0:T(8,128)S(1)} %get-tuple-element.56.refs_3_.refs_6_.refs_4_), channel_id=1, source_target_pairs={{0,4},{8,12},{16,20},{24,28},{4,0},{12,8},{20,16},{28,24},{1,5},{9... | collective-permute-start | bytes 393224 | tf_op jit(solution)/shard_map/ppermute | solution.py:493
  44.2 2.1 %collective-permute-start.10 = (f32[256,384]{1,0:T(8,128)S(1)}, f32[256,384]{1,0:T(8,128)S(1)}, u32[]{:S(2)}, u32[]{:S(2)}) collective-permute-start(f32[256,384]{1,0:T(8,128)S(1)} %get-tuple-element.64.mine), channel_id=1, source_target_pairs={{0,1},{1,0},{2,3},{3,2},{4,5},{5,4},{6,7},{7,6},{8,9},{9,8},{10,11... | collective-permute-start | bytes 1179656 | tf_op jit(solution)/shard_map/ppermute | solution.py:508
  44.2 14.7 %collective-permute-start.13 = (f32[512,256]{1,0:T(8,128)S(1)}, f32[512,256]{1,0:T(8,128)S(1)}, u32[]{:S(2)}, u32[]{:S(2)}) collective-permute-start(f32[512,256]{1,0:T(8,128)S(1)} %get-tuple-element.70.mine), channel_id=1, source_target_pairs={{0,2},{1,3},{2,0},{3,1},{4,6},{5,7},{6,4},{7,5},{8,10},{9,11},{10,... | collective-permute-start | bytes 1572872 | tf_op jit(solution)/shard_map/ppermute | solution.py:508
  47.3 13.6 %collective-permute-start.11 = (f32[256,128]{1,0:T(8,128)S(1)}, f32[256,128]{1,0:T(8,128)S(1)}, u32[]{:S(2)}, u32[]{:S(2)}) collective-permute-start(f32[256,128]{1,0:T(8,128)S(1)} %sweep.2.refs_7_), channel_id=1, source_target_pairs={{4,8},{12,16},{20,24},{8,4},{16,12},{24,20},{5,9},{13,17},{21,25},... | collective-permute-start | bytes 393224 | tf_op jit(solution)/shard_map/ppermute | solution.py:494
  50.6 10.4 %collective-permute-start.12 = (f32[256,128]{1,0:T(8,128)S(1)}, f32[256,128]{1,0:T(8,128)S(1)}, u32[]{:S(2)}, u32[]{:S(2)}) collective-permute-start(f32[256,128]{1,0:T(8,128)S(1)} %sweep.2.refs_7_), channel_id=1, source_target_pairs={{0,4},{8,12},{16,20},{24,28},{4,0},{12,8},{20,16},{28,24},{1,5},{9... | collective-permute-start | bytes 393224 | tf_op jit(solution)/shard_map/ppermute | solution.py:493
  60.9 6.3 %collective-permute-start.14 = (f32[512,384]{1,0:T(8,128)S(1)}, f32[512,384]{1,0:T(8,128)S(1)}, u32[]{:S(2)}, u32[]{:S(2)}) collective-permute-start(f32[512,384]{1,0:T(8,128)S(1)} %lift_half.1.mine), channel_id=1, source_target_pairs={{0,1},{1,0},{2,3},{3,2},{4,5},{5,4},{6,7},{7,6},{8,9},{9,8},{10,11... | collective-permute-start | bytes 2359304 | tf_op jit(solution)/shard_map/ppermute | solution.py:508
  61.9 8.8 %collective-permute-start.15 = (f32[256,128]{1,0:T(8,128)S(1)}, f32[256,128]{1,0:T(8,128)S(1)}, u32[]{:S(2)}, u32[]{:S(2)}) collective-permute-start(f32[256,128]{1,0:T(8,128)S(1)} %sweep.3.own), channel_id=1, source_target_pairs={{4,8},{12,16},{20,24},{8,4},{16,12},{24,20},{5,9},{13,17},{21,25},... | collective-permute-start | bytes 393224 | tf_op jit(solution)/shard_map/ppermute | solution.py:494
  65.2 8.2 %collective-permute-start.16 = (f32[256,128]{1,0:T(8,128)S(1)}, f32[256,128]{1,0:T(8,128)S(1)}, u32[]{:S(2)}, u32[]{:S(2)}) collective-permute-start(f32[256,128]{1,0:T(8,128)S(1)} %sweep.3.own), channel_id=1, source_target_pairs={{0,4},{8,12},{16,20},{24,28},{4,0},{12,8},{20,16},{28,24},{1,5},{9... | collective-permute-start | bytes 393224 | tf_op jit(solution)/shard_map/ppermute | solution.py:493

commit v7 on v5

--- a/solution.py
+++ b/solution.py
@@ -190,13 +190,19 @@
 
 
 def own_kernel(
-    agg_of, prolong, field, right, pair, pair_other, side_ref, half_ref, image_ref, rt_high, rt_low, q_high, q_low
+    agg_of, prolong, field, right, pair, pair_other,
+    side_ref, half_ref, coarse_ref, image_ref, weight_ref, rt_high, rt_low, q_high, q_low
 ):
     start = lax.axis_index("slab") * ROWS
     core = lax.axis_index("sub") & 1
 
     @pl.when(pl.program_id(0) == 0)
     def _():
+        for a in range(GROUPS):
+            members = jnp.zeros((), jnp.int32)
+            for e in range(ROWS):
+                members += jnp.where(agg_of[start + e] == a, 1, 0)
+            weight_ref[span(a), :] = COARSE_WEIGHT / jnp.full((DOF, COLS), members.astype(F32))
         restrict_rows = []
         for e in range(ROWS):
             group = agg_of[start + e]
@@ -208,10 +214,14 @@
         high, low = halves(jnp.concatenate(restrict_rows, axis=0).T)
         rt_high[...] = high
         rt_low[...] = low
+        coarse_ref[...] = jnp.zeros_like(coarse_ref)
 
     side_ref[...] = pair[:, WIDE:] + pair_other[:, WIDE:]
     own = halves(pair[:, :WIDE] + pair_other[:, :WIDE])
-    half_ref[...] = product(own, (q_high[...], q_low[...]))
+    half = product(own, (q_high[...], q_low[...]))
+    half_ref[...] = half
+    lanes = aligned(pl.program_id(0), half.shape[0])
+    coarse_ref[...] += narrow_product((rt_high[:, lanes], rt_low[:, lanes]), half)
     total = product(own, halves(field[...]))
     image_ref[:, :COLS] = total[:, :COLS] - right[...]
     image_ref[:, COLS:] = total[:, COLS:]
@@ -225,11 +235,13 @@
         own_kernel,
         grid=(steps,),
         in_specs=[SMEM, whole(*prolong.shape), whole(WIDE, 2 * COLS), part(COLS)] + [part(2 * WIDE)] * 2,
-        out_specs=[part(WIDE), part(PAIR), part(2 * COLS)] + [whole(COARSE, WIDE)] * 2,
+        out_specs=[part(WIDE), part(PAIR), whole(COARSE, PAIR), part(2 * COLS), whole(COARSE, COLS)] + [whole(COARSE, WIDE)] * 2,
         out_shape=[
             shape(WIDE, WIDE),
             shape(WIDE, PAIR),
+            shape(COARSE, PAIR),
             shape(WIDE, 2 * COLS),
+            shape(COARSE, COLS),
             shape(COARSE, WIDE, dtype=BF16),
             shape(COARSE, WIDE, dtype=BF16),
         ],
@@ -291,47 +303,48 @@
     )(agg_of, d_high, d_low, mine, other)
 
 
-def scaled_by_weight(agg_of, value):
-    start = lax.axis_index("slab") * ROWS
-    pieces = []
-    for a in range(GROUPS):
-        members = jnp.zeros((), jnp.int32)
-        for e in range(ROWS):
-            members += jnp.where(agg_of[start + e] == a, 1, 0)
-        piece = value[span(a), :]
-        pieces.append(piece * (COARSE_WEIGHT / jnp.full(piece.shape, members.astype(F32))))
-    return jnp.concatenate(pieces, axis=0)
-
-
-def coarse_kernel(own, own_received, side, side_received, rt_high, rt_low, g_ref, coarse_ref):
+def near_and_far(mine, received):
     is_near = ((lax.axis_index("sub") >> 1) & 1) == 0
-    g_ref[:, span(0, PAIR)] = jnp.where(is_near, side[...], side_received[...])
-    g_ref[:, span(1, PAIR)] = own[...] + own_received[...]
-    g_ref[:, span(2, PAIR)] = jnp.where(is_near, side_received[...], side[...])
-    coarse_ref[...] = product((rt_high[...], rt_low[...]), halves(g_ref[...]))
+    return jnp.where(is_near, mine, received), jnp.where(is_near, received, mine)
+
+
+def coarse_kernel(own, own_received, side, side_received, rt_high, rt_low, *refs):
+    regions, (high_ref, low_ref) = refs[:3], refs[3:]
+    sides = jnp.concatenate(near_and_far(side[...], side_received[...]), axis=1)
+    sides = product((rt_high[...], rt_low[...]), halves(sides))
+    values = (sides[:, :PAIR], own[...] + own_received[...], sides[:, PAIR:])
+    for region, (ref, value) in enumerate(zip(regions, values)):
+        ref[...] = value
+        high, low = halves(value)
+        high_ref[:, span(region, PAIR)] = high
+        low_ref[:, span(region, PAIR)] = low
 
 
 def coarse_half(own, own_received, side, side_received, rt_high, rt_low):
     return pl.pallas_call(
         coarse_kernel,
         in_specs=[VMEM] * 6,
-        out_specs=[VMEM] * 2,
-        out_shape=[shape(WIDE, 3 * PAIR), shape(COARSE, 3 * PAIR)],
+        out_specs=[VMEM] * 5,
+        out_shape=[shape(COARSE, PAIR)] * 3 + [shape(COARSE, 3 * PAIR, dtype=BF16)] * 2,
         compiler_params=params(),
         name="coarse_half",
     )(own, own_received, side, side_received, rt_high, rt_low)
 
 
-def share_kernel(mine, other, op_ref, natural):
+def share_kernel(*refs):
+    mine, other, (op_ref, high_ref, low_ref, natural) = refs[:3], refs[3:6], refs[6:]
     sub = lax.axis_index("sub")
     odd = lax.axis_index("slab") & 1
     is_first = (sub & 1) == 0
-    first = jnp.where(is_first, mine[...], other[...])
-    second = jnp.where(is_first, other[...], mine[...])
     places = (2 * (1 - odd), 1, 2 * odd)
     for region, place in enumerate(places):
-        value = jnp.concatenate([first[:, span(region, PAIR)], second[:, span(region, PAIR)]], axis=1)
-        natural[:, aligned(place, COARSE)] = value
+        own_value, other_value = mine[region][...], other[region][...]
+        first = jnp.where(is_first, own_value, other_value)
+        second = jnp.where(is_first, other_value, own_value)
+        natural[:, aligned(place, COARSE)] = jnp.concatenate([first, second], axis=1)
+        high, low = halves(other_value)
+        high_ref[:, span(region, PAIR)] = high
+        low_ref[:, span(region, PAIR)] = low
     share = op_ref.shape[1]
     for k in range(BANDS // share):
 
@@ -345,49 +358,52 @@
 def coarse_share(mine, other):
     return pl.pallas_call(
         share_kernel,
-        in_specs=[VMEM] * 2,
-        out_specs=VMEM,
-        out_shape=shape(GROUPS, BANDS // SUBS, DOF, DOF),
+        in_specs=[VMEM] * 6,
+        out_specs=[VMEM] * 3,
+        out_shape=[shape(GROUPS, BANDS // SUBS, DOF, DOF)] + [shape(COARSE, 3 * PAIR, dtype=BF16)] * 2,
         scratch_shapes=[pltpu.VMEM((COARSE, 3 * COARSE), F32)],
         compiler_params=params(),
         name="coarse_share",
-    )(mine, other)
-
-
-def lift_kernel(agg_of, g_half, smoother, prolong, w_ref):
+    )(*mine, *other)
+
+
+def lift_kernel(agg_of, own, own_received, side, side_received, smoother, prolong, w_ref):
     start = lax.axis_index("slab") * ROWS
     core = lax.axis_index("sub") & 1
     for e in range(ROWS):
-        w_ref[span(e), :] = -product(halves(smoother[e]), halves(g_half[span(e), :]))
-        w_ref[span(e), span(1, PAIR)] += placed(prolong[e], agg_of[start + e] - 2 * core)
-
-
-def lift_half(agg_of, g_half, smoother, prolong):
+        rows = span(e)
+        near, far = near_and_far(side[rows, :], side_received[rows, :])
+        g_half = jnp.concatenate([near, own[rows, :] + own_received[rows, :], far], axis=1)
+        w_ref[rows, :] = -product(halves(smoother[e]), halves(g_half))
+        w_ref[rows, span(1, PAIR)] += placed(prolong[e], agg_of[start + e] - 2 * core)
+
+
+def lift_half(agg_of, own, own_received, side, side_received, smoother, prolong):
     return pl.pallas_call(
         lift_kernel,
-        in_specs=[SMEM] + [VMEM] * 3,
+        in_specs=[SMEM] + [VMEM] * 6,
         out_specs=VMEM,
         out_shape=shape(WIDE, 3 * PAIR),
         compiler_params=params(),
         name="lift_half",
-    )(agg_of, g_half, smoother, prolong)
-
-
-def residual_kernel(agg_of, keep, received, rt_high, rt_low, residual_ref, first_ref):
+    )(agg_of, own, own_received, side, side_received, smoother, prolong)
+
+
+def residual_kernel(keep, received, weight, rt_high, rt_low, residual_ref, first_ref):
     residual = -(keep[...] + received[...])
     residual_ref[...] = residual
-    first_ref[...] = scaled_by_weight(agg_of, narrow_product((rt_high[...], rt_low[...]), residual))
-
-
-def residual_step(agg_of, keep, received, rt_high, rt_low):
+    first_ref[...] = weight[...] * narrow_product((rt_high[...], rt_low[...]), residual)
+
+
+def residual_step(keep, received, weight, rt_high, rt_low):
     return pl.pallas_call(
         residual_kernel,
-        in_specs=[SMEM] + [VMEM] * 4,
+        in_specs=[VMEM] * 5,
         out_specs=[VMEM] * 2,
         out_shape=[shape(WIDE, COLS), shape(COARSE, COLS)],
         compiler_params=params(),
         name="residual_step",
-    )(agg_of, keep, received, rt_high, rt_low)
+    )(keep, received, weight, rt_high, rt_low)
 
 
 def base_kernel(smoother, message, residual, base_ref):
@@ -413,23 +429,29 @@
         yield jnp.concatenate([field[aligned(which, PAIR), :] for field in fields], axis=0)
 
 
-def sweep_kernel(agg_of, mine, other, first, near, own, far, next_ref):
+def sweep_kernel(*refs):
+    operators, (first, weight, near, own, far, next_ref) = refs[:-6], refs[-6:]
+    mine = (operators[0][...], operators[1][...])
+    if len(operators) == 5:
+        other = halves(jnp.concatenate([region[...] for region in operators[2:]], axis=1))
+    else:
+        other = (operators[2][...], operators[3][...])
     total = None
     for operator, field in zip((mine, other), core_parts(near, own, far)):
-        part = narrow_product(halves(operator[...]), field)
+        part = narrow_product(operator, field)
         total = part if total is None else total + part
-    next_ref[...] = own[...] + first[...] - scaled_by_weight(agg_of, total)
-
-
-def sweep(agg_of, mine, other, first, near, own, far):
+    next_ref[...] = own[...] + first[...] - weight[...] * total
+
+
+def sweep(operators, first, weight, near, own, far):
     return pl.pallas_call(
         sweep_kernel,
-        in_specs=[SMEM] + [VMEM] * 6,
+        in_specs=[VMEM] * (len(operators) + 5),
         out_specs=VMEM,
         out_shape=shape(COARSE, COLS),
         compiler_params=params(),
         name="sweep",
-    )(agg_of, mine, other, first, near, own, far)
+    )(*operators, first, weight, near, own, far)
 
 
 def lifted_kernel(mine, other, base, own, base_ref, high_ref, low_ref):
@@ -503,29 +525,37 @@
     theirs = swapped(theirs, 1)
     received = swapped(mine + theirs, 2)
     pair, theirs = lax.optimization_barrier((pair, theirs))
-    side, own_half, own_image, rt_high, rt_low = own_step(agg_of, prolong, message, right, pair, swapped(pair, 1))
-    received, side, own_half = lax.optimization_barrier((received, side, own_half))
-    own_received = swapped(own_half, 2)
+    side, own_half, own_coarse, own_image, weight, rt_high, rt_low = own_step(
+        agg_of, prolong, message, right, pair, swapped(pair, 1)
+    )
+    received, side, own_coarse = lax.optimization_barrier((received, side, own_coarse))
+    own_coarse_received = swapped(own_coarse, 2)
     keep, send, d_high, d_low = image(own_image, side, received, swapped(received, 1), side_message)
-    send, own_received = lax.optimization_barrier((send, own_received))
     image_received = swapped(send, 2)
     ghosts = side_message[WIDE:]
+    ghosts, own_coarse_received = lax.optimization_barrier((ghosts, own_coarse_received))
     side_half = ghost_step(agg_of, d_high, d_low, ghosts, swapped(ghosts, 1))
     side_received = swapped(side_half, 2)
-    residual, first = residual_step(agg_of, keep, image_received, rt_high, rt_low)
+    residual, first = residual_step(keep, image_received, weight, rt_high, rt_low)
     base = base_step(smoother, message, residual)
     near, far = from_neighbours(first)
-    g_half, coarse = coarse_half(own_half, own_received, side_half, side_received, rt_high, rt_low)
-    near, far, coarse = lax.optimization_barrier((near, far, coarse))
-    coarse_other = swapped(coarse, 1)
-    coarse_op = coarse_share(coarse, coarse_other)
-    lift = lift_half(agg_of, g_half, smoother, prolong)
-    correction = first
-    for index in range(COARSE_SWEEPS - 1):
-        if index > 0:
-            near, far = from_neighbours(correction)
-            lift, near, far = lax.optimization_barrier((lift, near, far))
-        correction = sweep(agg_of, coarse, coarse_other, first, near, correction, far)
+    own_half, side_received = lax.optimization_barrier((own_half, side_received))
+    own_received = swapped(own_half, 2)
+    *coarse, mine_high, mine_low = coarse_half(
+        own_coarse, own_coarse_received, side_half, side_received, rt_high, rt_low
+    )
+    coarse_other = [swapped(region, 1) for region in coarse]
+    near, far, coarse_other = lax.optimization_barrier((near, far, coarse_other))
+    correction = sweep((mine_high, mine_low, *coarse_other), first, weight, near, first, far)
+    coarse_op, other_high, other_low = coarse_share(coarse, coarse_other)
+    lift = lift_half(agg_of, own_half, own_received, side_half, side_received, smoother, prolong)
+    for index in range(1, COARSE_SWEEPS - 1):
+        near, far = from_neighbours(correction)
+        if index == 1:
+            shadowed = (near, far, lift, other_high, other_low)
+            near, far, lift, other_high, other_low = lax.optimization_barrier(shadowed)
+        operators = (mine_high, mine_low, other_high, other_low)
+        correction = sweep(operators, first, weight, near, correction, far)
     lift_other = swapped(lift, 1)
     near, far = from_neighbours(correction)
     base, w_high, w_low = lifted(lift, lift_other, base, correction)

time: 73 us -> 65.5 us (0.90)
  waiting for transfers between devices: 37.8 us -> 25.6 us
  starting transfers between devices: 18.2 us -> 23.5 us
  Pallas kernels: 15.7 us -> 14.4 us
    ppermute x10 -> x13, waiting for transfers between devices: 20 us -> 13.5 us  [swapped(): return lax.ppermute(value, 'sub', [(i, i ^ bit) for i in range(size)])]
    ppermute x10 -> x13, starting transfers between devices: 5.32 us -> 8.39 us  [swapped(): return lax.ppermute(value, 'sub', [(i, i ^ bit) for i in range(size)])]
    ppermute x3, waiting for transfers between devices: 9.91 us -> 6.85 us  [from_neighbours(): far = lax.ppermute(value, 'slab', swaps(size, 1))]
    ppermute x3, waiting for transfers between devices: 4.86 us -> 2.26 us  [from_neighbours(): near = lax.ppermute(value, 'slab', swaps(size, 0))]
    ppermute x3, starting transfers between devices: 5.73 us -> 8.26 us  [from_neighbours(): far = lax.ppermute(value, 'slab', swaps(size, 1))]
    pallas_call x6, Pallas kernels: 5.27 us -> 3.57 us  [the longest x1 1.06 us: lift_half(): pl.pallas_call(lift_kernel, in_specs=[SMEM] + [VMEM] * 6, out_specs=VMEM,...]
  transfers between devices with their start and end apart: 17 -> 20, of which waited for: 14 -> 11; matrix products, arithmetic and copies ran while one was open for 0% -> 0% of each run, Pallas kernels for 13% -> 14%
where the time goes in v7:
time: 65.5 us; the launch traced here: 64.5 us
  waiting for transfers between devices  25.6 us (39%)
  starting transfers between devices  23.5 us (36%)
  Pallas kernels  14.4 us (22%)
  between operations  0.86 us (1%)
    ppermute x13, waiting for transfers between devices, swapped(): return lax.ppermute(value, 'sub', [(i, i ^ bit) for i in range(size)])  13.5 us
    ppermute x13, starting transfers between devices, swapped(): return lax.ppermute(value, 'sub', [(i, i ^ bit) for i in range(size)])  8.39 us
    ppermute x3, starting transfers between devices, from_neighbours(): far = lax.ppermute(value, 'slab', swaps(size, 1))  8.26 us
    ppermute x3, waiting for transfers between devices, from_neighbours(): far = lax.ppermute(value, 'slab', swaps(size, 1))  6.85 us
    pallas_call x1, Pallas kernels, start_step(): pl.pallas_call(start_kernel, in_specs=[HBM] * 7, out_specs=[VMEM] * 5, ou...  4.17 us
    ppermute x3, starting transfers between devices, from_neighbours(): near = lax.ppermute(value, 'slab', swaps(size, 0))  3.43 us
    ppermute x1, starting transfers between devices, from_side(): return lax.ppermute(value, ('slab', 'sub'), pairs)  3.41 us
    ppermute x1, waiting for transfers between devices, from_side(): return lax.ppermute(value, ('slab', 'sub'), pairs)  3 us
  transfers between devices with their start and end apart: 20, of which 11 were waited for; matrix products, arithmetic and copies ran while one was open for 0% of the time, Pallas kernels for 14%

profile of v7, /device:TPU:8, one launch (start us, length us, event | category | flops | bytes accessed | tf_op | source)
XLA Modules:
  0.0 64.5 jit_solution(1689776670941825085)
XLA Ops:
  0.6 0.0 copy-start
  0.6 0.0 copy-start.2
  0.7 4.2 %start_step.1 = (f32[512,1024]{1,0:T(8,128)S(1)}, f32[256,512]{1,0:T(8,128)S(1)}, f32[256,512]{1,0:T(8,128)S(1)}, f32[576,256]{1,0:T(8,128)S(1)}, f32[512,128]{1,0:T(8,128)S(1)}) custom-call(s32[8,16]{1,0:T(8,128)} %col_hbm.1, s32[8,4,2,8]{3,2,1,0:T(2,128)} %rows_hbm.1, s32[4,2,8]{2,1,0:T(2,128)} %bitcast.3, f32[8,16,64,64]{3,2,1,0:T(8,128)} %blocks_hbm.1, ...), custom_call_target="tpu_custom_call" | custom-call | tf_op jit(solution)/shard_map/start_step/pallas_call | solution.py:156
  4.8 0.1 collective-permute-start
  4.9 1.9 %collective-permute-done = f32[256,512]{1,0:T(8,128)S(1)} collective-permute-done((f32[256,512]{1,0:T(8,128)S(1)}, f32[256,512]{1,0:T(8,128)S(1)}, u32[]{:S(2)}, u32[]{:S(2)}) %collective-permute-start) | collective-permute-done | bytes 524320 | tf_op jit(solution)/shard_map/ppermute | solution.py:517
  6.8 0.1 collective-permute-start.2
  6.9 0.1 add.3
  7.0 1.6 %collective-permute-start.1 = (f32[256,512]{1,0:T(8,128)S(1)}, f32[256,512]{1,0:T(8,128)S(1)}, u32[]{:S(2)}, u32[]{:S(2)}) collective-permute-start(f32[256,512]{1,0:T(8,128)S(1)} %add.3), channel_id=1, source_target_pairs={{0,2},{1,3},{2,0},{3,1},{4,6},{5,7},{6,4},{7,5},{8,10},{9,11},{10,... | collective-permute-start | bytes 1572872 | tf_op jit(solution)/shard_map/ppermute | solution.py:517
  8.6 3.4 %collective-permute-start.3 = (f32[576,256]{1,0:T(8,128)S(1)}, f32[576,256]{1,0:T(8,128)S(1)}, u32[]{:S(2)}, u32[]{:S(2)}) collective-permute-start(f32[576,256]{1,0:T(8,128)S(1)} %get-tuple-element.51.field.message), channel_id=1, source_target_pairs={{0,4},{8,12},{16,20},{24,28},{4,0},{12,8},{20,16},{28,24},{1,5},{9... | collective-permute-start | bytes 1769480 | tf_op jit(solution)/shard_map/ppermute | solution.py:512
  12.0 0.0 collective-permute-done.2.pair_other
  12.0 0.0 copy-done
  12.0 0.0 copy-done.2
  12.0 2.7 %own_step.1 = (f32[512,512]{1,0:T(8,128)S(1)}, f32[512,128]{1,0:T(8,128)S(1)}, f32[256,128]{1,0:T(8,128)S(1)}, f32[512,256]{1,0:T(8,128)S(1)}, f32[256,128]{1,0:...) custom-call(s32[64]{0:T(128)S(1)} %copy-done.2, f32[8,64,64]{2,1,0:T(8,128)S(1)} %copy-done, ...), custom_call_target="tpu_custom_call" | custom-call | tf_op jit(solution)/shard_map/own_step/pallas_call | solution.py:234
  14.7 6.6 %collective-permute-done.1.received = f32[256,512]{1,0:T(8,128)S(1)} collective-permute-done((f32[256,512]{1,0:T(8,128)S(1)}, f32[256,512]{1,0:T(8,128)S(1)}, u32[]{:S(2)}, u32[]{:S(2)}) %collective-permute-start.1) | collective-permute-done | bytes 524320 | tf_op jit(solution)/shard_map/ppermute | solution.py:517
  21.3 0.0 collective-permute-start.5
  21.3 1.5 %collective-permute-start.4 = (f32[256,128]{1,0:T(8,128)S(1)}, f32[256,128]{1,0:T(8,128)S(1)}, u32[]{:S(2)}, u32[]{:S(2)}) collective-permute-start(f32[256,128]{1,0:T(8,128)S(1)} %get-tuple-element.57.own), channel_id=1, source_target_pairs={{0,2},{1,3},{2,0},{3,1},{4,6},{5,7},{6,4},{7,5},{8,10},{9,11},{10,... | collective-permute-start | bytes 393224 | tf_op jit(solution)/shard_map/ppermute | solution.py:517
  22.8 3.0 %collective-permute-done.3.message = f32[576,256]{1,0:T(8,128)S(1)} collective-permute-done((f32[576,256]{1,0:T(8,128)S(1)}, f32[576,256]{1,0:T(8,128)S(1)}, u32[]{:S(2)}, u32[]{:S(2)}) %collective-permute-start.3) | collective-permute-done | bytes 589856 | tf_op jit(solution)/shard_map/ppermute | solution.py:512
  25.8 0.0 collective-permute-done.5.received_other
  25.8 0.7 %image.1 = (f32[512,128]{1,0:T(8,128)S(1)}, f32[512,128]{1,0:T(8,128)S(1)}, bf16[512,512]{1,0:T(8,128)(2,1)S(1)}, bf16[512,512]{1,0:T(8,128)(2,1)S(1)}) custom-call(f32[512,256]{1,0:T(8,128)S(1)} %get-tuple-element.59.own_image, f32[512,512]{1,0:T(8,128)S(1)} %get-tuple-element.60.side, f32[256,512]{1,0:T(8,128)S(1)} %collective-permute-done.1.received, ...), custom_call_target="tpu_custom_call" | custom-call | tf_op jit(solution)/shard_map/image/pallas_call | solution.py:270
  26.5 1.5 %collective-permute-start.8 = (f32[512,128]{1,0:T(8,128)S(1)}, f32[512,128]{1,0:T(8,128)S(1)}, u32[]{:S(2)}, u32[]{:S(2)}) collective-permute-start(f32[512,128]{1,0:T(8,128)S(1)} %get-tuple-element.73), channel_id=1, source_target_pairs={{0,2},{1,3},{2,0},{3,1},{4,6},{5,7},{6,4},{7,5},{8,10},{9,11},{10,... | collective-permute-start | bytes 786440 | tf_op jit(solution)/shard_map/ppermute | solution.py:517
  28.0 0.0 collective-permute-done.4.own_received
  28.0 0.1 collective-permute-start.6
  28.1 1.2 %collective-permute-done.6.other = f32[64,256]{1,0:T(8,128)S(1)} collective-permute-done((f32[64,256]{1,0:T(8,128)S(1)}, f32[64,256]{1,0:T(8,128)S(1)}, u32[]{:S(2)}, u32[]{:S(2)}) %collective-permute-start.6) | collective-permute-done | bytes 65568 | tf_op jit(solution)/shard_map/ppermute | solution.py:517
  29.3 1.2 %ghost_step.1.side = f32[512,128]{1,0:T(8,128)S(1)} custom-call(s32[64]{0:T(128)S(1)} %copy-done.2, bf16[512,512]{1,0:T(8,128)(2,1)S(1)} %get-tuple-element.62.d_high, bf16[512,512]{1,0:T(8,128)(2,1)S(1)} %get-tuple-element.63.d_low, f32[64,256]{1,0:T(8,128)S(1)} %slice.4.mine, f32[64,256]{1,0:T(8,128)S(1)} %collective-permute-done.6.other), custom_call_target="tpu_custom_call" | custom-call | tf_op jit(solution)/shard_map/ghost_step/pallas_call | solution.py:295
  30.6 0.6 %collective-permute-start.7 = (f32[512,128]{1,0:T(8,128)S(1)}, f32[512,128]{1,0:T(8,128)S(1)}, u32[]{:S(2)}, u32[]{:S(2)}) collective-permute-start(f32[512,128]{1,0:T(8,128)S(1)} %ghost_step.1.side), channel_id=1, source_target_pairs={{0,2},{1,3},{2,0},{3,1},{4,6},{5,7},{6,4},{7,5},{8,10},{9,11},{10,... | collective-permute-start | bytes 786440 | tf_op jit(solution)/shard_map/ppermute | solution.py:517
  31.3 3.3 %collective-permute-done.8.received = f32[512,128]{1,0:T(8,128)S(1)} collective-permute-done((f32[512,128]{1,0:T(8,128)S(1)}, f32[512,128]{1,0:T(8,128)S(1)}, u32[]{:S(2)}, u32[]{:S(2)}) %collective-permute-start.8) | collective-permute-done | bytes 262176 | tf_op jit(solution)/shard_map/ppermute | solution.py:517
  34.5 0.3 residual_step.1
  34.8 0.0 copy-start.1
  34.9 1.6 %collective-permute-start.9 = (f32[256,128]{1,0:T(8,128)S(1)}, f32[256,128]{1,0:T(8,128)S(1)}, u32[]{:S(2)}, u32[]{:S(2)}) collective-permute-start(f32[256,128]{1,0:T(8,128)S(1)} %get-tuple-element.75.refs_5_.refs_8_.refs_4_), channel_id=1, source_target_pairs={{0,4},{8,12},{16,20},{24,28},{4,0},{12,8},{20,16},{28,24},{1,5},{9... | collective-permute-start | bytes 393224 | tf_op jit(solution)/shard_map/ppermute | solution.py:502
  36.4 3.5 %collective-permute-start.10 = (f32[256,128]{1,0:T(8,128)S(1)}, f32[256,128]{1,0:T(8,128)S(1)}, u32[]{:S(2)}, u32[]{:S(2)}) collective-permute-start(f32[256,128]{1,0:T(8,128)S(1)} %get-tuple-element.75.refs_5_.refs_8_.refs_4_), channel_id=1, source_target_pairs={{4,8},{12,16},{20,24},{8,4},{16,12},{24,20},{5,9},{13,17},{21,25},... | collective-permute-start | bytes 393224 | tf_op jit(solution)/shard_map/ppermute | solution.py:503
  39.9 0.0 collective-permute-done.7.side_received
  39.9 0.4 coarse_half.1
  40.4 0.1 collective-permute-start.11
  40.4 0.5 collective-permute-start.12
  40.9 0.1 collective-permute-start.13
  41.0 0.3 collective-permute-done.9.refs_7_
  41.3 2.3 %collective-permute-start.16 = (f32[512,128]{1,0:T(8,128)S(1)}, f32[512,128]{1,0:T(8,128)S(1)}, u32[]{:S(2)}, u32[]{:S(2)}) collective-permute-start(f32[512,128]{1,0:T(8,128)S(1)} %get-tuple-element.84.own), channel_id=1, source_target_pairs={{0,2},{1,3},{2,0},{3,1},{4,6},{5,7},{6,4},{7,5},{8,10},{9,11},{10,... | collective-permute-start | bytes 786440 | tf_op jit(solution)/shard_map/ppermute | solution.py:517
  43.6 0.6 collective-permute-done.10.refs_9_
  44.2 0.0 collective-permute-done.11.refs_3_.refs_2_
  44.2 0.0 collective-permute-done.12.refs_4_.refs_3_
  44.2 0.0 collective-permute-done.13.refs_5_.refs_4_
  44.2 0.4 sweep.2.refs_7_
  44.6 0.7 %collective-permute-start.14 = (f32[256,128]{1,0:T(8,128)S(1)}, f32[256,128]{1,0:T(8,128)S(1)}, u32[]{:S(2)}, u32[]{:S(2)}) collective-permute-start(f32[256,128]{1,0:T(8,128)S(1)} %sweep.2.refs_7_), channel_id=1, source_target_pairs={{0,4},{8,12},{16,20},{24,28},{4,0},{12,8},{20,16},{28,24},{1,5},{9... | collective-permute-start | bytes 393224 | tf_op jit(solution)/shard_map/ppermute | solution.py:502
  45.3 2.9 %collective-permute-start.15 = (f32[256,128]{1,0:T(8,128)S(1)}, f32[256,128]{1,0:T(8,128)S(1)}, u32[]{:S(2)}, u32[]{:S(2)}) collective-permute-start(f32[256,128]{1,0:T(8,128)S(1)} %sweep.2.refs_7_), channel_id=1, source_target_pairs={{4,8},{12,16},{20,24},{8,4},{16,12},{24,20},{5,9},{13,17},{21,25},... | collective-permute-start | bytes 393224 | tf_op jit(solution)/shard_map/ppermute | solution.py:503
  48.2 1.0 %coarse_share.1 = (f32[4,3,64,64]{3,2,1,0:T(8,128)}, bf16[256,384]{1,0:T(8,128)(2,1)S(1)}, bf16[256,384]{1,0:T(8,128)(2,1)S(1)}) custom-call(f32[256,128]{1,0:T(8,128)S(1)} %get-tuple-element.69.refs_0_, f32[256,128]{1,0:T(8,128)S(1)} %get-tuple-element.70.refs_1_, f32[256,128]{1,0:T(8,128)S(1)} %get-tuple-element.71.refs_2_, ...), custom_call_target="tpu_custom_call" | custom-call | tf_op jit(solution)/shard_map/coarse_share/pallas_call | solution.py:359
  49.1 0.5 collective-permute-done.16.own_received
  49.7 0.0 copy-done.1
  49.7 1.1 %lift_half.1.mine = f32[512,384]{1,0:T(8,128)S(1)} custom-call(s32[64]{0:T(128)S(1)} %copy-done.2, f32[512,128]{1,0:T(8,128)S(1)} %get-tuple-element.84.own, f32[512,128]{1,0:T(8,128)S(1)} %collective-permute-done.16.own_received, f32[512,128]{1,0:T(8,128)S(1)} %ghost_step.1.side, f32[512,128]{1,0:T(8,128)S(1)} %collective-permute-done.7.side_received, ...), custom_call_target="tpu_custom_call" | custom-call | tf_op jit(solution)/shard_map/lift_half/pallas_call | solution.py:382
  50.7 0.0 collective-permute-done.14.refs_6_
  50.7 2.6 %collective-permute-done.15.refs_8_ = f32[256,128]{1,0:T(8,128)S(1)} collective-permute-done((f32[256,128]{1,0:T(8,128)S(1)}, f32[256,128]{1,0:T(8,128)S(1)}, u32[]{:S(2)}, u32[]{:S(2)}) %collective-permute-start.15) | collective-permute-done | bytes 131104 | tf_op jit(solution)/shard_map/ppermute | solution.py:503
  53.3 0.0 collective-permute-start.17
  53.4 0.4 sweep.3.own
  53.8 1.2 %collective-permute-start.18 = (f32[256,128]{1,0:T(8,128)S(1)}, f32[256,128]{1,0:T(8,128)S(1)}, u32[]{:S(2)}, u32[]{:S(2)}) collective-permute-start(f32[256,128]{1,0:T(8,128)S(1)} %sweep.3.own), channel_id=1, source_target_pairs={{0,4},{8,12},{16,20},{24,28},{4,0},{12,8},{20,16},{28,24},{1,5},{9... | collective-permute-start | bytes 393224 | tf_op jit(solution)/shard_map/ppermute | solution.py:502
  54.9 1.9 %collective-permute-start.19 = (f32[256,128]{1,0:T(8,128)S(1)}, f32[256,128]{1,0:T(8,128)S(1)}, u32[]{:S(2)}, u32[]{:S(2)}) collective-permute-start(f32[256,128]{1,0:T(8,128)S(1)} %sweep.3.own), channel_id=1, source_target_pairs={{4,8},{12,16},{20,24},{8,4},{16,12},{24,20},{5,9},{13,17},{21,25},... | collective-permute-start | bytes 393224 | tf_op jit(solution)/shard_map/ppermute | solution.py:503
  56.9 0.3 base_step.1.base
  57.1 0.0 collective-permute-done.17.other
  57.1 0.6 lifted.1
  57.7 2.0 %collective-permute-done.18.near = f32[256,128]{1,0:T(8,128)S(1)} collective-permute-done((f32[256,128]{1,0:T(8,128)S(1)}, f32[256,128]{1,0:T(8,128)S(1)}, u32[]{:S(2)}, u32[]{:S(2)}) %collective-permute-start.18) | collective-permute-done | bytes 131104 | tf_op jit(solution)/shard_map/ppermute | solution.py:502
  59.7 3.6 %collective-permute-done.19.far = f32[256,128]{1,0:T(8,128)S(1)} collective-permute-done((f32[256,128]{1,0:T(8,128)S(1)}, f32[256,128]{1,0:T(8,128)S(1)}, u32[]{:S(2)}, u32[]{:S(2)}) %collective-permute-start.19) | collective-permute-done | bytes 131104 | tf_op jit(solution)/shard_map/ppermute | solution.py:503
  63.4 1.1 %last_step.1 = f32[512,128]{1,0:T(8,128)} custom-call(bf16[512,512]{1,0:T(8,128)(2,1)S(1)} %get-tuple-element.93.w_high, bf16[512,512]{1,0:T(8,128)(2,1)S(1)} %get-tuple-element.94.w_low, f32[512,128]{1,0:T(8,128)S(1)} %get-tuple-element.95.base, f32[256,128]{1,0:T(8,128)S(1)} %collective-permute-done.18.near, f32[256,128]{1,0:T(8,128)S(1)} %collective-permute-done.19.far), custom_call_target="tpu_custom_call" | custom-call | tf_op jit(solution)/shard_map/last_step/pallas_call | solution.py:485
  (1 shorter events, 0.0 us)
Async XLA Ops:
  0.6 11.4 %copy-start = (f32[8,64,64]{2,1,0:T(8,128)S(1)}, f32[8,64,64]{2,1,0:T(8,128)}, u32[]{:S(2)}) copy-start(f32[8,64,64]{2,1,0:T(8,128)} %prolong.3) | copy-start | bytes 393220
  0.6 11.4 %copy-start.2 = (s32[64]{0:T(128)S(1)}, s32[64]{0:T(128)}, u32[]{:S(2)}) copy-start(s32[64]{0:T(128)} %agg_of.5) | copy-start | bytes 772
  4.8 2.0 %collective-permute-start = (f32[256,512]{1,0:T(8,128)S(1)}, f32[256,512]{1,0:T(8,128)S(1)}, u32[]{:S(2)}, u32[]{:S(2)}) collective-permute-start(f32[256,512]{1,0:T(8,128)S(1)} %get-tuple-element.50), channel_id=1, source_target_pairs={{0,1},{1,0},{2,3},{3,2},{4,5},{5,4},{6,7},{7,6},{8,9},{9,8},{10,11... | collective-permute-start | bytes 1572872 | tf_op jit(solution)/shard_map/ppermute | solution.py:517
  6.8 5.2 %collective-permute-start.2 = (f32[512,1024]{1,0:T(8,128)S(1)}, f32[512,1024]{1,0:T(8,128)S(1)}, u32[]{:S(2)}, u32[]{:S(2)}) collective-permute-start(f32[512,1024]{1,0:T(8,128)S(1)} %get-tuple-element.54.pair), channel_id=1, source_target_pairs={{0,1},{1,0},{2,3},{3,2},{4,5},{5,4},{6,7},{7,6},{8,9},{9,8},{10,11... | collective-permute-start | bytes 6291464 | tf_op jit(solution)/shard_map/ppermute | solution.py:517
  7.0 14.3 %collective-permute-start.1 = (f32[256,512]{1,0:T(8,128)S(1)}, f32[256,512]{1,0:T(8,128)S(1)}, u32[]{:S(2)}, u32[]{:S(2)}) collective-permute-start(f32[256,512]{1,0:T(8,128)S(1)} %add.3), channel_id=1, source_target_pairs={{0,2},{1,3},{2,0},{3,1},{4,6},{5,7},{6,4},{7,5},{8,10},{9,11},{10,... | collective-permute-start | bytes 1572872 | tf_op jit(solution)/shard_map/ppermute | solution.py:517
  8.6 17.2 %collective-permute-start.3 = (f32[576,256]{1,0:T(8,128)S(1)}, f32[576,256]{1,0:T(8,128)S(1)}, u32[]{:S(2)}, u32[]{:S(2)}) collective-permute-start(f32[576,256]{1,0:T(8,128)S(1)} %get-tuple-element.51.field.message), channel_id=1, source_target_pairs={{0,4},{8,12},{16,20},{24,28},{4,0},{12,8},{20,16},{28,24},{1,5},{9... | collective-permute-start | bytes 1769480 | tf_op jit(solution)/shard_map/ppermute | solution.py:512
  21.3 4.5 %collective-permute-start.5 = (f32[256,512]{1,0:T(8,128)S(1)}, f32[256,512]{1,0:T(8,128)S(1)}, u32[]{:S(2)}, u32[]{:S(2)}) collective-permute-start(f32[256,512]{1,0:T(8,128)S(1)} %collective-permute-done.1.received), channel_id=1, source_target_pairs={{0,1},{1,0},{2,3},{3,2},{4,5},{5,4},{6,7},{7,6},{8,9},{9,8},{10,11... | collective-permute-start | bytes 1572872 | tf_op jit(solution)/shard_map/ppermute | solution.py:517
  21.3 6.7 %collective-permute-start.4 = (f32[256,128]{1,0:T(8,128)S(1)}, f32[256,128]{1,0:T(8,128)S(1)}, u32[]{:S(2)}, u32[]{:S(2)}) collective-permute-start(f32[256,128]{1,0:T(8,128)S(1)} %get-tuple-element.57.own), channel_id=1, source_target_pairs={{0,2},{1,3},{2,0},{3,1},{4,6},{5,7},{6,4},{7,5},{8,10},{9,11},{10,... | collective-permute-start | bytes 393224 | tf_op jit(solution)/shard_map/ppermute | solution.py:517
  26.5 8.0 %collective-permute-start.8 = (f32[512,128]{1,0:T(8,128)S(1)}, f32[512,128]{1,0:T(8,128)S(1)}, u32[]{:S(2)}, u32[]{:S(2)}) collective-permute-start(f32[512,128]{1,0:T(8,128)S(1)} %get-tuple-element.73), channel_id=1, source_target_pairs={{0,2},{1,3},{2,0},{3,1},{4,6},{5,7},{6,4},{7,5},{8,10},{9,11},{10,... | collective-permute-start | bytes 786440 | tf_op jit(solution)/shard_map/ppermute | solution.py:517
  28.0 1.3 %collective-permute-start.6 = (f32[64,256]{1,0:T(8,128)S(1)}, f32[64,256]{1,0:T(8,128)S(1)}, u32[]{:S(2)}, u32[]{:S(2)}) collective-permute-start(f32[64,256]{1,0:T(8,128)S(1)} %slice.4.mine), channel_id=1, source_target_pairs={{0,1},{1,0},{2,3},{3,2},{4,5},{5,4},{6,7},{7,6},{8,9},{9,8},{10,11... | collective-permute-start | bytes 196616 | tf_op jit(solution)/shard_map/ppermute | solution.py:517
  30.6 9.3 %collective-permute-start.7 = (f32[512,128]{1,0:T(8,128)S(1)}, f32[512,128]{1,0:T(8,128)S(1)}, u32[]{:S(2)}, u32[]{:S(2)}) collective-permute-start(f32[512,128]{1,0:T(8,128)S(1)} %ghost_step.1.side), channel_id=1, source_target_pairs={{0,2},{1,3},{2,0},{3,1},{4,6},{5,7},{6,4},{7,5},{8,10},{9,11},{10,... | collective-permute-start | bytes 786440 | tf_op jit(solution)/shard_map/ppermute | solution.py:517
  34.8 14.8 %copy-start.1 = (f32[8,64,64]{2,1,0:T(8,128)S(1)}, f32[8,64,64]{2,1,0:T(8,128)}, u32[]{:S(2)}) copy-start(f32[8,64,64]{2,1,0:T(8,128)} %smoother.3) | copy-start | bytes 393220
  34.9 6.4 %collective-permute-start.9 = (f32[256,128]{1,0:T(8,128)S(1)}, f32[256,128]{1,0:T(8,128)S(1)}, u32[]{:S(2)}, u32[]{:S(2)}) collective-permute-start(f32[256,128]{1,0:T(8,128)S(1)} %get-tuple-element.75.refs_5_.refs_8_.refs_4_), channel_id=1, source_target_pairs={{0,4},{8,12},{16,20},{24,28},{4,0},{12,8},{20,16},{28,24},{1,5},{9... | collective-permute-start | bytes 393224 | tf_op jit(solution)/shard_map/ppermute | solution.py:502
  36.4 7.7 %collective-permute-start.10 = (f32[256,128]{1,0:T(8,128)S(1)}, f32[256,128]{1,0:T(8,128)S(1)}, u32[]{:S(2)}, u32[]{:S(2)}) collective-permute-start(f32[256,128]{1,0:T(8,128)S(1)} %get-tuple-element.75.refs_5_.refs_8_.refs_4_), channel_id=1, source_target_pairs={{4,8},{12,16},{20,24},{8,4},{16,12},{24,20},{5,9},{13,17},{21,25},... | collective-permute-start | bytes 393224 | tf_op jit(solution)/shard_map/ppermute | solution.py:503
  40.4 3.8 %collective-permute-start.11 = (f32[256,128]{1,0:T(8,128)S(1)}, f32[256,128]{1,0:T(8,128)S(1)}, u32[]{:S(2)}, u32[]{:S(2)}) collective-permute-start(f32[256,128]{1,0:T(8,128)S(1)} %get-tuple-element.69.refs_0_), channel_id=1, source_target_pairs={{0,1},{1,0},{2,3},{3,2},{4,5},{5,4},{6,7},{7,6},{8,9},{9,8},{10,11... | collective-permute-start | bytes 393224 | tf_op jit(solution)/shard_map/ppermute | solution.py:517
  40.4 3.8 %collective-permute-start.12 = (f32[256,128]{1,0:T(8,128)S(1)}, f32[256,128]{1,0:T(8,128)S(1)}, u32[]{:S(2)}, u32[]{:S(2)}) collective-permute-start(f32[256,128]{1,0:T(8,128)S(1)} %get-tuple-element.70.refs_1_), channel_id=1, source_target_pairs={{0,1},{1,0},{2,3},{3,2},{4,5},{5,4},{6,7},{7,6},{8,9},{9,8},{10,11... | collective-permute-start | bytes 393224 | tf_op jit(solution)/shard_map/ppermute | solution.py:517
  40.9 3.3 %collective-permute-start.13 = (f32[256,128]{1,0:T(8,128)S(1)}, f32[256,128]{1,0:T(8,128)S(1)}, u32[]{:S(2)}, u32[]{:S(2)}) collective-permute-start(f32[256,128]{1,0:T(8,128)S(1)} %get-tuple-element.71.refs_2_), channel_id=1, source_target_pairs={{0,1},{1,0},{2,3},{3,2},{4,5},{5,4},{6,7},{7,6},{8,9},{9,8},{10,11... | collective-permute-start | bytes 393224 | tf_op jit(solution)/shard_map/ppermute | solution.py:517
  41.3 8.4 %collective-permute-start.16 = (f32[512,128]{1,0:T(8,128)S(1)}, f32[512,128]{1,0:T(8,128)S(1)}, u32[]{:S(2)}, u32[]{:S(2)}) collective-permute-start(f32[512,128]{1,0:T(8,128)S(1)} %get-tuple-element.84.own), channel_id=1, source_target_pairs={{0,2},{1,3},{2,0},{3,1},{4,6},{5,7},{6,4},{7,5},{8,10},{9,11},{10,... | collective-permute-start | bytes 786440 | tf_op jit(solution)/shard_map/ppermute | solution.py:517
  44.6 6.1 %collective-permute-start.14 = (f32[256,128]{1,0:T(8,128)S(1)}, f32[256,128]{1,0:T(8,128)S(1)}, u32[]{:S(2)}, u32[]{:S(2)}) collective-permute-start(f32[256,128]{1,0:T(8,128)S(1)} %sweep.2.refs_7_), channel_id=1, source_target_pairs={{0,4},{8,12},{16,20},{24,28},{4,0},{12,8},{20,16},{28,24},{1,5},{9... | collective-permute-start | bytes 393224 | tf_op jit(solution)/shard_map/ppermute | solution.py:502
  45.3 8.1 %collective-permute-start.15 = (f32[256,128]{1,0:T(8,128)S(1)}, f32[256,128]{1,0:T(8,128)S(1)}, u32[]{:S(2)}, u32[]{:S(2)}) collective-permute-start(f32[256,128]{1,0:T(8,128)S(1)} %sweep.2.refs_7_), channel_id=1, source_target_pairs={{4,8},{12,16},{20,24},{8,4},{16,12},{24,20},{5,9},{13,17},{21,25},... | collective-permute-start | bytes 393224 | tf_op jit(solution)/shard_map/ppermute | solution.py:503
  53.3 3.8 %collective-permute-start.17 = (f32[512,384]{1,0:T(8,128)S(1)}, f32[512,384]{1,0:T(8,128)S(1)}, u32[]{:S(2)}, u32[]{:S(2)}) collective-permute-start(f32[512,384]{1,0:T(8,128)S(1)} %lift_half.1.mine), channel_id=1, source_target_pairs={{0,1},{1,0},{2,3},{3,2},{4,5},{5,4},{6,7},{7,6},{8,9},{9,8},{10,11... | collective-permute-start | bytes 2359304 | tf_op jit(solution)/shard_map/ppermute | solution.py:517
  53.8 6.0 %collective-permute-start.18 = (f32[256,128]{1,0:T(8,128)S(1)}, f32[256,128]{1,0:T(8,128)S(1)}, u32[]{:S(2)}, u32[]{:S(2)}) collective-permute-start(f32[256,128]{1,0:T(8,128)S(1)} %sweep.3.own), channel_id=1, source_target_pairs={{0,4},{8,12},{16,20},{24,28},{4,0},{12,8},{20,16},{28,24},{1,5},{9... | collective-permute-start | bytes 393224 | tf_op jit(solution)/shard_map/ppermute | solution.py:502
  54.9 8.4 %collective-permute-start.19 = (f32[256,128]{1,0:T(8,128)S(1)}, f32[256,128]{1,0:T(8,128)S(1)}, u32[]{:S(2)}, u32[]{:S(2)}) collective-permute-start(f32[256,128]{1,0:T(8,128)S(1)} %sweep.3.own), channel_id=1, source_target_pairs={{4,8},{12,16},{20,24},{8,4},{16,12},{24,20},{5,9},{13,17},{21,25},... | collective-permute-start | bytes 393224 | tf_op jit(solution)/shard_map/ppermute | solution.py:503

commit v8 on v7

--- a/solution.py
+++ b/solution.py
@@ -251,10 +251,14 @@
     )(agg_of, prolong, message, right, pair, pair_other)
 
 
-def image_kernel(own_image, side, received, received_other, message, keep_ref, send_ref, high_ref, low_ref):
+def image_kernel(
+    own_image, side, received, received_other, message, rt_high, rt_low,
+    keep_ref, send_ref, rhs_keep_ref, rhs_send_ref, high_ref, low_ref
+):
     core = lax.axis_index("sub") & 1
     field = halves(message[:WIDE, :])
     rows = WIDE // 2
+    rhs = None
     for group in range(2):
         part = span(group, rows)
         extra = jnp.where(core == group, received[...], received_other[...])
@@ -264,20 +268,24 @@
         total = own_image[part, :] + product((high, low), field)
         keep_ref[part, :] = total[:, :COLS]
         send_ref[part, :] = total[:, COLS:]
-
-
-def image(own_image, side, received, received_other, message):
+        term = product((rt_high[:, part], rt_low[:, part]), halves(total))
+        rhs = term if rhs is None else rhs + term
+    rhs_keep_ref[...] = rhs[:, :COLS]
+    rhs_send_ref[...] = rhs[:, COLS:]
+
+
+def image(own_image, side, received, received_other, message, rt_high, rt_low):
     return pl.pallas_call(
         image_kernel,
-        in_specs=[VMEM] * 5,
-        out_specs=[VMEM] * 4,
-        out_shape=[shape(WIDE, COLS)] * 2 + [shape(WIDE, WIDE, dtype=BF16)] * 2,
+        in_specs=[VMEM] * 7,
+        out_specs=[VMEM] * 6,
+        out_shape=[shape(WIDE, COLS)] * 2 + [shape(COARSE, COLS)] * 2 + [shape(WIDE, WIDE, dtype=BF16)] * 2,
         compiler_params=params(),
         name="image",
-    )(own_image, side, received, received_other, message)
-
-
-def ghost_kernel(agg_of, d_high, d_low, mine, other, half_ref, q_high, q_low):
+    )(own_image, side, received, received_other, message, rt_high, rt_low)
+
+
+def ghost_kernel(agg_of, d_high, d_low, mine, other, upper_ref, lower_ref, q_high, q_low):
     _, near, far = neighbours()
     sub = lax.axis_index("sub")
     core = sub & 1
@@ -288,15 +296,17 @@
         high, low = halves(placed(piece, agg_of[start + r] - 2 * core))
         q_high[span(r), :] = high
         q_low[span(r), :] = low
-    half_ref[...] = product((d_high[...], d_low[...]), (q_high[...], q_low[...]))
+    for group, ref in enumerate((upper_ref, lower_ref)):
+        part = span(group, WIDE // 2)
+        ref[...] = product((d_high[part, :], d_low[part, :]), (q_high[...], q_low[...]))
 
 
 def ghost_step(agg_of, d_high, d_low, mine, other):
     return pl.pallas_call(
         ghost_kernel,
         in_specs=[SMEM] + [VMEM] * 4,
-        out_specs=VMEM,
-        out_shape=shape(WIDE, PAIR),
+        out_specs=[VMEM] * 2,
+        out_shape=[shape(WIDE // 2, PAIR)] * 2,
         scratch_shapes=[pltpu.VMEM((WIDE, PAIR), BF16)] * 2,
         compiler_params=params(),
         name="ghost_step",
@@ -308,9 +318,11 @@
     return jnp.where(is_near, mine, received), jnp.where(is_near, received, mine)
 
 
-def coarse_kernel(own, own_received, side, side_received, rt_high, rt_low, *refs):
+def coarse_kernel(own, own_received, upper, lower, upper_received, lower_received, rt_high, rt_low, *refs):
     regions, (high_ref, low_ref) = refs[:3], refs[3:]
-    sides = jnp.concatenate(near_and_far(side[...], side_received[...]), axis=1)
+    side = jnp.concatenate([upper[...], lower[...]], axis=0)
+    side_received = jnp.concatenate([upper_received[...], lower_received[...]], axis=0)
+    sides = jnp.concatenate(near_and_far(side, side_received), axis=1)
     sides = product((rt_high[...], rt_low[...]), halves(sides))
     values = (sides[:, :PAIR], own[...] + own_received[...], sides[:, PAIR:])
     for region, (ref, value) in enumerate(zip(regions, values)):
@@ -323,12 +335,12 @@
 def coarse_half(own, own_received, side, side_received, rt_high, rt_low):
     return pl.pallas_call(
         coarse_kernel,
-        in_specs=[VMEM] * 6,
+        in_specs=[VMEM] * 8,
         out_specs=[VMEM] * 5,
         out_shape=[shape(COARSE, PAIR)] * 3 + [shape(COARSE, 3 * PAIR, dtype=BF16)] * 2,
         compiler_params=params(),
         name="coarse_half",
-    )(own, own_received, side, side_received, rt_high, rt_low)
+    )(own, own_received, *side, *side_received, rt_high, rt_low)
 
 
 def share_kernel(*refs):
@@ -367,12 +379,13 @@
     )(*mine, *other)
 
 
-def lift_kernel(agg_of, own, own_received, side, side_received, smoother, prolong, w_ref):
+def lift_kernel(agg_of, own, own_received, upper, lower, upper_received, lower_received, smoother, prolong, w_ref):
     start = lax.axis_index("slab") * ROWS
     core = lax.axis_index("sub") & 1
     for e in range(ROWS):
         rows = span(e)
-        near, far = near_and_far(side[rows, :], side_received[rows, :])
+        side, side_received = ((upper, upper_received), (lower, lower_received))[e // HALF_ROWS]
+        near, far = near_and_far(side[span(e % HALF_ROWS), :], side_received[span(e % HALF_ROWS), :])
         g_half = jnp.concatenate([near, own[rows, :] + own_received[rows, :], far], axis=1)
         w_ref[rows, :] = -product(halves(smoother[e]), halves(g_half))
         w_ref[rows, span(1, PAIR)] += placed(prolong[e], agg_of[start + e] - 2 * core)
@@ -381,46 +394,44 @@
 def lift_half(agg_of, own, own_received, side, side_received, smoother, prolong):
     return pl.pallas_call(
         lift_kernel,
-        in_specs=[SMEM] + [VMEM] * 6,
+        in_specs=[SMEM] + [VMEM] * 8,
         out_specs=VMEM,
         out_shape=shape(WIDE, 3 * PAIR),
         compiler_params=params(),
         name="lift_half",
-    )(agg_of, own, own_received, side, side_received, smoother, prolong)
-
-
-def residual_kernel(keep, received, weight, rt_high, rt_low, residual_ref, first_ref):
-    residual = -(keep[...] + received[...])
-    residual_ref[...] = residual
-    first_ref[...] = weight[...] * narrow_product((rt_high[...], rt_low[...]), residual)
-
-
-def residual_step(keep, received, weight, rt_high, rt_low):
-    return pl.pallas_call(
-        residual_kernel,
-        in_specs=[VMEM] * 5,
-        out_specs=[VMEM] * 2,
-        out_shape=[shape(WIDE, COLS), shape(COARSE, COLS)],
-        compiler_params=params(),
-        name="residual_step",
-    )(keep, received, weight, rt_high, rt_low)
-
-
-def base_kernel(smoother, message, residual, base_ref):
-    for e in range(ROWS):
-        smoothed = narrow_product(halves(smoother[e]), residual[span(e), :])
-        base_ref[span(e), :] = message[span(e), :COLS] + smoothed
-
-
-def base_step(smoother, message, residual):
-    return pl.pallas_call(
-        base_kernel,
+    )(agg_of, own, own_received, *side, *side_received, smoother, prolong)
+
+
+def first_kernel(keep, received, weight, first_ref):
+    first_ref[...] = -weight[...] * (keep[...] + received[...])
+
+
+def first_correction(keep, received, weight):
+    return pl.pallas_call(
+        first_kernel,
         in_specs=[VMEM] * 3,
         out_specs=VMEM,
+        out_shape=shape(COARSE, COLS),
+        compiler_params=params(),
+        name="first_correction",
+    )(keep, received, weight)
+
+
+def base_kernel(smoother, message, keep, received, base_ref):
+    for e in range(ROWS):
+        residual = -(keep[span(e), :] + received[span(e), :])
+        base_ref[span(e), :] = message[span(e), :COLS] + narrow_product(halves(smoother[e]), residual)
+
+
+def base_step(smoother, message, keep, received):
+    return pl.pallas_call(
+        base_kernel,
+        in_specs=[VMEM] * 4,
+        out_specs=VMEM,
         out_shape=shape(WIDE, COLS),
         compiler_params=params(),
         name="base_step",
-    )(smoother, message, residual)
+    )(smoother, message, keep, received)
 
 
 def core_parts(*fields):
@@ -530,17 +541,20 @@
     )
     received, side, own_coarse = lax.optimization_barrier((received, side, own_coarse))
     own_coarse_received = swapped(own_coarse, 2)
-    keep, send, d_high, d_low = image(own_image, side, received, swapped(received, 1), side_message)
-    image_received = swapped(send, 2)
+    keep, send, rhs_keep, rhs_send, d_high, d_low = image(
+        own_image, side, received, swapped(received, 1), side_message, rt_high, rt_low
+    )
+    rhs_received = swapped(rhs_send, 2)
     ghosts = side_message[WIDE:]
     ghosts, own_coarse_received = lax.optimization_barrier((ghosts, own_coarse_received))
     side_half = ghost_step(agg_of, d_high, d_low, ghosts, swapped(ghosts, 1))
-    side_received = swapped(side_half, 2)
-    residual, first = residual_step(keep, image_received, weight, rt_high, rt_low)
-    base = base_step(smoother, message, residual)
+    side_received = [swapped(part, 2) for part in side_half]
+    first = first_correction(rhs_keep, rhs_received, weight)
     near, far = from_neighbours(first)
     own_half, side_received = lax.optimization_barrier((own_half, side_received))
     own_received = swapped(own_half, 2)
+    send, side_received = lax.optimization_barrier((send, side_received))
+    base = base_step(smoother, message, keep, swapped(send, 2))
     *coarse, mine_high, mine_low = coarse_half(
         own_coarse, own_coarse_received, side_half, side_received, rt_high, rt_low
     )

time: 65.5 us -> 63.2 us (0.965); the launches traced: 64.5 us -> 63 us
  starting transfers between devices: 23.5 us -> 21.3 us
  waiting for transfers between devices: 25.6 us -> 26.3 us
    ppermute x13 -> x15, waiting for transfers between devices: 13.5 us -> 19.9 us  [swapped(): return lax.ppermute(value, 'sub', [(i, i ^ bit) for i in range(size)])]
    ppermute x3, waiting for transfers between devices: 6.85 us -> 3.38 us  [from_neighbours(): far = lax.ppermute(value, 'slab', swaps(size, 1))]
    ppermute x3, starting transfers between devices: 8.26 us -> 5.73 us  [from_neighbours(): far = lax.ppermute(value, 'slab', swaps(size, 1))]
    ppermute x3, waiting for transfers between devices: 2.26 us -> 0.01 us  [from_neighbours(): near = lax.ppermute(value, 'slab', swaps(size, 0))]
    ppermute x13 -> x15, starting transfers between devices: 8.39 us -> 8.98 us  [swapped(): return lax.ppermute(value, 'sub', [(i, i ^ bit) for i in range(size)])]
  transfers between devices with their start and end apart: 20 -> 22, of which waited for: 11 -> 11; matrix products, arithmetic and copies ran while one was open for 0% -> 0% of each run, Pallas kernels for 14% -> 15%
where the time goes in v8:
time: 63.2 us; the launch traced here: 63 us
  waiting for transfers between devices  26.3 us (42%)
  starting transfers between devices  21.3 us (34%)
  Pallas kernels  14.4 us (23%)
  between operations  0.86 us (1%)
    ppermute x15, waiting for transfers between devices, swapped(): return lax.ppermute(value, 'sub', [(i, i ^ bit) for i in range(size)])  19.9 us
    ppermute x15, starting transfers between devices, swapped(): return lax.ppermute(value, 'sub', [(i, i ^ bit) for i in range(size)])  8.98 us
    ppermute x3, starting transfers between devices, from_neighbours(): far = lax.ppermute(value, 'slab', swaps(size, 1))  5.73 us
    pallas_call x1, Pallas kernels, start_step(): pl.pallas_call(start_kernel, in_specs=[HBM] * 7, out_specs=[VMEM] * 5, ou...  4.15 us
    ppermute x3, waiting for transfers between devices, from_neighbours(): far = lax.ppermute(value, 'slab', swaps(size, 1))  3.38 us
    ppermute x1, starting transfers between devices, from_side(): return lax.ppermute(value, ('slab', 'sub'), pairs)  3.38 us
    ppermute x3, starting transfers between devices, from_neighbours(): near = lax.ppermute(value, 'slab', swaps(size, 0))  3.2 us
    ppermute x1, waiting for transfers between devices, from_side(): return lax.ppermute(value, ('slab', 'sub'), pairs)  3 us
  transfers between devices with their start and end apart: 22, of which 11 were waited for; matrix products, arithmetic and copies ran while one was open for 0% of the time, Pallas kernels for 15%

profile of v8, /device:TPU:8, one launch (start us, length us, event | category | flops | bytes accessed | tf_op | source)
XLA Modules:
  0.0 63.0 jit_solution(4209232650320390590)
XLA Ops:
  0.6 0.0 copy-start
  0.6 0.0 copy-start.2
  0.7 4.1 %start_step.1 = (f32[512,1024]{1,0:T(8,128)S(1)}, f32[256,512]{1,0:T(8,128)S(1)}, f32[256,512]{1,0:T(8,128)S(1)}, f32[576,256]{1,0:T(8,128)S(1)}, f32[512,128]{1,0:T(8,128)S(1)}) custom-call(s32[8,16]{1,0:T(8,128)} %col_hbm.1, s32[8,4,2,8]{3,2,1,0:T(2,128)} %rows_hbm.1, s32[4,2,8]{2,1,0:T(2,128)} %bitcast.3, f32[8,16,64,64]{3,2,1,0:T(8,128)} %blocks_hbm.1, ...), custom_call_target="tpu_custom_call" | custom-call | tf_op jit(solution)/shard_map/start_step/pallas_call | solution.py:156
  4.8 0.1 collective-permute-start
  4.9 1.9 %collective-permute-done = f32[256,512]{1,0:T(8,128)S(1)} collective-permute-done((f32[256,512]{1,0:T(8,128)S(1)}, f32[256,512]{1,0:T(8,128)S(1)}, u32[]{:S(2)}, u32[]{:S(2)}) %collective-permute-start) | collective-permute-done | bytes 524320 | tf_op jit(solution)/shard_map/ppermute | solution.py:528
  6.8 0.1 collective-permute-start.2
  6.9 0.1 add.3
  7.0 1.6 %collective-permute-start.1 = (f32[256,512]{1,0:T(8,128)S(1)}, f32[256,512]{1,0:T(8,128)S(1)}, u32[]{:S(2)}, u32[]{:S(2)}) collective-permute-start(f32[256,512]{1,0:T(8,128)S(1)} %add.3), channel_id=1, source_target_pairs={{0,2},{1,3},{2,0},{3,1},{4,6},{5,7},{6,4},{7,5},{8,10},{9,11},{10,... | collective-permute-start | bytes 1572872 | tf_op jit(solution)/shard_map/ppermute | solution.py:528
  8.6 3.4 %collective-permute-start.3 = (f32[576,256]{1,0:T(8,128)S(1)}, f32[576,256]{1,0:T(8,128)S(1)}, u32[]{:S(2)}, u32[]{:S(2)}) collective-permute-start(f32[576,256]{1,0:T(8,128)S(1)} %get-tuple-element.57.field.message), channel_id=1, source_target_pairs={{0,4},{8,12},{16,20},{24,28},{4,0},{12,8},{20,16},{28,24},{1,5},{9... | collective-permute-start | bytes 1769480 | tf_op jit(solution)/shard_map/ppermute | solution.py:523
  12.0 0.0 collective-permute-done.2.pair_other
  12.0 0.0 copy-done
  12.0 0.0 copy-done.2
  12.0 2.7 %own_step.1 = (f32[512,512]{1,0:T(8,128)S(1)}, f32[512,128]{1,0:T(8,128)S(1)}, f32[256,128]{1,0:T(8,128)S(1)}, f32[512,256]{1,0:T(8,128)S(1)}, f32[256,128]{1,0:...) custom-call(s32[64]{0:T(128)S(1)} %copy-done.2, f32[8,64,64]{2,1,0:T(8,128)S(1)} %copy-done, ...), custom_call_target="tpu_custom_call" | custom-call | tf_op jit(solution)/shard_map/own_step/pallas_call | solution.py:234
  14.7 6.6 %collective-permute-done.1.received = f32[256,512]{1,0:T(8,128)S(1)} collective-permute-done((f32[256,512]{1,0:T(8,128)S(1)}, f32[256,512]{1,0:T(8,128)S(1)}, u32[]{:S(2)}, u32[]{:S(2)}) %collective-permute-start.1) | collective-permute-done | bytes 524320 | tf_op jit(solution)/shard_map/ppermute | solution.py:528
  21.3 0.0 collective-permute-start.5
  21.3 1.5 %collective-permute-start.4 = (f32[256,128]{1,0:T(8,128)S(1)}, f32[256,128]{1,0:T(8,128)S(1)}, u32[]{:S(2)}, u32[]{:S(2)}) collective-permute-start(f32[256,128]{1,0:T(8,128)S(1)} %get-tuple-element.63.own), channel_id=1, source_target_pairs={{0,2},{1,3},{2,0},{3,1},{4,6},{5,7},{6,4},{7,5},{8,10},{9,11},{10,... | collective-permute-start | bytes 393224 | tf_op jit(solution)/shard_map/ppermute | solution.py:528
  22.8 3.0 %collective-permute-done.3.message = f32[576,256]{1,0:T(8,128)S(1)} collective-permute-done((f32[576,256]{1,0:T(8,128)S(1)}, f32[576,256]{1,0:T(8,128)S(1)}, u32[]{:S(2)}, u32[]{:S(2)}) %collective-permute-start.3) | collective-permute-done | bytes 589856 | tf_op jit(solution)/shard_map/ppermute | solution.py:523
  25.8 0.0 collective-permute-done.5.received_other
  25.8 1.1 %image.1 = (f32[512,128]{1,0:T(8,128)S(1)}, f32[512,128]{1,0:T(8,128)S(1)}, f32[256,128]{1,0:T(8,128)S(1)}, f32[256,128]{1,0:T(8,128)S(1)}, bf16[512,512]{1,0:T(8,128)(2,1)S(1)}, /*index=5*/bf16[512,512]{1,0:T(8,128)(2,1)S(1)}) custom-call(f32[512,256]{1,0:T(8,128)S(1)} %get-tuple-element.65.own_image, f32[512,512]{1,0:T(8,128)S(1)} %get-tuple-element.66.side, ...), custom_call_target="tpu_custom_call" | custom-call | tf_op jit(solution)/shard_map/image/pallas_call | solution.py:278
  26.9 1.5 %collective-permute-start.9 = (f32[256,128]{1,0:T(8,128)S(1)}, f32[256,128]{1,0:T(8,128)S(1)}, u32[]{:S(2)}, u32[]{:S(2)}) collective-permute-start(f32[256,128]{1,0:T(8,128)S(1)} %get-tuple-element.85), channel_id=1, source_target_pairs={{0,2},{1,3},{2,0},{3,1},{4,6},{5,7},{6,4},{7,5},{8,10},{9,11},{10,... | collective-permute-start | bytes 393224 | tf_op jit(solution)/shard_map/ppermute | solution.py:528
  28.3 0.0 collective-permute-done.4.own_received
  28.3 0.1 collective-permute-start.6
  28.4 1.2 %collective-permute-done.6.other = f32[64,256]{1,0:T(8,128)S(1)} collective-permute-done((f32[64,256]{1,0:T(8,128)S(1)}, f32[64,256]{1,0:T(8,128)S(1)}, u32[]{:S(2)}, u32[]{:S(2)}) %collective-permute-start.6) | collective-permute-done | bytes 65568 | tf_op jit(solution)/shard_map/ppermute | solution.py:528
  29.7 1.3 %ghost_step.1 = (f32[256,128]{1,0:T(8,128)S(1)}, f32[256,128]{1,0:T(8,128)S(1)}) custom-call(s32[64]{0:T(128)S(1)} %copy-done.2, bf16[512,512]{1,0:T(8,128)(2,1)S(1)} %get-tuple-element.70.d_high, bf16[512,512]{1,0:T(8,128)(2,1)S(1)} %get-tuple-element.71.d_low, f32[64,256]{1,0:T(8,128)S(1)} %slice.4.mine, f32[64,256]{1,0:T(8,128)S(1)} %collective-permute-done.6.other), custom_call_target="tpu_custom_call" | custom-call | tf_op jit(solution)/shard_map/ghost_step/pallas_call | solution.py:305
  30.9 0.7 %collective-permute-start.7 = (f32[256,128]{1,0:T(8,128)S(1)}, f32[256,128]{1,0:T(8,128)S(1)}, u32[]{:S(2)}, u32[]{:S(2)}) collective-permute-start(f32[256,128]{1,0:T(8,128)S(1)} %get-tuple-element.73.upper), channel_id=1, source_target_pairs={{0,2},{1,3},{2,0},{3,1},{4,6},{5,7},{6,4},{7,5},{8,10},{9,11},{10,... | collective-permute-start | bytes 393224 | tf_op jit(solution)/shard_map/ppermute | solution.py:528
  31.6 1.4 %collective-permute-start.8 = (f32[256,128]{1,0:T(8,128)S(1)}, f32[256,128]{1,0:T(8,128)S(1)}, u32[]{:S(2)}, u32[]{:S(2)}) collective-permute-start(f32[256,128]{1,0:T(8,128)S(1)} %get-tuple-element.74.lower), channel_id=1, source_target_pairs={{0,2},{1,3},{2,0},{3,1},{4,6},{5,7},{6,4},{7,5},{8,10},{9,11},{10,... | collective-permute-start | bytes 393224 | tf_op jit(solution)/shard_map/ppermute | solution.py:528
  33.0 0.0 collective-permute-done.9.received
  33.0 0.0 copy-start.1
  33.1 1.6 %collective-permute-start.10 = (f32[256,128]{1,0:T(8,128)S(1)}, f32[256,128]{1,0:T(8,128)S(1)}, u32[]{:S(2)}, u32[]{:S(2)}) collective-permute-start(f32[256,128]{1,0:T(8,128)S(1)} %first_correction.1.refs_5_.refs_8_.refs_4_), channel_id=1, source_target_pairs={{0,4},{8,12},{16,20},{24,28},{4,0},{12,8},{20,16},{28,24},{1,5},{9... | collective-permute-start | bytes 393224 | tf_op jit(solution)/shard_map/ppermute | solution.py:513
  34.7 1.9 %collective-permute-start.11 = (f32[256,128]{1,0:T(8,128)S(1)}, f32[256,128]{1,0:T(8,128)S(1)}, u32[]{:S(2)}, u32[]{:S(2)}) collective-permute-start(f32[256,128]{1,0:T(8,128)S(1)} %first_correction.1.refs_5_.refs_8_.refs_4_), channel_id=1, source_target_pairs={{4,8},{12,16},{20,24},{8,4},{16,12},{24,20},{5,9},{13,17},{21,25},... | collective-permute-start | bytes 393224 | tf_op jit(solution)/shard_map/ppermute | solution.py:514
  36.6 0.8 %collective-permute-done.7.upper_received = f32[256,128]{1,0:T(8,128)S(1)} collective-permute-done((f32[256,128]{1,0:T(8,128)S(1)}, f32[256,128]{1,0:T(8,128)S(1)}, u32[]{:S(2)}, u32[]{:S(2)}) %collective-permute-start.7) | collective-permute-done | bytes 131104 | tf_op jit(solution)/shard_map/ppermute | solution.py:528
  37.3 2.0 %collective-permute-done.8.lower_received = f32[256,128]{1,0:T(8,128)S(1)} collective-permute-done((f32[256,128]{1,0:T(8,128)S(1)}, f32[256,128]{1,0:T(8,128)S(1)}, u32[]{:S(2)}, u32[]{:S(2)}) %collective-permute-start.8) | collective-permute-done | bytes 131104 | tf_op jit(solution)/shard_map/ppermute | solution.py:528
  39.4 0.4 coarse_half.1
  39.8 0.1 collective-permute-start.12
  39.9 0.5 collective-permute-start.13
  40.4 0.1 collective-permute-start.14
  40.5 0.0 collective-permute-done.10.refs_7_
  40.5 0.6 collective-permute-start.17
  41.1 1.3 %collective-permute-done.11.refs_9_ = f32[256,128]{1,0:T(8,128)S(1)} collective-permute-done((f32[256,128]{1,0:T(8,128)S(1)}, f32[256,128]{1,0:T(8,128)S(1)}, u32[]{:S(2)}, u32[]{:S(2)}) %collective-permute-start.11) | collective-permute-done | bytes 131104 | tf_op jit(solution)/shard_map/ppermute | solution.py:514
  42.4 0.0 collective-permute-done.12.refs_3_.refs_2_
  42.4 0.0 collective-permute-done.13.refs_4_.refs_3_
  42.4 0.0 collective-permute-done.14.refs_5_.refs_4_
  42.4 0.4 sweep.2.refs_7_
  42.8 0.9 %collective-permute-start.15 = (f32[256,128]{1,0:T(8,128)S(1)}, f32[256,128]{1,0:T(8,128)S(1)}, u32[]{:S(2)}, u32[]{:S(2)}) collective-permute-start(f32[256,128]{1,0:T(8,128)S(1)} %sweep.2.refs_7_), channel_id=1, source_target_pairs={{0,4},{8,12},{16,20},{24,28},{4,0},{12,8},{20,16},{28,24},{1,5},{9... | collective-permute-start | bytes 393224 | tf_op jit(solution)/shard_map/ppermute | solution.py:513
  43.7 1.9 %collective-permute-start.16 = (f32[256,128]{1,0:T(8,128)S(1)}, f32[256,128]{1,0:T(8,128)S(1)}, u32[]{:S(2)}, u32[]{:S(2)}) collective-permute-start(f32[256,128]{1,0:T(8,128)S(1)} %sweep.2.refs_7_), channel_id=1, source_target_pairs={{4,8},{12,16},{20,24},{8,4},{16,12},{24,20},{5,9},{13,17},{21,25},... | collective-permute-start | bytes 393224 | tf_op jit(solution)/shard_map/ppermute | solution.py:514
  45.7 1.0 %coarse_share.1 = (f32[4,3,64,64]{3,2,1,0:T(8,128)}, bf16[256,384]{1,0:T(8,128)(2,1)S(1)}, bf16[256,384]{1,0:T(8,128)(2,1)S(1)}) custom-call(f32[256,128]{1,0:T(8,128)S(1)} %get-tuple-element.81.refs_0_, f32[256,128]{1,0:T(8,128)S(1)} %get-tuple-element.82.refs_1_, f32[256,128]{1,0:T(8,128)S(1)} %get-tuple-element.83.refs_2_, ...), custom_call_target="tpu_custom_call" | custom-call | tf_op jit(solution)/shard_map/coarse_share/pallas_call | solution.py:371
  46.6 2.5 %collective-permute-done.17.own_received = f32[512,128]{1,0:T(8,128)S(1)} collective-permute-done((f32[512,128]{1,0:T(8,128)S(1)}, f32[512,128]{1,0:T(8,128)S(1)}, u32[]{:S(2)}, u32[]{:S(2)}) %collective-permute-start.17) | collective-permute-done | bytes 262176 | tf_op jit(solution)/shard_map/ppermute | solution.py:528
  49.1 0.0 copy-done.1
  49.1 1.0 %lift_half.1.mine = f32[512,384]{1,0:T(8,128)S(1)} custom-call(s32[64]{0:T(128)S(1)} %copy-done.2, f32[512,128]{1,0:T(8,128)S(1)} %get-tuple-element.95.own, f32[512,128]{1,0:T(8,128)S(1)} %collective-permute-done.17.own_received, f32[256,128]{1,0:T(8,128)S(1)} %get-tuple-element.73.upper, f32[256,128]{1,0:T(8,128)S(1)} %get-tuple-element.74.lower, ...), custom_call_target="tpu_custom_call" | custom-call | tf_op jit(solution)/shard_map/lift_half/pallas_call | solution.py:395
  50.1 0.0 collective-permute-done.15.refs_6_
  50.2 1.7 %collective-permute-done.16.refs_8_ = f32[256,128]{1,0:T(8,128)S(1)} collective-permute-done((f32[256,128]{1,0:T(8,128)S(1)}, f32[256,128]{1,0:T(8,128)S(1)}, u32[]{:S(2)}, u32[]{:S(2)}) %collective-permute-start.16) | collective-permute-done | bytes 131104 | tf_op jit(solution)/shard_map/ppermute | solution.py:514
  51.8 0.0 collective-permute-start.18
  51.8 0.8 %collective-permute-start.19 = (f32[512,128]{1,0:T(8,128)S(1)}, f32[512,128]{1,0:T(8,128)S(1)}, u32[]{:S(2)}, u32[]{:S(2)}) collective-permute-start(f32[512,128]{1,0:T(8,128)S(1)} %get-tuple-element.100), channel_id=1, source_target_pairs={{0,2},{1,3},{2,0},{3,1},{4,6},{5,7},{6,4},{7,5},{8,10},{9,11},{10,... | collective-permute-start | bytes 786440 | tf_op jit(solution)/shard_map/ppermute | solution.py:528
  52.6 0.4 sweep.3.own
  53.0 0.7 %collective-permute-start.20 = (f32[256,128]{1,0:T(8,128)S(1)}, f32[256,128]{1,0:T(8,128)S(1)}, u32[]{:S(2)}, u32[]{:S(2)}) collective-permute-start(f32[256,128]{1,0:T(8,128)S(1)} %sweep.3.own), channel_id=1, source_target_pairs={{0,4},{8,12},{16,20},{24,28},{4,0},{12,8},{20,16},{28,24},{1,5},{9... | collective-permute-start | bytes 393224 | tf_op jit(solution)/shard_map/ppermute | solution.py:513
  53.7 1.9 %collective-permute-start.21 = (f32[256,128]{1,0:T(8,128)S(1)}, f32[256,128]{1,0:T(8,128)S(1)}, u32[]{:S(2)}, u32[]{:S(2)}) collective-permute-start(f32[256,128]{1,0:T(8,128)S(1)} %sweep.3.own), channel_id=1, source_target_pairs={{4,8},{12,16},{20,24},{8,4},{16,12},{24,20},{5,9},{13,17},{21,25},... | collective-permute-start | bytes 393224 | tf_op jit(solution)/shard_map/ppermute | solution.py:514
  55.6 4.9 %collective-permute-done.19.received = f32[512,128]{1,0:T(8,128)S(1)} collective-permute-done((f32[512,128]{1,0:T(8,128)S(1)}, f32[512,128]{1,0:T(8,128)S(1)}, u32[]{:S(2)}, u32[]{:S(2)}) %collective-permute-start.19) | collective-permute-done | bytes 262176 | tf_op jit(solution)/shard_map/ppermute | solution.py:528
  60.5 0.3 base_step.1.base
  60.8 0.0 collective-permute-done.18.other
  60.8 0.6 lifted.1
  61.4 0.0 collective-permute-done.20.near
  61.4 0.4 collective-permute-done.21.far
  61.8 1.1 %last_step.1 = f32[512,128]{1,0:T(8,128)} custom-call(bf16[512,512]{1,0:T(8,128)(2,1)S(1)} %get-tuple-element.105.w_high, bf16[512,512]{1,0:T(8,128)(2,1)S(1)} %get-tuple-element.106.w_low, f32[512,128]{1,0:T(8,128)S(1)} %get-tuple-element.107.base, f32[256,128]{1,0:T(8,128)S(1)} %collective-permute-done.20.near, f32[256,128]{1,0:T(8,128)S(1)} %collective-permute-done.21.far), custom_call_target="tpu_custom_call" | custom-call | tf_op jit(solution)/shard_map/last_step/pallas_call | solution.py:496
  (2 shorter events, 0.0 us)
Async XLA Ops:
  0.6 11.4 %copy-start = (f32[8,64,64]{2,1,0:T(8,128)S(1)}, f32[8,64,64]{2,1,0:T(8,128)}, u32[]{:S(2)}) copy-start(f32[8,64,64]{2,1,0:T(8,128)} %prolong.3) | copy-start | bytes 393220
  0.6 11.4 %copy-start.2 = (s32[64]{0:T(128)S(1)}, s32[64]{0:T(128)}, u32[]{:S(2)}) copy-start(s32[64]{0:T(128)} %agg_of.5) | copy-start | bytes 772
  4.8 2.0 %collective-permute-start = (f32[256,512]{1,0:T(8,128)S(1)}, f32[256,512]{1,0:T(8,128)S(1)}, u32[]{:S(2)}, u32[]{:S(2)}) collective-permute-start(f32[256,512]{1,0:T(8,128)S(1)} %get-tuple-element.56), channel_id=1, source_target_pairs={{0,1},{1,0},{2,3},{3,2},{4,5},{5,4},{6,7},{7,6},{8,9},{9,8},{10,11... | collective-permute-start | bytes 1572872 | tf_op jit(solution)/shard_map/ppermute | solution.py:528
  6.8 5.2 %collective-permute-start.2 = (f32[512,1024]{1,0:T(8,128)S(1)}, f32[512,1024]{1,0:T(8,128)S(1)}, u32[]{:S(2)}, u32[]{:S(2)}) collective-permute-start(f32[512,1024]{1,0:T(8,128)S(1)} %get-tuple-element.60.pair), channel_id=1, source_target_pairs={{0,1},{1,0},{2,3},{3,2},{4,5},{5,4},{6,7},{7,6},{8,9},{9,8},{10,11... | collective-permute-start | bytes 6291464 | tf_op jit(solution)/shard_map/ppermute | solution.py:528
  7.0 14.3 %collective-permute-start.1 = (f32[256,512]{1,0:T(8,128)S(1)}, f32[256,512]{1,0:T(8,128)S(1)}, u32[]{:S(2)}, u32[]{:S(2)}) collective-permute-start(f32[256,512]{1,0:T(8,128)S(1)} %add.3), channel_id=1, source_target_pairs={{0,2},{1,3},{2,0},{3,1},{4,6},{5,7},{6,4},{7,5},{8,10},{9,11},{10,... | collective-permute-start | bytes 1572872 | tf_op jit(solution)/shard_map/ppermute | solution.py:528
  8.6 17.2 %collective-permute-start.3 = (f32[576,256]{1,0:T(8,128)S(1)}, f32[576,256]{1,0:T(8,128)S(1)}, u32[]{:S(2)}, u32[]{:S(2)}) collective-permute-start(f32[576,256]{1,0:T(8,128)S(1)} %get-tuple-element.57.field.message), channel_id=1, source_target_pairs={{0,4},{8,12},{16,20},{24,28},{4,0},{12,8},{20,16},{28,24},{1,5},{9... | collective-permute-start | bytes 1769480 | tf_op jit(solution)/shard_map/ppermute | solution.py:523
  21.3 4.5 %collective-permute-start.5 = (f32[256,512]{1,0:T(8,128)S(1)}, f32[256,512]{1,0:T(8,128)S(1)}, u32[]{:S(2)}, u32[]{:S(2)}) collective-permute-start(f32[256,512]{1,0:T(8,128)S(1)} %collective-permute-done.1.received), channel_id=1, source_target_pairs={{0,1},{1,0},{2,3},{3,2},{4,5},{5,4},{6,7},{7,6},{8,9},{9,8},{10,11... | collective-permute-start | bytes 1572872 | tf_op jit(solution)/shard_map/ppermute | solution.py:528
  21.3 7.1 %collective-permute-start.4 = (f32[256,128]{1,0:T(8,128)S(1)}, f32[256,128]{1,0:T(8,128)S(1)}, u32[]{:S(2)}, u32[]{:S(2)}) collective-permute-start(f32[256,128]{1,0:T(8,128)S(1)} %get-tuple-element.63.own), channel_id=1, source_target_pairs={{0,2},{1,3},{2,0},{3,1},{4,6},{5,7},{6,4},{7,5},{8,10},{9,11},{10,... | collective-permute-start | bytes 393224 | tf_op jit(solution)/shard_map/ppermute | solution.py:528
  26.9 6.2 %collective-permute-start.9 = (f32[256,128]{1,0:T(8,128)S(1)}, f32[256,128]{1,0:T(8,128)S(1)}, u32[]{:S(2)}, u32[]{:S(2)}) collective-permute-start(f32[256,128]{1,0:T(8,128)S(1)} %get-tuple-element.85), channel_id=1, source_target_pairs={{0,2},{1,3},{2,0},{3,1},{4,6},{5,7},{6,4},{7,5},{8,10},{9,11},{10,... | collective-permute-start | bytes 393224 | tf_op jit(solution)/shard_map/ppermute | solution.py:528
  28.3 1.3 %collective-permute-start.6 = (f32[64,256]{1,0:T(8,128)S(1)}, f32[64,256]{1,0:T(8,128)S(1)}, u32[]{:S(2)}, u32[]{:S(2)}) collective-permute-start(f32[64,256]{1,0:T(8,128)S(1)} %slice.4.mine), channel_id=1, source_target_pairs={{0,1},{1,0},{2,3},{3,2},{4,5},{5,4},{6,7},{7,6},{8,9},{9,8},{10,11... | collective-permute-start | bytes 196616 | tf_op jit(solution)/shard_map/ppermute | solution.py:528
  30.9 6.4 %collective-permute-start.7 = (f32[256,128]{1,0:T(8,128)S(1)}, f32[256,128]{1,0:T(8,128)S(1)}, u32[]{:S(2)}, u32[]{:S(2)}) collective-permute-start(f32[256,128]{1,0:T(8,128)S(1)} %get-tuple-element.73.upper), channel_id=1, source_target_pairs={{0,2},{1,3},{2,0},{3,1},{4,6},{5,7},{6,4},{7,5},{8,10},{9,11},{10,... | collective-permute-start | bytes 393224 | tf_op jit(solution)/shard_map/ppermute | solution.py:528
  31.6 7.8 %collective-permute-start.8 = (f32[256,128]{1,0:T(8,128)S(1)}, f32[256,128]{1,0:T(8,128)S(1)}, u32[]{:S(2)}, u32[]{:S(2)}) collective-permute-start(f32[256,128]{1,0:T(8,128)S(1)} %get-tuple-element.74.lower), channel_id=1, source_target_pairs={{0,2},{1,3},{2,0},{3,1},{4,6},{5,7},{6,4},{7,5},{8,10},{9,11},{10,... | collective-permute-start | bytes 393224 | tf_op jit(solution)/shard_map/ppermute | solution.py:528
  33.0 16.1 %copy-start.1 = (f32[8,64,64]{2,1,0:T(8,128)S(1)}, f32[8,64,64]{2,1,0:T(8,128)}, u32[]{:S(2)}) copy-start(f32[8,64,64]{2,1,0:T(8,128)} %smoother.3) | copy-start | bytes 393220
  33.1 7.4 %collective-permute-start.10 = (f32[256,128]{1,0:T(8,128)S(1)}, f32[256,128]{1,0:T(8,128)S(1)}, u32[]{:S(2)}, u32[]{:S(2)}) collective-permute-start(f32[256,128]{1,0:T(8,128)S(1)} %first_correction.1.refs_5_.refs_8_.refs_4_), channel_id=1, source_target_pairs={{0,4},{8,12},{16,20},{24,28},{4,0},{12,8},{20,16},{28,24},{1,5},{9... | collective-permute-start | bytes 393224 | tf_op jit(solution)/shard_map/ppermute | solution.py:513
  34.7 7.7 %collective-permute-start.11 = (f32[256,128]{1,0:T(8,128)S(1)}, f32[256,128]{1,0:T(8,128)S(1)}, u32[]{:S(2)}, u32[]{:S(2)}) collective-permute-start(f32[256,128]{1,0:T(8,128)S(1)} %first_correction.1.refs_5_.refs_8_.refs_4_), channel_id=1, source_target_pairs={{4,8},{12,16},{20,24},{8,4},{16,12},{24,20},{5,9},{13,17},{21,25},... | collective-permute-start | bytes 393224 | tf_op jit(solution)/shard_map/ppermute | solution.py:514
  39.8 2.6 %collective-permute-start.12 = (f32[256,128]{1,0:T(8,128)S(1)}, f32[256,128]{1,0:T(8,128)S(1)}, u32[]{:S(2)}, u32[]{:S(2)}) collective-permute-start(f32[256,128]{1,0:T(8,128)S(1)} %get-tuple-element.81.refs_0_), channel_id=1, source_target_pairs={{0,1},{1,0},{2,3},{3,2},{4,5},{5,4},{6,7},{7,6},{8,9},{9,8},{10,11... | collective-permute-start | bytes 393224 | tf_op jit(solution)/shard_map/ppermute | solution.py:528
  39.9 2.5 %collective-permute-start.13 = (f32[256,128]{1,0:T(8,128)S(1)}, f32[256,128]{1,0:T(8,128)S(1)}, u32[]{:S(2)}, u32[]{:S(2)}) collective-permute-start(f32[256,128]{1,0:T(8,128)S(1)} %get-tuple-element.82.refs_1_), channel_id=1, source_target_pairs={{0,1},{1,0},{2,3},{3,2},{4,5},{5,4},{6,7},{7,6},{8,9},{9,8},{10,11... | collective-permute-start | bytes 393224 | tf_op jit(solution)/shard_map/ppermute | solution.py:528
  40.4 2.0 %collective-permute-start.14 = (f32[256,128]{1,0:T(8,128)S(1)}, f32[256,128]{1,0:T(8,128)S(1)}, u32[]{:S(2)}, u32[]{:S(2)}) collective-permute-start(f32[256,128]{1,0:T(8,128)S(1)} %get-tuple-element.83.refs_2_), channel_id=1, source_target_pairs={{0,1},{1,0},{2,3},{3,2},{4,5},{5,4},{6,7},{7,6},{8,9},{9,8},{10,11... | collective-permute-start | bytes 393224 | tf_op jit(solution)/shard_map/ppermute | solution.py:528
  40.5 8.7 %collective-permute-start.17 = (f32[512,128]{1,0:T(8,128)S(1)}, f32[512,128]{1,0:T(8,128)S(1)}, u32[]{:S(2)}, u32[]{:S(2)}) collective-permute-start(f32[512,128]{1,0:T(8,128)S(1)} %get-tuple-element.95.own), channel_id=1, source_target_pairs={{0,2},{1,3},{2,0},{3,1},{4,6},{5,7},{6,4},{7,5},{8,10},{9,11},{10,... | collective-permute-start | bytes 786440 | tf_op jit(solution)/shard_map/ppermute | solution.py:528
  42.8 7.3 %collective-permute-start.15 = (f32[256,128]{1,0:T(8,128)S(1)}, f32[256,128]{1,0:T(8,128)S(1)}, u32[]{:S(2)}, u32[]{:S(2)}) collective-permute-start(f32[256,128]{1,0:T(8,128)S(1)} %sweep.2.refs_7_), channel_id=1, source_target_pairs={{0,4},{8,12},{16,20},{24,28},{4,0},{12,8},{20,16},{28,24},{1,5},{9... | collective-permute-start | bytes 393224 | tf_op jit(solution)/shard_map/ppermute | solution.py:513
  43.7 8.1 %collective-permute-start.16 = (f32[256,128]{1,0:T(8,128)S(1)}, f32[256,128]{1,0:T(8,128)S(1)}, u32[]{:S(2)}, u32[]{:S(2)}) collective-permute-start(f32[256,128]{1,0:T(8,128)S(1)} %sweep.2.refs_7_), channel_id=1, source_target_pairs={{4,8},{12,16},{20,24},{8,4},{16,12},{24,20},{5,9},{13,17},{21,25},... | collective-permute-start | bytes 393224 | tf_op jit(solution)/shard_map/ppermute | solution.py:514
  51.8 9.0 %collective-permute-start.18 = (f32[512,384]{1,0:T(8,128)S(1)}, f32[512,384]{1,0:T(8,128)S(1)}, u32[]{:S(2)}, u32[]{:S(2)}) collective-permute-start(f32[512,384]{1,0:T(8,128)S(1)} %lift_half.1.mine), channel_id=1, source_target_pairs={{0,1},{1,0},{2,3},{3,2},{4,5},{5,4},{6,7},{7,6},{8,9},{9,8},{10,11... | collective-permute-start | bytes 2359304 | tf_op jit(solution)/shard_map/ppermute | solution.py:528
  51.8 8.7 %collective-permute-start.19 = (f32[512,128]{1,0:T(8,128)S(1)}, f32[512,128]{1,0:T(8,128)S(1)}, u32[]{:S(2)}, u32[]{:S(2)}) collective-permute-start(f32[512,128]{1,0:T(8,128)S(1)} %get-tuple-element.100), channel_id=1, source_target_pairs={{0,2},{1,3},{2,0},{3,1},{4,6},{5,7},{6,4},{7,5},{8,10},{9,11},{10,... | collective-permute-start | bytes 786440 | tf_op jit(solution)/shard_map/ppermute | solution.py:528
  53.0 8.4 %collective-permute-start.20 = (f32[256,128]{1,0:T(8,128)S(1)}, f32[256,128]{1,0:T(8,128)S(1)}, u32[]{:S(2)}, u32[]{:S(2)}) collective-permute-start(f32[256,128]{1,0:T(8,128)S(1)} %sweep.3.own), channel_id=1, source_target_pairs={{0,4},{8,12},{16,20},{24,28},{4,0},{12,8},{20,16},{28,24},{1,5},{9... | collective-permute-start | bytes 393224 | tf_op jit(solution)/shard_map/ppermute | solution.py:513
  53.7 8.1 %collective-permute-start.21 = (f32[256,128]{1,0:T(8,128)S(1)}, f32[256,128]{1,0:T(8,128)S(1)}, u32[]{:S(2)}, u32[]{:S(2)}) collective-permute-start(f32[256,128]{1,0:T(8,128)S(1)} %sweep.3.own), channel_id=1, source_target_pairs={{4,8},{12,16},{20,24},{8,4},{16,12},{24,20},{5,9},{13,17},{21,25},... | collective-permute-start | bytes 393224 | tf_op jit(solution)/shard_map/ppermute | solution.py:514

commit v9 on v8

--- a/solution.py
+++ b/solution.py
@@ -191,7 +191,7 @@
 
 def own_kernel(
     agg_of, prolong, field, right, pair, pair_other,
-    side_ref, half_ref, coarse_ref, image_ref, weight_ref, rt_high, rt_low, q_high, q_low
+    side_ref, half_ref, image_ref, weight_ref, rt_high, rt_low, q_high, q_low
 ):
     start = lax.axis_index("slab") * ROWS
     core = lax.axis_index("sub") & 1
@@ -214,14 +214,10 @@
         high, low = halves(jnp.concatenate(restrict_rows, axis=0).T)
         rt_high[...] = high
         rt_low[...] = low
-        coarse_ref[...] = jnp.zeros_like(coarse_ref)
 
     side_ref[...] = pair[:, WIDE:] + pair_other[:, WIDE:]
     own = halves(pair[:, :WIDE] + pair_other[:, :WIDE])
-    half = product(own, (q_high[...], q_low[...]))
-    half_ref[...] = half
-    lanes = aligned(pl.program_id(0), half.shape[0])
-    coarse_ref[...] += narrow_product((rt_high[:, lanes], rt_low[:, lanes]), half)
+    half_ref[...] = product(own, (q_high[...], q_low[...]))
     total = product(own, halves(field[...]))
     image_ref[:, :COLS] = total[:, :COLS] - right[...]
     image_ref[:, COLS:] = total[:, COLS:]
@@ -235,11 +231,10 @@
         own_kernel,
         grid=(steps,),
         in_specs=[SMEM, whole(*prolong.shape), whole(WIDE, 2 * COLS), part(COLS)] + [part(2 * WIDE)] * 2,
-        out_specs=[part(WIDE), part(PAIR), whole(COARSE, PAIR), part(2 * COLS), whole(COARSE, COLS)] + [whole(COARSE, WIDE)] * 2,
+        out_specs=[part(WIDE), part(PAIR), part(2 * COLS), whole(COARSE, COLS)] + [whole(COARSE, WIDE)] * 2,
         out_shape=[
             shape(WIDE, WIDE),
             shape(WIDE, PAIR),
-            shape(COARSE, PAIR),
             shape(WIDE, 2 * COLS),
             shape(COARSE, COLS),
             shape(COARSE, WIDE, dtype=BF16),
@@ -324,7 +319,8 @@
     side_received = jnp.concatenate([upper_received[...], lower_received[...]], axis=0)
     sides = jnp.concatenate(near_and_far(side, side_received), axis=1)
     sides = product((rt_high[...], rt_low[...]), halves(sides))
-    values = (sides[:, :PAIR], own[...] + own_received[...], sides[:, PAIR:])
+    centre = narrow_product((rt_high[...], rt_low[...]), own[...] + own_received[...])
+    values = (sides[:, :PAIR], centre, sides[:, PAIR:])
     for region, (ref, value) in enumerate(zip(regions, values)):
         ref[...] = value
         high, low = halves(value)
@@ -536,27 +532,24 @@
     theirs = swapped(theirs, 1)
     received = swapped(mine + theirs, 2)
     pair, theirs = lax.optimization_barrier((pair, theirs))
-    side, own_half, own_coarse, own_image, weight, rt_high, rt_low = own_step(
+    side, own_half, own_image, weight, rt_high, rt_low = own_step(
         agg_of, prolong, message, right, pair, swapped(pair, 1)
     )
-    received, side, own_coarse = lax.optimization_barrier((received, side, own_coarse))
-    own_coarse_received = swapped(own_coarse, 2)
+    received, side, own_half = lax.optimization_barrier((received, side, own_half))
+    own_received = swapped(own_half, 2)
     keep, send, rhs_keep, rhs_send, d_high, d_low = image(
         own_image, side, received, swapped(received, 1), side_message, rt_high, rt_low
     )
     rhs_received = swapped(rhs_send, 2)
     ghosts = side_message[WIDE:]
-    ghosts, own_coarse_received = lax.optimization_barrier((ghosts, own_coarse_received))
     side_half = ghost_step(agg_of, d_high, d_low, ghosts, swapped(ghosts, 1))
     side_received = [swapped(part, 2) for part in side_half]
     first = first_correction(rhs_keep, rhs_received, weight)
     near, far = from_neighbours(first)
-    own_half, side_received = lax.optimization_barrier((own_half, side_received))
-    own_received = swapped(own_half, 2)
     send, side_received = lax.optimization_barrier((send, side_received))
     base = base_step(smoother, message, keep, swapped(send, 2))
     *coarse, mine_high, mine_low = coarse_half(
-        own_coarse, own_coarse_received, side_half, side_received, rt_high, rt_low
+        own_half, own_received, side_half, side_received, rt_high, rt_low
     )
     coarse_other = [swapped(region, 1) for region in coarse]
     near, far, coarse_other = lax.optimization_barrier((near, far, coarse_other))
@@ -566,8 +559,8 @@
     for index in range(1, COARSE_SWEEPS - 1):
         near, far = from_neighbours(correction)
         if index == 1:
-            shadowed = (near, far, lift, other_high, other_low)
-            near, far, lift, other_high, other_low = lax.optimization_barrier(shadowed)
+            shadowed = (near, far, lift, base, other_high, other_low)
+            near, far, lift, base, other_high, other_low = lax.optimization_barrier(shadowed)
         operators = (mine_high, mine_low, other_high, other_low)
         correction = sweep(operators, first, weight, near, correction, far)
     lift_other = swapped(lift, 1)

time: 63.2 us -> 62.8 us (level)
    ppermute x15 -> x14, waiting for transfers between devices: 19.9 us -> 14.4 us  [swapped(): return lax.ppermute(value, 'sub', [(i, i ^ bit) for i in range(size)])]
    ppermute x3, waiting for transfers between devices: 3.38 us -> 6.75 us  [from_neighbours(): far = lax.ppermute(value, 'slab', swaps(size, 1))]
    ppermute x3, waiting for transfers between devices: 0.01 us -> 2.67 us  [from_neighbours(): near = lax.ppermute(value, 'slab', swaps(size, 0))]
    ppermute x15 -> x14, starting transfers between devices: 8.98 us -> 8.17 us  [swapped(): return lax.ppermute(value, 'sub', [(i, i ^ bit) for i in range(size)])]
  transfers between devices with their start and end apart: 22 -> 21, of which waited for: 11 -> 11; matrix products, arithmetic and copies ran while one was open for 0% -> 0% of each run, Pallas kernels for 15% -> 14%
where the time goes in v9:
time: 62.8 us; the launch traced here: 62.6 us
  waiting for transfers between devices  26.8 us (43%)
  starting transfers between devices  20.7 us (33%)
  Pallas kernels  14.2 us (23%)
  between operations  0.85 us (1%)
    ppermute x14, waiting for transfers between devices, swapped(): return lax.ppermute(value, 'sub', [(i, i ^ bit) for i in range(size)])  14.4 us
    ppermute x14, starting transfers between devices, swapped(): return lax.ppermute(value, 'sub', [(i, i ^ bit) for i in range(size)])  8.17 us
    ppermute x3, waiting for transfers between devices, from_neighbours(): far = lax.ppermute(value, 'slab', swaps(size, 1))  6.75 us
    ppermute x3, starting transfers between devices, from_neighbours(): far = lax.ppermute(value, 'slab', swaps(size, 1))  5.73 us
    pallas_call x1, Pallas kernels, start_step(): pl.pallas_call(start_kernel, in_specs=[HBM] * 7, out_specs=[VMEM] * 5, ou...  4.14 us
    ppermute x1, starting transfers between devices, from_side(): return lax.ppermute(value, ('slab', 'sub'), pairs)  3.4 us
    ppermute x3, starting transfers between devices, from_neighbours(): near = lax.ppermute(value, 'slab', swaps(size, 0))  3.39 us
    ppermute x1, waiting for transfers between devices, from_side(): return lax.ppermute(value, ('slab', 'sub'), pairs)  3 us
  transfers between devices with their start and end apart: 21, of which 11 were waited for; matrix products, arithmetic and copies ran while one was open for 0% of the time, Pallas kernels for 14%

profile of v9, /device:TPU:8, one launch (start us, length us, event | category | flops | bytes accessed | tf_op | source)
XLA Modules:
  0.0 62.6 jit_solution(5535703916477560829)
XLA Ops:
  0.6 0.0 copy-start
  0.6 0.0 copy-start.2
  0.7 4.1 %start_step.1 = (f32[512,1024]{1,0:T(8,128)S(1)}, f32[256,512]{1,0:T(8,128)S(1)}, f32[256,512]{1,0:T(8,128)S(1)}, f32[576,256]{1,0:T(8,128)S(1)}, f32[512,128]{1,0:T(8,128)S(1)}) custom-call(s32[8,16]{1,0:T(8,128)} %col_hbm.1, s32[8,4,2,8]{3,2,1,0:T(2,128)} %rows_hbm.1, s32[4,2,8]{2,1,0:T(2,128)} %bitcast.3, f32[8,16,64,64]{3,2,1,0:T(8,128)} %blocks_hbm.1, ...), custom_call_target="tpu_custom_call" | custom-call | tf_op jit(solution)/shard_map/start_step/pallas_call | solution.py:156
  4.8 0.1 collective-permute-start
  4.9 1.9 %collective-permute-done = f32[256,512]{1,0:T(8,128)S(1)} collective-permute-done((f32[256,512]{1,0:T(8,128)S(1)}, f32[256,512]{1,0:T(8,128)S(1)}, u32[]{:S(2)}, u32[]{:S(2)}) %collective-permute-start) | collective-permute-done | bytes 524320 | tf_op jit(solution)/shard_map/ppermute | solution.py:524
  6.8 0.1 collective-permute-start.2
  6.9 0.1 add.3
  7.0 1.6 %collective-permute-start.1 = (f32[256,512]{1,0:T(8,128)S(1)}, f32[256,512]{1,0:T(8,128)S(1)}, u32[]{:S(2)}, u32[]{:S(2)}) collective-permute-start(f32[256,512]{1,0:T(8,128)S(1)} %add.3), channel_id=1, source_target_pairs={{0,2},{1,3},{2,0},{3,1},{4,6},{5,7},{6,4},{7,5},{8,10},{9,11},{10,... | collective-permute-start | bytes 1572872 | tf_op jit(solution)/shard_map/ppermute | solution.py:524
  8.6 3.4 %collective-permute-start.5 = (f32[576,256]{1,0:T(8,128)S(1)}, f32[576,256]{1,0:T(8,128)S(1)}, u32[]{:S(2)}, u32[]{:S(2)}) collective-permute-start(f32[576,256]{1,0:T(8,128)S(1)} %get-tuple-element.52.field.message), channel_id=1, source_target_pairs={{0,4},{8,12},{16,20},{24,28},{4,0},{12,8},{20,16},{28,24},{1,5},{9... | collective-permute-start | bytes 1769480 | tf_op jit(solution)/shard_map/ppermute | solution.py:519
  12.0 0.0 collective-permute-done.2.pair_other
  12.0 0.0 copy-done
  12.0 0.0 copy-done.2
  12.0 2.3 %own_step.1 = (f32[512,512]{1,0:T(8,128)S(1)}, f32[512,128]{1,0:T(8,128)S(1)}, f32[512,256]{1,0:T(8,128)S(1)}, f32[256,128]{1,0:T(8,128)S(1)}, bf16[256,512]{1,0...) custom-call(s32[64]{0:T(128)S(1)} %copy-done.2, f32[8,64,64]{2,1,0:T(8,128)S(1)} %copy-done, ...), custom_call_target="tpu_custom_call" | custom-call | tf_op jit(solution)/shard_map/own_step/pallas_call | solution.py:230
  14.3 6.9 %collective-permute-done.1.received = f32[256,512]{1,0:T(8,128)S(1)} collective-permute-done((f32[256,512]{1,0:T(8,128)S(1)}, f32[256,512]{1,0:T(8,128)S(1)}, u32[]{:S(2)}, u32[]{:S(2)}) %collective-permute-start.1) | collective-permute-done | bytes 524320 | tf_op jit(solution)/shard_map/ppermute | solution.py:524
  21.3 0.0 collective-permute-start.4
  21.3 1.5 %collective-permute-start.3 = (f32[512,128]{1,0:T(8,128)S(1)}, f32[512,128]{1,0:T(8,128)S(1)}, u32[]{:S(2)}, u32[]{:S(2)}) collective-permute-start(f32[512,128]{1,0:T(8,128)S(1)} %get-tuple-element.58.own), channel_id=1, source_target_pairs={{0,2},{1,3},{2,0},{3,1},{4,6},{5,7},{6,4},{7,5},{8,10},{9,11},{10,... | collective-permute-start | bytes 786440 | tf_op jit(solution)/shard_map/ppermute | solution.py:524
  22.8 3.0 %collective-permute-done.5.message = f32[576,256]{1,0:T(8,128)S(1)} collective-permute-done((f32[576,256]{1,0:T(8,128)S(1)}, f32[576,256]{1,0:T(8,128)S(1)}, u32[]{:S(2)}, u32[]{:S(2)}) %collective-permute-start.5) | collective-permute-done | bytes 589856 | tf_op jit(solution)/shard_map/ppermute | solution.py:519
  25.8 0.0 collective-permute-done.4.received_other
  25.8 1.0 %image.1 = (f32[512,128]{1,0:T(8,128)S(1)}, f32[512,128]{1,0:T(8,128)S(1)}, f32[256,128]{1,0:T(8,128)S(1)}, f32[256,128]{1,0:T(8,128)S(1)}, bf16[512,512]{1,0:T(8,128)(2,1)S(1)}, /*index=5*/bf16[512,512]{1,0:T(8,128)(2,1)S(1)}) custom-call(f32[512,256]{1,0:T(8,128)S(1)} %get-tuple-element.59.own_image, f32[512,512]{1,0:T(8,128)S(1)} %get-tuple-element.60.side, ...), custom_call_target="tpu_custom_call" | custom-call | tf_op jit(solution)/shard_map/image/pallas_call | solution.py:273
  26.8 1.5 %collective-permute-start.9 = (f32[256,128]{1,0:T(8,128)S(1)}, f32[256,128]{1,0:T(8,128)S(1)}, u32[]{:S(2)}, u32[]{:S(2)}) collective-permute-start(f32[256,128]{1,0:T(8,128)S(1)} %get-tuple-element.75), channel_id=1, source_target_pairs={{0,2},{1,3},{2,0},{3,1},{4,6},{5,7},{6,4},{7,5},{8,10},{9,11},{10,... | collective-permute-start | bytes 393224 | tf_op jit(solution)/shard_map/ppermute | solution.py:524
  28.3 0.0 collective-permute-start.6
  28.3 1.2 %collective-permute-done.6.other = f32[64,256]{1,0:T(8,128)S(1)} collective-permute-done((f32[64,256]{1,0:T(8,128)S(1)}, f32[64,256]{1,0:T(8,128)S(1)}, u32[]{:S(2)}, u32[]{:S(2)}) %collective-permute-start.6) | collective-permute-done | bytes 65568 | tf_op jit(solution)/shard_map/ppermute | solution.py:524
  29.6 1.3 %ghost_step.1 = (f32[256,128]{1,0:T(8,128)S(1)}, f32[256,128]{1,0:T(8,128)S(1)}) custom-call(s32[64]{0:T(128)S(1)} %copy-done.2, bf16[512,512]{1,0:T(8,128)(2,1)S(1)} %get-tuple-element.64.d_high, bf16[512,512]{1,0:T(8,128)(2,1)S(1)} %get-tuple-element.65.d_low, f32[64,256]{1,0:T(8,128)S(1)} %slice.4.mine, f32[64,256]{1,0:T(8,128)S(1)} %collective-permute-done.6.other), custom_call_target="tpu_custom_call" | custom-call | tf_op jit(solution)/shard_map/ghost_step/pallas_call | solution.py:300
  30.8 0.0 copy-start.1
  30.9 0.7 %collective-permute-start.7 = (f32[256,128]{1,0:T(8,128)S(1)}, f32[256,128]{1,0:T(8,128)S(1)}, u32[]{:S(2)}, u32[]{:S(2)}) collective-permute-start(f32[256,128]{1,0:T(8,128)S(1)} %get-tuple-element.66.upper), channel_id=1, source_target_pairs={{0,2},{1,3},{2,0},{3,1},{4,6},{5,7},{6,4},{7,5},{8,10},{9,11},{10,... | collective-permute-start | bytes 393224 | tf_op jit(solution)/shard_map/ppermute | solution.py:524
  31.5 1.4 %collective-permute-start.8 = (f32[256,128]{1,0:T(8,128)S(1)}, f32[256,128]{1,0:T(8,128)S(1)}, u32[]{:S(2)}, u32[]{:S(2)}) collective-permute-start(f32[256,128]{1,0:T(8,128)S(1)} %get-tuple-element.67.lower), channel_id=1, source_target_pairs={{0,2},{1,3},{2,0},{3,1},{4,6},{5,7},{6,4},{7,5},{8,10},{9,11},{10,... | collective-permute-start | bytes 393224 | tf_op jit(solution)/shard_map/ppermute | solution.py:524
  32.9 0.0 collective-permute-done.9.received
  33.0 1.6 %collective-permute-start.10 = (f32[256,128]{1,0:T(8,128)S(1)}, f32[256,128]{1,0:T(8,128)S(1)}, u32[]{:S(2)}, u32[]{:S(2)}) collective-permute-start(f32[256,128]{1,0:T(8,128)S(1)} %first_correction.1.refs_5_.refs_8_.refs_4_), channel_id=1, source_target_pairs={{0,4},{8,12},{16,20},{24,28},{4,0},{12,8},{20,16},{28,24},{1,5},{9... | collective-permute-start | bytes 393224 | tf_op jit(solution)/shard_map/ppermute | solution.py:509
  34.6 1.9 %collective-permute-start.11 = (f32[256,128]{1,0:T(8,128)S(1)}, f32[256,128]{1,0:T(8,128)S(1)}, u32[]{:S(2)}, u32[]{:S(2)}) collective-permute-start(f32[256,128]{1,0:T(8,128)S(1)} %first_correction.1.refs_5_.refs_8_.refs_4_), channel_id=1, source_target_pairs={{4,8},{12,16},{20,24},{8,4},{16,12},{24,20},{5,9},{13,17},{21,25},... | collective-permute-start | bytes 393224 | tf_op jit(solution)/shard_map/ppermute | solution.py:510
  36.5 0.8 %collective-permute-done.7.upper_received = f32[256,128]{1,0:T(8,128)S(1)} collective-permute-done((f32[256,128]{1,0:T(8,128)S(1)}, f32[256,128]{1,0:T(8,128)S(1)}, u32[]{:S(2)}, u32[]{:S(2)}) %collective-permute-start.7) | collective-permute-done | bytes 131104 | tf_op jit(solution)/shard_map/ppermute | solution.py:524
  37.3 2.0 %collective-permute-done.8.lower_received = f32[256,128]{1,0:T(8,128)S(1)} collective-permute-done((f32[256,128]{1,0:T(8,128)S(1)}, f32[256,128]{1,0:T(8,128)S(1)}, u32[]{:S(2)}, u32[]{:S(2)}) %collective-permute-start.8) | collective-permute-done | bytes 131104 | tf_op jit(solution)/shard_map/ppermute | solution.py:524
  39.3 0.0 collective-permute-done.3.own_received
  39.3 0.6 coarse_half.1
  39.9 0.1 collective-permute-start.12
  40.0 0.5 collective-permute-start.13
  40.5 0.1 collective-permute-start.14
  40.5 0.0 collective-permute-done.10.refs_7_
  40.5 0.6 %collective-permute-start.17 = (f32[512,128]{1,0:T(8,128)S(1)}, f32[512,128]{1,0:T(8,128)S(1)}, u32[]{:S(2)}, u32[]{:S(2)}) collective-permute-start(f32[512,128]{1,0:T(8,128)S(1)} %get-tuple-element.86), channel_id=1, source_target_pairs={{0,2},{1,3},{2,0},{3,1},{4,6},{5,7},{6,4},{7,5},{8,10},{9,11},{10,... | collective-permute-start | bytes 786440 | tf_op jit(solution)/shard_map/ppermute | solution.py:524
  41.2 1.1 %collective-permute-done.11.refs_9_ = f32[256,128]{1,0:T(8,128)S(1)} collective-permute-done((f32[256,128]{1,0:T(8,128)S(1)}, f32[256,128]{1,0:T(8,128)S(1)}, u32[]{:S(2)}, u32[]{:S(2)}) %collective-permute-start.11) | collective-permute-done | bytes 131104 | tf_op jit(solution)/shard_map/ppermute | solution.py:510
  42.3 0.0 collective-permute-done.12.refs_3_.refs_2_
  42.3 0.0 collective-permute-done.13.refs_4_.refs_3_
  42.3 0.0 collective-permute-done.14.refs_5_.refs_4_
  42.3 0.4 sweep.2.refs_7_
  42.7 1.1 %collective-permute-start.15 = (f32[256,128]{1,0:T(8,128)S(1)}, f32[256,128]{1,0:T(8,128)S(1)}, u32[]{:S(2)}, u32[]{:S(2)}) collective-permute-start(f32[256,128]{1,0:T(8,128)S(1)} %sweep.2.refs_7_), channel_id=1, source_target_pairs={{0,4},{8,12},{16,20},{24,28},{4,0},{12,8},{20,16},{28,24},{1,5},{9... | collective-permute-start | bytes 393224 | tf_op jit(solution)/shard_map/ppermute | solution.py:509
  43.8 1.9 %collective-permute-start.16 = (f32[256,128]{1,0:T(8,128)S(1)}, f32[256,128]{1,0:T(8,128)S(1)}, u32[]{:S(2)}, u32[]{:S(2)}) collective-permute-start(f32[256,128]{1,0:T(8,128)S(1)} %sweep.2.refs_7_), channel_id=1, source_target_pairs={{4,8},{12,16},{20,24},{8,4},{16,12},{24,20},{5,9},{13,17},{21,25},... | collective-permute-start | bytes 393224 | tf_op jit(solution)/shard_map/ppermute | solution.py:510
  45.7 0.0 copy-done.1
  45.7 1.0 %lift_half.1.mine = f32[512,384]{1,0:T(8,128)S(1)} custom-call(s32[64]{0:T(128)S(1)} %copy-done.2, f32[512,128]{1,0:T(8,128)S(1)} %get-tuple-element.58.own, f32[512,128]{1,0:T(8,128)S(1)} %collective-permute-done.3.own_received, f32[256,128]{1,0:T(8,128)S(1)} %get-tuple-element.66.upper, f32[256,128]{1,0:T(8,128)S(1)} %get-tuple-element.67.lower, ...), custom_call_target="tpu_custom_call" | custom-call | tf_op jit(solution)/shard_map/lift_half/pallas_call | solution.py:391
  46.8 1.0 %coarse_share.1 = (f32[4,3,64,64]{3,2,1,0:T(8,128)}, bf16[256,384]{1,0:T(8,128)(2,1)S(1)}, bf16[256,384]{1,0:T(8,128)(2,1)S(1)}) custom-call(f32[256,128]{1,0:T(8,128)S(1)} %get-tuple-element.71.refs_0_, f32[256,128]{1,0:T(8,128)S(1)} %get-tuple-element.72.refs_1_, f32[256,128]{1,0:T(8,128)S(1)} %get-tuple-element.73.refs_2_, ...), custom_call_target="tpu_custom_call" | custom-call | tf_op jit(solution)/shard_map/coarse_share/pallas_call | solution.py:367
  47.7 1.5 %collective-permute-done.17.received = f32[512,128]{1,0:T(8,128)S(1)} collective-permute-done((f32[512,128]{1,0:T(8,128)S(1)}, f32[512,128]{1,0:T(8,128)S(1)}, u32[]{:S(2)}, u32[]{:S(2)}) %collective-permute-start.17) | collective-permute-done | bytes 262176 | tf_op jit(solution)/shard_map/ppermute | solution.py:524
  49.2 0.3 base_step.1.base
  49.5 0.0 collective-permute-done.15.refs_6_
  49.5 2.4 %collective-permute-done.16.refs_8_ = f32[256,128]{1,0:T(8,128)S(1)} collective-permute-done((f32[256,128]{1,0:T(8,128)S(1)}, f32[256,128]{1,0:T(8,128)S(1)}, u32[]{:S(2)}, u32[]{:S(2)}) %collective-permute-start.16) | collective-permute-done | bytes 131104 | tf_op jit(solution)/shard_map/ppermute | solution.py:510
  51.9 0.0 collective-permute-start.18
  51.9 0.4 sweep.3.own
  52.3 0.8 %collective-permute-start.19 = (f32[256,128]{1,0:T(8,128)S(1)}, f32[256,128]{1,0:T(8,128)S(1)}, u32[]{:S(2)}, u32[]{:S(2)}) collective-permute-start(f32[256,128]{1,0:T(8,128)S(1)} %sweep.3.own), channel_id=1, source_target_pairs={{0,4},{8,12},{16,20},{24,28},{4,0},{12,8},{20,16},{28,24},{1,5},{9... | collective-permute-start | bytes 393224 | tf_op jit(solution)/shard_map/ppermute | solution.py:509
  53.1 1.9 %collective-permute-start.20 = (f32[256,128]{1,0:T(8,128)S(1)}, f32[256,128]{1,0:T(8,128)S(1)}, u32[]{:S(2)}, u32[]{:S(2)}) collective-permute-start(f32[256,128]{1,0:T(8,128)S(1)} %sweep.3.own), channel_id=1, source_target_pairs={{4,8},{12,16},{20,24},{8,4},{16,12},{24,20},{5,9},{13,17},{21,25},... | collective-permute-start | bytes 393224 | tf_op jit(solution)/shard_map/ppermute | solution.py:510
  55.0 0.0 collective-permute-done.18.other
  55.0 0.6 lifted.1
  55.6 2.7 %collective-permute-done.19.near = f32[256,128]{1,0:T(8,128)S(1)} collective-permute-done((f32[256,128]{1,0:T(8,128)S(1)}, f32[256,128]{1,0:T(8,128)S(1)}, u32[]{:S(2)}, u32[]{:S(2)}) %collective-permute-start.19) | collective-permute-done | bytes 131104 | tf_op jit(solution)/shard_map/ppermute | solution.py:509
  58.3 3.2 %collective-permute-done.20.far = f32[256,128]{1,0:T(8,128)S(1)} collective-permute-done((f32[256,128]{1,0:T(8,128)S(1)}, f32[256,128]{1,0:T(8,128)S(1)}, u32[]{:S(2)}, u32[]{:S(2)}) %collective-permute-start.20) | collective-permute-done | bytes 131104 | tf_op jit(solution)/shard_map/ppermute | solution.py:510
  61.5 1.1 %last_step.1 = f32[512,128]{1,0:T(8,128)} custom-call(bf16[512,512]{1,0:T(8,128)(2,1)S(1)} %get-tuple-element.95.w_high, bf16[512,512]{1,0:T(8,128)(2,1)S(1)} %get-tuple-element.96.w_low, f32[512,128]{1,0:T(8,128)S(1)} %get-tuple-element.97.base, f32[256,128]{1,0:T(8,128)S(1)} %collective-permute-done.19.near, f32[256,128]{1,0:T(8,128)S(1)} %collective-permute-done.20.far), custom_call_target="tpu_custom_call" | custom-call | tf_op jit(solution)/shard_map/last_step/pallas_call | solution.py:492
  (2 shorter events, 0.0 us)
Async XLA Ops:
  0.6 11.4 %copy-start = (f32[8,64,64]{2,1,0:T(8,128)S(1)}, f32[8,64,64]{2,1,0:T(8,128)}, u32[]{:S(2)}) copy-start(f32[8,64,64]{2,1,0:T(8,128)} %prolong.3) | copy-start | bytes 393220
  0.6 11.4 %copy-start.2 = (s32[64]{0:T(128)S(1)}, s32[64]{0:T(128)}, u32[]{:S(2)}) copy-start(s32[64]{0:T(128)} %agg_of.5) | copy-start | bytes 772
  4.8 2.0 %collective-permute-start = (f32[256,512]{1,0:T(8,128)S(1)}, f32[256,512]{1,0:T(8,128)S(1)}, u32[]{:S(2)}, u32[]{:S(2)}) collective-permute-start(f32[256,512]{1,0:T(8,128)S(1)} %get-tuple-element.51), channel_id=1, source_target_pairs={{0,1},{1,0},{2,3},{3,2},{4,5},{5,4},{6,7},{7,6},{8,9},{9,8},{10,11... | collective-permute-start | bytes 1572872 | tf_op jit(solution)/shard_map/ppermute | solution.py:524
  6.8 5.2 %collective-permute-start.2 = (f32[512,1024]{1,0:T(8,128)S(1)}, f32[512,1024]{1,0:T(8,128)S(1)}, u32[]{:S(2)}, u32[]{:S(2)}) collective-permute-start(f32[512,1024]{1,0:T(8,128)S(1)} %get-tuple-element.55.pair), channel_id=1, source_target_pairs={{0,1},{1,0},{2,3},{3,2},{4,5},{5,4},{6,7},{7,6},{8,9},{9,8},{10,11... | collective-permute-start | bytes 6291464 | tf_op jit(solution)/shard_map/ppermute | solution.py:524
  7.0 14.3 %collective-permute-start.1 = (f32[256,512]{1,0:T(8,128)S(1)}, f32[256,512]{1,0:T(8,128)S(1)}, u32[]{:S(2)}, u32[]{:S(2)}) collective-permute-start(f32[256,512]{1,0:T(8,128)S(1)} %add.3), channel_id=1, source_target_pairs={{0,2},{1,3},{2,0},{3,1},{4,6},{5,7},{6,4},{7,5},{8,10},{9,11},{10,... | collective-permute-start | bytes 1572872 | tf_op jit(solution)/shard_map/ppermute | solution.py:524
  8.6 17.2 %collective-permute-start.5 = (f32[576,256]{1,0:T(8,128)S(1)}, f32[576,256]{1,0:T(8,128)S(1)}, u32[]{:S(2)}, u32[]{:S(2)}) collective-permute-start(f32[576,256]{1,0:T(8,128)S(1)} %get-tuple-element.52.field.message), channel_id=1, source_target_pairs={{0,4},{8,12},{16,20},{24,28},{4,0},{12,8},{20,16},{28,24},{1,5},{9... | collective-permute-start | bytes 1769480 | tf_op jit(solution)/shard_map/ppermute | solution.py:519
  21.3 4.5 %collective-permute-start.4 = (f32[256,512]{1,0:T(8,128)S(1)}, f32[256,512]{1,0:T(8,128)S(1)}, u32[]{:S(2)}, u32[]{:S(2)}) collective-permute-start(f32[256,512]{1,0:T(8,128)S(1)} %collective-permute-done.1.received), channel_id=1, source_target_pairs={{0,1},{1,0},{2,3},{3,2},{4,5},{5,4},{6,7},{7,6},{8,9},{9,8},{10,11... | collective-permute-start | bytes 1572872 | tf_op jit(solution)/shard_map/ppermute | solution.py:524
  21.3 18.0 %collective-permute-start.3 = (f32[512,128]{1,0:T(8,128)S(1)}, f32[512,128]{1,0:T(8,128)S(1)}, u32[]{:S(2)}, u32[]{:S(2)}) collective-permute-start(f32[512,128]{1,0:T(8,128)S(1)} %get-tuple-element.58.own), channel_id=1, source_target_pairs={{0,2},{1,3},{2,0},{3,1},{4,6},{5,7},{6,4},{7,5},{8,10},{9,11},{10,... | collective-permute-start | bytes 786440 | tf_op jit(solution)/shard_map/ppermute | solution.py:524
  26.8 6.1 %collective-permute-start.9 = (f32[256,128]{1,0:T(8,128)S(1)}, f32[256,128]{1,0:T(8,128)S(1)}, u32[]{:S(2)}, u32[]{:S(2)}) collective-permute-start(f32[256,128]{1,0:T(8,128)S(1)} %get-tuple-element.75), channel_id=1, source_target_pairs={{0,2},{1,3},{2,0},{3,1},{4,6},{5,7},{6,4},{7,5},{8,10},{9,11},{10,... | collective-permute-start | bytes 393224 | tf_op jit(solution)/shard_map/ppermute | solution.py:524
  28.3 1.3 %collective-permute-start.6 = (f32[64,256]{1,0:T(8,128)S(1)}, f32[64,256]{1,0:T(8,128)S(1)}, u32[]{:S(2)}, u32[]{:S(2)}) collective-permute-start(f32[64,256]{1,0:T(8,128)S(1)} %slice.4.mine), channel_id=1, source_target_pairs={{0,1},{1,0},{2,3},{3,2},{4,5},{5,4},{6,7},{7,6},{8,9},{9,8},{10,11... | collective-permute-start | bytes 196616 | tf_op jit(solution)/shard_map/ppermute | solution.py:524
  30.8 14.9 %copy-start.1 = (f32[8,64,64]{2,1,0:T(8,128)S(1)}, f32[8,64,64]{2,1,0:T(8,128)}, u32[]{:S(2)}) copy-start(f32[8,64,64]{2,1,0:T(8,128)} %smoother.3) | copy-start | bytes 393220
  30.9 6.4 %collective-permute-start.7 = (f32[256,128]{1,0:T(8,128)S(1)}, f32[256,128]{1,0:T(8,128)S(1)}, u32[]{:S(2)}, u32[]{:S(2)}) collective-permute-start(f32[256,128]{1,0:T(8,128)S(1)} %get-tuple-element.66.upper), channel_id=1, source_target_pairs={{0,2},{1,3},{2,0},{3,1},{4,6},{5,7},{6,4},{7,5},{8,10},{9,11},{10,... | collective-permute-start | bytes 393224 | tf_op jit(solution)/shard_map/ppermute | solution.py:524
  31.5 7.8 %collective-permute-start.8 = (f32[256,128]{1,0:T(8,128)S(1)}, f32[256,128]{1,0:T(8,128)S(1)}, u32[]{:S(2)}, u32[]{:S(2)}) collective-permute-start(f32[256,128]{1,0:T(8,128)S(1)} %get-tuple-element.67.lower), channel_id=1, source_target_pairs={{0,2},{1,3},{2,0},{3,1},{4,6},{5,7},{6,4},{7,5},{8,10},{9,11},{10,... | collective-permute-start | bytes 393224 | tf_op jit(solution)/shard_map/ppermute | solution.py:524
  33.0 7.6 %collective-permute-start.10 = (f32[256,128]{1,0:T(8,128)S(1)}, f32[256,128]{1,0:T(8,128)S(1)}, u32[]{:S(2)}, u32[]{:S(2)}) collective-permute-start(f32[256,128]{1,0:T(8,128)S(1)} %first_correction.1.refs_5_.refs_8_.refs_4_), channel_id=1, source_target_pairs={{0,4},{8,12},{16,20},{24,28},{4,0},{12,8},{20,16},{28,24},{1,5},{9... | collective-permute-start | bytes 393224 | tf_op jit(solution)/shard_map/ppermute | solution.py:509
  34.6 7.7 %collective-permute-start.11 = (f32[256,128]{1,0:T(8,128)S(1)}, f32[256,128]{1,0:T(8,128)S(1)}, u32[]{:S(2)}, u32[]{:S(2)}) collective-permute-start(f32[256,128]{1,0:T(8,128)S(1)} %first_correction.1.refs_5_.refs_8_.refs_4_), channel_id=1, source_target_pairs={{4,8},{12,16},{20,24},{8,4},{16,12},{24,20},{5,9},{13,17},{21,25},... | collective-permute-start | bytes 393224 | tf_op jit(solution)/shard_map/ppermute | solution.py:510
  39.9 2.4 %collective-permute-start.12 = (f32[256,128]{1,0:T(8,128)S(1)}, f32[256,128]{1,0:T(8,128)S(1)}, u32[]{:S(2)}, u32[]{:S(2)}) collective-permute-start(f32[256,128]{1,0:T(8,128)S(1)} %get-tuple-element.71.refs_0_), channel_id=1, source_target_pairs={{0,1},{1,0},{2,3},{3,2},{4,5},{5,4},{6,7},{7,6},{8,9},{9,8},{10,11... | collective-permute-start | bytes 393224 | tf_op jit(solution)/shard_map/ppermute | solution.py:524
  40.0 2.4 %collective-permute-start.13 = (f32[256,128]{1,0:T(8,128)S(1)}, f32[256,128]{1,0:T(8,128)S(1)}, u32[]{:S(2)}, u32[]{:S(2)}) collective-permute-start(f32[256,128]{1,0:T(8,128)S(1)} %get-tuple-element.72.refs_1_), channel_id=1, source_target_pairs={{0,1},{1,0},{2,3},{3,2},{4,5},{5,4},{6,7},{7,6},{8,9},{9,8},{10,11... | collective-permute-start | bytes 393224 | tf_op jit(solution)/shard_map/ppermute | solution.py:524
  40.5 1.9 %collective-permute-start.14 = (f32[256,128]{1,0:T(8,128)S(1)}, f32[256,128]{1,0:T(8,128)S(1)}, u32[]{:S(2)}, u32[]{:S(2)}) collective-permute-start(f32[256,128]{1,0:T(8,128)S(1)} %get-tuple-element.73.refs_2_), channel_id=1, source_target_pairs={{0,1},{1,0},{2,3},{3,2},{4,5},{5,4},{6,7},{7,6},{8,9},{9,8},{10,11... | collective-permute-start | bytes 393224 | tf_op jit(solution)/shard_map/ppermute | solution.py:524
  40.5 8.7 %collective-permute-start.17 = (f32[512,128]{1,0:T(8,128)S(1)}, f32[512,128]{1,0:T(8,128)S(1)}, u32[]{:S(2)}, u32[]{:S(2)}) collective-permute-start(f32[512,128]{1,0:T(8,128)S(1)} %get-tuple-element.86), channel_id=1, source_target_pairs={{0,2},{1,3},{2,0},{3,1},{4,6},{5,7},{6,4},{7,5},{8,10},{9,11},{10,... | collective-permute-start | bytes 786440 | tf_op jit(solution)/shard_map/ppermute | solution.py:524
  42.7 6.7 %collective-permute-start.15 = (f32[256,128]{1,0:T(8,128)S(1)}, f32[256,128]{1,0:T(8,128)S(1)}, u32[]{:S(2)}, u32[]{:S(2)}) collective-permute-start(f32[256,128]{1,0:T(8,128)S(1)} %sweep.2.refs_7_), channel_id=1, source_target_pairs={{0,4},{8,12},{16,20},{24,28},{4,0},{12,8},{20,16},{28,24},{1,5},{9... | collective-permute-start | bytes 393224 | tf_op jit(solution)/shard_map/ppermute | solution.py:509
  43.8 8.1 %collective-permute-start.16 = (f32[256,128]{1,0:T(8,128)S(1)}, f32[256,128]{1,0:T(8,128)S(1)}, u32[]{:S(2)}, u32[]{:S(2)}) collective-permute-start(f32[256,128]{1,0:T(8,128)S(1)} %sweep.2.refs_7_), channel_id=1, source_target_pairs={{4,8},{12,16},{20,24},{8,4},{16,12},{24,20},{5,9},{13,17},{21,25},... | collective-permute-start | bytes 393224 | tf_op jit(solution)/shard_map/ppermute | solution.py:510
  51.9 3.1 %collective-permute-start.18 = (f32[512,384]{1,0:T(8,128)S(1)}, f32[512,384]{1,0:T(8,128)S(1)}, u32[]{:S(2)}, u32[]{:S(2)}) collective-permute-start(f32[512,384]{1,0:T(8,128)S(1)} %lift_half.1.mine), channel_id=1, source_target_pairs={{0,1},{1,0},{2,3},{3,2},{4,5},{5,4},{6,7},{7,6},{8,9},{9,8},{10,11... | collective-permute-start | bytes 2359304 | tf_op jit(solution)/shard_map/ppermute | solution.py:524
  52.3 6.0 %collective-permute-start.19 = (f32[256,128]{1,0:T(8,128)S(1)}, f32[256,128]{1,0:T(8,128)S(1)}, u32[]{:S(2)}, u32[]{:S(2)}) collective-permute-start(f32[256,128]{1,0:T(8,128)S(1)} %sweep.3.own), channel_id=1, source_target_pairs={{0,4},{8,12},{16,20},{24,28},{4,0},{12,8},{20,16},{28,24},{1,5},{9... | collective-permute-start | bytes 393224 | tf_op jit(solution)/shard_map/ppermute | solution.py:509
  53.1 8.4 %collective-permute-start.20 = (f32[256,128]{1,0:T(8,128)S(1)}, f32[256,128]{1,0:T(8,128)S(1)}, u32[]{:S(2)}, u32[]{:S(2)}) collective-permute-start(f32[256,128]{1,0:T(8,128)S(1)} %sweep.3.own), channel_id=1, source_target_pairs={{4,8},{12,16},{20,24},{8,4},{16,12},{24,20},{5,9},{13,17},{21,25},... | collective-permute-start | bytes 393224 | tf_op jit(solution)/shard_map/ppermute | solution.py:510

commit v10 on v9

--- a/solution.py
+++ b/solution.py
@@ -483,17 +483,25 @@
     )(mine, other, base, own)
 
 
-def last_kernel(w_high, w_low, base, near, far, out_ref):
+def last_kernel(w_high, w_low, base, near, far, out_hbm, out, sems):
     field = jnp.concatenate(list(core_parts(near, far)), axis=0)
-    out_ref[...] = base[...] + narrow_product((w_high[...], w_low[...]), field)
+    copies = []
+    for group in range(2):
+        part = span(group, WIDE // 2)
+        out[part, :] = base[part, :] + narrow_product((w_high[part, :], w_low[part, :]), field)
+        copies.append(pltpu.make_async_copy(out.at[part], out_hbm.at[part], sems.at[group]))
+        copies[-1].start()
+    for copy in copies:
+        copy.wait()
 
 
 def last_step(w_high, w_low, base, near, far):
     return pl.pallas_call(
         last_kernel,
         in_specs=[VMEM] * 5,
-        out_specs=VMEM,
+        out_specs=HBM,
         out_shape=shape(WIDE, COLS),
+        scratch_shapes=[pltpu.VMEM((WIDE, COLS), F32), pltpu.SemaphoreType.DMA((2,))],
         compiler_params=params(),
         name="last_step",
     )(w_high, w_low, base, near, far)

time: 62.8 us -> 62.8 us (level)
  no operation moved by 1% of the time
where the time goes in v10:
time: 62.8 us; the launch traced here: 62.6 us
  waiting for transfers between devices  26.8 us (43%)
  starting transfers between devices  20.7 us (33%)
  Pallas kernels  14.2 us (23%)
  between operations  0.85 us (1%)
    ppermute x14, waiting for transfers between devices, swapped(): return lax.ppermute(value, 'sub', [(i, i ^ bit) for i in range(size)])  14.4 us
    ppermute x14, starting transfers between devices, swapped(): return lax.ppermute(value, 'sub', [(i, i ^ bit) for i in range(size)])  8.16 us
    ppermute x3, waiting for transfers between devices, from_neighbours(): far = lax.ppermute(value, 'slab', swaps(size, 1))  6.76 us
    ppermute x3, starting transfers between devices, from_neighbours(): far = lax.ppermute(value, 'slab', swaps(size, 1))  5.73 us
    pallas_call x1, Pallas kernels, start_step(): pl.pallas_call(start_kernel, in_specs=[HBM] * 7, out_specs=[VMEM] * 5, ou...  4.15 us
    ppermute x3, starting transfers between devices, from_neighbours(): near = lax.ppermute(value, 'slab', swaps(size, 0))  3.4 us
    ppermute x1, starting transfers between devices, from_side(): return lax.ppermute(value, ('slab', 'sub'), pairs)  3.37 us
    ppermute x1, waiting for transfers between devices, from_side(): return lax.ppermute(value, ('slab', 'sub'), pairs)  3 us
  transfers between devices with their start and end apart: 21, of which 11 were waited for; matrix products, arithmetic and copies ran while one was open for 0% of the time, Pallas kernels for 14%

profile of v10, /device:TPU:8, one launch (start us, length us, event | category | flops | bytes accessed | tf_op | source)
XLA Modules:
  0.0 62.6 jit_solution(17803340492172877863)
XLA Ops:
  0.6 0.0 copy-start
  0.6 0.0 copy-start.2
  0.7 4.2 %start_step.1 = (f32[512,1024]{1,0:T(8,128)S(1)}, f32[256,512]{1,0:T(8,128)S(1)}, f32[256,512]{1,0:T(8,128)S(1)}, f32[576,256]{1,0:T(8,128)S(1)}, f32[512,128]{1,0:T(8,128)S(1)}) custom-call(s32[8,16]{1,0:T(8,128)} %col_hbm.1, s32[8,4,2,8]{3,2,1,0:T(2,128)} %rows_hbm.1, s32[4,2,8]{2,1,0:T(2,128)} %bitcast.3, f32[8,16,64,64]{3,2,1,0:T(8,128)} %blocks_hbm.1, ...), custom_call_target="tpu_custom_call" | custom-call | tf_op jit(solution)/shard_map/start_step/pallas_call | solution.py:156
  4.8 0.1 collective-permute-start
  4.9 1.9 %collective-permute-done = f32[256,512]{1,0:T(8,128)S(1)} collective-permute-done((f32[256,512]{1,0:T(8,128)S(1)}, f32[256,512]{1,0:T(8,128)S(1)}, u32[]{:S(2)}, u32[]{:S(2)}) %collective-permute-start) | collective-permute-done | bytes 524320 | tf_op jit(solution)/shard_map/ppermute | solution.py:532
  6.8 0.1 collective-permute-start.2
  6.9 0.1 add.3
  7.0 1.6 %collective-permute-start.1 = (f32[256,512]{1,0:T(8,128)S(1)}, f32[256,512]{1,0:T(8,128)S(1)}, u32[]{:S(2)}, u32[]{:S(2)}) collective-permute-start(f32[256,512]{1,0:T(8,128)S(1)} %add.3), channel_id=1, source_target_pairs={{0,2},{1,3},{2,0},{3,1},{4,6},{5,7},{6,4},{7,5},{8,10},{9,11},{10,... | collective-permute-start | bytes 1572872 | tf_op jit(solution)/shard_map/ppermute | solution.py:532
  8.6 3.4 %collective-permute-start.5 = (f32[576,256]{1,0:T(8,128)S(1)}, f32[576,256]{1,0:T(8,128)S(1)}, u32[]{:S(2)}, u32[]{:S(2)}) collective-permute-start(f32[576,256]{1,0:T(8,128)S(1)} %get-tuple-element.52.field.message), channel_id=1, source_target_pairs={{0,4},{8,12},{16,20},{24,28},{4,0},{12,8},{20,16},{28,24},{1,5},{9... | collective-permute-start | bytes 1769480 | tf_op jit(solution)/shard_map/ppermute | solution.py:527
  12.0 0.0 collective-permute-done.2.pair_other
  12.0 0.0 copy-done
  12.0 0.0 copy-done.2
  12.0 2.3 %own_step.1 = (f32[512,512]{1,0:T(8,128)S(1)}, f32[512,128]{1,0:T(8,128)S(1)}, f32[512,256]{1,0:T(8,128)S(1)}, f32[256,128]{1,0:T(8,128)S(1)}, bf16[256,512]{1,0...) custom-call(s32[64]{0:T(128)S(1)} %copy-done.2, f32[8,64,64]{2,1,0:T(8,128)S(1)} %copy-done, ...), custom_call_target="tpu_custom_call" | custom-call | tf_op jit(solution)/shard_map/own_step/pallas_call | solution.py:230
  14.3 7.0 %collective-permute-done.1.received = f32[256,512]{1,0:T(8,128)S(1)} collective-permute-done((f32[256,512]{1,0:T(8,128)S(1)}, f32[256,512]{1,0:T(8,128)S(1)}, u32[]{:S(2)}, u32[]{:S(2)}) %collective-permute-start.1) | collective-permute-done | bytes 524320 | tf_op jit(solution)/shard_map/ppermute | solution.py:532
  21.3 0.0 collective-permute-start.4
  21.3 1.5 %collective-permute-start.3 = (f32[512,128]{1,0:T(8,128)S(1)}, f32[512,128]{1,0:T(8,128)S(1)}, u32[]{:S(2)}, u32[]{:S(2)}) collective-permute-start(f32[512,128]{1,0:T(8,128)S(1)} %get-tuple-element.58.own), channel_id=1, source_target_pairs={{0,2},{1,3},{2,0},{3,1},{4,6},{5,7},{6,4},{7,5},{8,10},{9,11},{10,... | collective-permute-start | bytes 786440 | tf_op jit(solution)/shard_map/ppermute | solution.py:532
  22.8 3.0 %collective-permute-done.5.message = f32[576,256]{1,0:T(8,128)S(1)} collective-permute-done((f32[576,256]{1,0:T(8,128)S(1)}, f32[576,256]{1,0:T(8,128)S(1)}, u32[]{:S(2)}, u32[]{:S(2)}) %collective-permute-start.5) | collective-permute-done | bytes 589856 | tf_op jit(solution)/shard_map/ppermute | solution.py:527
  25.8 0.0 collective-permute-done.4.received_other
  25.8 1.0 %image.1 = (f32[512,128]{1,0:T(8,128)S(1)}, f32[512,128]{1,0:T(8,128)S(1)}, f32[256,128]{1,0:T(8,128)S(1)}, f32[256,128]{1,0:T(8,128)S(1)}, bf16[512,512]{1,0:T(8,128)(2,1)S(1)}, /*index=5*/bf16[512,512]{1,0:T(8,128)(2,1)S(1)}) custom-call(f32[512,256]{1,0:T(8,128)S(1)} %get-tuple-element.59.own_image, f32[512,512]{1,0:T(8,128)S(1)} %get-tuple-element.60.side, ...), custom_call_target="tpu_custom_call" | custom-call | tf_op jit(solution)/shard_map/image/pallas_call | solution.py:273
  26.8 1.5 %collective-permute-start.9 = (f32[256,128]{1,0:T(8,128)S(1)}, f32[256,128]{1,0:T(8,128)S(1)}, u32[]{:S(2)}, u32[]{:S(2)}) collective-permute-start(f32[256,128]{1,0:T(8,128)S(1)} %get-tuple-element.75), channel_id=1, source_target_pairs={{0,2},{1,3},{2,0},{3,1},{4,6},{5,7},{6,4},{7,5},{8,10},{9,11},{10,... | collective-permute-start | bytes 393224 | tf_op jit(solution)/shard_map/ppermute | solution.py:532
  28.3 0.0 collective-permute-start.6
  28.3 1.2 %collective-permute-done.6.other = f32[64,256]{1,0:T(8,128)S(1)} collective-permute-done((f32[64,256]{1,0:T(8,128)S(1)}, f32[64,256]{1,0:T(8,128)S(1)}, u32[]{:S(2)}, u32[]{:S(2)}) %collective-permute-start.6) | collective-permute-done | bytes 65568 | tf_op jit(solution)/shard_map/ppermute | solution.py:532
  29.6 1.3 %ghost_step.1 = (f32[256,128]{1,0:T(8,128)S(1)}, f32[256,128]{1,0:T(8,128)S(1)}) custom-call(s32[64]{0:T(128)S(1)} %copy-done.2, bf16[512,512]{1,0:T(8,128)(2,1)S(1)} %get-tuple-element.64.d_high, bf16[512,512]{1,0:T(8,128)(2,1)S(1)} %get-tuple-element.65.d_low, f32[64,256]{1,0:T(8,128)S(1)} %slice.4.mine, f32[64,256]{1,0:T(8,128)S(1)} %collective-permute-done.6.other), custom_call_target="tpu_custom_call" | custom-call | tf_op jit(solution)/shard_map/ghost_step/pallas_call | solution.py:300
  30.9 0.0 copy-start.1
  30.9 0.7 %collective-permute-start.7 = (f32[256,128]{1,0:T(8,128)S(1)}, f32[256,128]{1,0:T(8,128)S(1)}, u32[]{:S(2)}, u32[]{:S(2)}) collective-permute-start(f32[256,128]{1,0:T(8,128)S(1)} %get-tuple-element.66.upper), channel_id=1, source_target_pairs={{0,2},{1,3},{2,0},{3,1},{4,6},{5,7},{6,4},{7,5},{8,10},{9,11},{10,... | collective-permute-start | bytes 393224 | tf_op jit(solution)/shard_map/ppermute | solution.py:532
  31.5 1.4 %collective-permute-start.8 = (f32[256,128]{1,0:T(8,128)S(1)}, f32[256,128]{1,0:T(8,128)S(1)}, u32[]{:S(2)}, u32[]{:S(2)}) collective-permute-start(f32[256,128]{1,0:T(8,128)S(1)} %get-tuple-element.67.lower), channel_id=1, source_target_pairs={{0,2},{1,3},{2,0},{3,1},{4,6},{5,7},{6,4},{7,5},{8,10},{9,11},{10,... | collective-permute-start | bytes 393224 | tf_op jit(solution)/shard_map/ppermute | solution.py:532
  33.0 0.0 collective-permute-done.9.received
  33.0 1.6 %collective-permute-start.10 = (f32[256,128]{1,0:T(8,128)S(1)}, f32[256,128]{1,0:T(8,128)S(1)}, u32[]{:S(2)}, u32[]{:S(2)}) collective-permute-start(f32[256,128]{1,0:T(8,128)S(1)} %first_correction.1.refs_5_.refs_8_.refs_4_), channel_id=1, source_target_pairs={{0,4},{8,12},{16,20},{24,28},{4,0},{12,8},{20,16},{28,24},{1,5},{9... | collective-permute-start | bytes 393224 | tf_op jit(solution)/shard_map/ppermute | solution.py:517
  34.6 1.9 %collective-permute-start.11 = (f32[256,128]{1,0:T(8,128)S(1)}, f32[256,128]{1,0:T(8,128)S(1)}, u32[]{:S(2)}, u32[]{:S(2)}) collective-permute-start(f32[256,128]{1,0:T(8,128)S(1)} %first_correction.1.refs_5_.refs_8_.refs_4_), channel_id=1, source_target_pairs={{4,8},{12,16},{20,24},{8,4},{16,12},{24,20},{5,9},{13,17},{21,25},... | collective-permute-start | bytes 393224 | tf_op jit(solution)/shard_map/ppermute | solution.py:518
  36.5 0.8 %collective-permute-done.7.upper_received = f32[256,128]{1,0:T(8,128)S(1)} collective-permute-done((f32[256,128]{1,0:T(8,128)S(1)}, f32[256,128]{1,0:T(8,128)S(1)}, u32[]{:S(2)}, u32[]{:S(2)}) %collective-permute-start.7) | collective-permute-done | bytes 131104 | tf_op jit(solution)/shard_map/ppermute | solution.py:532
  37.3 2.0 %collective-permute-done.8.lower_received = f32[256,128]{1,0:T(8,128)S(1)} collective-permute-done((f32[256,128]{1,0:T(8,128)S(1)}, f32[256,128]{1,0:T(8,128)S(1)}, u32[]{:S(2)}, u32[]{:S(2)}) %collective-permute-start.8) | collective-permute-done | bytes 131104 | tf_op jit(solution)/shard_map/ppermute | solution.py:532
  39.3 0.0 collective-permute-done.3.own_received
  39.3 0.6 coarse_half.1
  39.9 0.1 collective-permute-start.12
  40.0 0.5 collective-permute-start.13
  40.5 0.1 collective-permute-start.14
  40.5 0.0 collective-permute-done.10.refs_7_
  40.6 0.6 %collective-permute-start.17 = (f32[512,128]{1,0:T(8,128)S(1)}, f32[512,128]{1,0:T(8,128)S(1)}, u32[]{:S(2)}, u32[]{:S(2)}) collective-permute-start(f32[512,128]{1,0:T(8,128)S(1)} %get-tuple-element.86), channel_id=1, source_target_pairs={{0,2},{1,3},{2,0},{3,1},{4,6},{5,7},{6,4},{7,5},{8,10},{9,11},{10,... | collective-permute-start | bytes 786440 | tf_op jit(solution)/shard_map/ppermute | solution.py:532
  41.2 1.1 %collective-permute-done.11.refs_9_ = f32[256,128]{1,0:T(8,128)S(1)} collective-permute-done((f32[256,128]{1,0:T(8,128)S(1)}, f32[256,128]{1,0:T(8,128)S(1)}, u32[]{:S(2)}, u32[]{:S(2)}) %collective-permute-start.11) | collective-permute-done | bytes 131104 | tf_op jit(solution)/shard_map/ppermute | solution.py:518
  42.3 0.0 collective-permute-done.12.refs_3_.refs_2_
  42.3 0.0 collective-permute-done.13.refs_4_.refs_3_
  42.3 0.0 collective-permute-done.14.refs_5_.refs_4_
  42.3 0.4 sweep.2.refs_7_
  42.8 1.1 %collective-permute-start.15 = (f32[256,128]{1,0:T(8,128)S(1)}, f32[256,128]{1,0:T(8,128)S(1)}, u32[]{:S(2)}, u32[]{:S(2)}) collective-permute-start(f32[256,128]{1,0:T(8,128)S(1)} %sweep.2.refs_7_), channel_id=1, source_target_pairs={{0,4},{8,12},{16,20},{24,28},{4,0},{12,8},{20,16},{28,24},{1,5},{9... | collective-permute-start | bytes 393224 | tf_op jit(solution)/shard_map/ppermute | solution.py:517
  43.8 1.9 %collective-permute-start.16 = (f32[256,128]{1,0:T(8,128)S(1)}, f32[256,128]{1,0:T(8,128)S(1)}, u32[]{:S(2)}, u32[]{:S(2)}) collective-permute-start(f32[256,128]{1,0:T(8,128)S(1)} %sweep.2.refs_7_), channel_id=1, source_target_pairs={{4,8},{12,16},{20,24},{8,4},{16,12},{24,20},{5,9},{13,17},{21,25},... | collective-permute-start | bytes 393224 | tf_op jit(solution)/shard_map/ppermute | solution.py:518
  45.7 0.0 copy-done.1
  45.7 1.0 %lift_half.1.mine = f32[512,384]{1,0:T(8,128)S(1)} custom-call(s32[64]{0:T(128)S(1)} %copy-done.2, f32[512,128]{1,0:T(8,128)S(1)} %get-tuple-element.58.own, f32[512,128]{1,0:T(8,128)S(1)} %collective-permute-done.3.own_received, f32[256,128]{1,0:T(8,128)S(1)} %get-tuple-element.66.upper, f32[256,128]{1,0:T(8,128)S(1)} %get-tuple-element.67.lower, ...), custom_call_target="tpu_custom_call" | custom-call | tf_op jit(solution)/shard_map/lift_half/pallas_call | solution.py:391
  46.8 1.0 %coarse_share.1 = (f32[4,3,64,64]{3,2,1,0:T(8,128)}, bf16[256,384]{1,0:T(8,128)(2,1)S(1)}, bf16[256,384]{1,0:T(8,128)(2,1)S(1)}) custom-call(f32[256,128]{1,0:T(8,128)S(1)} %get-tuple-element.71.refs_0_, f32[256,128]{1,0:T(8,128)S(1)} %get-tuple-element.72.refs_1_, f32[256,128]{1,0:T(8,128)S(1)} %get-tuple-element.73.refs_2_, ...), custom_call_target="tpu_custom_call" | custom-call | tf_op jit(solution)/shard_map/coarse_share/pallas_call | solution.py:367
  47.8 1.5 %collective-permute-done.17.received = f32[512,128]{1,0:T(8,128)S(1)} collective-permute-done((f32[512,128]{1,0:T(8,128)S(1)}, f32[512,128]{1,0:T(8,128)S(1)}, u32[]{:S(2)}, u32[]{:S(2)}) %collective-permute-start.17) | collective-permute-done | bytes 262176 | tf_op jit(solution)/shard_map/ppermute | solution.py:532
  49.2 0.3 base_step.1.base
  49.5 0.0 collective-permute-done.15.refs_6_
  49.5 2.4 %collective-permute-done.16.refs_8_ = f32[256,128]{1,0:T(8,128)S(1)} collective-permute-done((f32[256,128]{1,0:T(8,128)S(1)}, f32[256,128]{1,0:T(8,128)S(1)}, u32[]{:S(2)}, u32[]{:S(2)}) %collective-permute-start.16) | collective-permute-done | bytes 131104 | tf_op jit(solution)/shard_map/ppermute | solution.py:518
  51.9 0.0 collective-permute-start.18
  51.9 0.4 sweep.3.own
  52.3 0.8 %collective-permute-start.19 = (f32[256,128]{1,0:T(8,128)S(1)}, f32[256,128]{1,0:T(8,128)S(1)}, u32[]{:S(2)}, u32[]{:S(2)}) collective-permute-start(f32[256,128]{1,0:T(8,128)S(1)} %sweep.3.own), channel_id=1, source_target_pairs={{0,4},{8,12},{16,20},{24,28},{4,0},{12,8},{20,16},{28,24},{1,5},{9... | collective-permute-start | bytes 393224 | tf_op jit(solution)/shard_map/ppermute | solution.py:517
  53.1 1.9 %collective-permute-start.20 = (f32[256,128]{1,0:T(8,128)S(1)}, f32[256,128]{1,0:T(8,128)S(1)}, u32[]{:S(2)}, u32[]{:S(2)}) collective-permute-start(f32[256,128]{1,0:T(8,128)S(1)} %sweep.3.own), channel_id=1, source_target_pairs={{4,8},{12,16},{20,24},{8,4},{16,12},{24,20},{5,9},{13,17},{21,25},... | collective-permute-start | bytes 393224 | tf_op jit(solution)/shard_map/ppermute | solution.py:518
  55.0 0.0 collective-permute-done.18.other
  55.0 0.6 lifted.1
  55.6 2.7 %collective-permute-done.19.near = f32[256,128]{1,0:T(8,128)S(1)} collective-permute-done((f32[256,128]{1,0:T(8,128)S(1)}, f32[256,128]{1,0:T(8,128)S(1)}, u32[]{:S(2)}, u32[]{:S(2)}) %collective-permute-start.19) | collective-permute-done | bytes 131104 | tf_op jit(solution)/shard_map/ppermute | solution.py:517
  58.3 3.2 %collective-permute-done.20.far = f32[256,128]{1,0:T(8,128)S(1)} collective-permute-done((f32[256,128]{1,0:T(8,128)S(1)}, f32[256,128]{1,0:T(8,128)S(1)}, u32[]{:S(2)}, u32[]{:S(2)}) %collective-permute-start.20) | collective-permute-done | bytes 131104 | tf_op jit(solution)/shard_map/ppermute | solution.py:518
  61.5 1.1 %last_step.1 = f32[512,128]{1,0:T(8,128)} custom-call(bf16[512,512]{1,0:T(8,128)(2,1)S(1)} %get-tuple-element.95.w_high, bf16[512,512]{1,0:T(8,128)(2,1)S(1)} %get-tuple-element.96.w_low, f32[512,128]{1,0:T(8,128)S(1)} %get-tuple-element.97.base, f32[256,128]{1,0:T(8,128)S(1)} %collective-permute-done.19.near, f32[256,128]{1,0:T(8,128)S(1)} %collective-permute-done.20.far), custom_call_target="tpu_custom_call" | custom-call | tf_op jit(solution)/shard_map/last_step/pallas_call | solution.py:499
  (2 shorter events, 0.0 us)
Async XLA Ops:
  0.6 11.4 %copy-start = (f32[8,64,64]{2,1,0:T(8,128)S(1)}, f32[8,64,64]{2,1,0:T(8,128)}, u32[]{:S(2)}) copy-start(f32[8,64,64]{2,1,0:T(8,128)} %prolong.3) | copy-start | bytes 393220
  0.6 11.4 %copy-start.2 = (s32[64]{0:T(128)S(1)}, s32[64]{0:T(128)}, u32[]{:S(2)}) copy-start(s32[64]{0:T(128)} %agg_of.5) | copy-start | bytes 772
  4.8 2.0 %collective-permute-start = (f32[256,512]{1,0:T(8,128)S(1)}, f32[256,512]{1,0:T(8,128)S(1)}, u32[]{:S(2)}, u32[]{:S(2)}) collective-permute-start(f32[256,512]{1,0:T(8,128)S(1)} %get-tuple-element.51), channel_id=1, source_target_pairs={{0,1},{1,0},{2,3},{3,2},{4,5},{5,4},{6,7},{7,6},{8,9},{9,8},{10,11... | collective-permute-start | bytes 1572872 | tf_op jit(solution)/shard_map/ppermute | solution.py:532
  6.8 5.2 %collective-permute-start.2 = (f32[512,1024]{1,0:T(8,128)S(1)}, f32[512,1024]{1,0:T(8,128)S(1)}, u32[]{:S(2)}, u32[]{:S(2)}) collective-permute-start(f32[512,1024]{1,0:T(8,128)S(1)} %get-tuple-element.55.pair), channel_id=1, source_target_pairs={{0,1},{1,0},{2,3},{3,2},{4,5},{5,4},{6,7},{7,6},{8,9},{9,8},{10,11... | collective-permute-start | bytes 6291464 | tf_op jit(solution)/shard_map/ppermute | solution.py:532
  7.0 14.3 %collective-permute-start.1 = (f32[256,512]{1,0:T(8,128)S(1)}, f32[256,512]{1,0:T(8,128)S(1)}, u32[]{:S(2)}, u32[]{:S(2)}) collective-permute-start(f32[256,512]{1,0:T(8,128)S(1)} %add.3), channel_id=1, source_target_pairs={{0,2},{1,3},{2,0},{3,1},{4,6},{5,7},{6,4},{7,5},{8,10},{9,11},{10,... | collective-permute-start | bytes 1572872 | tf_op jit(solution)/shard_map/ppermute | solution.py:532
  8.6 17.2 %collective-permute-start.5 = (f32[576,256]{1,0:T(8,128)S(1)}, f32[576,256]{1,0:T(8,128)S(1)}, u32[]{:S(2)}, u32[]{:S(2)}) collective-permute-start(f32[576,256]{1,0:T(8,128)S(1)} %get-tuple-element.52.field.message), channel_id=1, source_target_pairs={{0,4},{8,12},{16,20},{24,28},{4,0},{12,8},{20,16},{28,24},{1,5},{9... | collective-permute-start | bytes 1769480 | tf_op jit(solution)/shard_map/ppermute | solution.py:527
  21.3 4.5 %collective-permute-start.4 = (f32[256,512]{1,0:T(8,128)S(1)}, f32[256,512]{1,0:T(8,128)S(1)}, u32[]{:S(2)}, u32[]{:S(2)}) collective-permute-start(f32[256,512]{1,0:T(8,128)S(1)} %collective-permute-done.1.received), channel_id=1, source_target_pairs={{0,1},{1,0},{2,3},{3,2},{4,5},{5,4},{6,7},{7,6},{8,9},{9,8},{10,11... | collective-permute-start | bytes 1572872 | tf_op jit(solution)/shard_map/ppermute | solution.py:532
  21.3 18.0 %collective-permute-start.3 = (f32[512,128]{1,0:T(8,128)S(1)}, f32[512,128]{1,0:T(8,128)S(1)}, u32[]{:S(2)}, u32[]{:S(2)}) collective-permute-start(f32[512,128]{1,0:T(8,128)S(1)} %get-tuple-element.58.own), channel_id=1, source_target_pairs={{0,2},{1,3},{2,0},{3,1},{4,6},{5,7},{6,4},{7,5},{8,10},{9,11},{10,... | collective-permute-start | bytes 786440 | tf_op jit(solution)/shard_map/ppermute | solution.py:532
  26.8 6.1 %collective-permute-start.9 = (f32[256,128]{1,0:T(8,128)S(1)}, f32[256,128]{1,0:T(8,128)S(1)}, u32[]{:S(2)}, u32[]{:S(2)}) collective-permute-start(f32[256,128]{1,0:T(8,128)S(1)} %get-tuple-element.75), channel_id=1, source_target_pairs={{0,2},{1,3},{2,0},{3,1},{4,6},{5,7},{6,4},{7,5},{8,10},{9,11},{10,... | collective-permute-start | bytes 393224 | tf_op jit(solution)/shard_map/ppermute | solution.py:532
  28.3 1.3 %collective-permute-start.6 = (f32[64,256]{1,0:T(8,128)S(1)}, f32[64,256]{1,0:T(8,128)S(1)}, u32[]{:S(2)}, u32[]{:S(2)}) collective-permute-start(f32[64,256]{1,0:T(8,128)S(1)} %slice.4.mine), channel_id=1, source_target_pairs={{0,1},{1,0},{2,3},{3,2},{4,5},{5,4},{6,7},{7,6},{8,9},{9,8},{10,11... | collective-permute-start | bytes 196616 | tf_op jit(solution)/shard_map/ppermute | solution.py:532
  30.9 14.9 %copy-start.1 = (f32[8,64,64]{2,1,0:T(8,128)S(1)}, f32[8,64,64]{2,1,0:T(8,128)}, u32[]{:S(2)}) copy-start(f32[8,64,64]{2,1,0:T(8,128)} %smoother.3) | copy-start | bytes 393220
  30.9 6.4 %collective-permute-start.7 = (f32[256,128]{1,0:T(8,128)S(1)}, f32[256,128]{1,0:T(8,128)S(1)}, u32[]{:S(2)}, u32[]{:S(2)}) collective-permute-start(f32[256,128]{1,0:T(8,128)S(1)} %get-tuple-element.66.upper), channel_id=1, source_target_pairs={{0,2},{1,3},{2,0},{3,1},{4,6},{5,7},{6,4},{7,5},{8,10},{9,11},{10,... | collective-permute-start | bytes 393224 | tf_op jit(solution)/shard_map/ppermute | solution.py:532
  31.5 7.8 %collective-permute-start.8 = (f32[256,128]{1,0:T(8,128)S(1)}, f32[256,128]{1,0:T(8,128)S(1)}, u32[]{:S(2)}, u32[]{:S(2)}) collective-permute-start(f32[256,128]{1,0:T(8,128)S(1)} %get-tuple-element.67.lower), channel_id=1, source_target_pairs={{0,2},{1,3},{2,0},{3,1},{4,6},{5,7},{6,4},{7,5},{8,10},{9,11},{10,... | collective-permute-start | bytes 393224 | tf_op jit(solution)/shard_map/ppermute | solution.py:532
  33.0 7.6 %collective-permute-start.10 = (f32[256,128]{1,0:T(8,128)S(1)}, f32[256,128]{1,0:T(8,128)S(1)}, u32[]{:S(2)}, u32[]{:S(2)}) collective-permute-start(f32[256,128]{1,0:T(8,128)S(1)} %first_correction.1.refs_5_.refs_8_.refs_4_), channel_id=1, source_target_pairs={{0,4},{8,12},{16,20},{24,28},{4,0},{12,8},{20,16},{28,24},{1,5},{9... | collective-permute-start | bytes 393224 | tf_op jit(solution)/shard_map/ppermute | solution.py:517
  34.6 7.7 %collective-permute-start.11 = (f32[256,128]{1,0:T(8,128)S(1)}, f32[256,128]{1,0:T(8,128)S(1)}, u32[]{:S(2)}, u32[]{:S(2)}) collective-permute-start(f32[256,128]{1,0:T(8,128)S(1)} %first_correction.1.refs_5_.refs_8_.refs_4_), channel_id=1, source_target_pairs={{4,8},{12,16},{20,24},{8,4},{16,12},{24,20},{5,9},{13,17},{21,25},... | collective-permute-start | bytes 393224 | tf_op jit(solution)/shard_map/ppermute | solution.py:518
  39.9 2.4 %collective-permute-start.12 = (f32[256,128]{1,0:T(8,128)S(1)}, f32[256,128]{1,0:T(8,128)S(1)}, u32[]{:S(2)}, u32[]{:S(2)}) collective-permute-start(f32[256,128]{1,0:T(8,128)S(1)} %get-tuple-element.71.refs_0_), channel_id=1, source_target_pairs={{0,1},{1,0},{2,3},{3,2},{4,5},{5,4},{6,7},{7,6},{8,9},{9,8},{10,11... | collective-permute-start | bytes 393224 | tf_op jit(solution)/shard_map/ppermute | solution.py:532
  40.0 2.4 %collective-permute-start.13 = (f32[256,128]{1,0:T(8,128)S(1)}, f32[256,128]{1,0:T(8,128)S(1)}, u32[]{:S(2)}, u32[]{:S(2)}) collective-permute-start(f32[256,128]{1,0:T(8,128)S(1)} %get-tuple-element.72.refs_1_), channel_id=1, source_target_pairs={{0,1},{1,0},{2,3},{3,2},{4,5},{5,4},{6,7},{7,6},{8,9},{9,8},{10,11... | collective-permute-start | bytes 393224 | tf_op jit(solution)/shard_map/ppermute | solution.py:532
  40.5 1.9 %collective-permute-start.14 = (f32[256,128]{1,0:T(8,128)S(1)}, f32[256,128]{1,0:T(8,128)S(1)}, u32[]{:S(2)}, u32[]{:S(2)}) collective-permute-start(f32[256,128]{1,0:T(8,128)S(1)} %get-tuple-element.73.refs_2_), channel_id=1, source_target_pairs={{0,1},{1,0},{2,3},{3,2},{4,5},{5,4},{6,7},{7,6},{8,9},{9,8},{10,11... | collective-permute-start | bytes 393224 | tf_op jit(solution)/shard_map/ppermute | solution.py:532
  40.6 8.7 %collective-permute-start.17 = (f32[512,128]{1,0:T(8,128)S(1)}, f32[512,128]{1,0:T(8,128)S(1)}, u32[]{:S(2)}, u32[]{:S(2)}) collective-permute-start(f32[512,128]{1,0:T(8,128)S(1)} %get-tuple-element.86), channel_id=1, source_target_pairs={{0,2},{1,3},{2,0},{3,1},{4,6},{5,7},{6,4},{7,5},{8,10},{9,11},{10,... | collective-permute-start | bytes 786440 | tf_op jit(solution)/shard_map/ppermute | solution.py:532
  42.8 6.7 %collective-permute-start.15 = (f32[256,128]{1,0:T(8,128)S(1)}, f32[256,128]{1,0:T(8,128)S(1)}, u32[]{:S(2)}, u32[]{:S(2)}) collective-permute-start(f32[256,128]{1,0:T(8,128)S(1)} %sweep.2.refs_7_), channel_id=1, source_target_pairs={{0,4},{8,12},{16,20},{24,28},{4,0},{12,8},{20,16},{28,24},{1,5},{9... | collective-permute-start | bytes 393224 | tf_op jit(solution)/shard_map/ppermute | solution.py:517
  43.8 8.1 %collective-permute-start.16 = (f32[256,128]{1,0:T(8,128)S(1)}, f32[256,128]{1,0:T(8,128)S(1)}, u32[]{:S(2)}, u32[]{:S(2)}) collective-permute-start(f32[256,128]{1,0:T(8,128)S(1)} %sweep.2.refs_7_), channel_id=1, source_target_pairs={{4,8},{12,16},{20,24},{8,4},{16,12},{24,20},{5,9},{13,17},{21,25},... | collective-permute-start | bytes 393224 | tf_op jit(solution)/shard_map/ppermute | solution.py:518
  51.9 3.1 %collective-permute-start.18 = (f32[512,384]{1,0:T(8,128)S(1)}, f32[512,384]{1,0:T(8,128)S(1)}, u32[]{:S(2)}, u32[]{:S(2)}) collective-permute-start(f32[512,384]{1,0:T(8,128)S(1)} %lift_half.1.mine), channel_id=1, source_target_pairs={{0,1},{1,0},{2,3},{3,2},{4,5},{5,4},{6,7},{7,6},{8,9},{9,8},{10,11... | collective-permute-start | bytes 2359304 | tf_op jit(solution)/shard_map/ppermute | solution.py:532
  52.3 6.0 %collective-permute-start.19 = (f32[256,128]{1,0:T(8,128)S(1)}, f32[256,128]{1,0:T(8,128)S(1)}, u32[]{:S(2)}, u32[]{:S(2)}) collective-permute-start(f32[256,128]{1,0:T(8,128)S(1)} %sweep.3.own), channel_id=1, source_target_pairs={{0,4},{8,12},{16,20},{24,28},{4,0},{12,8},{20,16},{28,24},{1,5},{9... | collective-permute-start | bytes 393224 | tf_op jit(solution)/shard_map/ppermute | solution.py:517
  53.1 8.4 %collective-permute-start.20 = (f32[256,128]{1,0:T(8,128)S(1)}, f32[256,128]{1,0:T(8,128)S(1)}, u32[]{:S(2)}, u32[]{:S(2)}) collective-permute-start(f32[256,128]{1,0:T(8,128)S(1)} %sweep.3.own), channel_id=1, source_target_pairs={{4,8},{12,16},{20,24},{8,4},{16,12},{24,20},{5,9},{13,17},{21,25},... | collective-permute-start | bytes 393224 | tf_op jit(solution)/shard_map/ppermute | solution.py:518
